TPU v7x, 32 devices: a whole 2x2x4 slice. The times are simulated.
32 devices in a mesh: grp: 8 (over z, core), blk: 4 (over y, x).
Axes of the slice: x: 2, y: 2, z: 4, core: 2. Of those that a mesh axis runs over, the one named last changes fastest.
Arguments:
- slab: bfloat16 [2048, 32768], P(('grp', 'blk')), as said below
- pick_owner: int32 [2048, 1], P(('grp', 'blk')), may hold values from 0 to 3; in each aligned block of 64 rows (0 to 63, 64 to 127, ...) at most 32 rows name the same one
- pick_offset: int32 [2048], P(('grp', 'blk')), may hold values from 0 to 63
- wedge_id: int32 [2048], P(('grp', 'blk')), may hold values from 0 to 7
- live_count: int32 [32], P(('grp', 'blk')), may hold values from 16 to 64, as said below
- references: bfloat16 [192, 32768], P('blk')
- wedge: float32 [8, 32768], replicated, may hold values from 0.05 to 1
Outputs:
- new_refs: float32 [192, 32768], P('blk', 'grp')
Inputs may be any that keep to these rules, and one draw needn't show every extreme that they name: `pick_owner`: on one device at most 32 slots name the same owner. `live_count`: live slots are the first ones of a device; some device has all 64 live. `slab`: coefficients of the tomogram blocks.
All inputs are finite; a program needn't handle non-finite values.
Results may differ from a plain program's by a relative error of at most 0.0036.
Values may be sent and summed in bfloat16 or wider, within the bound.
No kernel may reach another device: no remote copies, remote signals or barrier semaphores. Data moves between devices by JAX's collectives and lax.ppermute only.
A program may use at most 128 MiB of HBM per device.

v0:
```python
import math

import jax
import jax.numpy as jnp
from jax import lax
from jax.sharding import PartitionSpec as P


def per_device(slab, pick_owner, pick_offset, wedge_id, live_count, references, wedge):
    highest = lax.Precision.HIGHEST
    slot_count, voxels = slab.shape
    group_count = lax.axis_size("grp")
    cycle_size = lax.axis_size("blk")
    capacity = 2 * slot_count // cycle_size
    owners = pick_owner[:, 0]
    owner_hot = (owners[:, None] == jnp.arange(cycle_size, dtype=jnp.int32)[None, :]).astype(
        jnp.int32
    )
    slot_rank = jnp.sum((jnp.cumsum(owner_hot, axis=0) - 1) * owner_hot, axis=1)
    requests = jnp.zeros((cycle_size, capacity), jnp.int32).at[owners, slot_rank].set(pick_offset)
    wanted = lax.all_to_all(requests, "blk", split_axis=0, concat_axis=0, tiled=True)
    amount = wanted.shape[1]
    blocks_out = jnp.take(slab, wanted.reshape(-1), axis=0).reshape(cycle_size, amount, voxels)
    fetched = lax.all_to_all(blocks_out, "blk", split_axis=0, concat_axis=0, tiled=True)
    blocks = fetched[owners, slot_rank]
    masks_hot = (wedge_id[:, None] == jnp.arange(wedge.shape[0], dtype=jnp.int32)[None, :]).astype(
        jnp.float32
    )
    weights = jnp.dot(masks_hot, wedge, precision=highest)
    scaled = (weights * blocks.astype(jnp.float32)).astype(jnp.bfloat16)
    per_ref = references.shape[0]
    inv_noise = 1.0 / (32.0 * math.sqrt(voxels))
    ref_piece = lax.all_gather(references, "blk", axis=0, tiled=True)
    correl = jnp.dot(scaled, ref_piece.T, preferred_element_type=jnp.float32)
    piece_float = ref_piece.astype(jnp.float32)
    piece_norms = jnp.dot(wedge, (piece_float * piece_float).T, precision=highest)
    chosen_norms = jnp.dot(masks_hot, piece_norms, precision=highest)
    folded = correl - 0.5 * chosen_norms
    posterior = jax.nn.softmax(folded * inv_noise, axis=1)
    live_mask = (jnp.arange(slot_count, dtype=jnp.int32) < live_count[0]).astype(jnp.float32)
    weighted = posterior * live_mask[:, None]
    weighted_b = weighted.astype(jnp.bfloat16)
    totals = lax.psum(jnp.dot(weighted.T, masks_hot, precision=highest), ("grp", "blk"))
    per_vox = voxels // group_count
    contract = (((0,), (0,)), ((), ()))
    columns = lax.all_to_all(scaled, "grp", split_axis=1, concat_axis=0, tiled=True)
    all_weights = lax.all_gather(weighted_b, "grp", axis=0, tiled=True)
    summed = lax.psum_scatter(
        lax.dot_general(all_weights, columns, contract, preferred_element_type=jnp.float32),
        "blk",
        scatter_dimension=0,
        tiled=True,
    )
    row_first = lax.axis_index("blk") * per_ref
    vox_first = lax.axis_index("grp") * per_vox
    own_totals = lax.dynamic_slice_in_dim(totals, row_first, per_ref, 0)
    wedge_cols = lax.dynamic_slice_in_dim(wedge, vox_first, per_vox, 1)
    weight_sum = jnp.dot(own_totals, wedge_cols, precision=highest)
    return summed / (weight_sum + 1.0)


def solution(mesh):
    placed = (
        P(("grp", "blk"), None),
        P(("grp", "blk"), None),
        P(("grp", "blk")),
        P(("grp", "blk")),
        P(("grp", "blk")),
        P("blk", None),
        P(),
    )
    return jax.shard_map(
        per_device, mesh=mesh, in_specs=placed, out_specs=P("blk", "grp"), check_vma=False
    )
```

profile of v0, /device:TPU:0, one launch (start us, length us, event | category | flops | bytes accessed | tf_op | source)
XLA Modules:
  0.0 415.8 jit_solution(10837172099122750557)
XLA Ops:
  6.5 0.8 fusion.9
  7.4 0.8 select_reduce_fusion
  8.3 0.7 fusion.18
  9.0 0.6 broadcast_in_dim.12
  9.5 10.1 %scatter_fusion = s32[4,32]{1,0:T(4,128)} fusion(s32[4,32]{1,0:T(4,128)} %broadcast_in_dim.12, s32[64]{0:T(128)S(1)} %get-tuple-element.7, s32[64]{0:T(128)} %param.9), kind=kCustom, calls=%fused_computation.2 | custom fusion | bytes 1280 | tf_op jit(solution)/shard_map/scatter | solution.py:20
  19.7 5.2 %all-to-all-start = ((s32[4,1,32]{2,1,0:T(1,128)}), s32[4,1,32]{2,1,0:T(1,128)S(1)}, u32[]{:S(2)}, u32[]{:S(2)}) async-start(s32[4,1,32]{2,1,0:T(1,128)} %bitcast.4), calls=%async_computation | async-start | bytes 4096 | tf_op jit(solution)/shard_map/all_to_all | solution.py:21
  24.9 0.7 all-gather.2.cloned.1.call-update
  25.6 3.9 all-to-all-done
  30.0 0.7 reduce.3
  30.7 19.2 %gather_fusion = bf16[128,32768]{1,0:T(8,128)(2,1)} fusion(bf16[64,32768]{1,0:T(8,128)(2,1)} %param.7, s32[1024]{0:T(1024)S(1)} %pad_clamp_fusion), kind=kCustom, calls=%fused_computation | custom fusion | bytes 16777728 | tf_op jit(solution)/shard_map/jit(_take)/gather | solution.py:23
  49.9 7.4 %broadcast_select_fusion = bf16[4,32,32768]{2,1,0:T(8,128)(2,1)} fusion(bf16[4,32,32768]{2,1,0:T(8,128)(2,1)} %bitcast.36, pred[4,32]{1,0:T(4,128)(4,1)S(1)} %compare_and_fusion), kind=kLoop, calls=%fused_computation.8 | loop fusion | flops 4194304 | bytes 16777344 | tf_op jit(solution)/shard_map/jit(_take)/select_n | solution.py:23
  57.4 171.9 %all_to_all.33 = bf16[4,32,32768]{2,1,0:T(8,128)(2,1)} all-to-all(bf16[4,32,32768]{2,1,0:T(8,128)(2,1)} %broadcast_select_fusion), channel_id=1, replica_groups=mesh['grp'=8,'blk'=4] {'blk'}, dimensions={0} | all-to-all | bytes 16777216 | tf_op jit(solution)/shard_map/all_to_all | solution.py:24
  229.3 12.5 %gather_fusion.1 = bf16[64,32768]{1,0:T(8,128)(2,1)} fusion(bf16[4,32,32768]{2,1,0:T(8,128)(2,1)} %all_to_all.33, s32[64]{0:T(128)S(1)} %bitcast.38), kind=kCustom, calls=%fused_computation.1 | custom fusion | bytes 8389120 | tf_op jit(solution)/shard_map/gather | solution.py:25
  241.8 5.5 %fusion = bf16[64,32768]{1,0:T(8,128)(2,1)S(1)} fusion(f32[8,32768]{1,0:T(8,128)S(1)} %copy-done, bf16[64,32768]{1,0:T(8,128)(2,1)} %gather_fusion.1, s32[64]{0:T(128)S(1)} %copy-done.3), kind=kOutput, calls=%fused_computation.4 | convolution fusion | flops 207618560 | bytes 9437440 | tf_op jit(solution)/shard_map/dot_general | solution.py:29
  247.4 2.0 copy-done.1
  249.3 2.2 copy.13
  251.5 4.6 %all-to-all-start.2 = ((bf16[64,8,4096]{2,0,1:T(8,128)(2,1)}), bf16[64,8,4096]{2,0,1:T(8,128)(2,1)}, u32[]{:S(2)}, u32[]{:S(2)}) async-start(bf16[64,8,4096]{2,0,1:T(8,128)(2,1)} %bitcast.37), calls=%async_computation.2 | async-start | bytes 8388608 | tf_op jit(solution)/shard_map/all_to_all | solution.py:46
  257.1 22.6 %fusion.1 = f32[192,8]{0,1:T(8,128)S(1)} fusion(f32[8,32768]{1,0:T(8,128)S(1)} %copy-done, bf16[192,32768]{1,0:T(8,128)(2,1)} %all-gather.2.cloned.1.call-done), kind=kOutput, calls=%fused_computation.5 | convolution fusion | flops 616562688 | bytes 13637632 | tf_op jit(solution)/shard_map/dot_general | solution.py:36
  279.7 8.7 %fusion.22 = f32[64,192]{1,0:T(8,128)S(1)} fusion(bf16[64,32768]{1,0:T(8,128)(2,1)S(1)} %copy-done.2, bf16[192,32768]{1,0:T(8,128)(2,1)} %all-gather.2.cloned.1.call-done), kind=kOutput, calls=%fused_computation.44 | convolution fusion | flops 805306368 | bytes 16826368 | tf_op jit(solution)/shard_map/dot_general | solution.py:34
  289.0 68.1 %all_gather.7 = bf16[512,192]{1,0:T(8,128)(2,1)S(1)} all-gather(bf16[64,192]{1,0:T(8,128)(2,1)S(1)} %get-tuple-element.5), channel_id=1, replica_groups=mesh['grp'=8,'blk'=4] {'grp'}, dimensions={0}, use_global_device_ids=true | all-gather | bytes 221184 | tf_op jit(solution)/shard_map/all_gather | solution.py:47
  357.1 4.9 %fusion.23 = f32[192,4096]{1,0:T(8,128)} fusion(bf16[512,192]{1,0:T(8,128)(2,1)S(1)} %all_gather.7, bf16[512,4096]{1,0:T(8,128)(2,1)} %bitcast.11), kind=kOutput, calls=%fused_computation.45 | convolution fusion | flops 805306368 | bytes 7536640 | tf_op jit(solution)/shard_map/dot_general | solution.py:49
  362.3 39.1 %psum.7 = f32[192,8]{0,1:T(8,128)S(1)} all-reduce(f32[192,8]{0,1:T(8,128)S(1)} %fusion.10), channel_id=1, replica_groups=mesh['grp'=8,'blk'=4] {'grp','blk'}, use_global_device_ids=true, to_apply=%region_6.7 | all-reduce | flops 1536 | bytes 12288 | tf_op jit(solution)/shard_map/psum | solution.py:43
  401.4 4.7 %reduce-scatter.2.cloned.1.call-done = f32[48,4096]{1,0:T(8,128)} async-done(((f32[192,4096]{1,0:T(8,128)}), f32[48,4096]{1,0:T(8,128)}) %reduce-scatter.2.cloned.1.call-update) | async-done | bytes 786448 | tf_op jit(solution)/shard_map/reduce_scatter | solution.py:48
  406.1 2.9 fusion.4
  (23 shorter events, 1.9 us)
Async XLA Ops:
  6.5 235.3 %copy-start = (f32[8,32768]{1,0:T(8,128)S(1)}, f32[8,32768]{1,0:T(8,128)}, u32[]{:S(2)}) copy-start(f32[8,32768]{1,0:T(8,128)} %param.13) | copy-start | bytes 3145732
  19.7 9.8 %all-to-all-start = ((s32[4,1,32]{2,1,0:T(1,128)}), s32[4,1,32]{2,1,0:T(1,128)S(1)}, u32[]{:S(2)}, u32[]{:S(2)}) async-start(s32[4,1,32]{2,1,0:T(1,128)} %bitcast.4), calls=%async_computation | async-start | bytes 4096 | tf_op jit(solution)/shard_map/all_to_all | solution.py:21
  24.9 232.2 %all-gather.2.cloned.1.call-start = ((), (), s32[]{:S(2)}) async-start(), calls=%async_computation.4 | async-start | bytes 15728640 | tf_op jit(solution)/shard_map/all_gather | solution.py:33
  229.3 12.5 %copy-start.3 = (s32[64]{0:T(128)S(1)}, s32[64]{0:T(128)}, u32[]{:S(2)}) copy-start(s32[64]{0:T(128)} %param.10) | copy-start | bytes 772
  247.3 2.0 copy-start.1
  251.5 105.6 %all-to-all-start.2 = ((bf16[64,8,4096]{2,0,1:T(8,128)(2,1)}), bf16[64,8,4096]{2,0,1:T(8,128)(2,1)}, u32[]{:S(2)}, u32[]{:S(2)}) async-start(bf16[64,8,4096]{2,0,1:T(8,128)(2,1)} %bitcast.37), calls=%async_computation.2 | async-start | bytes 8388608 | tf_op jit(solution)/shard_map/all_to_all | solution.py:46
  256.1 150.0 %reduce-scatter.2.cloned.1.call-start = ((), (), s32[]{:S(2)}) async-start(), calls=%async_computation.5 | async-start | bytes 3932160 | tf_op jit(solution)/shard_map/reduce_scatter | solution.py:48
  257.1 22.6 %copy-start.2 = (bf16[64,32768]{1,0:T(8,128)(2,1)S(1)}, bf16[64,32768]{1,0:T(8,128)(2,1)}, u32[]{:S(2)}) copy-start(bf16[64,32768]{1,0:T(8,128)(2,1)} %copy-done.1) | copy-start | bytes 12582916
Sparse Core Ops, SparseCore 0:
  27.5 206.4 all-gather.1
  362.1 43.9 reduce-scatter.1
where the time goes:
time: 417 us; the launch traced here: 416 us
  blocking collectives  279 us (67%)
  local copies, waits for them, and re-layouts  47.2 us (11%)
  matrix products  45.2 us (11%)
  between operations  14.2 us (3%)
  other arithmetic  10.8 us (3%)
  starting transfers between devices  10 us (2%)
  waiting for transfers between devices  9.34 us (2%)
    all_to_all x1, blocking collectives, per_device(): lax.all_to_all(blocks_out, 'blk', split_axis=0, concat_axis=0, tiled=True)  172 us
    all_gather x1, blocking collectives, per_device(): all_weights = lax.all_gather(weighted_b, 'grp', axis=0, tiled=True)  68.1 us
    psum x1, blocking collectives, per_device(): lax.psum(jnp.dot(weighted.T, masks_hot, precision=highest), ('grp', 'blk'))  39.1 us
    dot_general x1, matrix products, per_device(): jnp.dot(wedge, (piece_float * piece_float).T, precision=highest)  22.6 us
    gather x1, local copies, waits for them, and re-layouts, per_device(): jnp.take(slab, wanted.reshape(-1), axis=0)  19.2 us
    gather x1, local copies, waits for them, and re-layouts, per_device(): blocks = fetched[owners, slot_rank]  12.5 us
    scatter x1, local copies, waits for them, and re-layouts, per_device(): jnp.zeros((cycle_size, capacity), jnp.int32).at[owners, slot_rank]  10.1 us
    dot_general x1, matrix products, per_device(): correl = jnp.dot(scaled, ref_piece.T, preferred_element_type=jnp.float32)  8.69 us
  transfers between devices with their start and end apart: 4, of which 2 were waited for; matrix products, arithmetic and copies ran while one was open for 19% of the time, Pallas kernels for 0%

commit v1 on v0

v1 whole, which is shorter than its diff:
```python
import functools
import math

import jax
import jax.numpy as jnp
from jax import lax
from jax.experimental import pallas as pl
from jax.experimental.pallas import tpu as pltpu
from jax.sharding import PartitionSpec as P

F32 = jnp.float32
BF16 = jnp.bfloat16
ROWS = (((1,), (0,)), ((), ()))
LANES = (((1,), (1,)), ((), ()))


def dot(left, right, dims=ROWS):
    return lax.dot_general(left, right, dims, preferred_element_type=F32)


def pieces_of(value, count):
    parts = []
    for _ in range(count):
        part = value.astype(BF16)
        value = value - part.astype(F32)
        parts.append(part)
    return parts


def iota(shape, axis):
    return lax.broadcasted_iota(jnp.int32, shape, axis).astype(F32)


def correl_kernel(blocks, seeded, place, slab, mate, wedge, *rest):
    refs, rest = rest[:blocks], rest[blocks:]
    seeds, rest = (rest[:3], rest[3:]) if seeded else ((), rest)
    own, other, norms, scaled, table = rest
    masks, rows, count = own.shape
    per_ref = count // blocks

    @pl.when(pl.program_id(0) == 0)
    def _():
        for i, target in enumerate((own, other, norms)):
            target[...] = seeds[i][...] if seeded else jnp.zeros_like(target)

    for p in range(blocks):
        if per_ref % 16 == 0:
            first = pl.multiple_of(place[1 + p] * per_ref, 16)
        else:
            first = p * per_ref
        table[pl.ds(first, per_ref), :] = refs[p][...]
    weights = wedge[...]
    for side, source in enumerate((slab, mate)):
        values = source[...].astype(F32)
        for w in range(masks):
            first = (side * masks + w) * rows
            scaled[first : first + rows, :] = (weights[w : w + 1, :] * values).astype(BF16)
    every = table[...]
    got = dot(scaled[...], every, LANES)
    for side, target in enumerate((own, other)):
        for w in range(masks):
            first = (side * masks + w) * rows
            target[w] += got[first : first + rows, :]
    wide = every.astype(F32)
    high, low = pieces_of(wide * wide, 2)
    lined = jnp.concatenate(pieces_of(weights, 3), axis=0)
    sums = dot(lined, high, LANES) + dot(lined, low, LANES)
    norms[...] += sums[:masks] + sums[masks : 2 * masks] + sums[2 * masks :]


def correl(place, slab, mate, wedge, refs, begin, tile, seeds):
    blocks = len(refs)
    rows, voxels = slab.shape
    masks = wedge.shape[0]
    per_ref = refs[0].shape[0]
    count = blocks * per_ref
    half = voxels // 2
    span = half // 2
    steps = span // tile
    shift = begin // tile

    def local(t, s):
        return (0, s[0] * (half // tile) + shift + t)

    in_specs = [
        pl.BlockSpec((rows, tile), local),
        pl.BlockSpec((rows, tile), lambda t, s: (0, shift + t)),
        pl.BlockSpec((masks, tile), local),
    ]
    for ref in refs:
        whole = ref.shape[1] == voxels
        in_specs.append(
            pl.BlockSpec((per_ref, tile), local if whole else (lambda t, s: (0, t)))
        )
    fixed3 = pl.BlockSpec((masks, rows, count), lambda t, s: (0, 0, 0))
    fixed2 = pl.BlockSpec((masks, count), lambda t, s: (0, 0))
    outs = [fixed3, fixed3, fixed2]
    if seeds:
        in_specs += outs
    return pl.pallas_call(
        functools.partial(correl_kernel, blocks, bool(seeds)),
        grid_spec=pltpu.PrefetchScalarGridSpec(
            num_scalar_prefetch=1,
            grid=(steps,),
            in_specs=in_specs,
            out_specs=outs,
            scratch_shapes=[
                pltpu.VMEM((2 * masks * rows, tile), BF16),
                pltpu.VMEM((count, tile), BF16),
            ],
        ),
        out_shape=[
            jax.ShapeDtypeStruct((masks, rows, count), F32),
            jax.ShapeDtypeStruct((masks, rows, count), F32),
            jax.ShapeDtypeStruct((masks, count), F32),
        ],
        cost_estimate=pl.CostEstimate(
            flops=2 * 2 * masks * rows * count * span,
            bytes_accessed=2 * span * (2 * rows + count + 2 * masks),
            transcendentals=0,
        ),
        name="correl",
    )(place, slab, mate, wedge, *refs, *seeds)


def weigh_kernel(scale, cap, place, own, got, own_norms, got_norms, meta, out, post):
    masks, rows, count = own.shape
    slots = meta.shape[1]
    info = meta[...].astype(F32)
    named = jnp.logical_and(info[0:1] == place[0].astype(F32), info[3:4] > 0.0)
    chosen = named.astype(F32)
    earlier = (iota((slots, slots), 0) < iota((slots, slots), 1)).astype(BF16)
    eight = jnp.broadcast_to(chosen, (8, slots)).astype(BF16)
    rank = dot(eight, earlier)[0:1]
    hit = jnp.logical_and(iota((cap, slots), 0) == rank, named)
    order = hit.astype(F32).astype(BF16)
    offset, wedge_id = info[1:2], info[2:3]
    listed = jnp.concatenate(
        [offset * chosen, wedge_id * chosen, chosen, jnp.zeros((5, slots), F32)], axis=0
    )
    columns = dot(order, listed.astype(BF16), LANES)
    slot_row, slot_wedge, slot_live = columns[:, 0:1], columns[:, 1:2], columns[:, 2:3]
    at = slot_wedge * rows + slot_row
    pick = jnp.logical_and(iota((cap, masks * rows), 1) == at, slot_live > 0.0)
    row_hot = jnp.logical_and(iota((rows, slots), 0) == offset, named).astype(F32).astype(BF16)
    wedge_hot = (iota((masks, slots), 0) == wedge_id).astype(F32).astype(BF16)
    tally = dot(row_hot, wedge_hot, LANES)
    norms = own_norms[...] + got_norms[...]
    mass = []
    for w in range(masks):
        score = (own[w] + got[w] - 0.5 * norms[w : w + 1]) * scale
        score = jnp.exp(score - jnp.max(score, axis=1, keepdims=True))
        share = score / jnp.sum(score, axis=1, keepdims=True)
        post[w * rows : (w + 1) * rows, :] = share.astype(BF16)
        mass.append(jnp.sum(share * tally[:, w : w + 1], axis=0, keepdims=True))
    out[...] = jnp.zeros_like(out)
    out[:cap, :count] = dot(pick.astype(F32).astype(BF16), post[...]).astype(BF16)
    left = out.shape[1] - count
    lane = iota((cap, left), 1)
    tail = jnp.where(lane == 0.0, slot_row, jnp.where(lane == 1.0, slot_wedge, 0.0))
    out[:cap, count:] = tail.astype(BF16)
    for i, part in enumerate(pieces_of(jnp.concatenate(mass, axis=0), 3)):
        out[cap + i * masks : cap + (i + 1) * masks, :count] = part


def weigh(place, own, got, own_norms, got_norms, meta, scale, cap, height, width):
    masks, rows, count = own.shape
    memory = [pl.BlockSpec(memory_space=pltpu.SMEM)] + [pl.BlockSpec(memory_space=pltpu.VMEM)] * 5
    return pl.pallas_call(
        functools.partial(weigh_kernel, scale, cap),
        in_specs=memory,
        out_specs=pl.BlockSpec(memory_space=pltpu.VMEM),
        out_shape=jax.ShapeDtypeStruct((height, width), BF16),
        scratch_shapes=[pltpu.VMEM((masks * rows, count), BF16)],
        cost_estimate=pl.CostEstimate(
            flops=masks * rows * count * 300, bytes_accessed=1 << 20, transcendentals=0
        ),
        name="weigh",
    )(place, own, got, own_norms, got_norms, meta)


def gather_kernel(cap, count, place, slab, weights, wedge, out, rows_hot, wedge_hot, turned, scaled):
    groups = weights.shape[0]
    rows = slab.shape[0] // groups
    masks = wedge.shape[0]

    @pl.when(pl.program_id(0) == 0)
    def _():
        for g in range(groups):
            tail = weights[g, :cap, count : count + 2].astype(F32)
            rows_hot[g] = (iota((cap, rows), 1) == tail[:, 0:1]).astype(F32).astype(BF16)
            hot = (iota((cap, masks), 1) == tail[:, 1:2]).astype(F32)
            wedge_hot[g] = jnp.concatenate([hot] * 3, axis=1).astype(BF16)
            turned[:, g * cap : (g + 1) * cap] = (
                weights[g, :cap, :count].astype(F32).T.astype(BF16)
            )

    lined = jnp.concatenate(pieces_of(wedge[...], 3), axis=0)
    for g in range(groups):
        values = dot(rows_hot[g], slab[g * rows : (g + 1) * rows, :])
        scaled[g * cap : (g + 1) * cap, :] = (dot(wedge_hot[g], lined) * values).astype(BF16)
    sums = dot(turned[...], scaled[...]).astype(BF16)
    per_ref = out.shape[1]
    for p in range(out.shape[0]):
        out[p] = sums[p * per_ref : (p + 1) * per_ref, :]


def gather(place, slab, weights, wedge, cap, blocks, count, tile):
    groups, height, width = weights.shape
    total, span = slab.shape
    masks = wedge.shape[0]
    per_ref = count // blocks
    steps = span // tile
    return pl.pallas_call(
        functools.partial(gather_kernel, cap, count),
        grid_spec=pltpu.PrefetchScalarGridSpec(
            num_scalar_prefetch=1,
            grid=(steps,),
            in_specs=[
                pl.BlockSpec((total, tile), lambda t, s: (0, t)),
                pl.BlockSpec((groups, height, width), lambda t, s: (0, 0, 0)),
                pl.BlockSpec((masks, tile), lambda t, s: (0, s[0] * steps + t)),
            ],
            out_specs=pl.BlockSpec((blocks, per_ref, tile), lambda t, s: (0, 0, t)),
            scratch_shapes=[
                pltpu.VMEM((groups, cap, total // groups), BF16),
                pltpu.VMEM((groups, cap, 3 * masks), BF16),
                pltpu.VMEM((count, groups * cap), BF16),
                pltpu.VMEM((groups * cap, tile), BF16),
            ],
        ),
        out_shape=jax.ShapeDtypeStruct((blocks, per_ref, span), BF16),
        cost_estimate=pl.CostEstimate(
            flops=6 * groups * cap * count * span,
            bytes_accessed=2 * span * (total + count),
            transcendentals=0,
        ),
        name="gather",
    )(place, slab, weights, wedge)


def spread(value, axis):
    size = lax.axis_size(axis)
    copies = jnp.broadcast_to(value[None], (size, *value.shape))
    return lax.all_to_all(copies, axis, split_axis=0, concat_axis=0, tiled=True)


def per_device(slab, pick_owner, pick_offset, wedge_id, live_count, references, wedge):
    slot_count, voxels = slab.shape
    masks = wedge.shape[0]
    per_ref = references.shape[0]
    groups = lax.axis_size("grp")
    blocks = lax.axis_size("blk")
    count = per_ref * blocks
    per_vox = voxels // groups
    half = voxels // 2
    span = half // 2
    cap = 2 * slot_count
    height = -(-(cap + 3 * masks) // 16) * 16
    width = -(-(count + 2) // 128) * 128
    group = lax.axis_index("grp")
    block = lax.axis_index("blk")
    core = group % 2
    swap = [(g, g ^ 1) for g in range(groups)]

    columns = lax.all_to_all(slab, "grp", split_axis=1, concat_axis=0, tiled=True)

    live = (jnp.arange(slot_count, dtype=jnp.int32) < live_count[0]).astype(jnp.int32)
    mine = jnp.stack([pick_owner[:, 0], pick_offset, wedge_id, live])
    meta = spread(mine, "blk").transpose(1, 0, 2).reshape(4, blocks * slot_count)

    mate = lax.ppermute(lax.dynamic_slice_in_dim(slab, (1 - core) * half, half, 1), "grp", swap)
    stretches = [
        lax.dynamic_slice_in_dim(references, core * half + i * span, span, 1) for i in range(2)
    ]
    if blocks == 4:
        near = [[(b, b ^ 1) for b in range(4)], [(b, b ^ 2) for b in range(4)]]
        sides = [[lax.ppermute(s, "blk", near[i]) for i in range(2)] for s in stretches]
        across = [
            lax.ppermute(sides[0][0], "blk", near[1]),
            lax.ppermute(sides[1][1], "blk", near[0]),
        ]
        tables = [[references, *sides[i], across[i]] for i in range(2)]
        order = [block ^ p for p in range(4)]
    else:
        tables = []
        for s in stretches:
            everyone = spread(s, "blk")
            tables.append([everyone[p] for p in range(blocks)])
        order = [jnp.int32(p) for p in range(blocks)]
    place = jnp.stack([core, *order]).astype(jnp.int32)
    tile = min(1024, span)
    sums = ()
    for i in range(2):
        sums = correl(place, slab, mate, wedge, tables[i], i * span, tile, sums)
    own, other, norms = sums
    got = lax.ppermute(other, "grp", swap)
    got_norms = lax.ppermute(norms, "grp", swap)
    scale = 1.0 / (32.0 * math.sqrt(voxels))
    weights = weigh(
        block.reshape(1).astype(jnp.int32), own, got, norms, got_norms, meta, scale, cap, height, width
    )
    everyone = spread(weights, "grp")

    mass = everyone[:, cap : cap + 3 * masks, :count].astype(F32)
    mass = mass.reshape(groups * 3, masks, blocks, per_ref).sum(0).transpose(1, 0, 2)
    mass = lax.all_to_all(mass, "blk", split_axis=0, concat_axis=0, tiled=True).sum(0)

    shares = gather(
        group.reshape(1).astype(jnp.int32), columns, everyone, wedge, cap, blocks, count, min(512, per_vox)
    )
    shares = lax.all_to_all(shares, "blk", split_axis=0, concat_axis=0, tiled=True)
    summed = shares.astype(F32).sum(0)
    wedge_cols = lax.dynamic_slice_in_dim(wedge, group * per_vox, per_vox, 1)
    weight_sum = jnp.dot(mass.T, wedge_cols, precision=lax.Precision.HIGHEST)
    return summed / (weight_sum + 1.0)


def solution(mesh):
    placed = (
        P(("grp", "blk"), None),
        P(("grp", "blk"), None),
        P(("grp", "blk")),
        P(("grp", "blk")),
        P(("grp", "blk")),
        P("blk", None),
        P(),
    )
    return jax.shard_map(
        per_device, mesh=mesh, in_specs=placed, out_specs=P("blk", "grp"), check_vma=False
    )
```

time: 417 us -> 263 us (0.63)
  blocking collectives: 279 us -> 7.26 us
  waiting for transfers between devices: 9.34 us -> 171 us
  matrix products: 45.2 us -> 2.65 us
  Pallas kernels: 0 us -> 36.6 us
  local copies, waits for them, and re-layouts: 47.2 us -> 16.1 us
  starting transfers between devices: 10 us -> 26.1 us
  between operations: 14.2 us -> 0.79 us
  other arithmetic: 10.8 us -> 1.7 us
    all_to_all x1, blocking collectives: 172 us -> 7.26 us  [spread(): return lax.all_to_all(copies, axis, split_axis=0, concat_axis=0, tiled=True)]
    all_to_all x2 -> x4, waiting for transfers between devices: 3.88 us -> 124 us  [the longest x1 92.9 us: per_device(): lax.all_to_all(slab, 'grp', split_axis=1, concat_axis=0, tiled=True)]
    all_gather x1 -> x0, blocking collectives: 68.1 us -> none  [per_device(): all_weights = lax.all_gather(weighted_b, 'grp', axis=0, tiled=True)]
    ppermute x0 -> x9, waiting for transfers between devices: none -> 47.3 us  [the longest x4 31 us: per_device(): lax.ppermute(s, 'blk', near[i])]
    dot_general x7 -> x1, matrix products: 45.2 us -> 2.65 us  [per_device(): weight_sum = jnp.dot(mass.T, wedge_cols, precision=lax.Precision.HIGHEST)]
    psum x1 -> x0, blocking collectives: 39.1 us -> none  [per_device(): lax.psum(jnp.dot(weighted.T, masks_hot, precision=highest), ('grp', 'blk'))]
    pallas_call x0 -> x4, Pallas kernels: none -> 36.6 us  [the longest x2 23 us: correl(): pl.pallas_call(functools.partial(correl_kernel, blocks, bool(seeds)), gri...]
    gather x2 -> x0, local copies, waits for them, and re-layouts: 31.7 us -> none  [the longest x1 19.2 us: per_device(): jnp.take(slab, wanted.reshape(-1), axis=0)]
  transfers between devices with their start and end apart: 4 -> 13, of which waited for: 2 -> 6; matrix products, arithmetic and copies ran while one was open for 19% -> 4% of each run, Pallas kernels for 0% -> 8%
where the time goes in v1:
time: 263 us; the launch traced here: 262 us
  waiting for transfers between devices  171 us (65%)
  Pallas kernels  36.6 us (14%)
  starting transfers between devices  26.1 us (10%)
  local copies, waits for them, and re-layouts  16.1 us (6%)
  blocking collectives  7.26 us (3%)
  matrix products  2.65 us (1%)
    all_to_all x1, waiting for transfers between devices, per_device(): lax.all_to_all(slab, 'grp', split_axis=1, concat_axis=0, tiled=True)  92.9 us
    ppermute x4, waiting for transfers between devices, per_device(): lax.ppermute(s, 'blk', near[i])  31 us
    pallas_call x2, Pallas kernels, correl(): pl.pallas_call(functools.partial(correl_kernel, blocks, bool(seeds)), gri...  23 us
    all_to_all x1, waiting for transfers between devices, per_device(): lax.all_to_all(shares, 'blk', split_axis=0, concat_axis=0, tiled=True)  17.4 us
    ppermute x1, waiting for transfers between devices, per_device(): lax.ppermute(sides[0][0], 'blk', near[1])  16.2 us
    all_to_all x1, waiting for transfers between devices, spread(): return lax.all_to_all(copies, axis, split_axis=0, concat_axis=0, tiled=True)  13.5 us
    pallas_call x1, Pallas kernels, gather(): pl.pallas_call(functools.partial(gather_kernel, cap, count), grid_spec=pl...  10.9 us
    all_to_all x1, blocking collectives, spread(): return lax.all_to_all(copies, axis, split_axis=0, concat_axis=0, tiled=True)  7.26 us
  transfers between devices with their start and end apart: 13, of which 6 were waited for; matrix products, arithmetic and copies ran while one was open for 4% of the time, Pallas kernels for 8%

profile of v1, /device:TPU:0, one launch (start us, length us, event | category | flops | bytes accessed | tf_op | source)
XLA Modules:
  0.0 262.3 jit_solution(1212134504383830003)
XLA Ops:
  0.0 3.2 %constant_dynamic-slice_fusion.2 = bf16[64,16384]{1,0:T(8,128)(2,1)} fusion(bf16[64,32768]{1,0:T(8,128)(2,1)} %slab.3, s32[]{:T(128)S(6)} %select_n.20), kind=kLoop, calls=%fused_computation.11 | loop fusion | bytes 4194308 | tf_op jit(solution)/shard_map/dynamic_slice | solution.py:272
  3.7 1.3 constant_dynamic-slice_fusion
  5.0 2.5 collective-permute-start.4
  7.4 1.5 collective-permute-start.2
  9.5 16.4 %collective-permute-done.4.rest_1_ = bf16[48,8192]{1,0:T(8,128)(2,1)S(1)} collective-permute-done((bf16[48,8192]{1,0:T(8,128)(2,1)}, bf16[48,8192]{1,0:T(8,128)(2,1)S(1)}, u32[]{:S(2)}, u32[]{:S(2)}) %collective-permute-start.4) | collective-permute-done | bytes 786464 | tf_op jit(solution)/shard_map/ppermute | solution.py:278
  25.9 1.8 collective-permute-start.6
  27.6 1.5 collective-permute-start.1
  30.3 14.6 %collective-permute-done.5.rest_2_ = bf16[48,8192]{1,0:T(8,128)(2,1)S(1)} collective-permute-done((bf16[48,8192]{1,0:T(8,128)(2,1)}, bf16[48,8192]{1,0:T(8,128)(2,1)S(1)}, u32[]{:S(2)}, u32[]{:S(2)}) %collective-permute-start.5) | collective-permute-done | bytes 786464 | tf_op jit(solution)/shard_map/ppermute | solution.py:278
  44.9 16.2 %collective-permute-done.6.rest_3_ = bf16[48,8192]{1,0:T(8,128)(2,1)} collective-permute-done((bf16[48,8192]{1,0:T(8,128)(2,1)S(1)}, bf16[48,8192]{1,0:T(8,128)(2,1)}, u32[]{:S(2)}, u32[]{:S(2)}) %collective-permute-start.6) | collective-permute-done | bytes 786464 | tf_op jit(solution)/shard_map/ppermute | solution.py:280
  61.2 11.2 %correl.2 = (f32[8,64,192]{2,1,0:T(8,128)}, f32[8,64,192]{2,1,0:T(8,128)}, f32[8,192]{1,0:T(8,128)}) custom-call(s32[5]{0:T(128)} %stack.30.place, bf16[64,32768]{1,0:T(8,128)(2,1)} %slab.3, bf16[64,16384]{1,0:T(8,128)(2,1)} %collective-permute-done.mate, f32[8,32768]{1,0:T(8,128)} %wedge.5, bf16[48,32768]{1,0:T(8,128)(2,1)} %rest_0_.3, ...), custom_call_target="tpu_custom_call" | custom-call | flops 3221225472 | bytes 5505024 | tf_op jit(solution)/shard_map/correl/pallas_call | solution.py:100
  73.2 11.8 %correl.3 = (f32[8,64,192]{2,1,0:T(8,128)}, f32[8,64,192]{2,1,0:T(8,128)}, f32[8,192]{1,0:T(8,128)}) custom-call(s32[5]{0:T(128)} %stack.30.place, bf16[64,32768]{1,0:T(8,128)(2,1)} %slab.3, bf16[64,16384]{1,0:T(8,128)(2,1)} %collective-permute-done.mate, f32[8,32768]{1,0:T(8,128)} %wedge.5, bf16[48,32768]{1,0:T(8,128)(2,1)} %rest_0_.3, ...), custom_call_target="tpu_custom_call" | custom-call | flops 3221225472 | bytes 5505024 | tf_op jit(solution)/shard_map/correl/pallas_call | solution.py:100
  86.4 7.3 %all_to_all.39 = s32[4,1,256]{2,1,0:T(1,128)S(1)} all-to-all(s32[4,1,256]{2,1,0:T(1,128)S(1)} %reshape.38), channel_id=1, replica_groups=mesh['grp'=8,'blk'=4] {'blk'}, dimensions={0} | all-to-all | bytes 8192 | tf_op jit(solution)/shard_map/all_to_all | solution.py:245
  96.4 2.7 %weigh.1 = bf16[160,256]{1,0:T(8,128)(2,1)} custom-call(s32[1]{0:T(128)} %bitcast.3.place, f32[8,64,192]{2,1,0:T(8,128)} %get-tuple-element.14.own, f32[8,64,192]{2,1,0:T(8,128)} %copy-done.6, f32[8,192]{1,0:T(8,128)} %get-tuple-element.16.own_norms, f32[8,192]{1,0:T(8,128)} %copy-done.7, s32[4,256]{1,0:T(4,128)} %reshape.32.meta), custom_call_target="tpu_custom_call" | custom-call | flops 29491200 | bytes 1048576 | tf_op jit(solution)/shard_map/weigh/pallas_call | solution.py:169
  99.1 1.8 broadcast_in_dim.5
  100.9 4.9 %all-to-all-start.2 = ((bf16[8,160,256]{2,1,0:T(8,128)(2,1)}), bf16[8,160,256]{2,1,0:T(8,128)(2,1)S(1)}, u32[]{:S(2)}, u32[]{:S(2)}) async-start(bf16[8,160,256]{2,1,0:T(8,128)(2,1)} %broadcast_in_dim.5), calls=%async_computation.2 | async-start | bytes 1310720 | tf_op jit(solution)/shard_map/all_to_all | solution.py:245
  105.8 4.7 %copy.16 = bf16[8,8,8,4096]{3,2,0,1:T(8,128)(2,1)} copy(bf16[8,8,8,4096]{3,2,1,0:T(8,128)(2,1)} %bitcast.21) | data formatting | bytes 8388608 | tf_op jit(solution)/shard_map/all_to_all | solution.py:266
  110.4 13.5 %all-to-all-done.2.weights = bf16[8,160,256]{2,1,0:T(8,128)(2,1)S(1)} async-done(((bf16[8,160,256]{2,1,0:T(8,128)(2,1)}), bf16[8,160,256]{2,1,0:T(8,128)(2,1)S(1)}, u32[]{:S(2)}, u32[]{:S(2)}) %all-to-all-start.2) | async-done | bytes 655392 | tf_op jit(solution)/shard_map/all_to_all | solution.py:245
  123.9 4.5 %all-to-all-start = ((bf16[64,8,4096]{2,0,1:T(8,128)(2,1)}), bf16[64,8,4096]{2,0,1:T(8,128)(2,1)}, u32[]{:S(2)}, u32[]{:S(2)}) async-start(bf16[64,8,4096]{2,0,1:T(8,128)(2,1)} %bitcast.22), calls=%async_computation | async-start | bytes 8388608 | tf_op jit(solution)/shard_map/all_to_all | solution.py:266
  129.5 92.9 %all-to-all-done = bf16[64,8,4096]{2,0,1:T(8,128)(2,1)} async-done(((bf16[64,8,4096]{2,0,1:T(8,128)(2,1)}), bf16[64,8,4096]{2,0,1:T(8,128)(2,1)}, u32[]{:S(2)}, u32[]{:S(2)}) %all-to-all-start) | async-done | bytes 4194336 | tf_op jit(solution)/shard_map/all_to_all | solution.py:266
  222.4 3.2 %all-to-all-start.4 = ((f32[4,1,384]{2,1,0:T(1,128)}), f32[4,1,384]{2,1,0:T(1,128)S(1)}, u32[]{:S(2)}, u32[]{:S(2)}) async-start(f32[4,1,384]{2,1,0:T(1,128)} %reshape.40), calls=%async_computation.4 | async-start | bytes 12288 | tf_op jit(solution)/shard_map/all_to_all | solution.py:307
  225.6 10.9 %gather.1 = bf16[4,48,4096]{2,1,0:T(8,128)(2,1)} custom-call(s32[1]{0:T(128)} %bitcast.place, bf16[512,4096]{1,0:T(8,128)(2,1)} %bitcast.2.slab, bf16[8,160,256]{2,1,0:T(8,128)(2,1)} %copy-done.1, f32[8,32768]{1,0:T(8,128)} %wedge.5), custom_call_target="tpu_custom_call" | custom-call | flops 4831838208 | bytes 5767168 | tf_op jit(solution)/shard_map/gather/pallas_call | solution.py:214
  236.6 4.1 %all-to-all-start.3 = ((bf16[4,48,4096]{2,1,0:T(8,128)(2,1)}), bf16[4,48,4096]{2,1,0:T(8,128)(2,1)S(1)}, u32[]{:S(2)}, u32[]{:S(2)}) async-start(bf16[4,48,4096]{2,1,0:T(8,128)(2,1)} %gather.1), calls=%async_computation.3 | async-start | bytes 3145728 | tf_op jit(solution)/shard_map/all_to_all | solution.py:312
  242.0 17.4 %all-to-all-done.3 = bf16[4,48,4096]{2,1,0:T(8,128)(2,1)S(1)} async-done(((bf16[4,48,4096]{2,1,0:T(8,128)(2,1)}), bf16[4,48,4096]{2,1,0:T(8,128)(2,1)S(1)}, u32[]{:S(2)}, u32[]{:S(2)}) %all-to-all-start.3) | async-done | bytes 1572896 | tf_op jit(solution)/shard_map/all_to_all | solution.py:312
  259.6 2.6 %fusion = f32[48,4096]{1,0:T(8,128)} fusion(f32[48,4096]{1,0:T(8,128)S(1)} %convert_reduce_fusion, f32[8,48]{1,0:T(8,128)S(1)} %reduce_sum.29, f32[8,32768]{1,0:T(8,128)} %wedge.5, s32[]{:T(128)S(6)} %select_n.23), kind=kOutput, calls=%fused_computation.1 | convolution fusion | flops 19267584 | bytes 1705476 | tf_op jit(solution)/shard_map/dot_general | solution.py:315
  (54 shorter events, 9.0 us)
Async XLA Ops:
  0.0 3.7 %copy-start = (bf16[48,32768]{1,0:T(8,128)(2,1)S(1)}, bf16[48,32768]{1,0:T(8,128)(2,1)}, u32[]{:S(2)}) copy-start(bf16[48,32768]{1,0:T(8,128)(2,1)} %rest_0_.3) | copy-start | bytes 9437188
  3.2 57.9 %collective-permute-start = (bf16[64,16384]{1,0:T(8,128)(2,1)}, bf16[64,16384]{1,0:T(8,128)(2,1)}, u32[]{:S(2)}, u32[]{:S(2)}) collective-permute-start(bf16[64,16384]{1,0:T(8,128)(2,1)} %constant_dynamic-slice_fusion.2), channel_id=1, source_target_pairs={{0,4},{4,0},{8,12},{12,8},{16,20},{20,16},{24,28},{28,24},{1,5},{5... | collective-permute-start | bytes 6291464 | tf_op jit(solution)/shard_map/ppermute | solution.py:272
  5.0 20.9 %collective-permute-start.4 = (bf16[48,8192]{1,0:T(8,128)(2,1)}, bf16[48,8192]{1,0:T(8,128)(2,1)S(1)}, u32[]{:S(2)}, u32[]{:S(2)}) collective-permute-start(bf16[48,8192]{1,0:T(8,128)(2,1)} %get-tuple-element.17), channel_id=1, source_target_pairs={{0,1},{1,0},{2,3},{3,2},{4,5},{5,4},{6,7},{7,6},{8,9},{9,8},{10,11... | collective-permute-start | bytes 2359304 | tf_op jit(solution)/shard_map/ppermute | solution.py:278
  7.4 21.7 %collective-permute-start.2 = (bf16[48,8192]{1,0:T(8,128)(2,1)}, bf16[48,8192]{1,0:T(8,128)(2,1)S(1)}, u32[]{:S(2)}, u32[]{:S(2)}) collective-permute-start(bf16[48,8192]{1,0:T(8,128)(2,1)} %get-tuple-element.18), channel_id=1, source_target_pairs={{0,2},{1,3},{2,0},{3,1},{4,6},{5,7},{6,4},{7,5},{8,10},{9,11},{10,... | collective-permute-start | bytes 2359304 | tf_op jit(solution)/shard_map/ppermute | solution.py:278
  9.0 36.0 %collective-permute-start.5 = (bf16[48,8192]{1,0:T(8,128)(2,1)}, bf16[48,8192]{1,0:T(8,128)(2,1)S(1)}, u32[]{:S(2)}, u32[]{:S(2)}) collective-permute-start(bf16[48,8192]{1,0:T(8,128)(2,1)} %get-tuple-element.17), channel_id=1, source_target_pairs={{0,2},{1,3},{2,0},{3,1},{4,6},{5,7},{6,4},{7,5},{8,10},{9,11},{10,... | collective-permute-start | bytes 2359304 | tf_op jit(solution)/shard_map/ppermute | solution.py:278
  25.9 35.3 %copy-start.3 = (bf16[48,8192]{1,0:T(8,128)(2,1)}, bf16[48,8192]{1,0:T(8,128)(2,1)S(1)}, u32[]{:S(2)}) copy-start(bf16[48,8192]{1,0:T(8,128)(2,1)S(1)} %collective-permute-done.4.rest_1_) | copy-start | bytes 2359300
  25.9 35.3 %collective-permute-start.6 = (bf16[48,8192]{1,0:T(8,128)(2,1)S(1)}, bf16[48,8192]{1,0:T(8,128)(2,1)}, u32[]{:S(2)}, u32[]{:S(2)}) collective-permute-start(bf16[48,8192]{1,0:T(8,128)(2,1)S(1)} %collective-permute-done.4.rest_1_), channel_id=1, source_target_pairs={{0,2},{1,3},{2,0},{3,1},{4,6},{5,7},{6,4},{7,5},{8,10},{9,11},{10,... | collective-permute-start | bytes 2359304 | tf_op jit(solution)/shard_map/ppermute | solution.py:280
  27.6 44.7 %collective-permute-start.1 = (bf16[48,8192]{1,0:T(8,128)(2,1)}, bf16[48,8192]{1,0:T(8,128)(2,1)S(1)}, u32[]{:S(2)}, u32[]{:S(2)}) collective-permute-start(bf16[48,8192]{1,0:T(8,128)(2,1)} %get-tuple-element.18), channel_id=1, source_target_pairs={{0,1},{1,0},{2,3},{3,2},{4,5},{5,4},{6,7},{7,6},{8,9},{9,8},{10,11... | collective-permute-start | bytes 2359304 | tf_op jit(solution)/shard_map/ppermute | solution.py:278
  29.1 43.2 %copy-start.2 = (bf16[48,8192]{1,0:T(8,128)(2,1)}, bf16[48,8192]{1,0:T(8,128)(2,1)S(1)}, u32[]{:S(2)}) copy-start(bf16[48,8192]{1,0:T(8,128)(2,1)S(1)} %collective-permute-done.2.rest_2_) | copy-start | bytes 2359300
  29.1 43.2 %collective-permute-start.3 = (bf16[48,8192]{1,0:T(8,128)(2,1)S(1)}, bf16[48,8192]{1,0:T(8,128)(2,1)}, u32[]{:S(2)}, u32[]{:S(2)}) collective-permute-start(bf16[48,8192]{1,0:T(8,128)(2,1)S(1)} %collective-permute-done.2.rest_2_), channel_id=1, source_target_pairs={{0,1},{1,0},{2,3},{3,2},{4,5},{5,4},{6,7},{7,6},{8,9},{9,8},{10,11... | collective-permute-start | bytes 2359304 | tf_op jit(solution)/shard_map/ppermute | solution.py:281
  44.9 16.2 %copy-start.5 = (bf16[48,8192]{1,0:T(8,128)(2,1)}, bf16[48,8192]{1,0:T(8,128)(2,1)S(1)}, u32[]{:S(2)}) copy-start(bf16[48,8192]{1,0:T(8,128)(2,1)S(1)} %collective-permute-done.5.rest_2_) | copy-start | bytes 2359300
  72.4 0.9 copy-start.4
  73.2 13.1 %copy-start.8 = (s32[64]{0:T(128)S(1)}, s32[64]{0:T(128)}, u32[]{:S(2)}) copy-start(s32[64]{0:T(128)} %param.10) | copy-start | bytes 772
  73.2 13.1 %copy-start.9 = (s32[64]{0:T(128)S(1)}, s32[64]{0:T(128)}, u32[]{:S(2)}) copy-start(s32[64]{0:T(128)} %param.9) | copy-start | bytes 772
  73.2 13.1 %copy-start.10 = (s32[64,1]{0,1:T(1,128)S(1)}, s32[64,1]{0,1:T(1,128)}, u32[]{:S(2)}) copy-start(s32[64,1]{0,1:T(1,128)} %param.8) | copy-start | bytes 772
  85.0 10.6 %collective-permute-start.7 = (f32[8,64,192]{2,1,0:T(8,128)}, f32[8,64,192]{2,1,0:T(8,128)S(1)}, u32[]{:S(2)}, u32[]{:S(2)}) collective-permute-start(f32[8,64,192]{2,1,0:T(8,128)} %get-tuple-element.15), channel_id=1, source_target_pairs={{0,4},{4,0},{8,12},{12,8},{16,20},{20,16},{24,28},{28,24},{1,5},{5... | collective-permute-start | bytes 1179656 | tf_op jit(solution)/shard_map/ppermute | solution.py:297
  85.7 9.9 %collective-permute-start.8 = (f32[8,192]{1,0:T(8,128)}, f32[8,192]{1,0:T(8,128)S(1)}, u32[]{:S(2)}, u32[]{:S(2)}) collective-permute-start(f32[8,192]{1,0:T(8,128)} %get-tuple-element.16.own_norms), channel_id=1, source_target_pairs={{0,4},{4,0},{8,12},{12,8},{16,20},{20,16},{24,28},{28,24},{1,5},{5... | collective-permute-start | bytes 18440 | tf_op jit(solution)/shard_map/ppermute | solution.py:298
  95.6 0.6 copy-start.7
  95.6 0.8 copy-start.6
  100.9 23.0 %all-to-all-start.2 = ((bf16[8,160,256]{2,1,0:T(8,128)(2,1)}), bf16[8,160,256]{2,1,0:T(8,128)(2,1)S(1)}, u32[]{:S(2)}, u32[]{:S(2)}) async-start(bf16[8,160,256]{2,1,0:T(8,128)(2,1)} %broadcast_in_dim.5), calls=%async_computation.2 | async-start | bytes 1310720 | tf_op jit(solution)/shard_map/all_to_all | solution.py:245
  123.9 4.6 %copy-start.1 = (bf16[8,160,256]{2,1,0:T(8,128)(2,1)}, bf16[8,160,256]{2,1,0:T(8,128)(2,1)S(1)}, u32[]{:S(2)}) copy-start(bf16[8,160,256]{2,1,0:T(8,128)(2,1)S(1)} %all-to-all-done.2.weights) | copy-start | bytes 1966084
  123.9 98.5 %all-to-all-start = ((bf16[64,8,4096]{2,0,1:T(8,128)(2,1)}), bf16[64,8,4096]{2,0,1:T(8,128)(2,1)}, u32[]{:S(2)}, u32[]{:S(2)}) async-start(bf16[64,8,4096]{2,0,1:T(8,128)(2,1)} %bitcast.22), calls=%async_computation | async-start | bytes 8388608 | tf_op jit(solution)/shard_map/all_to_all | solution.py:266
  222.4 14.1 %all-to-all-start.4 = ((f32[4,1,384]{2,1,0:T(1,128)}), f32[4,1,384]{2,1,0:T(1,128)S(1)}, u32[]{:S(2)}, u32[]{:S(2)}) async-start(f32[4,1,384]{2,1,0:T(1,128)} %reshape.40), calls=%async_computation.4 | async-start | bytes 12288 | tf_op jit(solution)/shard_map/all_to_all | solution.py:307
  236.6 22.8 %all-to-all-start.3 = ((bf16[4,48,4096]{2,1,0:T(8,128)(2,1)}), bf16[4,48,4096]{2,1,0:T(8,128)(2,1)S(1)}, u32[]{:S(2)}, u32[]{:S(2)}) async-start(bf16[4,48,4096]{2,1,0:T(8,128)(2,1)} %gather.1), calls=%async_computation.3 | async-start | bytes 3145728 | tf_op jit(solution)/shard_map/all_to_all | solution.py:312

commit v2 on v0

v2 whole, which is shorter than its diff:
```python
import functools
import math

import jax
import jax.numpy as jnp
from jax import lax
from jax.experimental import pallas as pl
from jax.experimental.pallas import tpu as pltpu
from jax.sharding import Mesh
from jax.sharding import PartitionSpec as P

F32 = jnp.float32
BF16 = jnp.bfloat16
ROWS = (((1,), (0,)), ((), ()))
LANES = (((1,), (1,)), ((), ()))
VMEM = pl.BlockSpec(memory_space=pltpu.VMEM)
SMEM = pl.BlockSpec(memory_space=pltpu.SMEM)
SPLIT = 4


def dot(left, right, dims=ROWS):
    return lax.dot_general(left, right, dims, preferred_element_type=F32)


def pieces_of(value, count):
    parts = []
    for _ in range(count):
        part = value.astype(BF16)
        value = value - part.astype(F32)
        parts.append(part)
    return parts


def iota(shape, axis):
    return lax.broadcasted_iota(jnp.int32, shape, axis).astype(F32)


def hot(mask):
    return mask.astype(F32).astype(BF16)


def cost(flops, moved):
    return pl.CostEstimate(flops=int(flops), bytes_accessed=int(moved), transcendentals=0)


def cut_kernel(place, source, out):
    out[...] = source[...]


def cut(place, source, begin, count, per_vox):
    rows = source.shape[0]
    return pl.pallas_call(
        cut_kernel,
        grid_spec=pltpu.PrefetchScalarGridSpec(
            num_scalar_prefetch=1,
            grid=(count,),
            in_specs=[pl.BlockSpec((rows, per_vox), lambda t, s: (0, 2 * (begin + t) + s[0]))],
            out_specs=pl.BlockSpec((rows, per_vox), lambda t, s: (0, t)),
        ),
        out_shape=jax.ShapeDtypeStruct((rows, count * per_vox), source.dtype),
        cost_estimate=cost(0, 4 * rows * count * per_vox),
        name="cut",
    )(place, source)


def deal_kernel(place, source, *outs):
    for p, out in enumerate(outs):

        @pl.when(pl.program_id(0) == p)
        def _(out=out):
            out[...] = source[:, : out.shape[1]]


def deal(place, slab, groups, keep):
    rows, voxels = slab.shape
    return pl.pallas_call(
        deal_kernel,
        grid_spec=pltpu.PrefetchScalarGridSpec(
            num_scalar_prefetch=1,
            grid=(groups,),
            in_specs=[pl.BlockSpec((rows, voxels // groups), lambda t, s: (0, s[1] ^ t))],
            out_specs=[pl.BlockSpec((rows, keep), lambda t, s: (0, 0))] * groups,
        ),
        out_shape=[jax.ShapeDtypeStruct((rows, keep), slab.dtype)] * groups,
        cost_estimate=cost(0, 4 * rows * groups * keep),
        name="deal",
    )(place, slab)


def lists_kernel(place, meta, out):
    cap = out.shape[1]
    slots = meta.shape[1]
    info = meta[...].astype(F32)
    named = jnp.logical_and(info[0:1] == place[0].astype(F32), info[3:4] > 0.0)
    chosen = named.astype(F32)
    earlier = hot(iota((slots, slots), 0) < iota((slots, slots), 1))
    rank = dot(jnp.broadcast_to(chosen, (8, slots)).astype(BF16), earlier)[0:1]
    order = hot(jnp.logical_and(iota((cap, slots), 0) == rank, named))
    listed = jnp.concatenate(
        [info[1:2] * chosen, info[2:3] * chosen, chosen, jnp.zeros((5, slots), F32)], axis=0
    )
    out[...] = dot(listed.astype(BF16), order, LANES)


def lists_of(place, meta, cap):
    return pl.pallas_call(
        lists_kernel,
        in_specs=[SMEM, VMEM],
        out_specs=VMEM,
        out_shape=jax.ShapeDtypeStruct((8, cap), F32),
        cost_estimate=cost(1 << 22, 1 << 18),
        name="lists",
    )(place, meta)


def columns_of(listed):
    cap = listed.shape[1]
    eye = hot(iota((cap, cap), 0) == iota((cap, cap), 1))
    return dot(eye, listed.astype(BF16), LANES)


def select_kernel(sources, place, *rest):
    blocks, (listed, wedge, out, rows_hot, wedge_hot) = rest[:sources], rest[sources:]
    lists, cap, rows = rows_hot.shape
    masks = wedge.shape[0]

    @pl.when(pl.program_id(0) == 0)
    def _():
        for g in range(lists):
            columns = columns_of(listed[g])
            rows_hot[g] = hot(iota((cap, rows), 1) == columns[:, 0:1])
            marks = (iota((cap, masks), 1) == columns[:, 1:2]).astype(F32)
            wedge_hot[g] = jnp.concatenate([marks] * 3, axis=1).astype(BF16)

    lined = jnp.concatenate(pieces_of(wedge[...], 3), axis=0)
    for g in range(lists):
        values = dot(rows_hot[g], blocks[g][...])
        out[g * cap : (g + 1) * cap, :] = (dot(wedge_hot[g], lined) * values).astype(BF16)


def select(place, blocks, block_specs, listed, wedge, wedge_spec, rows, tile, steps):
    lists, _, cap = listed.shape
    masks = wedge.shape[0]
    return pl.pallas_call(
        functools.partial(select_kernel, len(blocks)),
        grid_spec=pltpu.PrefetchScalarGridSpec(
            num_scalar_prefetch=1,
            grid=(steps,),
            in_specs=[
                *block_specs,
                pl.BlockSpec((lists, 8, cap), lambda t, s: (0, 0, 0)),
                wedge_spec,
            ],
            out_specs=pl.BlockSpec((lists * cap, tile), lambda t, s: (0, t)),
            scratch_shapes=[
                pltpu.VMEM((lists, cap, rows), BF16),
                pltpu.VMEM((lists, cap, 3 * masks), BF16),
            ],
        ),
        out_shape=jax.ShapeDtypeStruct((lists * cap, steps * tile), BF16),
        cost_estimate=cost(
            4 * lists * cap * 256 * steps * tile, 2 * lists * (cap + rows) * steps * tile
        ),
        name="select",
    )(place, *blocks, listed, wedge)


def correl_kernel(blocks, seeded, place, scaled, wedge, *rest):
    refs, rest = rest[:blocks], rest[blocks:]
    seeds, rest = (rest[:3], rest[3:]) if seeded else ((), rest)
    own, other, norms, table = rest
    cap, count = own.shape
    masks = wedge.shape[0]
    per_ref = count // blocks

    @pl.when(pl.program_id(0) == 0)
    def _():
        for i, target in enumerate((own, other, norms)):
            target[...] = seeds[i][...] if seeded else jnp.zeros_like(target)

    for p in range(blocks):
        table[p * per_ref : (p + 1) * per_ref, :] = refs[p][...]
    every = table[...]
    got = dot(scaled[...], every, LANES)
    own[...] += got[:cap]
    other[...] += got[cap:]
    wide = every.astype(F32)
    high, low = pieces_of(wide * wide, 2)
    lined = jnp.concatenate(pieces_of(wedge[...], 3), axis=0)
    sums = dot(lined, high, LANES) + dot(lined, low, LANES)
    norms[...] += sums[:masks] + sums[masks : 2 * masks] + sums[2 * masks :]


def correl(place, scaled, wedge, wedge_spec, refs, shift, tile, steps, seeds):
    blocks = len(refs)
    cap = scaled.shape[0] // 2
    masks = wedge.shape[0]
    per_ref = refs[0].shape[0]
    count = blocks * per_ref
    in_specs = [pl.BlockSpec((2 * cap, tile), lambda t, s: (0, shift + t)), wedge_spec]
    in_specs += [pl.BlockSpec((per_ref, tile), lambda t, s: (0, t))] * blocks
    shapes = [(cap, count), (cap, count), (masks, count)]
    outs = [pl.BlockSpec(shape, lambda t, s: (0, 0)) for shape in shapes]
    if seeds:
        in_specs += outs
    return pl.pallas_call(
        functools.partial(correl_kernel, blocks, bool(seeds)),
        grid_spec=pltpu.PrefetchScalarGridSpec(
            num_scalar_prefetch=1,
            grid=(steps,),
            in_specs=in_specs,
            out_specs=outs,
            scratch_shapes=[pltpu.VMEM((count, tile), BF16)],
        ),
        out_shape=[jax.ShapeDtypeStruct(shape, F32) for shape in shapes],
        cost_estimate=cost(
            8 * cap * count * steps * tile, 2 * steps * tile * (2 * cap + count + 2 * masks)
        ),
        name="correl",
    )(place, scaled, wedge, *refs, *seeds)


def weigh_kernel(scale, masks, own, got, own_norms, got_norms, listed, out):
    cap = own.shape[0]
    columns = columns_of(listed[...])
    marks = (iota((cap, masks), 1) == columns[:, 1:2]).astype(F32)
    wedge_hot = jnp.concatenate([marks] * 3, axis=1).astype(BF16)
    norms = jnp.concatenate(pieces_of(own_norms[...] + got_norms[...], 3), axis=0)
    score = (own[...] + got[...] - 0.5 * dot(wedge_hot, norms)) * scale
    score = jnp.exp(score - jnp.max(score, axis=1, keepdims=True))
    share = score / jnp.sum(score, axis=1, keepdims=True) * columns[:, 2:3]
    out[...] = share.T.astype(BF16)


def weigh(own, got, own_norms, got_norms, listed, scale):
    cap, count = own.shape
    return pl.pallas_call(
        functools.partial(weigh_kernel, scale, own_norms.shape[0]),
        in_specs=[VMEM] * 5,
        out_specs=VMEM,
        out_shape=jax.ShapeDtypeStruct((count, cap), BF16),
        cost_estimate=cost(1 << 24, 1 << 18),
        name="weigh",
    )(own, got, own_norms, got_norms, listed)


def blend_kernel(lists, blocks, masks, place, *rest):
    weights, rest = rest[:lists], rest[lists:]
    listed, scaled, rest = rest[0], rest[1], rest[2:]
    outs, masses, turned = rest[:blocks], rest[blocks:-1], rest[-1]
    cap = weights[0].shape[1]
    per_ref = outs[0].shape[-2]

    @pl.when(pl.program_id(0) == 0)
    def _():
        for g in range(lists):
            turned[:, g * cap : (g + 1) * cap] = weights[g][...]
        for p, mass in enumerate(masses):
            total = jnp.zeros(mass.shape, F32)
            for g in range(lists):
                marks = hot(iota((masks, cap), 0) == listed[g, 1:2, :])
                total = total + dot(weights[g][p * per_ref : (p + 1) * per_ref, :], marks, LANES)
            mass[...] = total

    sums = dot(turned[...], scaled[...]).astype(BF16)
    for p, out in enumerate(outs):
        out[...] = sums[p * per_ref : (p + 1) * per_ref, :].reshape(out.shape)


def blend(place, weights, listed, scaled, masks, blocks, tile, steps, index, deep):
    lists = len(weights)
    count, cap = weights[0].shape
    per_ref = count // blocks
    if deep:
        shape = (steps, per_ref, tile)
        spec = pl.BlockSpec((1, per_ref, tile), lambda t, s: (t, 0, 0))
        masses = 0
    else:
        shape = (per_ref, steps * tile)
        spec = pl.BlockSpec((per_ref, tile), lambda t, s: (0, t))
        masses = blocks
    return pl.pallas_call(
        functools.partial(blend_kernel, lists, blocks, masks),
        grid_spec=pltpu.PrefetchScalarGridSpec(
            num_scalar_prefetch=1,
            grid=(steps,),
            in_specs=[pl.BlockSpec((count, cap), lambda t, s: (0, 0))] * lists
            + [
                pl.BlockSpec((lists, 8, cap), lambda t, s: (0, 0, 0)),
                pl.BlockSpec((lists * cap, tile), index),
            ],
            out_specs=[spec] * blocks
            + [pl.BlockSpec((per_ref, masks), lambda t, s: (0, 0))] * masses,
            scratch_shapes=[pltpu.VMEM((count, lists * cap), BF16)],
        ),
        out_shape=[jax.ShapeDtypeStruct(shape, BF16)] * blocks
        + [jax.ShapeDtypeStruct((per_ref, masks), F32)] * masses,
        cost_estimate=cost(
            2 * lists * cap * count * steps * tile, 2 * (lists * cap + count) * steps * tile
        ),
        name="blend",
    )(place, *weights, listed, scaled)


def fold_kernel(parts, *refs):
    sources, outs = refs[:parts], refs[parts:]
    for t, out in enumerate(outs):
        total = sources[0][t].astype(F32)
        for source in sources[1:]:
            total = total + source[t].astype(F32)
        out[...] = total.astype(BF16)


def fold(parts):
    layers, per_ref, tile = parts[0].shape
    return pl.pallas_call(
        functools.partial(fold_kernel, len(parts)),
        in_specs=[VMEM] * len(parts),
        out_specs=[VMEM] * layers,
        out_shape=[jax.ShapeDtypeStruct((per_ref, tile), BF16)] * layers,
        cost_estimate=cost(0, 2 * (len(parts) + 1) * layers * per_ref * tile),
        name="fold",
    )(*parts)


def finish_kernel(blocks, place, *rest):
    shares, masses, rest = rest[:blocks], rest[blocks : 2 * blocks], rest[2 * blocks :]
    apart, wedge, out = rest[:-2], rest[-2], rest[-1]
    mass = masses[0][...]
    for part in masses[1:]:
        mass = mass + part[...]
    below = jnp.ones(out.shape, F32)
    for w in range(wedge.shape[0]):
        below = below + mass[:, w : w + 1] * wedge[w : w + 1, :]

    def emit(parts):
        total = parts[0][...].astype(F32)
        for part in parts[1:]:
            total = total + part[...].astype(F32)
        out[...] = total / below

    last = pl.num_programs(0) - 1

    @pl.when(pl.program_id(0) < last)
    def _():
        emit(shares)

    @pl.when(pl.program_id(0) == last)
    def _():
        emit(apart)


def finish(place, shares, masses, apart, wedge, tile):
    per_ref = shares[0].shape[0]
    masks = wedge.shape[0]
    blocks = len(shares)
    return pl.pallas_call(
        functools.partial(finish_kernel, blocks),
        grid_spec=pltpu.PrefetchScalarGridSpec(
            num_scalar_prefetch=1,
            grid=(SPLIT,),
            in_specs=[pl.BlockSpec((per_ref, tile), lambda t, s: (0, jnp.minimum(t, SPLIT - 2)))]
            * blocks
            + [pl.BlockSpec((per_ref, masks), lambda t, s: (0, 0))] * blocks
            + [pl.BlockSpec((per_ref, tile), lambda t, s: (0, 0))] * len(apart)
            + [pl.BlockSpec((masks, tile), lambda t, s: (0, s[1] * SPLIT + t))],
            out_specs=pl.BlockSpec((per_ref, tile), lambda t, s: (0, t)),
        ),
        out_shape=jax.ShapeDtypeStruct((per_ref, SPLIT * tile), F32),
        cost_estimate=cost(0, 8 * per_ref * SPLIT * tile),
        name="finish",
    )(place, *shares, *masses, *apart, wedge)


GRP = ("lay", "core")


def passed(values, axis, size):
    return [values[0]] + [
        lax.ppermute(values[p], axis, [(d, d ^ p) for d in range(size)]) for p in range(1, size)
    ]


def per_device(slab, pick_owner, pick_offset, wedge_id, live_count, references, wedge):
    slot_count, voxels = slab.shape
    masks = wedge.shape[0]
    layers = lax.axis_size("lay")
    groups = 2 * layers
    blocks = lax.axis_size("blk")
    per_vox = voxels // groups
    tile = per_vox // SPLIT
    keep = per_vox - tile
    half_steps = voxels // 2 // tile
    cap = 2 * slot_count
    block = lax.axis_index("blk").astype(jnp.int32)
    core = lax.axis_index("core").astype(jnp.int32)
    layer = lax.axis_index("lay").astype(jnp.int32)
    place = jnp.stack([core, layer * 2 + core, layer, block])

    stretches = [cut(place[:1], references, i * layers // 2, layers // 2, per_vox) for i in range(2)]
    if blocks == 4:
        near = [[(b, b ^ 1) for b in range(4)], [(b, b ^ 2) for b in range(4)]]
        sides = [[lax.ppermute(stretches[0], "blk", near[i]) for i in range(2)]]
        sides += [[lax.ppermute(stretches[1], "blk", near[i]) for i in range(2)]]
        across = [
            lax.ppermute(sides[0][0], "blk", near[1]),
            lax.ppermute(sides[1][1], "blk", near[0]),
        ]
        tables = [[stretches[i], *sides[i], across[i]] for i in range(2)]
    else:
        tables = [passed([s] * blocks, "blk", blocks) for s in stretches]

    columns = passed(deal(place, slab, groups, keep), GRP, groups)
    live = (jnp.arange(slot_count, dtype=jnp.int32) < live_count[0]).astype(jnp.int32)
    mine = jnp.stack([pick_owner[:, 0], pick_offset, wedge_id, live])
    meta = jnp.concatenate(passed([mine] * blocks, "blk", blocks), axis=1)
    mate = lax.ppermute(
        cut(1 - place[:1], slab, 0, layers, per_vox), "core", [(0, 1), (1, 0)]
    )

    listed = lists_of(block.reshape(1), meta, cap)
    pair = jnp.stack(passed([listed] * 2, "core", 2))
    all_lists = jnp.concatenate(passed([pair] * layers, "lay", layers), axis=0)

    def local(t, s):
        return (0, (2 * (t // SPLIT) + s[0]) * SPLIT + t % SPLIT)

    scaled = select(
        place,
        [slab, mate],
        [
            pl.BlockSpec((slot_count, tile), local),
            pl.BlockSpec((slot_count, tile), lambda t, s: (0, t)),
        ],
        pair,
        wedge,
        pl.BlockSpec((masks, tile), local),
        slot_count,
        tile,
        half_steps,
    )
    sums = ()
    for i in range(2):
        shift = i * half_steps // 2
        spec = pl.BlockSpec((masks, tile), lambda t, s, shift=shift: local(shift + t, s))
        sums = correl(place, scaled, wedge, spec, tables[i], shift, tile, half_steps // 2, sums)
    own, other, norms = sums
    got = lax.ppermute(other, "core", [(0, 1), (1, 0)])
    got_norms = lax.ppermute(norms, "core", [(0, 1), (1, 0)])
    scale = 1.0 / (32.0 * math.sqrt(voxels))
    weights = weigh(own, got, norms, got_norms, listed, scale)
    all_weights = passed([weights] * groups, GRP, groups)

    chosen = select(
        place,
        columns,
        [pl.BlockSpec((slot_count, tile), lambda t, s: (0, t))] * groups,
        all_lists,
        wedge,
        pl.BlockSpec((masks, tile), lambda t, s: (0, s[1] * SPLIT + t)),
        slot_count,
        tile,
        SPLIT - 1,
    )

    apart = blend(
        place,
        all_weights[:2],
        pair,
        scaled,
        masks,
        blocks,
        tile,
        layers,
        lambda t, s: (0, (s[2] ^ t) * SPLIT + SPLIT - 1),
        True,
    )
    apart = passed(apart, "blk", blocks)
    apart = fold(apart)
    apart = passed(apart, "lay", layers)

    mixed = blend(
        place, all_weights, all_lists, chosen, masks, blocks, tile, SPLIT - 1,
        lambda t, s: (0, t), False,
    )
    shares = passed(mixed[:blocks], "blk", blocks)
    masses = passed(mixed[blocks:], "blk", blocks)
    return finish(place, shares, masses, apart, wedge, tile)


def solution(mesh):
    groups, blocks = mesh.shape["grp"], mesh.shape["blk"]
    fine = Mesh(mesh.devices.reshape(groups // 2, 2, blocks), ("lay", "core", "blk"))
    every = ("lay", "core", "blk")
    placed = (P(every, None), P(every, None), P(every), P(every), P(every), P("blk", None), P())

    return jax.shard_map(
        per_device, mesh=fine, in_specs=placed, out_specs=P("blk", GRP), check_vma=False
    )
```

time: 417 us -> 261 us (0.63)
  blocking collectives: 279 us -> 0 us
  waiting for transfers between devices: 9.34 us -> 111 us
  Pallas kernels: 0 us -> 79.1 us
  starting transfers between devices: 10 us -> 64.9 us
  matrix products: 45.2 us -> 0 us
  local copies, waits for them, and re-layouts: 47.2 us -> 2.33 us
  between operations: 14.2 us -> 0.94 us
  other arithmetic: 10.8 us -> 1.85 us
    all_to_all x1 -> x0, blocking collectives: 172 us -> none  [per_device(): lax.all_to_all(blocks_out, 'blk', split_axis=0, concat_axis=0, tiled=True)]
    ppermute x0 -> x42, waiting for transfers between devices: none -> 111 us  [the longest x33 96.8 us: passed(): lax.ppermute(values[p], axis, [(d, d ^ p) for d in range(size)])]
    pallas_call x0 -> x14, Pallas kernels: none -> 79.1 us  [the longest x2 24.3 us: select(): pl.pallas_call(functools.partial(select_kernel, len(blocks)), grid_spec=p...]
    all_gather x1 -> x0, blocking collectives: 68.1 us -> none  [per_device(): all_weights = lax.all_gather(weighted_b, 'grp', axis=0, tiled=True)]
    ppermute x0 -> x42, starting transfers between devices: none -> 64.9 us  [the longest x33 55.5 us: passed(): lax.ppermute(values[p], axis, [(d, d ^ p) for d in range(size)])]
    dot_general x7 -> x0, matrix products: 45.2 us -> none  [the longest x1 22.6 us: per_device(): jnp.dot(wedge, (piece_float * piece_float).T, precision=highest)]
    psum x1 -> x0, blocking collectives: 39.1 us -> none  [per_device(): lax.psum(jnp.dot(weighted.T, masks_hot, precision=highest), ('grp', 'blk'))]
    gather x2 -> x0, local copies, waits for them, and re-layouts: 31.7 us -> none  [the longest x1 19.2 us: per_device(): jnp.take(slab, wanted.reshape(-1), axis=0)]
  transfers between devices with their start and end apart: 4 -> 42, of which waited for: 2 -> 12; matrix products, arithmetic and copies ran while one was open for 19% -> 1% of each run, Pallas kernels for 0% -> 27%
where the time goes in v2:
time: 261 us; the launch traced here: 260 us
  waiting for transfers between devices  111 us (43%)
  Pallas kernels  79.1 us (30%)
  starting transfers between devices  64.9 us (25%)
    ppermute x33, waiting for transfers between devices, passed(): lax.ppermute(values[p], axis, [(d, d ^ p) for d in range(size)])  96.8 us
    ppermute x33, starting transfers between devices, passed(): lax.ppermute(values[p], axis, [(d, d ^ p) for d in range(size)])  55.5 us
    pallas_call x2, Pallas kernels, select(): pl.pallas_call(functools.partial(select_kernel, len(blocks)), grid_spec=p...  24.3 us
    pallas_call x2, Pallas kernels, correl(): pl.pallas_call(functools.partial(correl_kernel, blocks, bool(seeds)), gri...  17.8 us
    ppermute x2, waiting for transfers between devices, per_device(): sides = [[lax.ppermute(stretches[0], 'blk', near[i]) for i in range(2)]]  13.8 us
    pallas_call x2, Pallas kernels, blend(): pl.pallas_call(functools.partial(blend_kernel, lists, blocks, masks), gri...  11.6 us
    pallas_call x3, Pallas kernels, cut(): pl.pallas_call(cut_kernel, grid_spec=pltpu.PrefetchScalarGridSpec(num_sca...  7.65 us
    pallas_call x1, Pallas kernels, deal(): pl.pallas_call(deal_kernel, grid_spec=pltpu.PrefetchScalarGridSpec(num_sc...  7.02 us
  transfers between devices with their start and end apart: 42, of which 12 were waited for; matrix products, arithmetic and copies ran while one was open for 1% of the time, Pallas kernels for 27%

profile of v2, /device:TPU:0, one launch (start us, length us, event | category | flops | bytes accessed | tf_op | source)
XLA Modules:
  0.0 259.7 jit_solution(11214194875447974563)
XLA Ops:
  0.0 3.8 %cut.3 = bf16[64,16384]{1,0:T(8,128)(2,1)} custom-call(s32[1]{0:T(128)S(6)} %sub.3.place, bf16[64,32768]{1,0:T(8,128)(2,1)} %source.7), custom_call_target="tpu_custom_call" | custom-call | bytes 4194304 | tf_op jit(solution)/shard_map/cut/pallas_call | solution.py:52
  6.3 2.5 collective-permute-start.8
  13.4 13.8 %collective-permute-done.8.rest_1_ = bf16[48,8192]{1,0:T(8,128)(2,1)S(1)} collective-permute-done((bf16[48,8192]{1,0:T(8,128)(2,1)}, bf16[48,8192]{1,0:T(8,128)(2,1)S(1)}, u32[]{:S(2)}, u32[]{:S(2)}) %collective-permute-start.8) | collective-permute-done | bytes 786464 | tf_op jit(solution)/shard_map/ppermute | solution.py:403
  32.9 31.4 %collective-permute-done.2 = s32[4,64]{1,0:T(4,128)S(1)} collective-permute-done((s32[4,64]{1,0:T(4,128)S(1)}, s32[4,64]{1,0:T(4,128)S(1)}, u32[]{:S(2)}, u32[]{:S(2)}) %collective-permute-start.2) | collective-permute-done | bytes 1056 | tf_op jit(solution)/shard_map/ppermute | solution.py:380
  65.8 3.0 %collective-permute-done.3 = s32[4,64]{1,0:T(4,128)S(1)} collective-permute-done((s32[4,64]{1,0:T(4,128)S(1)}, s32[4,64]{1,0:T(4,128)S(1)}, u32[]{:S(2)}, u32[]{:S(2)}) %collective-permute-start.3) | collective-permute-done | bytes 1056 | tf_op jit(solution)/shard_map/ppermute | solution.py:380
  75.0 7.0 %deal.1 = (bf16[64,3072]{1,0:T(8,128)(2,1)}, bf16[64,3072]{1,0:T(8,128)(2,1)}, bf16[64,3072]{1,0:T(8,128)(2,1)}, bf16[64,3072]{1,0:T(8,128)(2,1)}, bf16[64,3072]...) custom-call(s32[4]{0:T(128)} %pad_add_fusion.2.place, ...), custom_call_target="tpu_custom_call" | custom-call | bytes 6291456 | tf_op jit(solution)/shard_map/deal/pallas_call | solution.py:76
  82.7 15.2 %select.2.scaled.rest_3_ = bf16[256,16384]{1,0:T(8,128)(2,1)} custom-call(s32[4]{0:T(128)} %pad_add_fusion.2.place, bf16[64,32768]{1,0:T(8,128)(2,1)} %source.7, bf16[64,16384]{1,0:T(8,128)(2,1)} %collective-permute-done.rest_1_, f32[2,8,128]{2,1,0:T(8,128)} %pad_maximum_fusion.rest_2_, f32[8,32768]{1,0:T(8,128)} %rest_12_.1), custom_call_target="tpu_custom_call" | custom-call | flops 4294967296 | bytes 12582912 | tf_op jit(solution)/shard_map/select/pallas_call | solution.py:144
  100.5 8.7 %correl.2 = (f32[128,192]{1,0:T(8,128)}, f32[128,192]{1,0:T(8,128)}, f32[8,192]{1,0:T(8,128)}) custom-call(s32[4]{0:T(128)} %pad_add_fusion.2.place, bf16[256,16384]{1,0:T(8,128)(2,1)} %select.2.scaled.rest_3_, f32[8,32768]{1,0:T(8,128)} %rest_12_.1, bf16[48,8192]{1,0:T(8,128)(2,1)} %cut.5.rest_0_, bf16[48,8192]{1,0:T(8,128)(2,1)} %copy-done.1, ...), custom_call_target="tpu_custom_call" | custom-call | flops 1610612736 | bytes 7602176 | tf_op jit(solution)/shard_map/correl/pallas_call | solution.py:206
  109.2 2.7 %collective-permute-start.21 = (f32[2,8,128]{2,1,0:T(8,128)S(1)}, f32[2,8,128]{2,1,0:T(8,128)S(1)}, u32[]{:S(2)}, u32[]{:S(2)}) collective-permute-start(f32[2,8,128]{2,1,0:T(8,128)S(1)} %copy-done.24), channel_id=1, source_target_pairs={{0,16},{8,24},{16,0},{24,8},{1,17},{9,25},{17,1},{25,9},{2,18},{10... | collective-permute-start | bytes 24584 | tf_op jit(solution)/shard_map/ppermute | solution.py:380
  112.9 9.1 %correl.3 = (f32[128,192]{1,0:T(8,128)}, f32[128,192]{1,0:T(8,128)}, f32[8,192]{1,0:T(8,128)}) custom-call(s32[4]{0:T(128)} %pad_add_fusion.2.place, bf16[256,16384]{1,0:T(8,128)(2,1)} %select.2.scaled.rest_3_, f32[8,32768]{1,0:T(8,128)} %rest_12_.1, bf16[48,8192]{1,0:T(8,128)(2,1)} %cut.4.rest_0_, bf16[48,8192]{1,0:T(8,128)(2,1)} %collective-permute-done.5.rest_1_, ...), custom_call_target="tpu_custom_call" | custom-call | flops 1610612736 | bytes 7602176 | tf_op jit(solution)/shard_map/correl/pallas_call | solution.py:206
  122.6 3.1 %collective-permute-start.26 = (bf16[64,3072]{1,0:T(8,128)(2,1)S(1)}, bf16[64,3072]{1,0:T(8,128)(2,1)}, u32[]{:S(2)}, u32[]{:S(2)}) collective-permute-start(bf16[64,3072]{1,0:T(8,128)(2,1)S(1)} %copy-done.36), channel_id=1, source_target_pairs={{0,16},{4,20},{8,24},{12,28},{16,0},{20,4},{24,8},{28,12},{1,17},{... | collective-permute-start | bytes 1179656 | tf_op jit(solution)/shard_map/ppermute | solution.py:380
  131.5 9.0 %collective-permute-done.25.rest_3_ = bf16[64,3072]{1,0:T(8,128)(2,1)S(1)} collective-permute-done((bf16[64,3072]{1,0:T(8,128)(2,1)S(1)}, bf16[64,3072]{1,0:T(8,128)(2,1)S(1)}, u32[]{:S(2)}, u32[]{:S(2)}) %collective-permute-start.25) | collective-permute-done | bytes 393248 | tf_op jit(solution)/shard_map/ppermute | solution.py:380
  140.5 29.0 %collective-permute-done.26.rest_4_ = bf16[64,3072]{1,0:T(8,128)(2,1)} collective-permute-done((bf16[64,3072]{1,0:T(8,128)(2,1)S(1)}, bf16[64,3072]{1,0:T(8,128)(2,1)}, u32[]{:S(2)}, u32[]{:S(2)}) %collective-permute-start.26) | collective-permute-done | bytes 393248 | tf_op jit(solution)/shard_map/ppermute | solution.py:380
  170.5 5.0 %blend.3 = (bf16[4,48,1024]{2,1,0:T(8,128)(2,1)}, bf16[4,48,1024]{2,1,0:T(8,128)(2,1)}, bf16[4,48,1024]{2,1,0:T(8,128)(2,1)}, bf16[4,48,1024]{2,1,0:T(8,128)(2,1)}) custom-call(s32[4]{0:T(128)} %pad_add_fusion.2.place, bf16[192,128]{1,0:T(8,128)(2,1)} %weigh.1.rest_0_, bf16[192,128]{1,0:T(8,128)(2,1)} %copy-done.11, f32[2,8,128]{2,1,0:T(8,128)} %pad_maximum_fusion.rest_2_, ...), custom_call_target="tpu_custom_call" | custom-call | flops 402653184 | bytes 3670016 | tf_op jit(solution)/shard_map/blend/pallas_call | solution.py:282
  178.5 9.3 %collective-permute-start.17 = (bf16[192,128]{1,0:T(8,128)(2,1)S(1)}, bf16[192,128]{1,0:T(8,128)(2,1)S(1)}, u32[]{:S(2)}, u32[]{:S(2)}) collective-permute-start(bf16[192,128]{1,0:T(8,128)(2,1)S(1)} %copy-done.4), channel_id=1, source_target_pairs={{0,20},{4,16},{8,28},{12,24},{16,4},{20,0},{24,12},{28,8},{1,21},{... | collective-permute-start | bytes 147464 | tf_op jit(solution)/shard_map/ppermute | solution.py:380
  189.6 3.0 %collective-permute-start.19 = (bf16[192,128]{1,0:T(8,128)(2,1)S(1)}, bf16[192,128]{1,0:T(8,128)(2,1)S(1)}, u32[]{:S(2)}, u32[]{:S(2)}) collective-permute-start(bf16[192,128]{1,0:T(8,128)(2,1)S(1)} %copy-done.4), channel_id=1, source_target_pairs={{0,28},{4,24},{8,20},{12,16},{16,12},{20,8},{24,4},{28,0},{1,29},{... | collective-permute-start | bytes 147464 | tf_op jit(solution)/shard_map/ppermute | solution.py:380
  193.1 9.1 %select.3.rest_9_ = bf16[1024,3072]{1,0:T(8,128)(2,1)} custom-call(s32[4]{0:T(128)} %pad_add_fusion.2.place, bf16[64,3072]{1,0:T(8,128)(2,1)} %get-tuple-element.41.rest_0_, bf16[64,3072]{1,0:T(8,128)(2,1)} %copy-done.32, bf16[64,3072]{1,0:T(8,128)(2,1)} %collective-permute-done.24.rest_2_, bf16[64,3072]{1,0:T(8,128)(2,1)} %copy-done.37, ...), custom_call_target="tpu_custom_call" | custom-call | flops 3221225472 | bytes 9437184 | tf_op jit(solution)/shard_map/select/pallas_call | solution.py:144
  206.6 6.6 %blend.2 = (bf16[48,3072]{1,0:T(8,128)(2,1)}, bf16[48,3072]{1,0:T(8,128)(2,1)}, bf16[48,3072]{1,0:T(8,128)(2,1)}, bf16[48,3072]{1,0:T(8,128)(2,1)}, f32[48,8]{1,...) custom-call(s32[4]{0:T(128)} %pad_add_fusion.2.place, bf16[192,128]{1,0:T(8,128)(2,1)} %weigh.1.rest_0_, ...), custom_call_target="tpu_custom_call" | custom-call | flops 1207959552 | bytes 7471104 | tf_op jit(solution)/shard_map/blend/pallas_call | solution.py:282
  215.2 5.9 %collective-permute-done.33.rest_5_ = f32[48,8]{1,0:T(8,128)S(1)} collective-permute-done((f32[48,8]{1,0:T(8,128)}, f32[48,8]{1,0:T(8,128)S(1)}, u32[]{:S(2)}, u32[]{:S(2)}) %collective-permute-start.33) | collective-permute-done | bytes 1568 | tf_op jit(solution)/shard_map/ppermute | solution.py:380
  228.4 6.7 %collective-permute-done.34.rest_6_ = f32[48,8]{1,0:T(8,128)S(1)} collective-permute-done((f32[48,8]{1,0:T(8,128)}, f32[48,8]{1,0:T(8,128)S(1)}, u32[]{:S(2)}, u32[]{:S(2)}) %collective-permute-start.34) | collective-permute-done | bytes 1568 | tf_op jit(solution)/shard_map/ppermute | solution.py:380
  235.1 10.7 %collective-permute-start.39 = (bf16[48,1024]{1,0:T(8,128)(2,1)}, bf16[48,1024]{1,0:T(8,128)(2,1)S(1)}, u32[]{:S(2)}, u32[]{:S(2)}) collective-permute-start(bf16[48,1024]{1,0:T(8,128)(2,1)} %get-tuple-element.62), channel_id=1, source_target_pairs={{0,8},{8,0},{16,24},{24,16},{1,9},{9,1},{17,25},{25,17},{2,10},{10... | collective-permute-start | bytes 294920 | tf_op jit(solution)/shard_map/ppermute | solution.py:380
  248.2 2.4 collective-permute-done.39.rest_9_
  250.6 3.8 %collective-permute-done.40.rest_10_ = bf16[48,1024]{1,0:T(8,128)(2,1)S(1)} collective-permute-done((bf16[48,1024]{1,0:T(8,128)(2,1)}, bf16[48,1024]{1,0:T(8,128)(2,1)S(1)}, u32[]{:S(2)}, u32[]{:S(2)}) %collective-permute-start.40) | collective-permute-done | bytes 98336 | tf_op jit(solution)/shard_map/ppermute | solution.py:380
  255.1 4.7 %finish.1 = f32[48,4096]{1,0:T(8,128)} custom-call(s32[4]{0:T(128)} %pad_add_fusion.2.place, bf16[48,3072]{1,0:T(8,128)(2,1)} %get-tuple-element.49.rest_0_, bf16[48,3072]{1,0:T(8,128)(2,1)} %copy-done.8, bf16[48,3072]{1,0:T(8,128)(2,1)} %copy-done.9, bf16[48,3072]{1,0:T(8,128)(2,1)} %copy-done.10, f32[48,8]{1,0:T(8,128)} %get-tuple-element.53.rest_4_, ...), custom_call_target="tpu_custom_call" | custom-call | bytes 1572864 | tf_op jit(solution)/shard_map/finish/pallas_call | solution.py:357
  (166 shorter events, 53.5 us)
Async XLA Ops:
  3.8 78.8 %collective-permute-start = (bf16[64,16384]{1,0:T(8,128)(2,1)}, bf16[64,16384]{1,0:T(8,128)(2,1)}, u32[]{:S(2)}, u32[]{:S(2)}) collective-permute-start(bf16[64,16384]{1,0:T(8,128)(2,1)} %cut.3), channel_id=1, source_target_pairs={{0,4},{4,0},{1,5},{5,1},{2,6},{6,2},{3,7},{7,3},{8,12},{12,8},{9,1... | collective-permute-start | bytes 6291464 | tf_op jit(solution)/shard_map/ppermute | solution.py:417
  10.7 62.0 %collective-permute-start.6 = (bf16[48,8192]{1,0:T(8,128)(2,1)}, bf16[48,8192]{1,0:T(8,128)(2,1)S(1)}, u32[]{:S(2)}, u32[]{:S(2)}) collective-permute-start(bf16[48,8192]{1,0:T(8,128)(2,1)} %cut.4.rest_0_), channel_id=1, source_target_pairs={{0,2},{1,3},{2,0},{3,1},{4,6},{5,7},{6,4},{7,5},{8,10},{9,11},{10,... | collective-permute-start | bytes 2359304 | tf_op jit(solution)/shard_map/ppermute | solution.py:404
  12.2 85.7 %collective-permute-start.9 = (bf16[48,8192]{1,0:T(8,128)(2,1)}, bf16[48,8192]{1,0:T(8,128)(2,1)S(1)}, u32[]{:S(2)}, u32[]{:S(2)}) collective-permute-start(bf16[48,8192]{1,0:T(8,128)(2,1)} %cut.5.rest_0_), channel_id=1, source_target_pairs={{0,2},{1,3},{2,0},{3,1},{4,6},{5,7},{6,4},{7,5},{8,10},{9,11},{10,... | collective-permute-start | bytes 2359304 | tf_op jit(solution)/shard_map/ppermute | solution.py:403
  27.2 72.4 %collective-permute-start.10 = (bf16[48,8192]{1,0:T(8,128)(2,1)S(1)}, bf16[48,8192]{1,0:T(8,128)(2,1)S(1)}, u32[]{:S(2)}, u32[]{:S(2)}) collective-permute-start(bf16[48,8192]{1,0:T(8,128)(2,1)S(1)} %collective-permute-done.8.rest_1_), channel_id=1, source_target_pairs={{0,2},{1,3},{2,0},{3,1},{4,6},{5,7},{6,4},{7,5},{8,10},{9,11},{10,... | collective-permute-start | bytes 2359304 | tf_op jit(solution)/shard_map/ppermute | solution.py:406
  32.7 31.7 %collective-permute-start.2 = (s32[4,64]{1,0:T(4,128)S(1)}, s32[4,64]{1,0:T(4,128)S(1)}, u32[]{:S(2)}, u32[]{:S(2)}) collective-permute-start(s32[4,64]{1,0:T(4,128)S(1)} %pad_add_fusion.1), channel_id=1, source_target_pairs={{0,2},{1,3},{2,0},{3,1},{4,6},{5,7},{6,4},{7,5},{8,10},{9,11},{10,... | collective-permute-start | bytes 3080 | tf_op jit(solution)/shard_map/ppermute | solution.py:380
  72.4 36.8 %collective-permute-start.5 = (bf16[48,8192]{1,0:T(8,128)(2,1)}, bf16[48,8192]{1,0:T(8,128)(2,1)}, u32[]{:S(2)}, u32[]{:S(2)}) collective-permute-start(bf16[48,8192]{1,0:T(8,128)(2,1)} %cut.4.rest_0_), channel_id=1, source_target_pairs={{0,1},{1,0},{2,3},{3,2},{4,5},{5,4},{6,7},{7,6},{8,9},{9,8},{10,11... | collective-permute-start | bytes 2359304 | tf_op jit(solution)/shard_map/ppermute | solution.py:404
  72.7 39.1 %collective-permute-start.7 = (bf16[48,8192]{1,0:T(8,128)(2,1)S(1)}, bf16[48,8192]{1,0:T(8,128)(2,1)}, u32[]{:S(2)}, u32[]{:S(2)}) collective-permute-start(bf16[48,8192]{1,0:T(8,128)(2,1)S(1)} %collective-permute-done.6.rest_2_), channel_id=1, source_target_pairs={{0,1},{1,0},{2,3},{3,2},{4,5},{5,4},{6,7},{7,6},{8,9},{9,8},{10,11... | collective-permute-start | bytes 2359304 | tf_op jit(solution)/shard_map/ppermute | solution.py:407
  82.7 39.9 %collective-permute-start.23 = (bf16[64,3072]{1,0:T(8,128)(2,1)}, bf16[64,3072]{1,0:T(8,128)(2,1)S(1)}, u32[]{:S(2)}, u32[]{:S(2)}) collective-permute-start(bf16[64,3072]{1,0:T(8,128)(2,1)} %get-tuple-element.42), channel_id=1, source_target_pairs={{0,4},{4,0},{8,12},{12,8},{16,20},{20,16},{24,28},{28,24},{1,5},{5... | collective-permute-start | bytes 1179656 | tf_op jit(solution)/shard_map/ppermute | solution.py:380
  97.9 27.7 %collective-permute-start.24 = (bf16[64,3072]{1,0:T(8,128)(2,1)}, bf16[64,3072]{1,0:T(8,128)(2,1)}, u32[]{:S(2)}, u32[]{:S(2)}) collective-permute-start(bf16[64,3072]{1,0:T(8,128)(2,1)} %get-tuple-element.43), channel_id=1, source_target_pairs={{0,8},{4,12},{8,0},{12,4},{16,24},{20,28},{24,16},{28,20},{1,9},{5... | collective-permute-start | bytes 1179656 | tf_op jit(solution)/shard_map/ppermute | solution.py:380
  99.6 22.3 %collective-permute-start.20 = (f32[2,8,128]{2,1,0:T(8,128)S(1)}, f32[2,8,128]{2,1,0:T(8,128)S(1)}, u32[]{:S(2)}, u32[]{:S(2)}) collective-permute-start(f32[2,8,128]{2,1,0:T(8,128)S(1)} %copy-done.24), channel_id=1, source_target_pairs={{0,8},{8,0},{16,24},{24,16},{1,9},{9,1},{17,25},{25,17},{2,10},{10... | collective-permute-start | bytes 24584 | tf_op jit(solution)/shard_map/ppermute | solution.py:380
  122.6 46.9 %collective-permute-start.26 = (bf16[64,3072]{1,0:T(8,128)(2,1)S(1)}, bf16[64,3072]{1,0:T(8,128)(2,1)}, u32[]{:S(2)}, u32[]{:S(2)}) collective-permute-start(bf16[64,3072]{1,0:T(8,128)(2,1)S(1)} %copy-done.36), channel_id=1, source_target_pairs={{0,16},{4,20},{8,24},{12,28},{16,0},{20,4},{24,8},{28,12},{1,17},{... | collective-permute-start | bytes 1179656 | tf_op jit(solution)/shard_map/ppermute | solution.py:380
  125.7 51.8 %collective-permute-start.27 = (bf16[64,3072]{1,0:T(8,128)(2,1)S(1)}, bf16[64,3072]{1,0:T(8,128)(2,1)}, u32[]{:S(2)}, u32[]{:S(2)}) collective-permute-start(bf16[64,3072]{1,0:T(8,128)(2,1)S(1)} %copy-done.35), channel_id=1, source_target_pairs={{0,20},{4,16},{8,28},{12,24},{16,4},{20,0},{24,12},{28,8},{1,21},{... | collective-permute-start | bytes 1179656 | tf_op jit(solution)/shard_map/ppermute | solution.py:380
  125.8 52.7 %collective-permute-start.28 = (bf16[64,3072]{1,0:T(8,128)(2,1)S(1)}, bf16[64,3072]{1,0:T(8,128)(2,1)}, u32[]{:S(2)}, u32[]{:S(2)}) collective-permute-start(bf16[64,3072]{1,0:T(8,128)(2,1)S(1)} %copy-done.34), channel_id=1, source_target_pairs={{0,24},{4,28},{8,16},{12,20},{16,8},{20,12},{24,0},{28,4},{1,25},{... | collective-permute-start | bytes 1179656 | tf_op jit(solution)/shard_map/ppermute | solution.py:380
  128.2 59.6 %collective-permute-start.29 = (bf16[64,3072]{1,0:T(8,128)(2,1)S(1)}, bf16[64,3072]{1,0:T(8,128)(2,1)}, u32[]{:S(2)}, u32[]{:S(2)}) collective-permute-start(bf16[64,3072]{1,0:T(8,128)(2,1)S(1)} %copy-done.33), channel_id=1, source_target_pairs={{0,28},{4,24},{8,20},{12,16},{16,12},{20,8},{24,4},{28,0},{1,29},{... | collective-permute-start | bytes 1179656 | tf_op jit(solution)/shard_map/ppermute | solution.py:380
  140.5 29.0 %collective-permute-start.13 = (bf16[192,128]{1,0:T(8,128)(2,1)}, bf16[192,128]{1,0:T(8,128)(2,1)S(1)}, u32[]{:S(2)}, u32[]{:S(2)}) collective-permute-start(bf16[192,128]{1,0:T(8,128)(2,1)} %weigh.1.rest_0_), channel_id=1, source_target_pairs={{0,4},{4,0},{8,12},{12,8},{16,20},{20,16},{24,28},{28,24},{1,5},{5... | collective-permute-start | bytes 147464 | tf_op jit(solution)/shard_map/ppermute | solution.py:380
  169.5 23.1 %collective-permute-start.15 = (bf16[192,128]{1,0:T(8,128)(2,1)}, bf16[192,128]{1,0:T(8,128)(2,1)S(1)}, u32[]{:S(2)}, u32[]{:S(2)}) collective-permute-start(bf16[192,128]{1,0:T(8,128)(2,1)} %weigh.1.rest_0_), channel_id=1, source_target_pairs={{0,12},{4,8},{8,4},{12,0},{16,28},{20,24},{24,20},{28,16},{1,13},{... | collective-permute-start | bytes 147464 | tf_op jit(solution)/shard_map/ppermute | solution.py:380
  177.5 24.7 %collective-permute-start.16 = (bf16[192,128]{1,0:T(8,128)(2,1)S(1)}, bf16[192,128]{1,0:T(8,128)(2,1)S(1)}, u32[]{:S(2)}, u32[]{:S(2)}) collective-permute-start(bf16[192,128]{1,0:T(8,128)(2,1)S(1)} %copy-done.4), channel_id=1, source_target_pairs={{0,16},{4,20},{8,24},{12,28},{16,0},{20,4},{24,8},{28,12},{1,17},{... | collective-permute-start | bytes 147464 | tf_op jit(solution)/shard_map/ppermute | solution.py:380
  178.5 25.3 %collective-permute-start.17 = (bf16[192,128]{1,0:T(8,128)(2,1)S(1)}, bf16[192,128]{1,0:T(8,128)(2,1)S(1)}, u32[]{:S(2)}, u32[]{:S(2)}) collective-permute-start(bf16[192,128]{1,0:T(8,128)(2,1)S(1)} %copy-done.4), channel_id=1, source_target_pairs={{0,20},{4,16},{8,28},{12,24},{16,4},{20,0},{24,12},{28,8},{1,21},{... | collective-permute-start | bytes 147464 | tf_op jit(solution)/shard_map/ppermute | solution.py:380
  192.6 30.1 %collective-permute-start.36 = (bf16[4,48,1024]{2,1,0:T(8,128)(2,1)}, bf16[4,48,1024]{2,1,0:T(8,128)(2,1)S(1)}, u32[]{:S(2)}, u32[]{:S(2)}) collective-permute-start(bf16[4,48,1024]{2,1,0:T(8,128)(2,1)} %get-tuple-element.58), channel_id=1, source_target_pairs={{0,1},{1,0},{2,3},{3,2},{4,5},{5,4},{6,7},{7,6},{8,9},{9,8},{10,11... | collective-permute-start | bytes 1179656 | tf_op jit(solution)/shard_map/ppermute | solution.py:380
  202.3 21.0 %collective-permute-start.37 = (bf16[4,48,1024]{2,1,0:T(8,128)(2,1)S(1)}, bf16[4,48,1024]{2,1,0:T(8,128)(2,1)S(1)}, u32[]{:S(2)}, u32[]{:S(2)}) collective-permute-start(bf16[4,48,1024]{2,1,0:T(8,128)(2,1)S(1)} %copy-done.40), channel_id=1, source_target_pairs={{0,2},{1,3},{2,0},{3,1},{4,6},{5,7},{6,4},{7,5},{8,10},{9,11},{10,... | collective-permute-start | bytes 1179656 | tf_op jit(solution)/shard_map/ppermute | solution.py:380
  203.8 21.0 %collective-permute-start.38 = (bf16[4,48,1024]{2,1,0:T(8,128)(2,1)S(1)}, bf16[4,48,1024]{2,1,0:T(8,128)(2,1)S(1)}, u32[]{:S(2)}, u32[]{:S(2)}) collective-permute-start(bf16[4,48,1024]{2,1,0:T(8,128)(2,1)S(1)} %copy-done.39), channel_id=1, source_target_pairs={{0,3},{1,2},{2,1},{3,0},{4,7},{5,6},{6,5},{7,4},{8,11},{9,10},{10,... | collective-permute-start | bytes 1179656 | tf_op jit(solution)/shard_map/ppermute | solution.py:380
  213.2 32.7 %collective-permute-start.30 = (bf16[48,3072]{1,0:T(8,128)(2,1)}, bf16[48,3072]{1,0:T(8,128)(2,1)S(1)}, u32[]{:S(2)}, u32[]{:S(2)}) collective-permute-start(bf16[48,3072]{1,0:T(8,128)(2,1)} %get-tuple-element.50), channel_id=1, source_target_pairs={{0,1},{1,0},{2,3},{3,2},{4,5},{5,4},{6,7},{7,6},{8,9},{9,8},{10,11... | collective-permute-start | bytes 884744 | tf_op jit(solution)/shard_map/ppermute | solution.py:380
  221.2 27.0 %collective-permute-start.31 = (bf16[48,3072]{1,0:T(8,128)(2,1)}, bf16[48,3072]{1,0:T(8,128)(2,1)S(1)}, u32[]{:S(2)}, u32[]{:S(2)}) collective-permute-start(bf16[48,3072]{1,0:T(8,128)(2,1)} %get-tuple-element.51), channel_id=1, source_target_pairs={{0,2},{1,3},{2,0},{3,1},{4,6},{5,7},{6,4},{7,5},{8,10},{9,11},{10,... | collective-permute-start | bytes 884744 | tf_op jit(solution)/shard_map/ppermute | solution.py:380
  222.7 25.5 %collective-permute-start.32 = (bf16[48,3072]{1,0:T(8,128)(2,1)}, bf16[48,3072]{1,0:T(8,128)(2,1)S(1)}, u32[]{:S(2)}, u32[]{:S(2)}) collective-permute-start(bf16[48,3072]{1,0:T(8,128)(2,1)} %get-tuple-element.52), channel_id=1, source_target_pairs={{0,3},{1,2},{2,1},{3,0},{4,7},{5,6},{6,5},{7,4},{8,11},{9,10},{10,... | collective-permute-start | bytes 884744 | tf_op jit(solution)/shard_map/ppermute | solution.py:380
  (59 other events, 753.9 us)

commit v3 on v2

v3 whole, which is shorter than its diff:
```python
import functools
import math

import jax
import jax.numpy as jnp
from jax import lax
from jax.experimental import pallas as pl
from jax.experimental.pallas import tpu as pltpu
from jax.sharding import Mesh
from jax.sharding import PartitionSpec as P

F32 = jnp.float32
BF16 = jnp.bfloat16
ROWS = (((1,), (0,)), ((), ()))
LANES = (((1,), (1,)), ((), ()))
VMEM = pl.BlockSpec(memory_space=pltpu.VMEM)
SMEM = pl.BlockSpec(memory_space=pltpu.SMEM)
SPLIT = 4


def dot(left, right, dims=ROWS):
    return lax.dot_general(left, right, dims, preferred_element_type=F32)


def pieces_of(value, count):
    parts = []
    for _ in range(count):
        part = value.astype(BF16)
        value = value - part.astype(F32)
        parts.append(part)
    return parts


def iota(shape, axis):
    return lax.broadcasted_iota(jnp.int32, shape, axis).astype(F32)


def hot(mask):
    return mask.astype(F32).astype(BF16)


def cost(flops, moved):
    return pl.CostEstimate(flops=int(flops), bytes_accessed=int(moved), transcendentals=0)


def cut_kernel(place, refs, slab, *rest):
    outs, held, came, went = rest[:3], rest[3:6], rest[6], rest[7]
    layers, per_vox = held[2].shape[0], held[2].shape[2]
    core = place[0]

    def start(which):
        source, side = (slab, 1 - core) if which == 2 else (refs, core)
        first = layers // 2 if which == 1 else 0
        copies = []
        for z in range(held[which].shape[0]):
            at = pl.multiple_of((2 * (first + z) + side) * per_vox, per_vox)
            copy = pltpu.make_async_copy(
                source.at[:, pl.ds(at, per_vox)], held[which].at[z], came.at[which, z]
            )
            copy.start()
            copies.append(copy)
        return copies

    coming = [start(which) for which in range(3)]
    going = []
    for which in range(3):
        for z, copy in enumerate(coming[which]):
            copy.wait()
            leave = pltpu.make_async_copy(
                held[which].at[z],
                outs[which].at[:, pl.ds(z * per_vox, per_vox)],
                went.at[which, z],
            )
            leave.start()
            going.append(leave)
    for leave in going:
        leave.wait()


def cut(place, refs, slab, layers, per_vox):
    anywhere = pl.BlockSpec(memory_space=pl.ANY)
    shapes = [
        (layers // 2, refs.shape[0]),
        (layers // 2, refs.shape[0]),
        (layers, slab.shape[0]),
    ]
    return pl.pallas_call(
        cut_kernel,
        in_specs=[SMEM, anywhere, anywhere],
        out_specs=[anywhere] * 3,
        out_shape=[jax.ShapeDtypeStruct((r, n * per_vox), BF16) for n, r in shapes],
        scratch_shapes=[pltpu.VMEM((n, r, per_vox), BF16) for n, r in shapes]
        + [pltpu.SemaphoreType.DMA((3, layers))] * 2,
        cost_estimate=cost(0, 4 * sum(n * r for n, r in shapes) * per_vox),
        name="cut",
    )(place, refs, slab)


def deal_kernel(place, slab, *rest):
    peers = len(rest) - 3
    outs, held, came, went = rest[:peers], rest[peers], rest[peers + 1], rest[peers + 2]
    keep = held.shape[2]
    per_vox = slab.shape[1] // (peers + 1)
    coming = []
    for p in range(peers):
        at = pl.multiple_of((place[1] ^ (p + 1)) * per_vox, per_vox)
        copy = pltpu.make_async_copy(slab.at[:, pl.ds(at, keep)], held.at[p], came.at[p])
        copy.start()
        coming.append(copy)
    going = []
    for p in range(peers):
        coming[p].wait()
        leave = pltpu.make_async_copy(held.at[p], outs[p], went.at[p])
        leave.start()
        going.append(leave)
    for leave in going:
        leave.wait()


def deal(place, slab, groups, keep):
    rows = slab.shape[0]
    anywhere = pl.BlockSpec(memory_space=pl.ANY)
    peers = groups - 1
    return pl.pallas_call(
        deal_kernel,
        in_specs=[SMEM, anywhere],
        out_specs=[anywhere] * peers,
        out_shape=[jax.ShapeDtypeStruct((rows, keep), BF16)] * peers,
        scratch_shapes=[pltpu.VMEM((peers, rows, keep), BF16)]
        + [pltpu.SemaphoreType.DMA((peers,))] * 2,
        cost_estimate=cost(0, 4 * rows * peers * keep),
        name="deal",
    )(place, slab)


def lists_kernel(place, meta, out):
    cap = out.shape[1]
    slots = meta.shape[1]
    info = meta[...].astype(F32)
    named = jnp.logical_and(info[0:1] == place[0].astype(F32), info[3:4] > 0.0)
    chosen = named.astype(F32)
    earlier = hot(iota((slots, slots), 0) < iota((slots, slots), 1))
    rank = dot(jnp.broadcast_to(chosen, (8, slots)).astype(BF16), earlier)[0:1]
    order = hot(jnp.logical_and(iota((cap, slots), 0) == rank, named))
    listed = jnp.concatenate(
        [info[1:2] * chosen, info[2:3] * chosen, chosen, jnp.zeros((5, slots), F32)], axis=0
    )
    out[...] = dot(listed.astype(BF16), order, LANES)


def lists_of(place, meta, cap):
    return pl.pallas_call(
        lists_kernel,
        in_specs=[SMEM, VMEM],
        out_specs=VMEM,
        out_shape=jax.ShapeDtypeStruct((8, cap), F32),
        cost_estimate=cost(1 << 22, 1 << 18),
        name="lists",
    )(place, meta)


def columns_of(listed):
    cap = listed.shape[1]
    eye = hot(iota((cap, cap), 0) == iota((cap, cap), 1))
    return dot(eye, listed.astype(BF16), LANES)


def select_kernel(count, place, *rest):
    blocks, pairs, wedge, out = rest[:count], rest[count:-4], rest[-4], rest[-3]
    rows_hot, wedge_hot = rest[-2:]
    bunches, height, depth = rows_hot.shape
    cap = wedge_hot.shape[0] // count
    rows = blocks[0].shape[0]
    bunch = depth // rows
    masks = wedge.shape[0]

    @pl.when(pl.program_id(0) == 0)
    def _():
        rows_hot[...] = jnp.zeros_like(rows_hot)
        for g in range(count):
            columns = columns_of(pairs[g // 2][g % 2])
            n, at = g // bunch, g % bunch
            rows_hot[n, at * cap : (at + 1) * cap, at * rows : (at + 1) * rows] = hot(
                iota((cap, rows), 1) == columns[:, 0:1]
            )
            marks = (iota((cap, masks), 1) == columns[:, 1:2]).astype(F32)
            wedge_hot[g * cap : (g + 1) * cap, :] = jnp.concatenate([marks] * 3, axis=1).astype(
                BF16
            )

    lined = jnp.concatenate(pieces_of(wedge[...], 3), axis=0)
    weights = dot(wedge_hot[...], lined)
    for n in range(bunches):
        stack = [blocks[n * bunch + i][...] for i in range(bunch)]
        values = dot(rows_hot[n], jnp.concatenate(stack, axis=0))
        part = slice(n * height, (n + 1) * height)
        out[part, :] = (weights[part] * values).astype(BF16)


def select(place, blocks, block_specs, pairs, wedge, wedge_spec, rows, tile, steps):
    count = len(blocks)
    cap = pairs[0].shape[2]
    masks = wedge.shape[0]
    bunch = min(count, 256 // rows)
    return pl.pallas_call(
        functools.partial(select_kernel, count),
        grid_spec=pltpu.PrefetchScalarGridSpec(
            num_scalar_prefetch=1,
            grid=(steps,),
            in_specs=[
                *block_specs,
                *[pl.BlockSpec((2, 8, cap), lambda t, s: (0, 0, 0))] * len(pairs),
                wedge_spec,
            ],
            out_specs=pl.BlockSpec((count * cap, tile), lambda t, s: (0, t)),
            scratch_shapes=[
                pltpu.VMEM((count // bunch, bunch * cap, bunch * rows), BF16),
                pltpu.VMEM((count * cap, 3 * masks), BF16),
            ],
        ),
        out_shape=jax.ShapeDtypeStruct((count * cap, steps * tile), BF16),
        cost_estimate=cost(
            4 * count * cap * 256 * steps * tile, 2 * count * (cap + rows) * steps * tile
        ),
        name="select",
    )(place, *blocks, *pairs, wedge)


def correl_kernel(blocks, seeded, place, scaled, wedge, *rest):
    refs, rest = rest[:blocks], rest[blocks:]
    seeds, rest = (rest[:3], rest[3:]) if seeded else ((), rest)
    own, other, norms, table = rest
    cap, count = own.shape
    masks = wedge.shape[0]
    per_ref = count // blocks

    @pl.when(pl.program_id(0) == 0)
    def _():
        for i, target in enumerate((own, other, norms)):
            target[...] = seeds[i][...] if seeded else jnp.zeros_like(target)

    for p in range(blocks):
        table[p * per_ref : (p + 1) * per_ref, :] = refs[p][...]
    every = table[...]
    got = dot(scaled[...], every, LANES)
    own[...] += got[:cap]
    other[:cap, :] += got[cap:]
    wide = every.astype(F32)
    high, low = pieces_of(wide * wide, 2)
    lined = jnp.concatenate(pieces_of(wedge[...], 3), axis=0)
    sums = dot(high, lined, LANES) + dot(low, lined, LANES)
    norms[:, :masks] += sums[:, :masks] + sums[:, masks : 2 * masks] + sums[:, 2 * masks :]

    @pl.when(pl.program_id(0) == pl.num_programs(0) - 1)
    def _():
        other[cap:, :] = norms[...].T[:masks]


def correl(place, scaled, wedge, wedge_spec, refs, shift, tile, steps, seeds):
    blocks = len(refs)
    cap = scaled.shape[0] // 2
    masks = wedge.shape[0]
    per_ref = refs[0].shape[0]
    count = blocks * per_ref
    in_specs = [pl.BlockSpec((2 * cap, tile), lambda t, s: (0, shift + t)), wedge_spec]
    in_specs += [pl.BlockSpec((per_ref, tile), lambda t, s: (0, t))] * blocks
    shapes = [(cap, count), (cap + masks, count), (count, 128)]
    outs = [pl.BlockSpec(shape, lambda t, s: (0, 0)) for shape in shapes]
    if seeds:
        in_specs += outs
    return pl.pallas_call(
        functools.partial(correl_kernel, blocks, bool(seeds)),
        grid_spec=pltpu.PrefetchScalarGridSpec(
            num_scalar_prefetch=1,
            grid=(steps,),
            in_specs=in_specs,
            out_specs=outs,
            scratch_shapes=[pltpu.VMEM((count, tile), BF16)],
        ),
        out_shape=[jax.ShapeDtypeStruct(shape, F32) for shape in shapes],
        cost_estimate=cost(
            8 * cap * count * steps * tile, 2 * steps * tile * (2 * cap + count + 2 * masks)
        ),
        name="correl",
    )(place, scaled, wedge, *refs, *seeds)


def weigh_kernel(scale, own, sent, got, pair, out):
    cap = own.shape[0]
    masks = sent.shape[0] - cap
    columns = columns_of(pair[0])
    marks = (iota((cap, masks), 1) == columns[:, 1:2]).astype(F32)
    wedge_hot = jnp.concatenate([marks] * 3, axis=1).astype(BF16)
    norms = jnp.concatenate(pieces_of(sent[cap:, :] + got[cap:, :], 3), axis=0)
    score = (own[...] + got[:cap, :] - 0.5 * dot(wedge_hot, norms)) * scale
    score = jnp.exp(score - jnp.max(score, axis=1, keepdims=True))
    share = score / jnp.sum(score, axis=1, keepdims=True) * columns[:, 2:3]
    out[...] = share.T.astype(BF16)


def weigh(own, sent, got, pair, scale):
    cap, count = own.shape
    return pl.pallas_call(
        functools.partial(weigh_kernel, scale),
        in_specs=[VMEM] * 4,
        out_specs=VMEM,
        out_shape=jax.ShapeDtypeStruct((count, cap), BF16),
        cost_estimate=cost(1 << 24, 1 << 18),
        name="weigh",
    )(own, sent, got, pair)


def blend_kernel(lists, blocks, masks, steps, place, *rest):
    weights, rest = rest[:lists], rest[lists:]
    pairs, scaled = rest[: -blocks - 2], rest[-blocks - 2]
    outs, turned = rest[-blocks - 1 : -1], rest[-1]
    cap = weights[0].shape[1]
    per_ref = outs[0].shape[-2]

    @pl.when(pl.program_id(0) == 0)
    def _():
        for g in range(lists):
            turned[:, g * cap : (g + 1) * cap] = weights[g][...]

    @pl.when(pl.program_id(0) < steps)
    def _():
        sums = dot(turned[...], scaled[...]).astype(BF16)
        for p, out in enumerate(outs):
            out[...] = sums[p * per_ref : (p + 1) * per_ref, :].reshape(out.shape)

    if pairs:

        @pl.when(pl.program_id(0) == steps)
        def _():
            total = jnp.zeros((turned.shape[0], masks), F32)
            for g in range(lists):
                marks = hot(iota((masks, cap), 0) == pairs[g // 2][g % 2, 1:2, :])
                total = total + dot(turned[:, g * cap : (g + 1) * cap], marks, LANES)
            parts = jnp.concatenate(pieces_of(total, 3), axis=1)
            for p, out in enumerate(outs):
                out[:, : 3 * masks] = parts[p * per_ref : (p + 1) * per_ref, :]


def blend(place, weights, pairs, scaled, masks, blocks, tile, steps, index):
    lists = len(weights)
    count, cap = weights[0].shape
    per_ref = count // blocks
    if pairs:
        shape = (per_ref, steps * tile + 128)
        spec = pl.BlockSpec((per_ref, tile), lambda t, s: (0, t))
    else:
        shape = (steps, per_ref, tile)
        spec = pl.BlockSpec((1, per_ref, tile), lambda t, s: (t, 0, 0))
    return pl.pallas_call(
        functools.partial(blend_kernel, lists, blocks, masks, steps),
        grid_spec=pltpu.PrefetchScalarGridSpec(
            num_scalar_prefetch=1,
            grid=(steps + (1 if pairs else 0),),
            in_specs=[pl.BlockSpec((count, cap), lambda t, s: (0, 0))] * lists
            + [pl.BlockSpec((2, 8, cap), lambda t, s: (0, 0, 0))] * len(pairs)
            + [pl.BlockSpec((lists * cap, tile), index)],
            out_specs=[spec] * blocks,
            scratch_shapes=[pltpu.VMEM((count, lists * cap), BF16)],
        ),
        out_shape=[jax.ShapeDtypeStruct(shape, BF16)] * blocks,
        cost_estimate=cost(
            2 * lists * cap * count * steps * tile, 2 * (lists * cap + count) * steps * tile
        ),
        name="blend",
    )(place, *weights, *pairs, scaled)


def fold_kernel(parts, *refs):
    sources, outs = refs[:parts], refs[parts:]
    for t, out in enumerate(outs):
        total = sources[0][t].astype(F32)
        for source in sources[1:]:
            total = total + source[t].astype(F32)
        out[...] = total.astype(BF16)


def fold(parts):
    layers, per_ref, tile = parts[0].shape
    return pl.pallas_call(
        functools.partial(fold_kernel, len(parts)),
        in_specs=[VMEM] * len(parts),
        out_specs=[VMEM] * layers,
        out_shape=[jax.ShapeDtypeStruct((per_ref, tile), BF16)] * layers,
        cost_estimate=cost(0, 2 * (len(parts) + 1) * layers * per_ref * tile),
        name="fold",
    )(*parts)


def finish_kernel(blocks, place, *rest):
    shares, masses, rest = rest[:blocks], rest[blocks : 2 * blocks], rest[2 * blocks :]
    apart, wedge, out = rest[:-2], rest[-2], rest[-1]
    masks = wedge.shape[0]
    mass = masses[0][...].astype(F32)
    for part in masses[1:]:
        mass = mass + part[...].astype(F32)
    mass = mass[:, :masks] + mass[:, masks : 2 * masks] + mass[:, 2 * masks : 3 * masks]
    below = jnp.ones(out.shape, F32)
    for w in range(masks):
        below = below + mass[:, w : w + 1] * wedge[w : w + 1, :]

    def emit(parts):
        total = parts[0][...].astype(F32)
        for part in parts[1:]:
            total = total + part[...].astype(F32)
        out[...] = total / below

    last = pl.num_programs(0) - 1

    @pl.when(pl.program_id(0) < last)
    def _():
        emit(shares)

    @pl.when(pl.program_id(0) == last)
    def _():
        emit(apart)


def finish(place, shares, apart, wedge, tile):
    per_ref, width = shares[0].shape
    masks = wedge.shape[0]
    blocks = len(shares)
    return pl.pallas_call(
        functools.partial(finish_kernel, blocks),
        grid_spec=pltpu.PrefetchScalarGridSpec(
            num_scalar_prefetch=1,
            grid=(SPLIT,),
            in_specs=[pl.BlockSpec((per_ref, tile), lambda t, s: (0, jnp.minimum(t, SPLIT - 2)))]
            * blocks
            + [pl.BlockSpec((per_ref, 128), lambda t, s: (0, width // 128 - 1))] * blocks
            + [pl.BlockSpec((per_ref, tile), lambda t, s: (0, 0))] * len(apart)
            + [pl.BlockSpec((masks, tile), lambda t, s: (0, s[1] * SPLIT + t))],
            out_specs=pl.BlockSpec((per_ref, tile), lambda t, s: (0, t)),
        ),
        out_shape=jax.ShapeDtypeStruct((per_ref, SPLIT * tile), F32),
        cost_estimate=cost(0, 8 * per_ref * SPLIT * tile),
        name="finish",
    )(place, *shares, *shares, *apart, wedge)


GRP = ("lay", "core")


def passed(values, axis, size):
    return [values[0]] + [
        lax.ppermute(values[p], axis, [(d, d ^ p) for d in range(size)]) for p in range(1, size)
    ]


def per_device(slab, pick_owner, pick_offset, wedge_id, live_count, references, wedge):
    slot_count, voxels = slab.shape
    masks = wedge.shape[0]
    layers = lax.axis_size("lay")
    groups = 2 * layers
    blocks = lax.axis_size("blk")
    per_vox = voxels // groups
    tile = per_vox // SPLIT
    keep = per_vox - tile
    half_steps = voxels // 2 // tile
    cap = 2 * slot_count
    block = lax.axis_index("blk").astype(jnp.int32)
    core = lax.axis_index("core").astype(jnp.int32)
    layer = lax.axis_index("lay").astype(jnp.int32)
    place = jnp.stack([core, layer * 2 + core, layer, block])

    live = (jnp.arange(slot_count, dtype=jnp.int32) < live_count[0]).astype(jnp.int32)
    mine = jnp.stack([pick_owner[:, 0], pick_offset, wedge_id, live])
    meta = jnp.concatenate(passed([mine] * blocks, "blk", blocks), axis=1)
    low, high, aside = cut(place, references, slab, layers, per_vox)
    stretches = [low, high]
    if blocks == 4:
        near = [[(b, b ^ 1) for b in range(4)], [(b, b ^ 2) for b in range(4)]]
        sides = [[lax.ppermute(low, "blk", near[i]) for i in range(2)]]
        sides += [[lax.ppermute(high, "blk", near[i]) for i in range(2)]]
        across = [
            lax.ppermute(sides[0][0], "blk", near[1]),
            lax.ppermute(sides[1][1], "blk", near[0]),
        ]
        tables = [[stretches[i], *sides[i], across[i]] for i in range(2)]
    else:
        tables = [passed([s] * blocks, "blk", blocks) for s in stretches]
    mate = lax.ppermute(aside, "core", [(0, 1), (1, 0)])
    columns = passed([slab, *deal(place, slab, groups, keep)], GRP, groups)

    listed = lists_of(block.reshape(1), meta, cap)
    pair = jnp.stack(passed([listed] * 2, "core", 2))
    pairs = passed([pair] * layers, "lay", layers)

    def local(t, s, split=SPLIT):
        return (0, (2 * (t // split) + s[0]) * split + t % split)

    wide = functools.partial(local, split=SPLIT // 2)
    scaled = select(
        place,
        [slab, mate],
        [
            pl.BlockSpec((slot_count, 2 * tile), wide),
            pl.BlockSpec((slot_count, 2 * tile), lambda t, s: (0, t)),
        ],
        [pair],
        wedge,
        pl.BlockSpec((masks, 2 * tile), wide),
        slot_count,
        2 * tile,
        half_steps // 2,
    )
    sums = ()
    for i in range(2):
        shift = i * half_steps // 2
        spec = pl.BlockSpec((masks, tile), lambda t, s, shift=shift: local(shift + t, s))
        sums = correl(place, scaled, wedge, spec, tables[i], shift, tile, half_steps // 2, sums)
    own, other, _ = sums
    got = lax.ppermute(other, "core", [(0, 1), (1, 0)])
    weights = weigh(own, other, got, pair, 1.0 / (32.0 * math.sqrt(voxels)))
    all_weights = passed([weights] * groups, GRP, groups)

    chosen = select(
        place,
        columns,
        [pl.BlockSpec((slot_count, tile), lambda t, s: (0, s[1] * SPLIT + t))]
        + [pl.BlockSpec((slot_count, tile), lambda t, s: (0, t))] * (groups - 1),
        pairs,
        wedge,
        pl.BlockSpec((masks, tile), lambda t, s: (0, s[1] * SPLIT + t)),
        slot_count,
        tile,
        SPLIT - 1,
    )

    apart = blend(
        place,
        all_weights[:2],
        [],
        scaled,
        masks,
        blocks,
        tile,
        layers,
        lambda t, s: (0, (s[2] ^ t) * SPLIT + SPLIT - 1),
    )
    apart = passed(apart, "blk", blocks)
    apart = fold(apart)
    apart = passed(apart, "lay", layers)

    shares = blend(
        place,
        all_weights,
        pairs,
        chosen,
        masks,
        blocks,
        tile,
        SPLIT - 1,
        lambda t, s: (0, jnp.minimum(t, SPLIT - 2)),
    )
    shares = passed(shares, "blk", blocks)
    return finish(place, shares, apart, wedge, tile)


def solution(mesh):
    groups, blocks = mesh.shape["grp"], mesh.shape["blk"]
    fine = Mesh(mesh.devices.reshape(groups // 2, 2, blocks), ("lay", "core", "blk"))
    every = ("lay", "core", "blk")
    placed = (P(every, None), P(every, None), P(every), P(every), P(every), P("blk", None), P())

    return jax.shard_map(
        per_device, mesh=fine, in_specs=placed, out_specs=P("blk", GRP), check_vma=False
    )
```

time: 261 us -> 267 us (1.023)
  waiting for transfers between devices: 111 us -> 125 us
  Pallas kernels: 79.1 us -> 69 us
    pallas_call x9 -> x7, Pallas kernels: 52.8 us -> 41.1 us  [the longest x2 20 us: select(): pl.pallas_call(functools.partial(select_kernel, count), grid_spec=pltpu.P...]
    ppermute x1, waiting for transfers between devices: 0.01 us -> 7.83 us  [per_device(): lax.ppermute(sides[1][1], 'blk', near[0])]
    ppermute x33 -> x30, waiting for transfers between devices: 96.8 us -> 101 us  [passed(): lax.ppermute(values[p], axis, [(d, d ^ p) for d in range(size)])]
    ppermute x6 -> x5, waiting for transfers between devices: 13.8 us -> 15.7 us  [the longest x2 15.7 us: per_device(): sides = [[lax.ppermute(low, 'blk', near[i]) for i in range(2)]]]
    ppermute x33 -> x30, starting transfers between devices: 55.5 us -> 55.9 us  [passed(): lax.ppermute(values[p], axis, [(d, d ^ p) for d in range(size)])]
    ppermute x6 -> x5, starting transfers between devices: 5.63 us -> 5.46 us  [the longest x2 3.06 us: per_device(): sides = [[lax.ppermute(low, 'blk', near[i]) for i in range(2)]]]
  transfers between devices with their start and end apart: 42 -> 38, of which waited for: 12 -> 14; matrix products, arithmetic and copies ran while one was open for 1% -> 0% of each run, Pallas kernels for 27% -> 23%
where the time goes in v3:
time: 267 us; the launch traced here: 266 us
  waiting for transfers between devices  125 us (47%)
  Pallas kernels  69 us (26%)
  starting transfers between devices  64.9 us (24%)
  local copies, waits for them, and re-layouts  4.3 us (2%)
    ppermute x30, waiting for transfers between devices, passed(): lax.ppermute(values[p], axis, [(d, d ^ p) for d in range(size)])  101 us
    ppermute x30, starting transfers between devices, passed(): lax.ppermute(values[p], axis, [(d, d ^ p) for d in range(size)])  55.9 us
    pallas_call x2, Pallas kernels, select(): pl.pallas_call(functools.partial(select_kernel, count), grid_spec=pltpu.P...  20 us
    pallas_call x2, Pallas kernels, correl(): pl.pallas_call(functools.partial(correl_kernel, blocks, bool(seeds)), gri...  19.2 us
    ppermute x2, waiting for transfers between devices, per_device(): sides = [[lax.ppermute(low, 'blk', near[i]) for i in range(2)]]  15.7 us
    pallas_call x2, Pallas kernels, blend(): pl.pallas_call(functools.partial(blend_kernel, lists, blocks, masks, step...  11.6 us
    ppermute x1, waiting for transfers between devices, per_device(): lax.ppermute(sides[1][1], 'blk', near[0])  7.83 us
  transfers between devices with their start and end apart: 38, of which 14 were waited for; matrix products, arithmetic and copies ran while one was open for 0% of the time, Pallas kernels for 23%

profile of v3, /device:TPU:0, one launch (start us, length us, event | category | flops | bytes accessed | tf_op | source)
XLA Modules:
  0.0 265.7 jit_solution(16513806188625914261)
XLA Ops:
  0.6 3.9 %cut.1 = (bf16[48,8192]{1,0:T(8,128)(2,1)}, bf16[48,8192]{1,0:T(8,128)(2,1)}, bf16[64,16384]{1,0:T(8,128)(2,1)}) custom-call(s32[4]{0:T(128)} %pad_add_fusion.2.place, bf16[48,32768]{1,0:T(8,128)(2,1)} %refs.1, bf16[64,32768]{1,0:T(8,128)(2,1)} %rest_0_.3), custom_call_target="tpu_custom_call" | custom-call | bytes 7340032 | tf_op jit(solution)/shard_map/cut/pallas_call | solution.py:87
  5.1 2.6 collective-permute-start.8
  10.3 15.7 %collective-permute-done.8.rest_1_ = bf16[48,8192]{1,0:T(8,128)(2,1)S(1)} collective-permute-done((bf16[48,8192]{1,0:T(8,128)(2,1)}, bf16[48,8192]{1,0:T(8,128)(2,1)S(1)}, u32[]{:S(2)}, u32[]{:S(2)}) %collective-permute-start.8) | collective-permute-done | bytes 786464 | tf_op jit(solution)/shard_map/ppermute | solution.py:477
  31.7 29.5 %collective-permute-done.2 = s32[4,64]{1,0:T(4,128)S(1)} collective-permute-done((s32[4,64]{1,0:T(4,128)S(1)}, s32[4,64]{1,0:T(4,128)S(1)}, u32[]{:S(2)}, u32[]{:S(2)}) %collective-permute-start.2) | collective-permute-done | bytes 1056 | tf_op jit(solution)/shard_map/ppermute | solution.py:450
  62.7 3.0 %collective-permute-done.3 = s32[4,64]{1,0:T(4,128)S(1)} collective-permute-done((s32[4,64]{1,0:T(4,128)S(1)}, s32[4,64]{1,0:T(4,128)S(1)}, u32[]{:S(2)}, u32[]{:S(2)}) %collective-permute-start.3) | collective-permute-done | bytes 1056 | tf_op jit(solution)/shard_map/ppermute | solution.py:450
  71.3 3.3 %deal.1 = (bf16[64,3072]{1,0:T(8,128)(2,1)}, bf16[64,3072]{1,0:T(8,128)(2,1)}, bf16[64,3072]{1,0:T(8,128)(2,1)}, bf16[64,3072]{1,0:T(8,128)(2,1)}, bf16[64,3072]...) custom-call(s32[4]{0:T(128)} %pad_add_fusion.2.place, bf16[64,32768]{1,0:T(8,128)(2,1)} %rest_0_.3), custom_call_target="tpu_custom_call" | custom-call | bytes 5505024 | tf_op jit(solution)/shard_map/deal/pallas_call | solution.py:124
  75.3 11.0 %select.2.scaled.rest_2_ = bf16[256,16384]{1,0:T(8,128)(2,1)} custom-call(s32[4]{0:T(128)} %pad_add_fusion.2.place, bf16[64,32768]{1,0:T(8,128)(2,1)} %rest_0_.3, bf16[64,16384]{1,0:T(8,128)(2,1)} %collective-permute-done.rest_1_, f32[2,8,128]{2,1,0:T(8,128)} %pad_maximum_fusion.rest_2_.pair.rest_8_, f32[8,32768]{1,0:T(8,128)} %rest_12_.3), custom_call_target="tpu_custom_call" | custom-call | flops 4294967296 | bytes 12582912 | tf_op jit(solution)/shard_map/select/pallas_call | solution.py:205
  88.8 9.4 %correl.2 = (f32[128,192]{1,0:T(8,128)}, f32[136,192]{1,0:T(8,128)}, f32[192,128]{1,0:T(8,128)}) custom-call(s32[4]{0:T(128)} %pad_add_fusion.2.place, bf16[256,16384]{1,0:T(8,128)(2,1)} %select.2.scaled.rest_2_, f32[8,32768]{1,0:T(8,128)} %rest_12_.3, bf16[48,8192]{1,0:T(8,128)(2,1)} %get-tuple-element.34.rest_0_, bf16[48,8192]{1,0:T(8,128)(2,1)} %copy-done.4, ...), custom_call_target="tpu_custom_call" | custom-call | flops 1610612736 | bytes 7602176 | tf_op jit(solution)/shard_map/correl/pallas_call | solution.py:271
  98.3 7.8 %collective-permute-done.7.rest_3_ = bf16[48,8192]{1,0:T(8,128)(2,1)} collective-permute-done((bf16[48,8192]{1,0:T(8,128)(2,1)S(1)}, bf16[48,8192]{1,0:T(8,128)(2,1)}, u32[]{:S(2)}, u32[]{:S(2)}) %collective-permute-start.7) | collective-permute-done | bytes 786464 | tf_op jit(solution)/shard_map/ppermute | solution.py:481
  106.1 9.8 %correl.3 = (f32[128,192]{1,0:T(8,128)}, f32[136,192]{1,0:T(8,128)}, f32[192,128]{1,0:T(8,128)}) custom-call(s32[4]{0:T(128)} %pad_add_fusion.2.place, bf16[256,16384]{1,0:T(8,128)(2,1)} %select.2.scaled.rest_2_, f32[8,32768]{1,0:T(8,128)} %rest_12_.3, bf16[48,8192]{1,0:T(8,128)(2,1)} %get-tuple-element.33.rest_0_, ...), custom_call_target="tpu_custom_call" | custom-call | flops 1610612736 | bytes 7602176 | tf_op jit(solution)/shard_map/correl/pallas_call | solution.py:271
  118.1 9.7 %collective-permute-done.19.rest_9_ = f32[2,8,128]{2,1,0:T(8,128)S(1)} collective-permute-done((f32[2,8,128]{2,1,0:T(8,128)S(1)}, f32[2,8,128]{2,1,0:T(8,128)S(1)}, u32[]{:S(2)}, u32[]{:S(2)}) %collective-permute-start.19) | collective-permute-done | bytes 8224 | tf_op jit(solution)/shard_map/ppermute | solution.py:450
  127.8 2.6 collective-permute-start.20
  132.4 3.6 %collective-permute-start.21 = (f32[2,8,128]{2,1,0:T(8,128)S(1)}, f32[2,8,128]{2,1,0:T(8,128)S(1)}, u32[]{:S(2)}, u32[]{:S(2)}) collective-permute-start(f32[2,8,128]{2,1,0:T(8,128)S(1)} %copy-done.19), channel_id=1, source_target_pairs={{0,24},{8,16},{16,8},{24,0},{1,25},{9,17},{17,9},{25,1},{2,26},{10... | collective-permute-start | bytes 24584 | tf_op jit(solution)/shard_map/ppermute | solution.py:450
  138.7 3.0 %collective-permute-start.27 = (bf16[64,3072]{1,0:T(8,128)(2,1)S(1)}, bf16[64,3072]{1,0:T(8,128)(2,1)S(1)}, u32[]{:S(2)}, u32[]{:S(2)}) collective-permute-start(bf16[64,3072]{1,0:T(8,128)(2,1)S(1)} %copy-done.37), channel_id=1, source_target_pairs={{0,24},{4,28},{8,16},{12,20},{16,8},{20,12},{24,0},{28,4},{1,25},{... | collective-permute-start | bytes 1179656 | tf_op jit(solution)/shard_map/ppermute | solution.py:450
  141.7 2.6 collective-permute-start.28
  147.4 34.4 %collective-permute-done.25.rest_4_ = bf16[64,3072]{1,0:T(8,128)(2,1)S(1)} collective-permute-done((bf16[64,3072]{1,0:T(8,128)(2,1)}, bf16[64,3072]{1,0:T(8,128)(2,1)S(1)}, u32[]{:S(2)}, u32[]{:S(2)}) %collective-permute-start.25) | collective-permute-done | bytes 393248 | tf_op jit(solution)/shard_map/ppermute | solution.py:450
  182.4 4.9 %blend.3 = (bf16[4,48,1024]{2,1,0:T(8,128)(2,1)}, bf16[4,48,1024]{2,1,0:T(8,128)(2,1)}, bf16[4,48,1024]{2,1,0:T(8,128)(2,1)}, bf16[4,48,1024]{2,1,0:T(8,128)(2,1)}) custom-call(s32[4]{0:T(128)} %pad_add_fusion.2.place, bf16[192,128]{1,0:T(8,128)(2,1)} %weigh.1.rest_0_, bf16[192,128]{1,0:T(8,128)(2,1)} %copy-done.17, bf16[256,16384]{1,0:T(8,128)(2,1)} %select.2.scaled.rest_2_), custom_call_target="tpu_custom_call" | custom-call | flops 402653184 | bytes 3670016 | tf_op jit(solution)/shard_map/blend/pallas_call | solution.py:354
  189.9 9.3 %collective-permute-start.16 = (bf16[192,128]{1,0:T(8,128)(2,1)S(1)}, bf16[192,128]{1,0:T(8,128)(2,1)S(1)}, u32[]{:S(2)}, u32[]{:S(2)}) collective-permute-start(bf16[192,128]{1,0:T(8,128)(2,1)S(1)} %copy-done.7), channel_id=1, source_target_pairs={{0,20},{4,16},{8,28},{12,24},{16,4},{20,0},{24,12},{28,8},{1,21},{... | collective-permute-start | bytes 147464 | tf_op jit(solution)/shard_map/ppermute | solution.py:450
  203.6 9.0 %select.3.rest_12_ = bf16[1024,3072]{1,0:T(8,128)(2,1)} custom-call(s32[4]{0:T(128)} %pad_add_fusion.2.place, bf16[64,32768]{1,0:T(8,128)(2,1)} %rest_0_.3, bf16[64,3072]{1,0:T(8,128)(2,1)} %copy-done.8, bf16[64,3072]{1,0:T(8,128)(2,1)} %collective-permute-done.23.rest_2_, bf16[64,3072]{1,0:T(8,128)(2,1)} %copy-done.9, bf16[64,3072]{1,0:T(8,128)(2,1)} %copy-done.10, ...), custom_call_target="tpu_custom_call" | custom-call | flops 3221225472 | bytes 9437184 | tf_op jit(solution)/shard_map/select/pallas_call | solution.py:205
  216.9 6.7 %blend.2 = (bf16[48,3200]{1,0:T(8,128)(2,1)}, bf16[48,3200]{1,0:T(8,128)(2,1)}, bf16[48,3200]{1,0:T(8,128)(2,1)}, bf16[48,3200]{1,0:T(8,128)(2,1)}) custom-call(s32[4]{0:T(128)} %pad_add_fusion.2.place, bf16[192,128]{1,0:T(8,128)(2,1)} %weigh.1.rest_0_, bf16[192,128]{1,0:T(8,128)(2,1)} %copy-done.17, bf16[192,128]{1,0:T(8,128)(2,1)} %copy-done.23, ...), custom_call_target="tpu_custom_call" | custom-call | flops 1207959552 | bytes 7471104 | tf_op jit(solution)/shard_map/blend/pallas_call | solution.py:354
  227.2 11.4 %collective-permute-done.33.refs_2_ = bf16[4,48,1024]{2,1,0:T(8,128)(2,1)S(1)} collective-permute-done((bf16[4,48,1024]{2,1,0:T(8,128)(2,1)S(1)}, bf16[4,48,1024]{2,1,0:T(8,128)(2,1)S(1)}, u32[]{:S(2)}, u32[]{:S(2)}) %collective-permute-start.33) | collective-permute-done | bytes 393248 | tf_op jit(solution)/shard_map/ppermute | solution.py:450
  241.7 11.2 %collective-permute-start.35 = (bf16[48,1024]{1,0:T(8,128)(2,1)}, bf16[48,1024]{1,0:T(8,128)(2,1)S(1)}, u32[]{:S(2)}, u32[]{:S(2)}) collective-permute-start(bf16[48,1024]{1,0:T(8,128)(2,1)} %get-tuple-element.56), channel_id=1, source_target_pairs={{0,8},{8,0},{16,24},{24,16},{1,9},{9,1},{17,25},{25,17},{2,10},{10... | collective-permute-start | bytes 294920 | tf_op jit(solution)/shard_map/ppermute | solution.py:450
  255.7 4.5 %collective-permute-done.36.rest_10_ = bf16[48,1024]{1,0:T(8,128)(2,1)S(1)} collective-permute-done((bf16[48,1024]{1,0:T(8,128)(2,1)}, bf16[48,1024]{1,0:T(8,128)(2,1)S(1)}, u32[]{:S(2)}, u32[]{:S(2)}) %collective-permute-start.36) | collective-permute-done | bytes 98336 | tf_op jit(solution)/shard_map/ppermute | solution.py:450
  260.9 4.9 %finish.1 = f32[48,4096]{1,0:T(8,128)} custom-call(s32[4]{0:T(128)} %pad_add_fusion.2.place, bf16[48,3200]{1,0:T(8,128)(2,1)} %get-tuple-element.47.rest_0_.rest_4_, bf16[48,3200]{1,0:T(8,128)(2,1)} %copy-done, bf16[48,3200]{1,0:T(8,128)(2,1)} %copy-done.1, bf16[48,3200]{1,0:T(8,128)(2,1)} %copy-done.2, bf16[48,3200]{1,0:T(8,128)(2,1)} %get-tuple-element.47.rest_0_.rest_4_, ...), custom_call_target="tpu_custom_call" | custom-call | bytes 1572864 | tf_op jit(solution)/shard_map/finish/pallas_call | solution.py:427
  (149 shorter events, 51.1 us)
Async XLA Ops:
  4.5 70.8 %collective-permute-start = (bf16[64,16384]{1,0:T(8,128)(2,1)}, bf16[64,16384]{1,0:T(8,128)(2,1)}, u32[]{:S(2)}, u32[]{:S(2)}) collective-permute-start(bf16[64,16384]{1,0:T(8,128)(2,1)} %get-tuple-element.32), channel_id=1, source_target_pairs={{0,4},{4,0},{1,5},{5,1},{2,6},{6,2},{3,7},{7,3},{8,12},{12,8},{9,1... | collective-permute-start | bytes 6291464 | tf_op jit(solution)/shard_map/ppermute | solution.py:486
  7.6 62.0 %collective-permute-start.6 = (bf16[48,8192]{1,0:T(8,128)(2,1)}, bf16[48,8192]{1,0:T(8,128)(2,1)S(1)}, u32[]{:S(2)}, u32[]{:S(2)}) collective-permute-start(bf16[48,8192]{1,0:T(8,128)(2,1)} %get-tuple-element.33.rest_0_), channel_id=1, source_target_pairs={{0,2},{1,3},{2,0},{3,1},{4,6},{5,7},{6,4},{7,5},{8,10},{9,11},{10,... | collective-permute-start | bytes 2359304 | tf_op jit(solution)/shard_map/ppermute | solution.py:478
  9.2 77.1 %collective-permute-start.9 = (bf16[48,8192]{1,0:T(8,128)(2,1)}, bf16[48,8192]{1,0:T(8,128)(2,1)S(1)}, u32[]{:S(2)}, u32[]{:S(2)}) collective-permute-start(bf16[48,8192]{1,0:T(8,128)(2,1)} %get-tuple-element.34.rest_0_), channel_id=1, source_target_pairs={{0,2},{1,3},{2,0},{3,1},{4,6},{5,7},{6,4},{7,5},{8,10},{9,11},{10,... | collective-permute-start | bytes 2359304 | tf_op jit(solution)/shard_map/ppermute | solution.py:477
  26.0 61.9 %collective-permute-start.10 = (bf16[48,8192]{1,0:T(8,128)(2,1)S(1)}, bf16[48,8192]{1,0:T(8,128)(2,1)S(1)}, u32[]{:S(2)}, u32[]{:S(2)}) collective-permute-start(bf16[48,8192]{1,0:T(8,128)(2,1)S(1)} %collective-permute-done.8.rest_1_), channel_id=1, source_target_pairs={{0,2},{1,3},{2,0},{3,1},{4,6},{5,7},{6,4},{7,5},{8,10},{9,11},{10,... | collective-permute-start | bytes 2359304 | tf_op jit(solution)/shard_map/ppermute | solution.py:480
  31.4 29.8 %collective-permute-start.2 = (s32[4,64]{1,0:T(4,128)S(1)}, s32[4,64]{1,0:T(4,128)S(1)}, u32[]{:S(2)}, u32[]{:S(2)}) collective-permute-start(s32[4,64]{1,0:T(4,128)S(1)} %pad_add_fusion.1), channel_id=1, source_target_pairs={{0,2},{1,3},{2,0},{3,1},{4,6},{5,7},{6,4},{7,5},{8,10},{9,11},{10,... | collective-permute-start | bytes 3080 | tf_op jit(solution)/shard_map/ppermute | solution.py:450
  69.3 28.9 %collective-permute-start.5 = (bf16[48,8192]{1,0:T(8,128)(2,1)}, bf16[48,8192]{1,0:T(8,128)(2,1)}, u32[]{:S(2)}, u32[]{:S(2)}) collective-permute-start(bf16[48,8192]{1,0:T(8,128)(2,1)} %get-tuple-element.33.rest_0_), channel_id=1, source_target_pairs={{0,1},{1,0},{2,3},{3,2},{4,5},{5,4},{6,7},{7,6},{8,9},{9,8},{10,11... | collective-permute-start | bytes 2359304 | tf_op jit(solution)/shard_map/ppermute | solution.py:478
  69.6 36.5 %collective-permute-start.7 = (bf16[48,8192]{1,0:T(8,128)(2,1)S(1)}, bf16[48,8192]{1,0:T(8,128)(2,1)}, u32[]{:S(2)}, u32[]{:S(2)}) collective-permute-start(bf16[48,8192]{1,0:T(8,128)(2,1)S(1)} %collective-permute-done.6.rest_2_), channel_id=1, source_target_pairs={{0,1},{1,0},{2,3},{3,2},{4,5},{5,4},{6,7},{7,6},{8,9},{9,8},{10,11... | collective-permute-start | bytes 2359304 | tf_op jit(solution)/shard_map/ppermute | solution.py:481
  75.3 63.4 %collective-permute-start.22 = (bf16[64,3072]{1,0:T(8,128)(2,1)}, bf16[64,3072]{1,0:T(8,128)(2,1)S(1)}, u32[]{:S(2)}, u32[]{:S(2)}) collective-permute-start(bf16[64,3072]{1,0:T(8,128)(2,1)} %get-tuple-element.40), channel_id=1, source_target_pairs={{0,4},{4,0},{8,12},{12,8},{16,20},{20,16},{24,28},{28,24},{1,5},{5... | collective-permute-start | bytes 1179656 | tf_op jit(solution)/shard_map/ppermute | solution.py:450
  86.3 52.4 %collective-permute-start.23 = (bf16[64,3072]{1,0:T(8,128)(2,1)}, bf16[64,3072]{1,0:T(8,128)(2,1)}, u32[]{:S(2)}, u32[]{:S(2)}) collective-permute-start(bf16[64,3072]{1,0:T(8,128)(2,1)} %get-tuple-element.41), channel_id=1, source_target_pairs={{0,8},{4,12},{8,0},{12,4},{16,24},{20,28},{24,16},{28,20},{1,9},{5... | collective-permute-start | bytes 1179656 | tf_op jit(solution)/shard_map/ppermute | solution.py:450
  115.9 25.8 %collective-permute-start.11 = (f32[136,192]{1,0:T(8,128)}, f32[136,192]{1,0:T(8,128)S(1)}, u32[]{:S(2)}, u32[]{:S(2)}) collective-permute-start(f32[136,192]{1,0:T(8,128)} %get-tuple-element.39.sent), channel_id=1, source_target_pairs={{0,4},{4,0},{1,5},{5,1},{2,6},{6,2},{3,7},{7,3},{8,12},{12,8},{9,1... | collective-permute-start | bytes 313352 | tf_op jit(solution)/shard_map/ppermute | solution.py:517
  116.0 30.6 %collective-permute-start.24 = (bf16[64,3072]{1,0:T(8,128)(2,1)}, bf16[64,3072]{1,0:T(8,128)(2,1)S(1)}, u32[]{:S(2)}, u32[]{:S(2)}) collective-permute-start(bf16[64,3072]{1,0:T(8,128)(2,1)} %get-tuple-element.42), channel_id=1, source_target_pairs={{0,12},{4,8},{8,4},{12,0},{16,28},{20,24},{24,20},{28,16},{1,13},{... | collective-permute-start | bytes 1179656 | tf_op jit(solution)/shard_map/ppermute | solution.py:450
  137.8 43.9 %collective-permute-start.25 = (bf16[64,3072]{1,0:T(8,128)(2,1)}, bf16[64,3072]{1,0:T(8,128)(2,1)S(1)}, u32[]{:S(2)}, u32[]{:S(2)}) collective-permute-start(bf16[64,3072]{1,0:T(8,128)(2,1)} %get-tuple-element.43), channel_id=1, source_target_pairs={{0,16},{4,20},{8,24},{12,28},{16,0},{20,4},{24,8},{28,12},{1,17},{... | collective-permute-start | bytes 1179656 | tf_op jit(solution)/shard_map/ppermute | solution.py:450
  138.6 49.6 %collective-permute-start.26 = (bf16[64,3072]{1,0:T(8,128)(2,1)}, bf16[64,3072]{1,0:T(8,128)(2,1)S(1)}, u32[]{:S(2)}, u32[]{:S(2)}) collective-permute-start(bf16[64,3072]{1,0:T(8,128)(2,1)} %get-tuple-element.44), channel_id=1, source_target_pairs={{0,20},{4,16},{8,28},{12,24},{16,4},{20,0},{24,12},{28,8},{1,21},{... | collective-permute-start | bytes 1179656 | tf_op jit(solution)/shard_map/ppermute | solution.py:450
  138.7 51.2 %collective-permute-start.27 = (bf16[64,3072]{1,0:T(8,128)(2,1)S(1)}, bf16[64,3072]{1,0:T(8,128)(2,1)S(1)}, u32[]{:S(2)}, u32[]{:S(2)}) collective-permute-start(bf16[64,3072]{1,0:T(8,128)(2,1)S(1)} %copy-done.37), channel_id=1, source_target_pairs={{0,24},{4,28},{8,16},{12,20},{16,8},{20,12},{24,0},{28,4},{1,25},{... | collective-permute-start | bytes 1179656 | tf_op jit(solution)/shard_map/ppermute | solution.py:450
  141.7 57.4 %collective-permute-start.28 = (bf16[64,3072]{1,0:T(8,128)(2,1)S(1)}, bf16[64,3072]{1,0:T(8,128)(2,1)S(1)}, u32[]{:S(2)}, u32[]{:S(2)}) collective-permute-start(bf16[64,3072]{1,0:T(8,128)(2,1)S(1)} %copy-done.36), channel_id=1, source_target_pairs={{0,28},{4,24},{8,20},{12,16},{16,12},{20,8},{24,4},{28,0},{1,29},{... | collective-permute-start | bytes 1179656 | tf_op jit(solution)/shard_map/ppermute | solution.py:450
  146.6 35.1 %collective-permute-start.12 = (bf16[192,128]{1,0:T(8,128)(2,1)}, bf16[192,128]{1,0:T(8,128)(2,1)S(1)}, u32[]{:S(2)}, u32[]{:S(2)}) collective-permute-start(bf16[192,128]{1,0:T(8,128)(2,1)} %weigh.1.rest_0_), channel_id=1, source_target_pairs={{0,4},{4,0},{8,12},{12,8},{16,20},{20,16},{24,28},{28,24},{1,5},{5... | collective-permute-start | bytes 147464 | tf_op jit(solution)/shard_map/ppermute | solution.py:450
  188.3 24.3 %collective-permute-start.15 = (bf16[192,128]{1,0:T(8,128)(2,1)S(1)}, bf16[192,128]{1,0:T(8,128)(2,1)S(1)}, u32[]{:S(2)}, u32[]{:S(2)}) collective-permute-start(bf16[192,128]{1,0:T(8,128)(2,1)S(1)} %copy-done.7), channel_id=1, source_target_pairs={{0,16},{4,20},{8,24},{12,28},{16,0},{20,4},{24,8},{28,12},{1,17},{... | collective-permute-start | bytes 147464 | tf_op jit(solution)/shard_map/ppermute | solution.py:450
  189.9 24.3 %collective-permute-start.16 = (bf16[192,128]{1,0:T(8,128)(2,1)S(1)}, bf16[192,128]{1,0:T(8,128)(2,1)S(1)}, u32[]{:S(2)}, u32[]{:S(2)}) collective-permute-start(bf16[192,128]{1,0:T(8,128)(2,1)S(1)} %copy-done.7), channel_id=1, source_target_pairs={{0,20},{4,16},{8,28},{12,24},{16,4},{20,0},{24,12},{28,8},{1,21},{... | collective-permute-start | bytes 147464 | tf_op jit(solution)/shard_map/ppermute | solution.py:450
  202.9 22.8 %collective-permute-start.32 = (bf16[4,48,1024]{2,1,0:T(8,128)(2,1)}, bf16[4,48,1024]{2,1,0:T(8,128)(2,1)S(1)}, u32[]{:S(2)}, u32[]{:S(2)}) collective-permute-start(bf16[4,48,1024]{2,1,0:T(8,128)(2,1)} %get-tuple-element.52), channel_id=1, source_target_pairs={{0,1},{1,0},{2,3},{3,2},{4,5},{5,4},{6,7},{7,6},{8,9},{9,8},{10,11... | collective-permute-start | bytes 1179656 | tf_op jit(solution)/shard_map/ppermute | solution.py:450
  212.6 26.0 %collective-permute-start.33 = (bf16[4,48,1024]{2,1,0:T(8,128)(2,1)S(1)}, bf16[4,48,1024]{2,1,0:T(8,128)(2,1)S(1)}, u32[]{:S(2)}, u32[]{:S(2)}) collective-permute-start(bf16[4,48,1024]{2,1,0:T(8,128)(2,1)S(1)} %copy-done.39), channel_id=1, source_target_pairs={{0,2},{1,3},{2,0},{3,1},{4,6},{5,7},{6,4},{7,5},{8,10},{9,11},{10,... | collective-permute-start | bytes 1179656 | tf_op jit(solution)/shard_map/ppermute | solution.py:450
  214.2 24.4 %collective-permute-start.34 = (bf16[4,48,1024]{2,1,0:T(8,128)(2,1)S(1)}, bf16[4,48,1024]{2,1,0:T(8,128)(2,1)S(1)}, u32[]{:S(2)}, u32[]{:S(2)}) collective-permute-start(bf16[4,48,1024]{2,1,0:T(8,128)(2,1)S(1)} %copy-done.38), channel_id=1, source_target_pairs={{0,3},{1,2},{2,1},{3,0},{4,7},{5,6},{6,5},{7,4},{8,11},{9,10},{10,... | collective-permute-start | bytes 1179656 | tf_op jit(solution)/shard_map/ppermute | solution.py:450
  223.6 29.3 %collective-permute-start.29 = (bf16[48,3200]{1,0:T(8,128)(2,1)}, bf16[48,3200]{1,0:T(8,128)(2,1)S(1)}, u32[]{:S(2)}, u32[]{:S(2)}) collective-permute-start(bf16[48,3200]{1,0:T(8,128)(2,1)} %get-tuple-element.48), channel_id=1, source_target_pairs={{0,1},{1,0},{2,3},{3,2},{4,5},{5,4},{6,7},{7,6},{8,9},{9,8},{10,11... | collective-permute-start | bytes 921608 | tf_op jit(solution)/shard_map/ppermute | solution.py:450
  224.2 31.1 %collective-permute-start.30 = (bf16[48,3200]{1,0:T(8,128)(2,1)}, bf16[48,3200]{1,0:T(8,128)(2,1)S(1)}, u32[]{:S(2)}, u32[]{:S(2)}) collective-permute-start(bf16[48,3200]{1,0:T(8,128)(2,1)} %get-tuple-element.49), channel_id=1, source_target_pairs={{0,2},{1,3},{2,0},{3,1},{4,6},{5,7},{6,4},{7,5},{8,10},{9,11},{10,... | collective-permute-start | bytes 921608 | tf_op jit(solution)/shard_map/ppermute | solution.py:450
  225.7 29.5 %collective-permute-start.31 = (bf16[48,3200]{1,0:T(8,128)(2,1)}, bf16[48,3200]{1,0:T(8,128)(2,1)S(1)}, u32[]{:S(2)}, u32[]{:S(2)}) collective-permute-start(bf16[48,3200]{1,0:T(8,128)(2,1)} %get-tuple-element.50), channel_id=1, source_target_pairs={{0,3},{1,2},{2,1},{3,0},{4,7},{5,6},{6,5},{7,4},{8,11},{9,10},{10,... | collective-permute-start | bytes 921608 | tf_op jit(solution)/shard_map/ppermute | solution.py:450
  (54 other events, 871.7 us)

commit v4 on v3

v4 whole, which is shorter than its diff:
```python
import functools
import math

import jax
import jax.numpy as jnp
from jax import lax
from jax.experimental import pallas as pl
from jax.experimental.pallas import tpu as pltpu
from jax.sharding import Mesh
from jax.sharding import PartitionSpec as P

F32 = jnp.float32
BF16 = jnp.bfloat16
ROWS = (((1,), (0,)), ((), ()))
LANES = (((1,), (1,)), ((), ()))
VMEM = pl.BlockSpec(memory_space=pltpu.VMEM)
SMEM = pl.BlockSpec(memory_space=pltpu.SMEM)
SPLIT = 4


def dot(left, right, dims=ROWS):
    return lax.dot_general(left, right, dims, preferred_element_type=F32)


def pieces_of(value, count):
    parts = []
    for _ in range(count):
        part = value.astype(BF16)
        value = value - part.astype(F32)
        parts.append(part)
    return parts


def iota(shape, axis):
    return lax.broadcasted_iota(jnp.int32, shape, axis).astype(F32)


def hot(mask):
    return mask.astype(F32).astype(BF16)


def cost(flops, moved):
    return pl.CostEstimate(flops=int(flops), bytes_accessed=int(moved), transcendentals=0)


def cut_kernel(place, refs, slab, *rest):
    outs, held, came, went = rest[:3], rest[3:6], rest[6], rest[7]
    layers, per_vox = held[2].shape[0], held[2].shape[2]
    core = place[0]

    def start(which):
        source, side = (slab, 1 - core) if which == 2 else (refs, core)
        first = layers // 2 if which == 1 else 0
        copies = []
        for z in range(held[which].shape[0]):
            at = pl.multiple_of((2 * (first + z) + side) * per_vox, per_vox)
            copy = pltpu.make_async_copy(
                source.at[:, pl.ds(at, per_vox)], held[which].at[z], came.at[which, z]
            )
            copy.start()
            copies.append(copy)
        return copies

    coming = [start(which) for which in range(3)]
    going = []
    for which in range(3):
        for z, copy in enumerate(coming[which]):
            copy.wait()
            leave = pltpu.make_async_copy(
                held[which].at[z],
                outs[which].at[:, pl.ds(z * per_vox, per_vox)],
                went.at[which, z],
            )
            leave.start()
            going.append(leave)
    for leave in going:
        leave.wait()


def cut(place, refs, slab, layers, per_vox):
    anywhere = pl.BlockSpec(memory_space=pl.ANY)
    shapes = [
        (layers // 2, refs.shape[0]),
        (layers // 2, refs.shape[0]),
        (layers, slab.shape[0]),
    ]
    return pl.pallas_call(
        cut_kernel,
        in_specs=[SMEM, anywhere, anywhere],
        out_specs=[anywhere] * 3,
        out_shape=[jax.ShapeDtypeStruct((r, n * per_vox), BF16) for n, r in shapes],
        scratch_shapes=[pltpu.VMEM((n, r, per_vox), BF16) for n, r in shapes]
        + [pltpu.SemaphoreType.DMA((3, layers))] * 2,
        cost_estimate=cost(0, 4 * sum(n * r for n, r in shapes) * per_vox),
        name="cut",
    )(place, refs, slab)


def deal_kernel(place, slab, mate, *rest):
    peers = len(rest) - 3
    outs, held, came, went = rest[:peers], rest[peers], rest[peers + 1], rest[peers + 2]
    rows = slab.shape[0]
    keep = held.shape[2]
    per_vox = mate.shape[1] // (peers + 1)
    coming = []
    for p in range(peers):
        layer = place[2] ^ (p + 1)
        mine = pl.multiple_of((2 * layer + place[0]) * per_vox, per_vox)
        theirs = pl.multiple_of(layer * per_vox, per_vox)
        pair = [
            pltpu.make_async_copy(
                slab.at[:, pl.ds(mine, keep)], held.at[p, pl.ds(0, rows)], came.at[p, 0]
            ),
            pltpu.make_async_copy(
                mate.at[:, pl.ds(theirs, keep)], held.at[p, pl.ds(rows, rows)], came.at[p, 1]
            ),
        ]
        for copy in pair:
            copy.start()
        coming.append(pair)
    going = []
    for p in range(peers):
        for copy in coming[p]:
            copy.wait()
        leave = pltpu.make_async_copy(held.at[p], outs[p], went.at[p])
        leave.start()
        going.append(leave)
    for leave in going:
        leave.wait()


def deal(place, slab, mate, layers, keep):
    rows = slab.shape[0]
    anywhere = pl.BlockSpec(memory_space=pl.ANY)
    peers = layers - 1
    return pl.pallas_call(
        deal_kernel,
        in_specs=[SMEM, anywhere, anywhere],
        out_specs=[anywhere] * peers,
        out_shape=[jax.ShapeDtypeStruct((2 * rows, keep), BF16)] * peers,
        scratch_shapes=[
            pltpu.VMEM((peers, 2 * rows, keep), BF16),
            pltpu.SemaphoreType.DMA((peers, 2)),
            pltpu.SemaphoreType.DMA((peers,)),
        ],
        cost_estimate=cost(0, 8 * rows * peers * keep),
        name="deal",
    )(place, slab, mate)


def brief_kernel(live, refs, wedge, owner, offset, wedge_id, out, sums):
    masks = wedge.shape[0]
    per_ref = refs.shape[0]
    slots = owner.shape[1]

    @pl.when(pl.program_id(0) == 0)
    def _():
        sums[...] = jnp.zeros_like(sums)

    wide = refs[...].astype(F32)
    high, low = pieces_of(wide * wide, 2)
    lined = jnp.concatenate(pieces_of(wedge[...], 3), axis=0)
    sums[...] += dot(lined, high, LANES) + dot(lined, low, LANES)

    @pl.when(pl.program_id(0) == pl.num_programs(0) - 1)
    def _():
        out[...] = jnp.zeros_like(out)
        out[0:1, :] = jnp.full((1, out.shape[1]), -1.0, F32)
        out[0:1, :slots] = owner[...].astype(F32)
        out[1:2, :slots] = offset[...].astype(F32)
        out[2:3, :slots] = wedge_id[...].astype(F32)
        out[3:4, :slots] = (iota((1, slots), 1) < live[0].astype(F32)).astype(F32)
        out[8 : 8 + masks, :per_ref] = (
            sums[:masks] + sums[masks : 2 * masks] + sums[2 * masks : 3 * masks]
        )


def brief(live, refs, wedge, owner, offset, wedge_id, tile):
    per_ref, voxels = refs.shape
    masks = wedge.shape[0]
    slots = owner.shape[1]
    height = -(-(8 + masks) // 8) * 8
    row = pl.BlockSpec((1, slots), lambda t, s: (0, 0))
    return pl.pallas_call(
        brief_kernel,
        grid_spec=pltpu.PrefetchScalarGridSpec(
            num_scalar_prefetch=1,
            grid=(voxels // tile,),
            in_specs=[
                pl.BlockSpec((per_ref, tile), lambda t, s: (0, t)),
                pl.BlockSpec((masks, tile), lambda t, s: (0, t)),
                row,
                row,
                row,
            ],
            out_specs=pl.BlockSpec((height, 128), lambda t, s: (0, 0)),
            scratch_shapes=[pltpu.VMEM((3 * masks, per_ref), F32)],
        ),
        out_shape=jax.ShapeDtypeStruct((height, 128), F32),
        cost_estimate=cost(12 * masks * per_ref * voxels, 2 * voxels * (per_ref + 2 * masks)),
        name="brief",
    )(live, refs, wedge, owner, offset, wedge_id)


def lists_kernel(place, *rest):
    notes, out = rest[:-1], rest[-1]
    cap = out.shape[1]
    slots = notes[0].shape[1]
    earlier = hot(iota((slots, slots), 0) < iota((slots, slots), 1))
    before = jnp.zeros((1, 1), F32)
    total = jnp.zeros(out.shape, F32)
    for note in notes:
        info = note[0:4, :]
        named = jnp.logical_and(info[0:1] == place[3].astype(F32), info[3:4] > 0.0)
        chosen = named.astype(F32)
        rank = dot(jnp.broadcast_to(chosen, (8, slots)).astype(BF16), earlier)[0:1] + before
        order = hot(jnp.logical_and(iota((cap, slots), 0) == rank, named))
        listed = jnp.concatenate(
            [info[1:2] * chosen, info[2:3] * chosen, chosen, jnp.zeros((5, slots), F32)], axis=0
        )
        total = total + dot(listed.astype(BF16), order, LANES)
        before = before + jnp.sum(chosen, axis=1, keepdims=True)
    out[...] = total


def lists_of(place, notes, cap):
    return pl.pallas_call(
        lists_kernel,
        in_specs=[SMEM] + [VMEM] * len(notes),
        out_specs=VMEM,
        out_shape=jax.ShapeDtypeStruct((8, cap), F32),
        cost_estimate=cost(1 << 22, 1 << 18),
        name="lists",
    )(place, *notes)


def columns_of(listed):
    cap = listed.shape[1]
    eye = hot(iota((cap, cap), 0) == iota((cap, cap), 1))
    return dot(eye, listed.astype(BF16), LANES)


def select_kernel(sources, place, *rest):
    blocks, pairs, wedge, out = rest[:sources], rest[sources:-4], rest[-4], rest[-3]
    rows_hot, wedge_hot = rest[-2:]
    bunches, height, depth = rows_hot.shape
    count = 2 * len(pairs)
    cap = wedge_hot.shape[0] // count
    bunch = height // cap
    rows = depth // bunch
    masks = wedge.shape[0]

    @pl.when(pl.program_id(0) == 0)
    def _():
        rows_hot[...] = jnp.zeros_like(rows_hot)
        for g in range(count):
            columns = columns_of(pairs[g // 2][g % 2])
            n, at = g // bunch, g % bunch
            rows_hot[n, at * cap : (at + 1) * cap, at * rows : (at + 1) * rows] = hot(
                iota((cap, rows), 1) == columns[:, 0:1]
            )
            marks = (iota((cap, masks), 1) == columns[:, 1:2]).astype(F32)
            wedge_hot[g * cap : (g + 1) * cap, :] = jnp.concatenate([marks] * 3, axis=1).astype(
                BF16
            )

    lined = jnp.concatenate(pieces_of(wedge[...], 3), axis=0)
    weights = dot(wedge_hot[...], lined)
    taken = 0
    for n in range(bunches):
        stack, have = [], 0
        while have < depth:
            stack.append(blocks[taken][...])
            have += blocks[taken].shape[0]
            taken += 1
        values = dot(rows_hot[n], jnp.concatenate(stack, axis=0) if len(stack) > 1 else stack[0])
        part = slice(n * height, (n + 1) * height)
        out[part, :] = (weights[part] * values).astype(BF16)


def select(place, blocks, block_specs, pairs, wedge, wedge_spec, rows, tile, steps):
    count = 2 * len(pairs)
    cap = pairs[0].shape[2]
    masks = wedge.shape[0]
    bunch = min(count, 256 // rows)
    return pl.pallas_call(
        functools.partial(select_kernel, len(blocks)),
        grid_spec=pltpu.PrefetchScalarGridSpec(
            num_scalar_prefetch=1,
            grid=(steps,),
            in_specs=[
                *block_specs,
                *[pl.BlockSpec((2, 8, cap), lambda t, s: (0, 0, 0))] * len(pairs),
                wedge_spec,
            ],
            out_specs=pl.BlockSpec((count * cap, tile), lambda t, s: (0, t)),
            scratch_shapes=[
                pltpu.VMEM((count // bunch, bunch * cap, bunch * rows), BF16),
                pltpu.VMEM((count * cap, 3 * masks), BF16),
            ],
        ),
        out_shape=jax.ShapeDtypeStruct((count * cap, steps * tile), BF16),
        cost_estimate=cost(
            4 * count * cap * 256 * steps * tile, 2 * count * (cap + rows) * steps * tile
        ),
        name="select",
    )(place, *blocks, *pairs, wedge)


def correl_kernel(blocks, scaled, *rest):
    refs, out, table = rest[:-2], rest[-2], rest[-1]
    per_ref = refs[0].shape[0]
    step = pl.program_id(0)
    half = pl.num_programs(0) // 2

    @pl.when(step == 0)
    def _():
        out[...] = jnp.zeros_like(out)

    def fill(side):
        for p in range(blocks):
            table[p * per_ref : (p + 1) * per_ref, :] = refs[2 * p + side][...]

    @pl.when(step < half)
    def _():
        fill(0)

    @pl.when(step >= half)
    def _():
        fill(1)

    out[...] += dot(scaled[...], table[...], LANES)


def correl(scaled, tables, tile):
    height, span = scaled.shape
    blocks = len(tables[0])
    per_ref = tables[0][0].shape[0]
    count = blocks * per_ref
    steps = span // tile
    half = steps // 2
    sides = [
        pl.BlockSpec((per_ref, tile), lambda t: (0, jnp.minimum(t, half - 1))),
        pl.BlockSpec((per_ref, tile), lambda t: (0, jnp.maximum(t - half, 0))),
    ]
    refs = [tables[i][p] for p in range(blocks) for i in range(2)]
    return pl.pallas_call(
        functools.partial(correl_kernel, blocks),
        grid=(steps,),
        in_specs=[pl.BlockSpec((height, tile), lambda t: (0, t))] + sides * blocks,
        out_specs=pl.BlockSpec((height, count), lambda t: (0, 0)),
        out_shape=jax.ShapeDtypeStruct((height, count), F32),
        scratch_shapes=[pltpu.VMEM((count, tile), BF16)],
        cost_estimate=cost(2 * height * count * span, 2 * span * (height + count)),
        name="correl",
    )(scaled, *refs)


def weigh_kernel(scale, masks, own, got, pair, *rest):
    notes, out = rest[:-1], rest[-1]
    count, cap = out.shape[1], out.shape[2]
    per_ref = count // len(notes)
    lanes = notes[0].shape[1]
    norms = jnp.zeros((3 * masks, count), F32)
    for p, note in enumerate(notes):
        parts = jnp.concatenate(pieces_of(note[8 : 8 + masks, :], 3), axis=0)
        shifted = hot(
            jnp.logical_and(
                iota((lanes, count), 0) + float(p * per_ref) == iota((lanes, count), 1),
                iota((lanes, count), 0) < float(per_ref),
            )
        )
        norms = norms + dot(parts, shifted)
    norms = norms.astype(BF16)
    for side in range(2):
        columns = columns_of(pair[side])
        marks = (iota((cap, masks), 1) == columns[:, 1:2]).astype(F32)
        wedge_hot = jnp.concatenate([marks] * 3, axis=1).astype(BF16)
        mine = own[side * cap : (side + 1) * cap, :] + got[(1 - side) * cap : (2 - side) * cap, :]
        score = (mine - 0.5 * dot(wedge_hot, norms)) * scale
        score = jnp.exp(score - jnp.max(score, axis=1, keepdims=True))
        share = score / jnp.sum(score, axis=1, keepdims=True) * columns[:, 2:3]
        out[side] = share.T.astype(BF16)


def weigh(own, got, pair, notes, masks, scale):
    cap, count = own.shape[0] // 2, own.shape[1]
    return pl.pallas_call(
        functools.partial(weigh_kernel, scale, masks),
        in_specs=[VMEM] * (3 + len(notes)),
        out_specs=VMEM,
        out_shape=jax.ShapeDtypeStruct((2, count, cap), BF16),
        cost_estimate=cost(1 << 24, 1 << 18),
        name="weigh",
    )(own, got, pair, *notes)


def blend_kernel(layers, parts, blocks, masks, steps, place, *rest):
    weights, rest = rest[:layers], rest[layers:]
    scaled, pairs = rest[:parts], rest[parts : -blocks - 1]
    outs, turned = rest[-blocks - 1 : -1], rest[-1]
    cap = weights[0].shape[2]
    per_ref = outs[0].shape[-2]

    @pl.when(pl.program_id(0) == 0)
    def _():
        for g in range(2 * layers):
            turned[:, g * cap : (g + 1) * cap] = weights[g // 2][g % 2]

    @pl.when(pl.program_id(0) < steps)
    def _():
        first = 0
        sums = 0.0
        for part in scaled:
            sums = sums + dot(turned[:, first : first + part.shape[0]], part[...])
            first += part.shape[0]
        sums = sums.astype(BF16)
        for p, out in enumerate(outs):
            out[...] = sums[p * per_ref : (p + 1) * per_ref, :].reshape(out.shape)

    if pairs:

        @pl.when(pl.program_id(0) == steps)
        def _():
            total = jnp.zeros((turned.shape[0], masks), F32)
            for g in range(2 * layers):
                marks = hot(iota((masks, cap), 0) == pairs[g // 2][g % 2, 1:2, :])
                total = total + dot(turned[:, g * cap : (g + 1) * cap], marks, LANES)
            split = jnp.concatenate(pieces_of(total, 3), axis=1)
            for p, out in enumerate(outs):
                out[:, : 3 * masks] = split[p * per_ref : (p + 1) * per_ref, :]


def blend(place, weights, pairs, scaled, masks, blocks, tile, steps, index):
    layers = len(weights)
    _, count, cap = weights[0].shape
    per_ref = count // blocks
    if pairs:
        shape = (per_ref, steps * tile + 128)
        spec = pl.BlockSpec((per_ref, tile), lambda t, s: (0, t))
    else:
        shape = (steps, per_ref, tile)
        spec = pl.BlockSpec((1, per_ref, tile), lambda t, s: (t, 0, 0))
    return pl.pallas_call(
        functools.partial(blend_kernel, layers, len(scaled), blocks, masks, steps),
        grid_spec=pltpu.PrefetchScalarGridSpec(
            num_scalar_prefetch=1,
            grid=(steps + (1 if pairs else 0),),
            in_specs=[pl.BlockSpec((2, count, cap), lambda t, s: (0, 0, 0))] * layers
            + [pl.BlockSpec((part.shape[0], tile), index) for part in scaled]
            + [pl.BlockSpec((2, 8, cap), lambda t, s: (0, 0, 0))] * len(pairs),
            out_specs=[spec] * blocks,
            scratch_shapes=[pltpu.VMEM((count, 2 * layers * cap), BF16)],
        ),
        out_shape=[jax.ShapeDtypeStruct(shape, BF16)] * blocks,
        cost_estimate=cost(
            4 * layers * cap * count * steps * tile, 2 * (2 * layers * cap + count) * steps * tile
        ),
        name="blend",
    )(place, *weights, *scaled, *pairs)


def fold_kernel(parts, *refs):
    sources, outs = refs[:parts], refs[parts:]
    for t, out in enumerate(outs):
        total = sources[0][t].astype(F32)
        for source in sources[1:]:
            total = total + source[t].astype(F32)
        out[...] = total.astype(BF16)


def fold(parts):
    layers, per_ref, tile = parts[0].shape
    return pl.pallas_call(
        functools.partial(fold_kernel, len(parts)),
        in_specs=[VMEM] * len(parts),
        out_specs=[VMEM] * layers,
        out_shape=[jax.ShapeDtypeStruct((per_ref, tile), BF16)] * layers,
        cost_estimate=cost(0, 2 * (len(parts) + 1) * layers * per_ref * tile),
        name="fold",
    )(*parts)


def finish_kernel(blocks, place, *rest):
    shares, apart = rest[:blocks], rest[blocks:-6]
    wedge, out, tables, held, came, went = rest[-6:]
    masks = wedge.shape[0]
    span = tables.shape[1]
    tile = held.shape[2]
    at = pl.multiple_of(place[1] * span, span)
    fetch = pltpu.make_async_copy(wedge.at[:, pl.ds(at, span)], tables, came)
    fetch.start()
    keep = span - tile
    mass = 0.0
    for part in shares:
        mass = mass + part[:, keep : keep + 3 * masks].astype(F32)
    mass = mass[:, :masks] + mass[:, masks : 2 * masks] + mass[:, 2 * masks : 3 * masks]
    fetch.wait()
    leaves = []
    for t in range(SPLIT):
        cols = slice(t * tile, (t + 1) * tile)
        below = jnp.ones(held.shape[1:], F32)
        for w in range(masks):
            below = below + mass[:, w : w + 1] * tables[w : w + 1, cols]
        total = 0.0
        for part in shares if t < SPLIT - 1 else apart:
            total = total + (part[:, cols] if t < SPLIT - 1 else part[...]).astype(F32)
        held[t] = total / below
        leave = pltpu.make_async_copy(held.at[t], out.at[:, pl.ds(t * tile, tile)], went.at[t])
        leave.start()
        leaves.append(leave)
    for leave in leaves:
        leave.wait()


def finish(place, shares, apart, wedge, tile):
    per_ref = shares[0].shape[0]
    masks = wedge.shape[0]
    blocks = len(shares)
    anywhere = pl.BlockSpec(memory_space=pl.ANY)
    return pl.pallas_call(
        functools.partial(finish_kernel, blocks),
        in_specs=[SMEM] + [VMEM] * (blocks + len(apart)) + [anywhere],
        out_specs=anywhere,
        out_shape=jax.ShapeDtypeStruct((per_ref, SPLIT * tile), F32),
        scratch_shapes=[
            pltpu.VMEM((masks, SPLIT * tile), F32),
            pltpu.VMEM((SPLIT, per_ref, tile), F32),
            pltpu.SemaphoreType.DMA,
            pltpu.SemaphoreType.DMA((SPLIT,)),
        ],
        cost_estimate=cost(0, 8 * per_ref * SPLIT * tile),
        name="finish",
    )(place, *shares, *apart, wedge)


GRP = ("lay", "core")


def passed(values, axis, size):
    return [values[0]] + [
        lax.ppermute(values[p], axis, [(d, d ^ p) for d in range(size)]) for p in range(1, size)
    ]


def per_device(slab, pick_owner, pick_offset, wedge_id, live_count, references, wedge):
    slot_count, voxels = slab.shape
    masks = wedge.shape[0]
    layers = lax.axis_size("lay")
    groups = 2 * layers
    blocks = lax.axis_size("blk")
    per_vox = voxels // groups
    tile = per_vox // SPLIT
    keep = per_vox - tile
    half_steps = voxels // 2 // tile
    cap = 2 * slot_count
    block = lax.axis_index("blk").astype(jnp.int32)
    core = lax.axis_index("core").astype(jnp.int32)
    layer = lax.axis_index("lay").astype(jnp.int32)
    place = jnp.stack([core, layer * 2 + core, layer, block])

    low, high, aside = cut(place, references, slab, layers, per_vox)
    mate = lax.ppermute(aside, "core", [(0, 1), (1, 0)])
    if blocks == 4:
        over_x, over_y = [(b, b ^ 1) for b in range(4)], [(b, b ^ 2) for b in range(4)]
        low_x = lax.ppermute(low, "blk", over_x)
        high_y = lax.ppermute(high, "blk", over_y)
        high_x = lax.ppermute(high, "blk", over_x)
        low_y = lax.ppermute(low, "blk", over_y)
        low_xy = lax.ppermute(low_x, "blk", over_y)
        high_xy = lax.ppermute(high_y, "blk", over_x)
        tables = [[low, low_x, low_y, low_xy], [high, high_x, high_y, high_xy]]
    else:
        tables = [passed([s] * blocks, "blk", blocks) for s in (low, high)]
    far = deal(place, slab, mate, layers, keep)
    nearby = layers // 2
    pieces = [None] * layers
    for p in range(1, layers):
        pieces[p] = lax.ppermute(far[p - 1], "lay", [(z, z ^ p) for z in range(layers)])
    note = brief(
        live_count,
        references,
        wedge,
        pick_owner.reshape(1, slot_count),
        pick_offset.reshape(1, slot_count),
        wedge_id.reshape(1, slot_count),
        per_vox,
    )
    notes = passed([note] * blocks, "blk", blocks)
    listed = lists_of(place, notes, cap)
    pair = jnp.stack(passed([listed] * 2, "core", 2))
    pairs = passed([pair] * layers, "lay", layers)

    def local(t, s, split=SPLIT):
        return (0, (2 * (t // split) + s[0]) * split + t % split)

    def here(t, s):
        return (0, s[1] * SPLIT + t)

    wide = functools.partial(local, split=SPLIT // 2)
    scaled = select(
        place,
        [slab, mate],
        [
            pl.BlockSpec((slot_count, 2 * tile), wide),
            pl.BlockSpec((slot_count, 2 * tile), lambda t, s: (0, t)),
        ],
        [pair],
        wedge,
        pl.BlockSpec((masks, 2 * tile), wide),
        slot_count,
        2 * tile,
        half_steps // 2,
    )
    sums = correl(scaled, tables, tile)
    got = lax.ppermute(sums, "core", [(0, 1), (1, 0)])
    weights = weigh(sums, got, pair, notes, masks, 1.0 / (32.0 * math.sqrt(voxels)))
    all_weights = passed([weights] * layers, "lay", layers)

    received = pl.BlockSpec((2 * slot_count, tile), lambda t, s: (0, t))
    near_rows = select(
        place,
        [slab, mate, *pieces[1:nearby]],
        [
            pl.BlockSpec((slot_count, tile), here),
            pl.BlockSpec((slot_count, tile), lambda t, s: (0, s[2] * SPLIT + t)),
        ]
        + [received] * (nearby - 1),
        pairs[:nearby],
        wedge,
        pl.BlockSpec((masks, tile), here),
        slot_count,
        tile,
        SPLIT - 1,
    )
    far_rows = select(
        place,
        pieces[nearby:],
        [received] * (layers - nearby),
        pairs[nearby:],
        wedge,
        pl.BlockSpec((masks, tile), here),
        slot_count,
        tile,
        SPLIT - 1,
    )

    apart = blend(
        place,
        all_weights[:1],
        [],
        [scaled],
        masks,
        blocks,
        tile,
        layers,
        lambda t, s: (0, (s[2] ^ t) * SPLIT + SPLIT - 1),
    )
    apart = passed(apart, "blk", blocks)
    apart = fold(apart)
    apart = passed(apart, "lay", layers)

    shares = blend(
        place,
        all_weights,
        pairs,
        [near_rows, far_rows],
        masks,
        blocks,
        tile,
        SPLIT - 1,
        lambda t, s: (0, jnp.minimum(t, SPLIT - 2)),
    )
    shares = passed(shares, "blk", blocks)
    return finish(place, shares, apart, wedge, tile)


def solution(mesh):
    groups, blocks = mesh.shape["grp"], mesh.shape["blk"]
    fine = Mesh(mesh.devices.reshape(groups // 2, 2, blocks), ("lay", "core", "blk"))
    every = ("lay", "core", "blk")
    placed = (P(every, None), P(every, None), P(every), P(every), P(every), P("blk", None), P())

    return jax.shard_map(
        per_device, mesh=fine, in_specs=placed, out_specs=P("blk", GRP), check_vma=False
    )
```

time: 267 us -> 180 us (0.67)
  waiting for transfers between devices: 125 us -> 52.4 us
  starting transfers between devices: 64.9 us -> 45.1 us
  Pallas kernels: 69 us -> 73.4 us
    ppermute x30 -> x19, waiting for transfers between devices: 101 us -> 40.5 us  [passed(): lax.ppermute(values[p], axis, [(d, d ^ p) for d in range(size)])]
    ppermute x30 -> x19, starting transfers between devices: 55.9 us -> 29.4 us  [passed(): lax.ppermute(values[p], axis, [(d, d ^ p) for d in range(size)])]
    ppermute x7 -> x10, waiting for transfers between devices: 23.5 us -> 11.9 us  [the longest x1 7.24 us: per_device(): high_x = lax.ppermute(high, 'blk', over_x)]
    ppermute x7 -> x10, starting transfers between devices: 8.44 us -> 15.2 us  [the longest x3 6.26 us: per_device(): lax.ppermute(far[p - 1], 'lay', [(z, z ^ p) for z in range(layers)])]
    pallas_call x10 -> x11, Pallas kernels: 62.9 us -> 67.3 us  [the longest x3 23 us: select(): pl.pallas_call(functools.partial(select_kernel, len(blocks)), grid_spec=p...]
    unnamed x80 -> x50, local copies, waits for them, and re-layouts: 4.3 us -> 5.61 us
  transfers between devices with their start and end apart: 38 -> 30, of which waited for: 14 -> 11; matrix products, arithmetic and copies ran while one was open for 0% -> 1% of each run, Pallas kernels for 23% -> 37%
where the time goes in v4:
time: 180 us; the launch traced here: 179 us
  Pallas kernels  73.4 us (41%)
  waiting for transfers between devices  52.4 us (29%)
  starting transfers between devices  45.1 us (25%)
  local copies, waits for them, and re-layouts  5.61 us (3%)
  other arithmetic  1.86 us (1%)
    ppermute x19, waiting for transfers between devices, passed(): lax.ppermute(values[p], axis, [(d, d ^ p) for d in range(size)])  40.5 us
    ppermute x19, starting transfers between devices, passed(): lax.ppermute(values[p], axis, [(d, d ^ p) for d in range(size)])  29.4 us
    pallas_call x3, Pallas kernels, select(): pl.pallas_call(functools.partial(select_kernel, len(blocks)), grid_spec=p...  23 us
    pallas_call x1, Pallas kernels, correl(): pl.pallas_call(functools.partial(correl_kernel, blocks), grid=(steps,), i...  13.9 us
    pallas_call x2, Pallas kernels, blend(): pl.pallas_call(functools.partial(blend_kernel, layers, len(scaled), block...  11.5 us
    ppermute x1, waiting for transfers between devices, per_device(): high_x = lax.ppermute(high, 'blk', over_x)  7.24 us
    pallas_call x1, Pallas kernels, brief(): pl.pallas_call(brief_kernel, grid_spec=pltpu.PrefetchScalarGridSpec(num_s...  6.87 us
    ppermute x3, starting transfers between devices, per_device(): lax.ppermute(far[p - 1], 'lay', [(z, z ^ p) for z in range(layers)])  6.26 us
  transfers between devices with their start and end apart: 30, of which 11 were waited for; matrix products, arithmetic and copies ran while one was open for 1% of the time, Pallas kernels for 37%

profile of v4, /device:TPU:0, one launch (start us, length us, event | category | flops | bytes accessed | tf_op | source)
XLA Modules:
  0.0 179.2 jit_solution(15686954906135344270)
XLA Ops:
  0.6 3.9 %cut.1 = (bf16[48,8192]{1,0:T(8,128)(2,1)}, bf16[48,8192]{1,0:T(8,128)(2,1)}, bf16[64,16384]{1,0:T(8,128)(2,1)}) custom-call(s32[4]{0:T(128)} %pad_add_fusion.place, bf16[48,32768]{1,0:T(8,128)(2,1)} %refs.3, bf16[64,32768]{1,0:T(8,128)(2,1)} %rest_0_.3), custom_call_target="tpu_custom_call" | custom-call | bytes 7340032 | tf_op jit(solution)/shard_map/cut/pallas_call | solution.py:87
  5.1 2.6 %collective-permute-start.8 = (bf16[48,8192]{1,0:T(8,128)(2,1)}, bf16[48,8192]{1,0:T(8,128)(2,1)}, u32[]{:S(2)}, u32[]{:S(2)}) collective-permute-start(bf16[48,8192]{1,0:T(8,128)(2,1)} %get-tuple-element.25.rest_1_), channel_id=1, source_target_pairs={{0,2},{1,3},{2,0},{3,1},{4,6},{5,7},{6,4},{7,5},{8,10},{9,11},{10,... | collective-permute-start | bytes 2359304 | tf_op jit(solution)/shard_map/ppermute | solution.py:567
  9.8 6.9 %brief.1.rest_0_ = f32[16,128]{1,0:T(8,128)} custom-call(s32[1]{0:T(128)S(6)} %copy.8.live, bf16[48,32768]{1,0:T(8,128)(2,1)} %refs.3, f32[8,32768]{1,0:T(8,128)} %rest_8_.1, s32[1,64]{1,0:T(1,128)} %bitcast.11, s32[1,64]{1,0:T(1,128)} %bitcast.12, s32[1,64]{1,0:T(1,128)} %bitcast.13), custom_call_target="tpu_custom_call" | custom-call | flops 150994944 | bytes 4194304 | tf_op jit(solution)/shard_map/brief/pallas_call | solution.py:184
  17.3 10.4 %collective-permute-done.1.rest_1_ = f32[16,128]{1,0:T(8,128)S(1)} collective-permute-done((f32[16,128]{1,0:T(8,128)}, f32[16,128]{1,0:T(8,128)S(1)}, u32[]{:S(2)}, u32[]{:S(2)}) %collective-permute-start.1) | collective-permute-done | bytes 8224 | tf_op jit(solution)/shard_map/ppermute | solution.py:542
  29.1 3.3 %collective-permute-done.3.rest_3_ = f32[16,128]{1,0:T(8,128)S(1)} collective-permute-done((f32[16,128]{1,0:T(8,128)}, f32[16,128]{1,0:T(8,128)S(1)}, u32[]{:S(2)}, u32[]{:S(2)}) %collective-permute-start.3) | collective-permute-done | bytes 8224 | tf_op jit(solution)/shard_map/ppermute | solution.py:542
  42.4 3.3 %deal.1 = (bf16[128,3072]{1,0:T(8,128)(2,1)}, bf16[128,3072]{1,0:T(8,128)(2,1)}, bf16[128,3072]{1,0:T(8,128)(2,1)}) custom-call(s32[4]{0:T(128)} %pad_add_fusion.place, bf16[64,32768]{1,0:T(8,128)(2,1)} %rest_0_.3, bf16[64,16384]{1,0:T(8,128)(2,1)} %copy-done), custom_call_target="tpu_custom_call" | custom-call | bytes 4718592 | tf_op jit(solution)/shard_map/deal/pallas_call | solution.py:136
  45.7 2.7 %collective-permute-start.17 = (bf16[128,3072]{1,0:T(8,128)(2,1)}, bf16[128,3072]{1,0:T(8,128)(2,1)S(1)}, u32[]{:S(2)}, u32[]{:S(2)}) collective-permute-start(bf16[128,3072]{1,0:T(8,128)(2,1)} %get-tuple-element.27), channel_id=1, source_target_pairs={{0,16},{8,24},{16,0},{24,8},{1,17},{9,25},{17,1},{25,9},{2,18},{10... | collective-permute-start | bytes 2359304 | tf_op jit(solution)/shard_map/ppermute | solution.py:579
  48.4 7.2 %collective-permute-done.6.rest_3_ = bf16[48,8192]{1,0:T(8,128)(2,1)} collective-permute-done((bf16[48,8192]{1,0:T(8,128)(2,1)}, bf16[48,8192]{1,0:T(8,128)(2,1)}, u32[]{:S(2)}, u32[]{:S(2)}) %collective-permute-start.6) | collective-permute-done | bytes 786464 | tf_op jit(solution)/shard_map/ppermute | solution.py:568
  55.6 3.6 %collective-permute-start.18 = (bf16[128,3072]{1,0:T(8,128)(2,1)}, bf16[128,3072]{1,0:T(8,128)(2,1)}, u32[]{:S(2)}, u32[]{:S(2)}) collective-permute-start(bf16[128,3072]{1,0:T(8,128)(2,1)} %get-tuple-element.28), channel_id=1, source_target_pairs={{0,24},{8,16},{16,8},{24,0},{1,25},{9,17},{17,9},{25,1},{2,26},{10... | collective-permute-start | bytes 2359304 | tf_op jit(solution)/shard_map/ppermute | solution.py:579
  59.2 10.9 %select.3.scaled.rest_1_ = bf16[256,16384]{1,0:T(8,128)(2,1)} custom-call(s32[4]{0:T(128)} %pad_add_fusion.place, bf16[64,32768]{1,0:T(8,128)(2,1)} %rest_0_.3, bf16[64,16384]{1,0:T(8,128)(2,1)} %copy-done, f32[2,8,128]{2,1,0:T(8,128)} %pad_maximum_fusion.rest_2_.pair.rest_3_.rest_6_, f32[8,32768]{1,0:T(8,128)} %rest_8_.1), custom_call_target="tpu_custom_call" | custom-call | flops 4294967296 | bytes 12582912 | tf_op jit(solution)/shard_map/select/pallas_call | solution.py:286
  73.0 13.9 %correl.1.own = f32[256,192]{1,0:T(8,128)} custom-call(bf16[256,16384]{1,0:T(8,128)(2,1)} %select.3.scaled.rest_1_, bf16[48,8192]{1,0:T(8,128)(2,1)} %get-tuple-element.24.rest_0_, bf16[48,8192]{1,0:T(8,128)(2,1)} %get-tuple-element.25.rest_1_, bf16[48,8192]{1,0:T(8,128)(2,1)} %collective-permute-done.5.rest_2_, ...), custom_call_target="tpu_custom_call" | custom-call | flops 1610612736 | bytes 14680064 | tf_op jit(solution)/shard_map/correl/pallas_call | solution.py:347
  89.4 2.8 %weigh.1.rest_0_ = bf16[2,192,128]{2,1,0:T(8,128)(2,1)} custom-call(f32[256,192]{1,0:T(8,128)} %correl.1.own, f32[256,192]{1,0:T(8,128)} %copy-done.10, f32[2,8,128]{2,1,0:T(8,128)} %pad_maximum_fusion.rest_2_.pair.rest_3_.rest_6_, f32[16,128]{1,0:T(8,128)} %brief.1.rest_0_, f32[16,128]{1,0:T(8,128)} %copy-done.18, f32[16,128]{1,0:T(8,128)} %copy-done.19, ...), custom_call_target="tpu_custom_call" | custom-call | flops 16777216 | bytes 262144 | tf_op jit(solution)/shard_map/weigh/pallas_call | solution.py:388
  93.8 2.6 %collective-permute-start.19 = (f32[2,8,128]{2,1,0:T(8,128)S(1)}, f32[2,8,128]{2,1,0:T(8,128)S(1)}, u32[]{:S(2)}, u32[]{:S(2)}) collective-permute-start(f32[2,8,128]{2,1,0:T(8,128)S(1)} %copy-done.11), channel_id=1, source_target_pairs={{0,16},{8,24},{16,0},{24,8},{1,17},{9,25},{17,1},{25,9},{2,18},{10... | collective-permute-start | bytes 24584 | tf_op jit(solution)/shard_map/ppermute | solution.py:542
  96.4 20.2 %collective-permute-done.19.rest_2_.rest_8_ = f32[2,8,128]{2,1,0:T(8,128)S(1)} collective-permute-done((f32[2,8,128]{2,1,0:T(8,128)S(1)}, f32[2,8,128]{2,1,0:T(8,128)S(1)}, u32[]{:S(2)}, u32[]{:S(2)}) %collective-permute-start.19) | collective-permute-done | bytes 8224 | tf_op jit(solution)/shard_map/ppermute | solution.py:542
  116.6 3.5 %collective-permute-start.20 = (f32[2,8,128]{2,1,0:T(8,128)S(1)}, f32[2,8,128]{2,1,0:T(8,128)S(1)}, u32[]{:S(2)}, u32[]{:S(2)}) collective-permute-start(f32[2,8,128]{2,1,0:T(8,128)S(1)} %copy-done.11), channel_id=1, source_target_pairs={{0,24},{8,16},{16,8},{24,0},{1,25},{9,17},{17,9},{25,1},{2,26},{10... | collective-permute-start | bytes 24584 | tf_op jit(solution)/shard_map/ppermute | solution.py:542
  122.1 4.9 %blend.3 = (bf16[4,48,1024]{2,1,0:T(8,128)(2,1)}, bf16[4,48,1024]{2,1,0:T(8,128)(2,1)}, bf16[4,48,1024]{2,1,0:T(8,128)(2,1)}, bf16[4,48,1024]{2,1,0:T(8,128)(2,1)}) custom-call(s32[4]{0:T(128)} %pad_add_fusion.place, bf16[2,192,128]{2,1,0:T(8,128)(2,1)} %weigh.1.rest_0_, bf16[256,16384]{1,0:T(8,128)(2,1)} %select.3.scaled.rest_1_), custom_call_target="tpu_custom_call" | custom-call | flops 402653184 | bytes 3670016 | tf_op jit(solution)/shard_map/blend/pallas_call | solution.py:444
  130.6 6.1 %select.4.rest_4_ = bf16[512,3072]{1,0:T(8,128)(2,1)} custom-call(s32[4]{0:T(128)} %pad_add_fusion.place, bf16[64,32768]{1,0:T(8,128)(2,1)} %rest_0_.3, bf16[64,16384]{1,0:T(8,128)(2,1)} %copy-done, bf16[128,3072]{1,0:T(8,128)(2,1)} %copy-done.3, f32[2,8,128]{2,1,0:T(8,128)} %pad_maximum_fusion.rest_2_.pair.rest_3_.rest_6_, f32[2,8,128]{2,1,0:T(8,128)} %copy-done.21, ...), custom_call_target="tpu_custom_call" | custom-call | flops 1610612736 | bytes 4718592 | tf_op jit(solution)/shard_map/select/pallas_call | solution.py:286
  136.8 4.1 %collective-permute-start.13 = (bf16[2,192,128]{2,1,0:T(8,128)(2,1)S(1)}, bf16[2,192,128]{2,1,0:T(8,128)(2,1)S(1)}, u32[]{:S(2)}, u32[]{:S(2)}) collective-permute-start(bf16[2,192,128]{2,1,0:T(8,128)(2,1)S(1)} %copy-done.1), channel_id=1, source_target_pairs={{0,16},{8,24},{16,0},{24,8},{1,17},{9,25},{17,1},{25,9},{2,18},{10... | collective-permute-start | bytes 294920 | tf_op jit(solution)/shard_map/ppermute | solution.py:542
  141.2 6.0 %select.5.rest_5_ = bf16[512,3072]{1,0:T(8,128)(2,1)} custom-call(s32[4]{0:T(128)} %pad_add_fusion.place, bf16[128,3072]{1,0:T(8,128)(2,1)} %copy-done.24, bf16[128,3072]{1,0:T(8,128)(2,1)} %collective-permute-done.18.rest_1_, f32[2,8,128]{2,1,0:T(8,128)} %copy-done.22, f32[2,8,128]{2,1,0:T(8,128)} %copy-done.23, f32[8,32768]{1,0:T(8,128)} %rest_8_.1), custom_call_target="tpu_custom_call" | custom-call | flops 1610612736 | bytes 4718592 | tf_op jit(solution)/shard_map/select/pallas_call | solution.py:286
  148.5 6.6 %blend.2 = (bf16[48,3200]{1,0:T(8,128)(2,1)}, bf16[48,3200]{1,0:T(8,128)(2,1)}, bf16[48,3200]{1,0:T(8,128)(2,1)}, bf16[48,3200]{1,0:T(8,128)(2,1)}) custom-call(s32[4]{0:T(128)} %pad_add_fusion.place, bf16[2,192,128]{2,1,0:T(8,128)(2,1)} %weigh.1.rest_0_, bf16[2,192,128]{2,1,0:T(8,128)(2,1)} %copy-done.15, bf16[2,192,128]{2,1,0:T(8,128)(2,1)} %copy-done.16, ...), custom_call_target="tpu_custom_call" | custom-call | flops 1207959552 | bytes 7471104 | tf_op jit(solution)/shard_map/blend/pallas_call | solution.py:444
  162.1 3.7 %collective-permute-start.28 = (bf16[48,1024]{1,0:T(8,128)(2,1)}, bf16[48,1024]{1,0:T(8,128)(2,1)S(1)}, u32[]{:S(2)}, u32[]{:S(2)}) collective-permute-start(bf16[48,1024]{1,0:T(8,128)(2,1)} %get-tuple-element.39), channel_id=1, source_target_pairs={{0,16},{8,24},{16,0},{24,8},{1,17},{9,25},{17,1},{25,9},{2,18},{10... | collective-permute-start | bytes 294920 | tf_op jit(solution)/shard_map/ppermute | solution.py:542
  167.5 4.1 %collective-permute-start.29 = (bf16[48,1024]{1,0:T(8,128)(2,1)}, bf16[48,1024]{1,0:T(8,128)(2,1)S(1)}, u32[]{:S(2)}, u32[]{:S(2)}) collective-permute-start(bf16[48,1024]{1,0:T(8,128)(2,1)} %get-tuple-element.40), channel_id=1, source_target_pairs={{0,24},{8,16},{16,8},{24,0},{1,25},{9,17},{17,9},{25,1},{2,26},{10... | collective-permute-start | bytes 294920 | tf_op jit(solution)/shard_map/ppermute | solution.py:542
  171.6 2.8 %collective-permute-done.29.rest_7_ = bf16[48,1024]{1,0:T(8,128)(2,1)S(1)} collective-permute-done((bf16[48,1024]{1,0:T(8,128)(2,1)}, bf16[48,1024]{1,0:T(8,128)(2,1)S(1)}, u32[]{:S(2)}, u32[]{:S(2)}) %collective-permute-start.29) | collective-permute-done | bytes 98336 | tf_op jit(solution)/shard_map/ppermute | solution.py:542
  175.3 3.9 %finish.1 = f32[48,4096]{1,0:T(8,128)} custom-call(s32[4]{0:T(128)} %pad_add_fusion.place, bf16[48,3200]{1,0:T(8,128)(2,1)} %get-tuple-element.29.rest_0_, bf16[48,3200]{1,0:T(8,128)(2,1)} %copy-done.7, bf16[48,3200]{1,0:T(8,128)(2,1)} %copy-done.8, bf16[48,3200]{1,0:T(8,128)(2,1)} %copy-done.9, bf16[48,1024]{1,0:T(8,128)(2,1)} %get-tuple-element.37.rest_4_, ...), custom_call_target="tpu_custom_call" | custom-call | bytes 1572864 | tf_op jit(solution)/shard_map/finish/pallas_call | solution.py:521
  (101 shorter events, 38.4 us)
Async XLA Ops:
  4.5 36.6 %collective-permute-start = (bf16[64,16384]{1,0:T(8,128)(2,1)}, bf16[64,16384]{1,0:T(8,128)(2,1)S(1)}, u32[]{:S(2)}, u32[]{:S(2)}) collective-permute-start(bf16[64,16384]{1,0:T(8,128)(2,1)} %get-tuple-element.23), channel_id=1, source_target_pairs={{0,4},{4,0},{1,5},{5,1},{2,6},{6,2},{3,7},{7,3},{8,12},{12,8},{9,1... | collective-permute-start | bytes 6291464 | tf_op jit(solution)/shard_map/ppermute | solution.py:563
  5.1 31.8 %collective-permute-start.8 = (bf16[48,8192]{1,0:T(8,128)(2,1)}, bf16[48,8192]{1,0:T(8,128)(2,1)}, u32[]{:S(2)}, u32[]{:S(2)}) collective-permute-start(bf16[48,8192]{1,0:T(8,128)(2,1)} %get-tuple-element.25.rest_1_), channel_id=1, source_target_pairs={{0,2},{1,3},{2,0},{3,1},{4,6},{5,7},{6,4},{7,5},{8,10},{9,11},{10,... | collective-permute-start | bytes 2359304 | tf_op jit(solution)/shard_map/ppermute | solution.py:567
  7.6 30.6 %collective-permute-start.5 = (bf16[48,8192]{1,0:T(8,128)(2,1)}, bf16[48,8192]{1,0:T(8,128)(2,1)}, u32[]{:S(2)}, u32[]{:S(2)}) collective-permute-start(bf16[48,8192]{1,0:T(8,128)(2,1)} %get-tuple-element.24.rest_0_), channel_id=1, source_target_pairs={{0,1},{1,0},{2,3},{3,2},{4,5},{5,4},{6,7},{7,6},{8,9},{9,8},{10,11... | collective-permute-start | bytes 2359304 | tf_op jit(solution)/shard_map/ppermute | solution.py:566
  16.7 11.0 %collective-permute-start.1 = (f32[16,128]{1,0:T(8,128)}, f32[16,128]{1,0:T(8,128)S(1)}, u32[]{:S(2)}, u32[]{:S(2)}) collective-permute-start(f32[16,128]{1,0:T(8,128)} %brief.1.rest_0_), channel_id=1, source_target_pairs={{0,1},{1,0},{2,3},{3,2},{4,5},{5,4},{6,7},{7,6},{8,9},{9,8},{10,11... | collective-permute-start | bytes 24584 | tf_op jit(solution)/shard_map/ppermute | solution.py:542
  17.2 11.9 %collective-permute-start.2 = (f32[16,128]{1,0:T(8,128)}, f32[16,128]{1,0:T(8,128)S(1)}, u32[]{:S(2)}, u32[]{:S(2)}) collective-permute-start(f32[16,128]{1,0:T(8,128)} %brief.1.rest_0_), channel_id=1, source_target_pairs={{0,2},{1,3},{2,0},{3,1},{4,6},{5,7},{6,4},{7,5},{8,10},{9,11},{10,... | collective-permute-start | bytes 24584 | tf_op jit(solution)/shard_map/ppermute | solution.py:542
  34.9 20.7 %collective-permute-start.6 = (bf16[48,8192]{1,0:T(8,128)(2,1)}, bf16[48,8192]{1,0:T(8,128)(2,1)}, u32[]{:S(2)}, u32[]{:S(2)}) collective-permute-start(bf16[48,8192]{1,0:T(8,128)(2,1)} %get-tuple-element.25.rest_1_), channel_id=1, source_target_pairs={{0,1},{1,0},{2,3},{3,2},{4,5},{5,4},{6,7},{7,6},{8,9},{9,8},{10,11... | collective-permute-start | bytes 2359304 | tf_op jit(solution)/shard_map/ppermute | solution.py:568
  36.4 22.8 %collective-permute-start.7 = (bf16[48,8192]{1,0:T(8,128)(2,1)S(1)}, bf16[48,8192]{1,0:T(8,128)(2,1)}, u32[]{:S(2)}, u32[]{:S(2)}) collective-permute-start(bf16[48,8192]{1,0:T(8,128)(2,1)S(1)} %copy-done.2), channel_id=1, source_target_pairs={{0,2},{1,3},{2,0},{3,1},{4,6},{5,7},{6,4},{7,5},{8,10},{9,11},{10,... | collective-permute-start | bytes 2359304 | tf_op jit(solution)/shard_map/ppermute | solution.py:569
  36.9 35.1 %collective-permute-start.10 = (bf16[48,8192]{1,0:T(8,128)(2,1)}, bf16[48,8192]{1,0:T(8,128)(2,1)}, u32[]{:S(2)}, u32[]{:S(2)}) collective-permute-start(bf16[48,8192]{1,0:T(8,128)(2,1)} %collective-permute-done.8.rest_5_), channel_id=1, source_target_pairs={{0,1},{1,0},{2,3},{3,2},{4,5},{5,4},{6,7},{7,6},{8,9},{9,8},{10,11... | collective-permute-start | bytes 2359304 | tf_op jit(solution)/shard_map/ppermute | solution.py:571
  38.3 34.7 %collective-permute-start.9 = (bf16[48,8192]{1,0:T(8,128)(2,1)}, bf16[48,8192]{1,0:T(8,128)(2,1)}, u32[]{:S(2)}, u32[]{:S(2)}) collective-permute-start(bf16[48,8192]{1,0:T(8,128)(2,1)} %collective-permute-done.5.rest_2_), channel_id=1, source_target_pairs={{0,2},{1,3},{2,0},{3,1},{4,6},{5,7},{6,4},{7,5},{8,10},{9,11},{10,... | collective-permute-start | bytes 2359304 | tf_op jit(solution)/shard_map/ppermute | solution.py:570
  45.7 91.0 %collective-permute-start.17 = (bf16[128,3072]{1,0:T(8,128)(2,1)}, bf16[128,3072]{1,0:T(8,128)(2,1)S(1)}, u32[]{:S(2)}, u32[]{:S(2)}) collective-permute-start(bf16[128,3072]{1,0:T(8,128)(2,1)} %get-tuple-element.27), channel_id=1, source_target_pairs={{0,16},{8,24},{16,0},{24,8},{1,17},{9,25},{17,1},{25,9},{2,18},{10... | collective-permute-start | bytes 2359304 | tf_op jit(solution)/shard_map/ppermute | solution.py:579
  55.6 85.3 %collective-permute-start.18 = (bf16[128,3072]{1,0:T(8,128)(2,1)}, bf16[128,3072]{1,0:T(8,128)(2,1)}, u32[]{:S(2)}, u32[]{:S(2)}) collective-permute-start(bf16[128,3072]{1,0:T(8,128)(2,1)} %get-tuple-element.28), channel_id=1, source_target_pairs={{0,24},{8,16},{16,8},{24,0},{1,25},{9,17},{17,9},{25,1},{2,26},{10... | collective-permute-start | bytes 2359304 | tf_op jit(solution)/shard_map/ppermute | solution.py:579
  59.2 69.1 %collective-permute-start.15 = (bf16[128,3072]{1,0:T(8,128)(2,1)}, bf16[128,3072]{1,0:T(8,128)(2,1)S(1)}, u32[]{:S(2)}, u32[]{:S(2)}) collective-permute-start(bf16[128,3072]{1,0:T(8,128)(2,1)} %get-tuple-element.26), channel_id=1, source_target_pairs={{0,8},{8,0},{16,24},{24,16},{1,9},{9,1},{17,25},{25,17},{2,10},{10... | collective-permute-start | bytes 2359304 | tf_op jit(solution)/shard_map/ppermute | solution.py:579
  92.3 35.6 %collective-permute-start.12 = (bf16[2,192,128]{2,1,0:T(8,128)(2,1)}, bf16[2,192,128]{2,1,0:T(8,128)(2,1)S(1)}, u32[]{:S(2)}, u32[]{:S(2)}) collective-permute-start(bf16[2,192,128]{2,1,0:T(8,128)(2,1)} %weigh.1.rest_0_), channel_id=1, source_target_pairs={{0,8},{8,0},{16,24},{24,16},{1,9},{9,1},{17,25},{25,17},{2,10},{10... | collective-permute-start | bytes 294920 | tf_op jit(solution)/shard_map/ppermute | solution.py:542
  93.8 22.8 %collective-permute-start.19 = (f32[2,8,128]{2,1,0:T(8,128)S(1)}, f32[2,8,128]{2,1,0:T(8,128)S(1)}, u32[]{:S(2)}, u32[]{:S(2)}) collective-permute-start(f32[2,8,128]{2,1,0:T(8,128)S(1)} %copy-done.11), channel_id=1, source_target_pairs={{0,16},{8,24},{16,0},{24,8},{1,17},{9,25},{17,1},{25,9},{2,18},{10... | collective-permute-start | bytes 24584 | tf_op jit(solution)/shard_map/ppermute | solution.py:542
  127.0 29.6 %collective-permute-start.24 = (bf16[4,48,1024]{2,1,0:T(8,128)(2,1)}, bf16[4,48,1024]{2,1,0:T(8,128)(2,1)S(1)}, u32[]{:S(2)}, u32[]{:S(2)}) collective-permute-start(bf16[4,48,1024]{2,1,0:T(8,128)(2,1)} %get-tuple-element.34), channel_id=1, source_target_pairs={{0,1},{1,0},{2,3},{3,2},{4,5},{5,4},{6,7},{7,6},{8,9},{9,8},{10,11... | collective-permute-start | bytes 1179656 | tf_op jit(solution)/shard_map/ppermute | solution.py:542
  127.8 30.8 %collective-permute-start.25 = (bf16[4,48,1024]{2,1,0:T(8,128)(2,1)}, bf16[4,48,1024]{2,1,0:T(8,128)(2,1)S(1)}, u32[]{:S(2)}, u32[]{:S(2)}) collective-permute-start(bf16[4,48,1024]{2,1,0:T(8,128)(2,1)} %get-tuple-element.35), channel_id=1, source_target_pairs={{0,2},{1,3},{2,0},{3,1},{4,6},{5,7},{6,4},{7,5},{8,10},{9,11},{10,... | collective-permute-start | bytes 1179656 | tf_op jit(solution)/shard_map/ppermute | solution.py:542
  128.3 30.3 %collective-permute-start.26 = (bf16[4,48,1024]{2,1,0:T(8,128)(2,1)}, bf16[4,48,1024]{2,1,0:T(8,128)(2,1)S(1)}, u32[]{:S(2)}, u32[]{:S(2)}) collective-permute-start(bf16[4,48,1024]{2,1,0:T(8,128)(2,1)} %get-tuple-element.36), channel_id=1, source_target_pairs={{0,3},{1,2},{2,1},{3,0},{4,7},{5,6},{6,5},{7,4},{8,11},{9,10},{10,... | collective-permute-start | bytes 1179656 | tf_op jit(solution)/shard_map/ppermute | solution.py:542
  136.8 10.5 %collective-permute-start.13 = (bf16[2,192,128]{2,1,0:T(8,128)(2,1)S(1)}, bf16[2,192,128]{2,1,0:T(8,128)(2,1)S(1)}, u32[]{:S(2)}, u32[]{:S(2)}) collective-permute-start(bf16[2,192,128]{2,1,0:T(8,128)(2,1)S(1)} %copy-done.1), channel_id=1, source_target_pairs={{0,16},{8,24},{16,0},{24,8},{1,17},{9,25},{17,1},{25,9},{2,18},{10... | collective-permute-start | bytes 294920 | tf_op jit(solution)/shard_map/ppermute | solution.py:542
  140.9 6.5 %collective-permute-start.14 = (bf16[2,192,128]{2,1,0:T(8,128)(2,1)S(1)}, bf16[2,192,128]{2,1,0:T(8,128)(2,1)S(1)}, u32[]{:S(2)}, u32[]{:S(2)}) collective-permute-start(bf16[2,192,128]{2,1,0:T(8,128)(2,1)S(1)} %copy-done.1), channel_id=1, source_target_pairs={{0,24},{8,16},{16,8},{24,0},{1,25},{9,17},{17,9},{25,1},{2,26},{10... | collective-permute-start | bytes 294920 | tf_op jit(solution)/shard_map/ppermute | solution.py:542
  155.1 19.3 %collective-permute-start.21 = (bf16[48,3200]{1,0:T(8,128)(2,1)}, bf16[48,3200]{1,0:T(8,128)(2,1)S(1)}, u32[]{:S(2)}, u32[]{:S(2)}) collective-permute-start(bf16[48,3200]{1,0:T(8,128)(2,1)} %get-tuple-element.30), channel_id=1, source_target_pairs={{0,1},{1,0},{2,3},{3,2},{4,5},{5,4},{6,7},{7,6},{8,9},{9,8},{10,11... | collective-permute-start | bytes 921608 | tf_op jit(solution)/shard_map/ppermute | solution.py:542
  155.9 18.5 %collective-permute-start.22 = (bf16[48,3200]{1,0:T(8,128)(2,1)}, bf16[48,3200]{1,0:T(8,128)(2,1)S(1)}, u32[]{:S(2)}, u32[]{:S(2)}) collective-permute-start(bf16[48,3200]{1,0:T(8,128)(2,1)} %get-tuple-element.31), channel_id=1, source_target_pairs={{0,2},{1,3},{2,0},{3,1},{4,6},{5,7},{6,4},{7,5},{8,10},{9,11},{10,... | collective-permute-start | bytes 921608 | tf_op jit(solution)/shard_map/ppermute | solution.py:542
  156.6 17.8 %collective-permute-start.23 = (bf16[48,3200]{1,0:T(8,128)(2,1)}, bf16[48,3200]{1,0:T(8,128)(2,1)S(1)}, u32[]{:S(2)}, u32[]{:S(2)}) collective-permute-start(bf16[48,3200]{1,0:T(8,128)(2,1)} %get-tuple-element.32), channel_id=1, source_target_pairs={{0,3},{1,2},{2,1},{3,0},{4,7},{5,6},{6,5},{7,4},{8,11},{9,10},{10,... | collective-permute-start | bytes 921608 | tf_op jit(solution)/shard_map/ppermute | solution.py:542
  162.1 9.4 %collective-permute-start.28 = (bf16[48,1024]{1,0:T(8,128)(2,1)}, bf16[48,1024]{1,0:T(8,128)(2,1)S(1)}, u32[]{:S(2)}, u32[]{:S(2)}) collective-permute-start(bf16[48,1024]{1,0:T(8,128)(2,1)} %get-tuple-element.39), channel_id=1, source_target_pairs={{0,16},{8,24},{16,0},{24,8},{1,17},{9,25},{17,1},{25,9},{2,18},{10... | collective-permute-start | bytes 294920 | tf_op jit(solution)/shard_map/ppermute | solution.py:542
  167.5 6.9 %collective-permute-start.29 = (bf16[48,1024]{1,0:T(8,128)(2,1)}, bf16[48,1024]{1,0:T(8,128)(2,1)S(1)}, u32[]{:S(2)}, u32[]{:S(2)}) collective-permute-start(bf16[48,1024]{1,0:T(8,128)(2,1)} %get-tuple-element.40), channel_id=1, source_target_pairs={{0,24},{8,16},{16,8},{24,0},{1,25},{9,17},{17,9},{25,1},{2,26},{10... | collective-permute-start | bytes 294920 | tf_op jit(solution)/shard_map/ppermute | solution.py:542
  (31 other events, 162.1 us)

commit v5 on v4

--- a/solution.py
+++ b/solution.py
@@ -264,13 +264,20 @@
                 BF16
             )
 
-    lined = jnp.concatenate(pieces_of(wedge[...], 3), axis=0)
+    tile = out.shape[1]
+
+    def part_of(ref):
+        if ref.shape[1] == tile:
+            return ref[...]
+        return ref[:, pl.ds(pl.multiple_of(pl.program_id(0) * tile, 128), tile)]
+
+    lined = jnp.concatenate(pieces_of(part_of(wedge), 3), axis=0)
     weights = dot(wedge_hot[...], lined)
     taken = 0
     for n in range(bunches):
         stack, have = [], 0
         while have < depth:
-            stack.append(blocks[taken][...])
+            stack.append(part_of(blocks[taken]))
             have += blocks[taken].shape[0]
             taken += 1
         values = dot(rows_hot[n], jnp.concatenate(stack, axis=0) if len(stack) > 1 else stack[0])
@@ -282,7 +289,7 @@
     count = 2 * len(pairs)
     cap = pairs[0].shape[2]
     masks = wedge.shape[0]
-    bunch = min(count, 256 // rows)
+    bunch = max(n for n in (2, 4) if count % n == 0 and n * rows <= 256)
     return pl.pallas_call(
         functools.partial(select_kernel, len(blocks)),
         grid_spec=pltpu.PrefetchScalarGridSpec(
@@ -552,7 +559,7 @@
     per_vox = voxels // groups
     tile = per_vox // SPLIT
     keep = per_vox - tile
-    half_steps = voxels // 2 // tile
+    half = voxels // 2
     cap = 2 * slot_count
     block = lax.axis_index("blk").astype(jnp.int32)
     core = lax.axis_index("core").astype(jnp.int32)
@@ -573,7 +580,6 @@
     else:
         tables = [passed([s] * blocks, "blk", blocks) for s in (low, high)]
     far = deal(place, slab, mate, layers, keep)
-    nearby = layers // 2
     pieces = [None] * layers
     for p in range(1, layers):
         pieces[p] = lax.ppermute(far[p - 1], "lay", [(z, z ^ p) for z in range(layers)])
@@ -584,65 +590,57 @@
         pick_owner.reshape(1, slot_count),
         pick_offset.reshape(1, slot_count),
         wedge_id.reshape(1, slot_count),
-        per_vox,
+        2 * per_vox,
     )
     notes = passed([note] * blocks, "blk", blocks)
     listed = lists_of(place, notes, cap)
     pair = jnp.stack(passed([listed] * 2, "core", 2))
-    pairs = passed([pair] * layers, "lay", layers)
-
-    def local(t, s, split=SPLIT):
-        return (0, (2 * (t // split) + s[0]) * split + t % split)
-
-    def here(t, s):
-        return (0, s[1] * SPLIT + t)
-
-    wide = functools.partial(local, split=SPLIT // 2)
+
     scaled = select(
         place,
         [slab, mate],
         [
-            pl.BlockSpec((slot_count, 2 * tile), wide),
-            pl.BlockSpec((slot_count, 2 * tile), lambda t, s: (0, t)),
+            pl.BlockSpec((slot_count, per_vox), lambda t, s: (0, 2 * t + s[0])),
+            pl.BlockSpec((slot_count, per_vox), lambda t, s: (0, t)),
         ],
         [pair],
         wedge,
-        pl.BlockSpec((masks, 2 * tile), wide),
+        pl.BlockSpec((masks, per_vox), lambda t, s: (0, 2 * t + s[0])),
         slot_count,
-        2 * tile,
-        half_steps // 2,
+        per_vox,
+        layers,
     )
-    sums = correl(scaled, tables, tile)
+    here = pl.BlockSpec((masks, per_vox), lambda t, s: (0, s[1]))
+    near_rows = select(
+        place,
+        [slab, mate],
+        [
+            pl.BlockSpec((slot_count, per_vox), lambda t, s: (0, s[1])),
+            pl.BlockSpec((slot_count, per_vox), lambda t, s: (0, s[2])),
+        ],
+        [pair],
+        wedge,
+        here,
+        slot_count,
+        keep // 2,
+        2,
+    )
+    pairs = passed([pair] * layers, "lay", layers)
+    sums = correl(scaled, tables, half // 4)
     got = lax.ppermute(sums, "core", [(0, 1), (1, 0)])
     weights = weigh(sums, got, pair, notes, masks, 1.0 / (32.0 * math.sqrt(voxels)))
     all_weights = passed([weights] * layers, "lay", layers)
 
-    received = pl.BlockSpec((2 * slot_count, tile), lambda t, s: (0, t))
-    near_rows = select(
-        place,
-        [slab, mate, *pieces[1:nearby]],
-        [
-            pl.BlockSpec((slot_count, tile), here),
-            pl.BlockSpec((slot_count, tile), lambda t, s: (0, s[2] * SPLIT + t)),
-        ]
-        + [received] * (nearby - 1),
-        pairs[:nearby],
-        wedge,
-        pl.BlockSpec((masks, tile), here),
-        slot_count,
-        tile,
-        SPLIT - 1,
-    )
     far_rows = select(
         place,
-        pieces[nearby:],
-        [received] * (layers - nearby),
-        pairs[nearby:],
+        pieces[1:],
+        [pl.BlockSpec((2 * slot_count, keep // 2), lambda t, s: (0, t))] * (layers - 1),
+        pairs[1:],
         wedge,
-        pl.BlockSpec((masks, tile), here),
+        here,
         slot_count,
-        tile,
-        SPLIT - 1,
+        keep // 2,
+        2,
     )
 
     apart = blend(
@@ -667,9 +665,9 @@
         [near_rows, far_rows],
         masks,
         blocks,
-        tile,
-        SPLIT - 1,
-        lambda t, s: (0, jnp.minimum(t, SPLIT - 2)),
+        keep // 2,
+        2,
+        lambda t, s: (0, jnp.minimum(t, 1)),
     )
     shares = passed(shares, "blk", blocks)
     return finish(place, shares, apart, wedge, tile)

time: 180 us -> 184 us (1.022)
  waiting for transfers between devices: 52.4 us -> 64.4 us
  Pallas kernels: 73.4 us -> 62.7 us
  starting transfers between devices: 45.1 us -> 47.6 us
    ppermute x19, waiting for transfers between devices: 40.5 us -> 52.9 us  [passed(): lax.ppermute(values[p], axis, [(d, d ^ p) for d in range(size)])]
    pallas_call x1, Pallas kernels: 13.9 us -> 8.14 us  [correl(): pl.pallas_call(functools.partial(correl_kernel, blocks), grid=(steps,), i...]
    ppermute x19, starting transfers between devices: 29.4 us -> 31.6 us  [passed(): lax.ppermute(values[p], axis, [(d, d ^ p) for d in range(size)])]
    pallas_call x3, Pallas kernels: 23 us -> 21 us  [select(): pl.pallas_call(functools.partial(select_kernel, len(blocks)), grid_spec=p...]
    unnamed x50 -> x54, local copies, waits for them, and re-layouts: 5.61 us -> 5.98 us
  transfers between devices with their start and end apart: 30 -> 30, of which waited for: 11 -> 10; matrix products, arithmetic and copies ran while one was open for 1% -> 1% of each run, Pallas kernels for 37% -> 30%
where the time goes in v5:
time: 184 us
  waiting for transfers between devices  64.4 us (35%)
  Pallas kernels  62.7 us (34%)
  starting transfers between devices  47.6 us (26%)
  local copies, waits for them, and re-layouts  5.98 us (3%)
  other arithmetic  1.93 us (1%)
    ppermute x19, waiting for transfers between devices, passed(): lax.ppermute(values[p], axis, [(d, d ^ p) for d in range(size)])  52.9 us
    ppermute x19, starting transfers between devices, passed(): lax.ppermute(values[p], axis, [(d, d ^ p) for d in range(size)])  31.6 us
    pallas_call x3, Pallas kernels, select(): pl.pallas_call(functools.partial(select_kernel, len(blocks)), grid_spec=p...  21 us
    pallas_call x2, Pallas kernels, blend(): pl.pallas_call(functools.partial(blend_kernel, layers, len(scaled), block...  10.5 us
    ppermute x1, waiting for transfers between devices, per_device(): high_x = lax.ppermute(high, 'blk', over_x)  8.31 us
    pallas_call x1, Pallas kernels, correl(): pl.pallas_call(functools.partial(correl_kernel, blocks), grid=(steps,), i...  8.14 us
    ppermute x3, starting transfers between devices, per_device(): lax.ppermute(far[p - 1], 'lay', [(z, z ^ p) for z in range(layers)])  6.53 us
    unnamed x54, local copies, waits for them, and re-layouts  5.98 us
  transfers between devices with their start and end apart: 30, of which 10 were waited for; matrix products, arithmetic and copies ran while one was open for 1% of the time, Pallas kernels for 30%

profile of v5, /device:TPU:0, one launch (start us, length us, event | category | flops | bytes accessed | tf_op | source)
XLA Modules:
  0.0 183.5 jit_solution(16163196121671169123)
XLA Ops:
  0.7 3.9 %cut.1 = (bf16[48,8192]{1,0:T(8,128)(2,1)}, bf16[48,8192]{1,0:T(8,128)(2,1)}, bf16[64,16384]{1,0:T(8,128)(2,1)}) custom-call(s32[4]{0:T(128)} %pad_add_fusion.place, bf16[48,32768]{1,0:T(8,128)(2,1)} %refs.3, bf16[64,32768]{1,0:T(8,128)(2,1)} %slab.3), custom_call_target="tpu_custom_call" | custom-call | bytes 7340032 | tf_op jit(solution)/shard_map/cut/pallas_call | solution.py:87
  5.1 2.6 %collective-permute-start.8 = (bf16[48,8192]{1,0:T(8,128)(2,1)}, bf16[48,8192]{1,0:T(8,128)(2,1)}, u32[]{:S(2)}, u32[]{:S(2)}) collective-permute-start(bf16[48,8192]{1,0:T(8,128)(2,1)} %get-tuple-element.25.rest_1_), channel_id=1, source_target_pairs={{0,2},{1,3},{2,0},{3,1},{4,6},{5,7},{6,4},{7,5},{8,10},{9,11},{10,... | collective-permute-start | bytes 2359304 | tf_op jit(solution)/shard_map/ppermute | solution.py:574
  9.8 5.1 %brief.1.rest_0_ = f32[16,128]{1,0:T(8,128)} custom-call(s32[1]{0:T(128)S(6)} %copy.8.live, bf16[48,32768]{1,0:T(8,128)(2,1)} %refs.3, f32[8,32768]{1,0:T(8,128)} %rest_8_.1, s32[1,64]{1,0:T(1,128)} %bitcast.11, s32[1,64]{1,0:T(1,128)} %bitcast.12, s32[1,64]{1,0:T(1,128)} %bitcast.13), custom_call_target="tpu_custom_call" | custom-call | flops 150994944 | bytes 4194304 | tf_op jit(solution)/shard_map/brief/pallas_call | solution.py:184
  15.6 12.1 %collective-permute-done.1.rest_1_ = f32[16,128]{1,0:T(8,128)S(1)} collective-permute-done((f32[16,128]{1,0:T(8,128)}, f32[16,128]{1,0:T(8,128)S(1)}, u32[]{:S(2)}, u32[]{:S(2)}) %collective-permute-start.1) | collective-permute-done | bytes 8224 | tf_op jit(solution)/shard_map/ppermute | solution.py:549
  29.1 3.3 %collective-permute-done.3.rest_3_ = f32[16,128]{1,0:T(8,128)S(1)} collective-permute-done((f32[16,128]{1,0:T(8,128)}, f32[16,128]{1,0:T(8,128)S(1)}, u32[]{:S(2)}, u32[]{:S(2)}) %collective-permute-start.3) | collective-permute-done | bytes 8224 | tf_op jit(solution)/shard_map/ppermute | solution.py:549
  42.5 3.3 %deal.1 = (bf16[128,3072]{1,0:T(8,128)(2,1)}, bf16[128,3072]{1,0:T(8,128)(2,1)}, bf16[128,3072]{1,0:T(8,128)(2,1)}) custom-call(s32[4]{0:T(128)} %pad_add_fusion.place, bf16[64,32768]{1,0:T(8,128)(2,1)} %slab.3, bf16[64,16384]{1,0:T(8,128)(2,1)} %copy-done), custom_call_target="tpu_custom_call" | custom-call | bytes 4718592 | tf_op jit(solution)/shard_map/deal/pallas_call | solution.py:136
  47.4 8.3 %collective-permute-done.6.rest_3_ = bf16[48,8192]{1,0:T(8,128)(2,1)} collective-permute-done((bf16[48,8192]{1,0:T(8,128)(2,1)}, bf16[48,8192]{1,0:T(8,128)(2,1)}, u32[]{:S(2)}, u32[]{:S(2)}) %collective-permute-start.6) | collective-permute-done | bytes 786464 | tf_op jit(solution)/shard_map/ppermute | solution.py:575
  55.7 2.6 %collective-permute-start.16 = (bf16[128,3072]{1,0:T(8,128)(2,1)}, bf16[128,3072]{1,0:T(8,128)(2,1)S(1)}, u32[]{:S(2)}, u32[]{:S(2)}) collective-permute-start(bf16[128,3072]{1,0:T(8,128)(2,1)} %get-tuple-element.27), channel_id=1, source_target_pairs={{0,16},{8,24},{16,0},{24,8},{1,17},{9,25},{17,1},{25,9},{2,18},{10... | collective-permute-start | bytes 2359304 | tf_op jit(solution)/shard_map/ppermute | solution.py:585
  60.6 9.4 %select.3.scaled.rest_1_ = bf16[256,16384]{1,0:T(8,128)(2,1)} custom-call(s32[4]{0:T(128)} %pad_add_fusion.place, bf16[64,32768]{1,0:T(8,128)(2,1)} %slab.3, bf16[64,16384]{1,0:T(8,128)(2,1)} %copy-done, f32[2,8,128]{2,1,0:T(8,128)} %pad_maximum_fusion.rest_2_.pair.rest_6_, f32[8,32768]{1,0:T(8,128)} %rest_8_.1), custom_call_target="tpu_custom_call" | custom-call | flops 4294967296 | bytes 12582912 | tf_op jit(solution)/shard_map/select/pallas_call | solution.py:293
  73.1 8.1 %correl.1.own = f32[256,192]{1,0:T(8,128)} custom-call(bf16[256,16384]{1,0:T(8,128)(2,1)} %select.3.scaled.rest_1_, bf16[48,8192]{1,0:T(8,128)(2,1)} %get-tuple-element.24.rest_0_, bf16[48,8192]{1,0:T(8,128)(2,1)} %get-tuple-element.25.rest_1_, bf16[48,8192]{1,0:T(8,128)(2,1)} %collective-permute-done.5.rest_2_, ...), custom_call_target="tpu_custom_call" | custom-call | flops 1610612736 | bytes 14680064 | tf_op jit(solution)/shard_map/correl/pallas_call | solution.py:354
  83.0 2.6 %collective-permute-start.19 = (f32[2,8,128]{2,1,0:T(8,128)S(1)}, f32[2,8,128]{2,1,0:T(8,128)S(1)}, u32[]{:S(2)}, u32[]{:S(2)}) collective-permute-start(f32[2,8,128]{2,1,0:T(8,128)S(1)} %copy-done.10), channel_id=1, source_target_pairs={{0,16},{8,24},{16,0},{24,8},{1,17},{9,25},{17,1},{25,9},{2,18},{10... | collective-permute-start | bytes 24584 | tf_op jit(solution)/shard_map/ppermute | solution.py:549
  85.6 2.8 %weigh.1.rest_0_ = bf16[2,192,128]{2,1,0:T(8,128)(2,1)} custom-call(f32[256,192]{1,0:T(8,128)} %correl.1.own, f32[256,192]{1,0:T(8,128)} %copy-done.9, f32[2,8,128]{2,1,0:T(8,128)} %pad_maximum_fusion.rest_2_.pair.rest_6_, f32[16,128]{1,0:T(8,128)} %brief.1.rest_0_, f32[16,128]{1,0:T(8,128)} %copy-done.18, f32[16,128]{1,0:T(8,128)} %copy-done.19, ...), custom_call_target="tpu_custom_call" | custom-call | flops 16777216 | bytes 262144 | tf_op jit(solution)/shard_map/weigh/pallas_call | solution.py:395
  88.4 9.5 %collective-permute-done.18.rest_3_.rest_7_ = f32[2,8,128]{2,1,0:T(8,128)S(1)} collective-permute-done((f32[2,8,128]{2,1,0:T(8,128)S(1)}, f32[2,8,128]{2,1,0:T(8,128)S(1)}, u32[]{:S(2)}, u32[]{:S(2)}) %collective-permute-start.18) | collective-permute-done | bytes 8224 | tf_op jit(solution)/shard_map/ppermute | solution.py:549
  98.0 4.3 %collective-permute-start.20 = (f32[2,8,128]{2,1,0:T(8,128)S(1)}, f32[2,8,128]{2,1,0:T(8,128)S(1)}, u32[]{:S(2)}, u32[]{:S(2)}) collective-permute-start(f32[2,8,128]{2,1,0:T(8,128)S(1)} %copy-done.11), channel_id=1, source_target_pairs={{0,24},{8,16},{16,8},{24,0},{1,25},{9,17},{17,9},{25,1},{2,26},{10... | collective-permute-start | bytes 24584 | tf_op jit(solution)/shard_map/ppermute | solution.py:549
  102.3 24.4 %collective-permute-done.19.rest_4_.rest_8_ = f32[2,8,128]{2,1,0:T(8,128)S(1)} collective-permute-done((f32[2,8,128]{2,1,0:T(8,128)S(1)}, f32[2,8,128]{2,1,0:T(8,128)S(1)}, u32[]{:S(2)}, u32[]{:S(2)}) %collective-permute-start.19) | collective-permute-done | bytes 8224 | tf_op jit(solution)/shard_map/ppermute | solution.py:549
  127.5 4.9 %blend.3 = (bf16[4,48,1024]{2,1,0:T(8,128)(2,1)}, bf16[4,48,1024]{2,1,0:T(8,128)(2,1)}, bf16[4,48,1024]{2,1,0:T(8,128)(2,1)}, bf16[4,48,1024]{2,1,0:T(8,128)(2,1)}) custom-call(s32[4]{0:T(128)} %pad_add_fusion.place, bf16[2,192,128]{2,1,0:T(8,128)(2,1)} %weigh.1.rest_0_, bf16[256,16384]{1,0:T(8,128)(2,1)} %select.3.scaled.rest_1_), custom_call_target="tpu_custom_call" | custom-call | flops 402653184 | bytes 3670016 | tf_op jit(solution)/shard_map/blend/pallas_call | solution.py:451
  134.0 4.3 %select.4.rest_4_ = bf16[256,3072]{1,0:T(8,128)(2,1)} custom-call(s32[4]{0:T(128)} %pad_add_fusion.place, bf16[64,32768]{1,0:T(8,128)(2,1)} %slab.3, bf16[64,16384]{1,0:T(8,128)(2,1)} %copy-done, f32[2,8,128]{2,1,0:T(8,128)} %pad_maximum_fusion.rest_2_.pair.rest_6_, f32[8,32768]{1,0:T(8,128)} %rest_8_.1), custom_call_target="tpu_custom_call" | custom-call | flops 805306368 | bytes 2359296 | tf_op jit(solution)/shard_map/select/pallas_call | solution.py:293
  138.4 3.4 %collective-permute-start.13 = (bf16[2,192,128]{2,1,0:T(8,128)(2,1)S(1)}, bf16[2,192,128]{2,1,0:T(8,128)(2,1)S(1)}, u32[]{:S(2)}, u32[]{:S(2)}) collective-permute-start(bf16[2,192,128]{2,1,0:T(8,128)(2,1)S(1)} %copy-done.1), channel_id=1, source_target_pairs={{0,16},{8,24},{16,0},{24,8},{1,17},{9,25},{17,1},{25,9},{2,18},{10... | collective-permute-start | bytes 294920 | tf_op jit(solution)/shard_map/ppermute | solution.py:549
  144.9 7.2 %select.5.rest_5_ = bf16[768,3072]{1,0:T(8,128)(2,1)} custom-call(s32[4]{0:T(128)} %pad_add_fusion.place, bf16[128,3072]{1,0:T(8,128)(2,1)} %copy-done.24, bf16[128,3072]{1,0:T(8,128)(2,1)} %copy-done.25, bf16[128,3072]{1,0:T(8,128)(2,1)} %collective-permute-done.17.rest_2_, f32[2,8,128]{2,1,0:T(8,128)} %copy-done.21, f32[2,8,128]{2,1,0:T(8,128)} %copy-done.22, ...), custom_call_target="tpu_custom_call" | custom-call | flops 2415919104 | bytes 7077888 | tf_op jit(solution)/shard_map/select/pallas_call | solution.py:293
  153.5 5.6 %blend.2 = (bf16[48,3200]{1,0:T(8,128)(2,1)}, bf16[48,3200]{1,0:T(8,128)(2,1)}, bf16[48,3200]{1,0:T(8,128)(2,1)}, bf16[48,3200]{1,0:T(8,128)(2,1)}) custom-call(s32[4]{0:T(128)} %pad_add_fusion.place, bf16[2,192,128]{2,1,0:T(8,128)(2,1)} %weigh.1.rest_0_, bf16[2,192,128]{2,1,0:T(8,128)(2,1)} %copy-done.15, bf16[2,192,128]{2,1,0:T(8,128)(2,1)} %copy-done.16, ...), custom_call_target="tpu_custom_call" | custom-call | flops 1207959552 | bytes 7471104 | tf_op jit(solution)/shard_map/blend/pallas_call | solution.py:451
  166.2 3.7 %collective-permute-start.28 = (bf16[48,1024]{1,0:T(8,128)(2,1)}, bf16[48,1024]{1,0:T(8,128)(2,1)S(1)}, u32[]{:S(2)}, u32[]{:S(2)}) collective-permute-start(bf16[48,1024]{1,0:T(8,128)(2,1)} %get-tuple-element.39), channel_id=1, source_target_pairs={{0,16},{8,24},{16,0},{24,8},{1,17},{9,25},{17,1},{25,9},{2,18},{10... | collective-permute-start | bytes 294920 | tf_op jit(solution)/shard_map/ppermute | solution.py:549
  170.6 5.2 %collective-permute-start.29 = (bf16[48,1024]{1,0:T(8,128)(2,1)}, bf16[48,1024]{1,0:T(8,128)(2,1)S(1)}, u32[]{:S(2)}, u32[]{:S(2)}) collective-permute-start(bf16[48,1024]{1,0:T(8,128)(2,1)} %get-tuple-element.40), channel_id=1, source_target_pairs={{0,24},{8,16},{16,8},{24,0},{1,25},{9,17},{17,9},{25,1},{2,26},{10... | collective-permute-start | bytes 294920 | tf_op jit(solution)/shard_map/ppermute | solution.py:549
  175.8 2.8 %collective-permute-done.29.rest_7_ = bf16[48,1024]{1,0:T(8,128)(2,1)S(1)} collective-permute-done((bf16[48,1024]{1,0:T(8,128)(2,1)}, bf16[48,1024]{1,0:T(8,128)(2,1)S(1)}, u32[]{:S(2)}, u32[]{:S(2)}) %collective-permute-start.29) | collective-permute-done | bytes 98336 | tf_op jit(solution)/shard_map/ppermute | solution.py:549
  179.6 3.9 %finish.1 = f32[48,4096]{1,0:T(8,128)} custom-call(s32[4]{0:T(128)} %pad_add_fusion.place, bf16[48,3200]{1,0:T(8,128)(2,1)} %get-tuple-element.29.rest_0_, bf16[48,3200]{1,0:T(8,128)(2,1)} %copy-done.6, bf16[48,3200]{1,0:T(8,128)(2,1)} %copy-done.7, bf16[48,3200]{1,0:T(8,128)(2,1)} %copy-done.8, bf16[48,1024]{1,0:T(8,128)(2,1)} %get-tuple-element.37.rest_4_, ...), custom_call_target="tpu_custom_call" | custom-call | bytes 1572864 | tf_op jit(solution)/shard_map/finish/pallas_call | solution.py:528
  (105 shorter events, 39.1 us)
Async XLA Ops:
  4.6 36.6 %collective-permute-start = (bf16[64,16384]{1,0:T(8,128)(2,1)}, bf16[64,16384]{1,0:T(8,128)(2,1)S(1)}, u32[]{:S(2)}, u32[]{:S(2)}) collective-permute-start(bf16[64,16384]{1,0:T(8,128)(2,1)} %get-tuple-element.23), channel_id=1, source_target_pairs={{0,4},{4,0},{1,5},{5,1},{2,6},{6,2},{3,7},{7,3},{8,12},{12,8},{9,1... | collective-permute-start | bytes 6291464 | tf_op jit(solution)/shard_map/ppermute | solution.py:570
  5.1 31.9 %collective-permute-start.8 = (bf16[48,8192]{1,0:T(8,128)(2,1)}, bf16[48,8192]{1,0:T(8,128)(2,1)}, u32[]{:S(2)}, u32[]{:S(2)}) collective-permute-start(bf16[48,8192]{1,0:T(8,128)(2,1)} %get-tuple-element.25.rest_1_), channel_id=1, source_target_pairs={{0,2},{1,3},{2,0},{3,1},{4,6},{5,7},{6,4},{7,5},{8,10},{9,11},{10,... | collective-permute-start | bytes 2359304 | tf_op jit(solution)/shard_map/ppermute | solution.py:574
  7.7 30.7 %collective-permute-start.5 = (bf16[48,8192]{1,0:T(8,128)(2,1)}, bf16[48,8192]{1,0:T(8,128)(2,1)}, u32[]{:S(2)}, u32[]{:S(2)}) collective-permute-start(bf16[48,8192]{1,0:T(8,128)(2,1)} %get-tuple-element.24.rest_0_), channel_id=1, source_target_pairs={{0,1},{1,0},{2,3},{3,2},{4,5},{5,4},{6,7},{7,6},{8,9},{9,8},{10,11... | collective-permute-start | bytes 2359304 | tf_op jit(solution)/shard_map/ppermute | solution.py:573
  15.0 12.7 %collective-permute-start.1 = (f32[16,128]{1,0:T(8,128)}, f32[16,128]{1,0:T(8,128)S(1)}, u32[]{:S(2)}, u32[]{:S(2)}) collective-permute-start(f32[16,128]{1,0:T(8,128)} %brief.1.rest_0_), channel_id=1, source_target_pairs={{0,1},{1,0},{2,3},{3,2},{4,5},{5,4},{6,7},{7,6},{8,9},{9,8},{10,11... | collective-permute-start | bytes 24584 | tf_op jit(solution)/shard_map/ppermute | solution.py:549
  15.5 13.6 %collective-permute-start.2 = (f32[16,128]{1,0:T(8,128)}, f32[16,128]{1,0:T(8,128)S(1)}, u32[]{:S(2)}, u32[]{:S(2)}) collective-permute-start(f32[16,128]{1,0:T(8,128)} %brief.1.rest_0_), channel_id=1, source_target_pairs={{0,2},{1,3},{2,0},{3,1},{4,6},{5,7},{6,4},{7,5},{8,10},{9,11},{10,... | collective-permute-start | bytes 24584 | tf_op jit(solution)/shard_map/ppermute | solution.py:549
  35.0 20.7 %collective-permute-start.6 = (bf16[48,8192]{1,0:T(8,128)(2,1)}, bf16[48,8192]{1,0:T(8,128)(2,1)}, u32[]{:S(2)}, u32[]{:S(2)}) collective-permute-start(bf16[48,8192]{1,0:T(8,128)(2,1)} %get-tuple-element.25.rest_1_), channel_id=1, source_target_pairs={{0,1},{1,0},{2,3},{3,2},{4,5},{5,4},{6,7},{7,6},{8,9},{9,8},{10,11... | collective-permute-start | bytes 2359304 | tf_op jit(solution)/shard_map/ppermute | solution.py:575
  36.5 21.8 %collective-permute-start.7 = (bf16[48,8192]{1,0:T(8,128)(2,1)S(1)}, bf16[48,8192]{1,0:T(8,128)(2,1)}, u32[]{:S(2)}, u32[]{:S(2)}) collective-permute-start(bf16[48,8192]{1,0:T(8,128)(2,1)S(1)} %copy-done.2), channel_id=1, source_target_pairs={{0,2},{1,3},{2,0},{3,1},{4,6},{5,7},{6,4},{7,5},{8,10},{9,11},{10,... | collective-permute-start | bytes 2359304 | tf_op jit(solution)/shard_map/ppermute | solution.py:576
  37.0 35.1 %collective-permute-start.10 = (bf16[48,8192]{1,0:T(8,128)(2,1)}, bf16[48,8192]{1,0:T(8,128)(2,1)}, u32[]{:S(2)}, u32[]{:S(2)}) collective-permute-start(bf16[48,8192]{1,0:T(8,128)(2,1)} %collective-permute-done.8.rest_5_), channel_id=1, source_target_pairs={{0,1},{1,0},{2,3},{3,2},{4,5},{5,4},{6,7},{7,6},{8,9},{9,8},{10,11... | collective-permute-start | bytes 2359304 | tf_op jit(solution)/shard_map/ppermute | solution.py:578
  38.4 34.7 %collective-permute-start.9 = (bf16[48,8192]{1,0:T(8,128)(2,1)}, bf16[48,8192]{1,0:T(8,128)(2,1)}, u32[]{:S(2)}, u32[]{:S(2)}) collective-permute-start(bf16[48,8192]{1,0:T(8,128)(2,1)} %collective-permute-done.5.rest_2_), channel_id=1, source_target_pairs={{0,2},{1,3},{2,0},{3,1},{4,6},{5,7},{6,4},{7,5},{8,10},{9,11},{10,... | collective-permute-start | bytes 2359304 | tf_op jit(solution)/shard_map/ppermute | solution.py:577
  45.7 96.1 %collective-permute-start.15 = (bf16[128,3072]{1,0:T(8,128)(2,1)}, bf16[128,3072]{1,0:T(8,128)(2,1)S(1)}, u32[]{:S(2)}, u32[]{:S(2)}) collective-permute-start(bf16[128,3072]{1,0:T(8,128)(2,1)} %get-tuple-element.26), channel_id=1, source_target_pairs={{0,8},{8,0},{16,24},{24,16},{1,9},{9,1},{17,25},{25,17},{2,10},{10... | collective-permute-start | bytes 2359304 | tf_op jit(solution)/shard_map/ppermute | solution.py:585
  55.7 86.3 %collective-permute-start.16 = (bf16[128,3072]{1,0:T(8,128)(2,1)}, bf16[128,3072]{1,0:T(8,128)(2,1)S(1)}, u32[]{:S(2)}, u32[]{:S(2)}) collective-permute-start(bf16[128,3072]{1,0:T(8,128)(2,1)} %get-tuple-element.27), channel_id=1, source_target_pairs={{0,16},{8,24},{16,0},{24,8},{1,17},{9,25},{17,1},{25,9},{2,18},{10... | collective-permute-start | bytes 2359304 | tf_op jit(solution)/shard_map/ppermute | solution.py:585
  58.3 85.2 %collective-permute-start.17 = (bf16[128,3072]{1,0:T(8,128)(2,1)}, bf16[128,3072]{1,0:T(8,128)(2,1)}, u32[]{:S(2)}, u32[]{:S(2)}) collective-permute-start(bf16[128,3072]{1,0:T(8,128)(2,1)} %get-tuple-element.28), channel_id=1, source_target_pairs={{0,24},{8,16},{16,8},{24,0},{1,25},{9,17},{17,9},{25,1},{2,26},{10... | collective-permute-start | bytes 2359304 | tf_op jit(solution)/shard_map/ppermute | solution.py:585
  81.3 16.7 %collective-permute-start.18 = (f32[2,8,128]{2,1,0:T(8,128)S(1)}, f32[2,8,128]{2,1,0:T(8,128)S(1)}, u32[]{:S(2)}, u32[]{:S(2)}) collective-permute-start(f32[2,8,128]{2,1,0:T(8,128)S(1)} %copy-done.10), channel_id=1, source_target_pairs={{0,8},{8,0},{16,24},{24,16},{1,9},{9,1},{17,25},{25,17},{2,10},{10... | collective-permute-start | bytes 24584 | tf_op jit(solution)/shard_map/ppermute | solution.py:549
  83.0 43.7 %collective-permute-start.19 = (f32[2,8,128]{2,1,0:T(8,128)S(1)}, f32[2,8,128]{2,1,0:T(8,128)S(1)}, u32[]{:S(2)}, u32[]{:S(2)}) collective-permute-start(f32[2,8,128]{2,1,0:T(8,128)S(1)} %copy-done.10), channel_id=1, source_target_pairs={{0,16},{8,24},{16,0},{24,8},{1,17},{9,25},{17,1},{25,9},{2,18},{10... | collective-permute-start | bytes 24584 | tf_op jit(solution)/shard_map/ppermute | solution.py:549
  98.0 34.4 %collective-permute-start.20 = (f32[2,8,128]{2,1,0:T(8,128)S(1)}, f32[2,8,128]{2,1,0:T(8,128)S(1)}, u32[]{:S(2)}, u32[]{:S(2)}) collective-permute-start(f32[2,8,128]{2,1,0:T(8,128)S(1)} %copy-done.11), channel_id=1, source_target_pairs={{0,24},{8,16},{16,8},{24,0},{1,25},{9,17},{17,9},{25,1},{2,26},{10... | collective-permute-start | bytes 24584 | tf_op jit(solution)/shard_map/ppermute | solution.py:549
  126.7 11.7 %collective-permute-start.12 = (bf16[2,192,128]{2,1,0:T(8,128)(2,1)}, bf16[2,192,128]{2,1,0:T(8,128)(2,1)S(1)}, u32[]{:S(2)}, u32[]{:S(2)}) collective-permute-start(bf16[2,192,128]{2,1,0:T(8,128)(2,1)} %weigh.1.rest_0_), channel_id=1, source_target_pairs={{0,8},{8,0},{16,24},{24,16},{1,9},{9,1},{17,25},{25,17},{2,10},{10... | collective-permute-start | bytes 294920 | tf_op jit(solution)/shard_map/ppermute | solution.py:549
  132.4 28.7 %collective-permute-start.24 = (bf16[4,48,1024]{2,1,0:T(8,128)(2,1)}, bf16[4,48,1024]{2,1,0:T(8,128)(2,1)S(1)}, u32[]{:S(2)}, u32[]{:S(2)}) collective-permute-start(bf16[4,48,1024]{2,1,0:T(8,128)(2,1)} %get-tuple-element.34), channel_id=1, source_target_pairs={{0,1},{1,0},{2,3},{3,2},{4,5},{5,4},{6,7},{7,6},{8,9},{9,8},{10,11... | collective-permute-start | bytes 1179656 | tf_op jit(solution)/shard_map/ppermute | solution.py:549
  138.4 13.8 %collective-permute-start.13 = (bf16[2,192,128]{2,1,0:T(8,128)(2,1)S(1)}, bf16[2,192,128]{2,1,0:T(8,128)(2,1)S(1)}, u32[]{:S(2)}, u32[]{:S(2)}) collective-permute-start(bf16[2,192,128]{2,1,0:T(8,128)(2,1)S(1)} %copy-done.1), channel_id=1, source_target_pairs={{0,16},{8,24},{16,0},{24,8},{1,17},{9,25},{17,1},{25,9},{2,18},{10... | collective-permute-start | bytes 294920 | tf_op jit(solution)/shard_map/ppermute | solution.py:549
  141.8 10.4 %collective-permute-start.14 = (bf16[2,192,128]{2,1,0:T(8,128)(2,1)S(1)}, bf16[2,192,128]{2,1,0:T(8,128)(2,1)S(1)}, u32[]{:S(2)}, u32[]{:S(2)}) collective-permute-start(bf16[2,192,128]{2,1,0:T(8,128)(2,1)S(1)} %copy-done.1), channel_id=1, source_target_pairs={{0,24},{8,16},{16,8},{24,0},{1,25},{9,17},{17,9},{25,1},{2,26},{10... | collective-permute-start | bytes 294920 | tf_op jit(solution)/shard_map/ppermute | solution.py:549
  142.9 19.7 %collective-permute-start.25 = (bf16[4,48,1024]{2,1,0:T(8,128)(2,1)}, bf16[4,48,1024]{2,1,0:T(8,128)(2,1)S(1)}, u32[]{:S(2)}, u32[]{:S(2)}) collective-permute-start(bf16[4,48,1024]{2,1,0:T(8,128)(2,1)} %get-tuple-element.35), channel_id=1, source_target_pairs={{0,2},{1,3},{2,0},{3,1},{4,6},{5,7},{6,4},{7,5},{8,10},{9,11},{10,... | collective-permute-start | bytes 1179656 | tf_op jit(solution)/shard_map/ppermute | solution.py:549
  143.5 19.2 %collective-permute-start.26 = (bf16[4,48,1024]{2,1,0:T(8,128)(2,1)S(1)}, bf16[4,48,1024]{2,1,0:T(8,128)(2,1)S(1)}, u32[]{:S(2)}, u32[]{:S(2)}) collective-permute-start(bf16[4,48,1024]{2,1,0:T(8,128)(2,1)S(1)} %copy-done.26), channel_id=1, source_target_pairs={{0,3},{1,2},{2,1},{3,0},{4,7},{5,6},{6,5},{7,4},{8,11},{9,10},{10,... | collective-permute-start | bytes 1179656 | tf_op jit(solution)/shard_map/ppermute | solution.py:549
  159.1 19.5 %collective-permute-start.21 = (bf16[48,3200]{1,0:T(8,128)(2,1)}, bf16[48,3200]{1,0:T(8,128)(2,1)S(1)}, u32[]{:S(2)}, u32[]{:S(2)}) collective-permute-start(bf16[48,3200]{1,0:T(8,128)(2,1)} %get-tuple-element.30), channel_id=1, source_target_pairs={{0,1},{1,0},{2,3},{3,2},{4,5},{5,4},{6,7},{7,6},{8,9},{9,8},{10,11... | collective-permute-start | bytes 921608 | tf_op jit(solution)/shard_map/ppermute | solution.py:549
  160.6 18.0 %collective-permute-start.22 = (bf16[48,3200]{1,0:T(8,128)(2,1)}, bf16[48,3200]{1,0:T(8,128)(2,1)S(1)}, u32[]{:S(2)}, u32[]{:S(2)}) collective-permute-start(bf16[48,3200]{1,0:T(8,128)(2,1)} %get-tuple-element.31), channel_id=1, source_target_pairs={{0,2},{1,3},{2,0},{3,1},{4,6},{5,7},{6,4},{7,5},{8,10},{9,11},{10,... | collective-permute-start | bytes 921608 | tf_op jit(solution)/shard_map/ppermute | solution.py:549
  161.1 17.5 %collective-permute-start.23 = (bf16[48,3200]{1,0:T(8,128)(2,1)}, bf16[48,3200]{1,0:T(8,128)(2,1)S(1)}, u32[]{:S(2)}, u32[]{:S(2)}) collective-permute-start(bf16[48,3200]{1,0:T(8,128)(2,1)} %get-tuple-element.32), channel_id=1, source_target_pairs={{0,3},{1,2},{2,1},{3,0},{4,7},{5,6},{6,5},{7,4},{8,11},{9,10},{10,... | collective-permute-start | bytes 921608 | tf_op jit(solution)/shard_map/ppermute | solution.py:549
  (33 other events, 213.8 us)

commit v6 on v5

--- a/solution.py
+++ b/solution.py
@@ -15,6 +15,7 @@
 LANES = (((1,), (1,)), ((), ()))
 VMEM = pl.BlockSpec(memory_space=pltpu.VMEM)
 SMEM = pl.BlockSpec(memory_space=pltpu.SMEM)
+HBM = pl.BlockSpec(memory_space=pltpu.HBM)
 SPLIT = 4
 
 
@@ -39,46 +40,37 @@
     return mask.astype(F32).astype(BF16)
 
 
+def room(mebibytes):
+    return pltpu.CompilerParams(vmem_limit_bytes=mebibytes << 20)
+
+
 def cost(flops, moved):
     return pl.CostEstimate(flops=int(flops), bytes_accessed=int(moved), transcendentals=0)
 
 
 def cut_kernel(place, refs, slab, *rest):
-    outs, held, came, went = rest[:3], rest[3:6], rest[6], rest[7]
-    layers, per_vox = held[2].shape[0], held[2].shape[2]
+    outs, came = rest[:3], rest[3]
+    layers = came.shape[1]
+    per_vox = outs[2].shape[1] // layers
     core = place[0]
-
-    def start(which):
+    copies = []
+    for which, out in enumerate(outs):
         source, side = (slab, 1 - core) if which == 2 else (refs, core)
         first = layers // 2 if which == 1 else 0
-        copies = []
-        for z in range(held[which].shape[0]):
+        for z in range(out.shape[1] // per_vox):
             at = pl.multiple_of((2 * (first + z) + side) * per_vox, per_vox)
             copy = pltpu.make_async_copy(
-                source.at[:, pl.ds(at, per_vox)], held[which].at[z], came.at[which, z]
+                source.at[:, pl.ds(at, per_vox)],
+                out.at[:, pl.ds(z * per_vox, per_vox)],
+                came.at[which, z],
             )
             copy.start()
             copies.append(copy)
-        return copies
-
-    coming = [start(which) for which in range(3)]
-    going = []
-    for which in range(3):
-        for z, copy in enumerate(coming[which]):
-            copy.wait()
-            leave = pltpu.make_async_copy(
-                held[which].at[z],
-                outs[which].at[:, pl.ds(z * per_vox, per_vox)],
-                went.at[which, z],
-            )
-            leave.start()
-            going.append(leave)
-    for leave in going:
-        leave.wait()
+    for copy in copies:
+        copy.wait()
 
 
 def cut(place, refs, slab, layers, per_vox):
-    anywhere = pl.BlockSpec(memory_space=pl.ANY)
     shapes = [
         (layers // 2, refs.shape[0]),
         (layers // 2, refs.shape[0]),
@@ -86,47 +78,38 @@
     ]
     return pl.pallas_call(
         cut_kernel,
-        in_specs=[SMEM, anywhere, anywhere],
-        out_specs=[anywhere] * 3,
+        in_specs=[SMEM, HBM, HBM],
+        out_specs=[VMEM] * 3,
         out_shape=[jax.ShapeDtypeStruct((r, n * per_vox), BF16) for n, r in shapes],
-        scratch_shapes=[pltpu.VMEM((n, r, per_vox), BF16) for n, r in shapes]
-        + [pltpu.SemaphoreType.DMA((3, layers))] * 2,
+        scratch_shapes=[pltpu.SemaphoreType.DMA((3, layers))],
+        compiler_params=room(16),
         cost_estimate=cost(0, 4 * sum(n * r for n, r in shapes) * per_vox),
         name="cut",
     )(place, refs, slab)
 
 
 def deal_kernel(place, slab, mate, *rest):
-    peers = len(rest) - 3
-    outs, held, came, went = rest[:peers], rest[peers], rest[peers + 1], rest[peers + 2]
+    outs, came = rest[:-1], rest[-1]
     rows = slab.shape[0]
-    keep = held.shape[2]
-    per_vox = mate.shape[1] // (peers + 1)
-    coming = []
-    for p in range(peers):
+    keep = outs[0].shape[1]
+    per_vox = mate.shape[1] // (len(outs) + 1)
+    copies = []
+    for p, out in enumerate(outs):
         layer = place[2] ^ (p + 1)
         mine = pl.multiple_of((2 * layer + place[0]) * per_vox, per_vox)
         theirs = pl.multiple_of(layer * per_vox, per_vox)
-        pair = [
+        copies += [
             pltpu.make_async_copy(
-                slab.at[:, pl.ds(mine, keep)], held.at[p, pl.ds(0, rows)], came.at[p, 0]
+                slab.at[:, pl.ds(mine, keep)], out.at[pl.ds(0, rows)], came.at[p, 0]
             ),
             pltpu.make_async_copy(
-                mate.at[:, pl.ds(theirs, keep)], held.at[p, pl.ds(rows, rows)], came.at[p, 1]
+                mate.at[:, pl.ds(theirs, keep)], out.at[pl.ds(rows, rows)], came.at[p, 1]
             ),
         ]
-        for copy in pair:
-            copy.start()
-        coming.append(pair)
-    going = []
-    for p in range(peers):
-        for copy in coming[p]:
-            copy.wait()
-        leave = pltpu.make_async_copy(held.at[p], outs[p], went.at[p])
-        leave.start()
-        going.append(leave)
-    for leave in going:
-        leave.wait()
+    for copy in copies:
+        copy.start()
+    for copy in copies:
+        copy.wait()
 
 
 def deal(place, slab, mate, layers, keep):
@@ -135,14 +118,11 @@
     peers = layers - 1
     return pl.pallas_call(
         deal_kernel,
-        in_specs=[SMEM, anywhere, anywhere],
-        out_specs=[anywhere] * peers,
+        in_specs=[SMEM, HBM, anywhere],
+        out_specs=[VMEM] * peers,
         out_shape=[jax.ShapeDtypeStruct((2 * rows, keep), BF16)] * peers,
-        scratch_shapes=[
-            pltpu.VMEM((peers, 2 * rows, keep), BF16),
-            pltpu.SemaphoreType.DMA((peers, 2)),
-            pltpu.SemaphoreType.DMA((peers,)),
-        ],
+        scratch_shapes=[pltpu.SemaphoreType.DMA((peers, 2))],
+        compiler_params=room(16),
         cost_estimate=cost(0, 8 * rows * peers * keep),
         name="deal",
     )(place, slab, mate)
@@ -198,6 +178,7 @@
         ),
         out_shape=jax.ShapeDtypeStruct((height, 128), F32),
         cost_estimate=cost(12 * masks * per_ref * voxels, 2 * voxels * (per_ref + 2 * masks)),
+        compiler_params=room(16),
         name="brief",
     )(live, refs, wedge, owner, offset, wedge_id)
 
@@ -230,6 +211,7 @@
         out_specs=VMEM,
         out_shape=jax.ShapeDtypeStruct((8, cap), F32),
         cost_estimate=cost(1 << 22, 1 << 18),
+        compiler_params=room(8),
         name="lists",
     )(place, *notes)
 
@@ -264,12 +246,13 @@
                 BF16
             )
 
-    tile = out.shape[1]
+    tile = out.shape[1] // pl.num_programs(0)
+    at = pl.multiple_of(pl.program_id(0) * tile, 128)
 
     def part_of(ref):
         if ref.shape[1] == tile:
             return ref[...]
-        return ref[:, pl.ds(pl.multiple_of(pl.program_id(0) * tile, 128), tile)]
+        return ref[:, pl.ds(at, tile)]
 
     lined = jnp.concatenate(pieces_of(part_of(wedge), 3), axis=0)
     weights = dot(wedge_hot[...], lined)
@@ -282,7 +265,7 @@
             taken += 1
         values = dot(rows_hot[n], jnp.concatenate(stack, axis=0) if len(stack) > 1 else stack[0])
         part = slice(n * height, (n + 1) * height)
-        out[part, :] = (weights[part] * values).astype(BF16)
+        out[part, pl.ds(at, tile)] = (weights[part] * values).astype(BF16)
 
 
 def select(place, blocks, block_specs, pairs, wedge, wedge_spec, rows, tile, steps):
@@ -300,7 +283,7 @@
                 *[pl.BlockSpec((2, 8, cap), lambda t, s: (0, 0, 0))] * len(pairs),
                 wedge_spec,
             ],
-            out_specs=pl.BlockSpec((count * cap, tile), lambda t, s: (0, t)),
+            out_specs=VMEM,
             scratch_shapes=[
                 pltpu.VMEM((count // bunch, bunch * cap, bunch * rows), BF16),
                 pltpu.VMEM((count * cap, 3 * masks), BF16),
@@ -310,54 +293,40 @@
         cost_estimate=cost(
             4 * count * cap * 256 * steps * tile, 2 * count * (cap + rows) * steps * tile
         ),
+        compiler_params=room(32),
         name="select",
     )(place, *blocks, *pairs, wedge)
 
 
-def correl_kernel(blocks, scaled, *rest):
+def correl_kernel(blocks, tile, scaled, *rest):
     refs, out, table = rest[:-2], rest[-2], rest[-1]
-    per_ref = refs[0].shape[0]
-    step = pl.program_id(0)
-    half = pl.num_programs(0) // 2
-
-    @pl.when(step == 0)
-    def _():
-        out[...] = jnp.zeros_like(out)
-
-    def fill(side):
-        for p in range(blocks):
-            table[p * per_ref : (p + 1) * per_ref, :] = refs[2 * p + side][...]
-
-    @pl.when(step < half)
-    def _():
-        fill(0)
-
-    @pl.when(step >= half)
-    def _():
-        fill(1)
-
-    out[...] += dot(scaled[...], table[...], LANES)
+    per_ref, span = refs[0].shape
+    out[...] = jnp.zeros_like(out)
+    for side in range(2):
+
+        def step(t, carry, side=side):
+            at = pl.multiple_of(t * tile, tile)
+            for p in range(blocks):
+                table[p * per_ref : (p + 1) * per_ref, :] = refs[2 * p + side][:, pl.ds(at, tile)]
+            rows = scaled[:, pl.ds(pl.multiple_of(side * span + t * tile, tile), tile)]
+            out[...] += dot(rows, table[...], LANES)
+            return carry
+
+        lax.fori_loop(0, span // tile, step, 0)
 
 
 def correl(scaled, tables, tile):
     height, span = scaled.shape
     blocks = len(tables[0])
-    per_ref = tables[0][0].shape[0]
-    count = blocks * per_ref
-    steps = span // tile
-    half = steps // 2
-    sides = [
-        pl.BlockSpec((per_ref, tile), lambda t: (0, jnp.minimum(t, half - 1))),
-        pl.BlockSpec((per_ref, tile), lambda t: (0, jnp.maximum(t - half, 0))),
-    ]
+    count = blocks * tables[0][0].shape[0]
     refs = [tables[i][p] for p in range(blocks) for i in range(2)]
     return pl.pallas_call(
-        functools.partial(correl_kernel, blocks),
-        grid=(steps,),
-        in_specs=[pl.BlockSpec((height, tile), lambda t: (0, t))] + sides * blocks,
-        out_specs=pl.BlockSpec((height, count), lambda t: (0, 0)),
+        functools.partial(correl_kernel, blocks, tile),
+        in_specs=[VMEM] * (1 + len(refs)),
+        out_specs=VMEM,
         out_shape=jax.ShapeDtypeStruct((height, count), F32),
         scratch_shapes=[pltpu.VMEM((count, tile), BF16)],
+        compiler_params=room(24),
         cost_estimate=cost(2 * height * count * span, 2 * span * (height + count)),
         name="correl",
     )(scaled, *refs)
@@ -398,68 +367,72 @@
         out_specs=VMEM,
         out_shape=jax.ShapeDtypeStruct((2, count, cap), BF16),
         cost_estimate=cost(1 << 24, 1 << 18),
+        compiler_params=room(16),
         name="weigh",
     )(own, got, pair, *notes)
 
 
-def blend_kernel(layers, parts, blocks, masks, steps, place, *rest):
+def blend_kernel(layers, parts, blocks, masks, starts, place, *rest):
     weights, rest = rest[:layers], rest[layers:]
     scaled, pairs = rest[:parts], rest[parts : -blocks - 1]
     outs, turned = rest[-blocks - 1 : -1], rest[-1]
     cap = weights[0].shape[2]
-    per_ref = outs[0].shape[-2]
-
-    @pl.when(pl.program_id(0) == 0)
-    def _():
+    per_ref, tile = outs[0].shape[1:] if not pairs else (outs[0].shape[0], starts[1])
+    for g in range(2 * layers):
+        turned[:, g * cap : (g + 1) * cap] = weights[g // 2][g % 2]
+
+    def mix(at):
+        first, sums = 0, 0.0
+        for part in scaled:
+            height = part.shape[0]
+            sums = sums + dot(turned[:, first : first + height], part[:, pl.ds(at, tile)])
+            first += height
+        return sums.astype(BF16)
+
+    if pairs:
+
+        def step(t, carry):
+            at = pl.multiple_of(t * tile, tile)
+            sums = mix(at)
+            for p, out in enumerate(outs):
+                out[:, pl.ds(at, tile)] = sums[p * per_ref : (p + 1) * per_ref, :]
+            return carry
+
+        lax.fori_loop(0, starts[0], step, 0)
+        total = jnp.zeros((turned.shape[0], masks), F32)
         for g in range(2 * layers):
-            turned[:, g * cap : (g + 1) * cap] = weights[g // 2][g % 2]
-
-    @pl.when(pl.program_id(0) < steps)
-    def _():
-        first = 0
-        sums = 0.0
-        for part in scaled:
-            sums = sums + dot(turned[:, first : first + part.shape[0]], part[...])
-            first += part.shape[0]
-        sums = sums.astype(BF16)
+            marks = hot(iota((masks, cap), 0) == pairs[g // 2][g % 2, 1:2, :])
+            total = total + dot(turned[:, g * cap : (g + 1) * cap], marks, LANES)
+        split = jnp.concatenate(pieces_of(total, 3), axis=1)
+        split = jnp.concatenate(
+            [split, jnp.zeros((split.shape[0], 128 - split.shape[1]), BF16)], axis=1
+        )
         for p, out in enumerate(outs):
-            out[...] = sums[p * per_ref : (p + 1) * per_ref, :].reshape(out.shape)
-
-    if pairs:
-
-        @pl.when(pl.program_id(0) == steps)
-        def _():
-            total = jnp.zeros((turned.shape[0], masks), F32)
-            for g in range(2 * layers):
-                marks = hot(iota((masks, cap), 0) == pairs[g // 2][g % 2, 1:2, :])
-                total = total + dot(turned[:, g * cap : (g + 1) * cap], marks, LANES)
-            split = jnp.concatenate(pieces_of(total, 3), axis=1)
+            out[:, starts[0] * tile :] = split[p * per_ref : (p + 1) * per_ref, :]
+    else:
+        stretch = scaled[0].shape[1] // starts[0]
+
+        def step(t, carry):
+            sums = mix(pl.multiple_of((place[2] ^ t) * stretch + stretch - tile, 128))
             for p, out in enumerate(outs):
-                out[:, : 3 * masks] = split[p * per_ref : (p + 1) * per_ref, :]
-
-
-def blend(place, weights, pairs, scaled, masks, blocks, tile, steps, index):
+                out[t] = sums[p * per_ref : (p + 1) * per_ref, :]
+            return carry
+
+        lax.fori_loop(0, starts[0], step, 0)
+
+
+def blend(place, weights, pairs, scaled, masks, blocks, tile, steps):
     layers = len(weights)
     _, count, cap = weights[0].shape
     per_ref = count // blocks
-    if pairs:
-        shape = (per_ref, steps * tile + 128)
-        spec = pl.BlockSpec((per_ref, tile), lambda t, s: (0, t))
-    else:
-        shape = (steps, per_ref, tile)
-        spec = pl.BlockSpec((1, per_ref, tile), lambda t, s: (t, 0, 0))
-    return pl.pallas_call(
-        functools.partial(blend_kernel, layers, len(scaled), blocks, masks, steps),
-        grid_spec=pltpu.PrefetchScalarGridSpec(
-            num_scalar_prefetch=1,
-            grid=(steps + (1 if pairs else 0),),
-            in_specs=[pl.BlockSpec((2, count, cap), lambda t, s: (0, 0, 0))] * layers
-            + [pl.BlockSpec((part.shape[0], tile), index) for part in scaled]
-            + [pl.BlockSpec((2, 8, cap), lambda t, s: (0, 0, 0))] * len(pairs),
-            out_specs=[spec] * blocks,
-            scratch_shapes=[pltpu.VMEM((count, 2 * layers * cap), BF16)],
-        ),
+    shape = (per_ref, steps * tile + 128) if pairs else (steps, per_ref, tile)
+    return pl.pallas_call(
+        functools.partial(blend_kernel, layers, len(scaled), blocks, masks, (steps, tile)),
+        in_specs=[SMEM] + [VMEM] * (layers + len(scaled) + len(pairs)),
+        out_specs=[VMEM] * blocks,
         out_shape=[jax.ShapeDtypeStruct(shape, BF16)] * blocks,
+        scratch_shapes=[pltpu.VMEM((count, 2 * layers * cap), BF16)],
+        compiler_params=room(24),
         cost_estimate=cost(
             4 * layers * cap * count * steps * tile, 2 * (2 * layers * cap + count) * steps * tile
         ),
@@ -484,6 +457,7 @@
         out_specs=[VMEM] * layers,
         out_shape=[jax.ShapeDtypeStruct((per_ref, tile), BF16)] * layers,
         cost_estimate=cost(0, 2 * (len(parts) + 1) * layers * per_ref * tile),
+        compiler_params=room(16),
         name="fold",
     )(*parts)
 
@@ -524,11 +498,10 @@
     per_ref = shares[0].shape[0]
     masks = wedge.shape[0]
     blocks = len(shares)
-    anywhere = pl.BlockSpec(memory_space=pl.ANY)
     return pl.pallas_call(
         functools.partial(finish_kernel, blocks),
-        in_specs=[SMEM] + [VMEM] * (blocks + len(apart)) + [anywhere],
-        out_specs=anywhere,
+        in_specs=[SMEM] + [VMEM] * (blocks + len(apart)) + [HBM],
+        out_specs=HBM,
         out_shape=jax.ShapeDtypeStruct((per_ref, SPLIT * tile), F32),
         scratch_shapes=[
             pltpu.VMEM((masks, SPLIT * tile), F32),
@@ -537,6 +510,7 @@
             pltpu.SemaphoreType.DMA((SPLIT,)),
         ],
         cost_estimate=cost(0, 8 * per_ref * SPLIT * tile),
+        compiler_params=room(16),
         name="finish",
     )(place, *shares, *apart, wedge)
 
@@ -626,7 +600,7 @@
         2,
     )
     pairs = passed([pair] * layers, "lay", layers)
-    sums = correl(scaled, tables, half // 4)
+    sums = correl(scaled, tables, half // 8)
     got = lax.ppermute(sums, "core", [(0, 1), (1, 0)])
     weights = weigh(sums, got, pair, notes, masks, 1.0 / (32.0 * math.sqrt(voxels)))
     all_weights = passed([weights] * layers, "lay", layers)
@@ -634,7 +608,7 @@
     far_rows = select(
         place,
         pieces[1:],
-        [pl.BlockSpec((2 * slot_count, keep // 2), lambda t, s: (0, t))] * (layers - 1),
+        [VMEM] * (layers - 1),
         pairs[1:],
         wedge,
         here,
@@ -643,31 +617,13 @@
         2,
     )
 
-    apart = blend(
-        place,
-        all_weights[:1],
-        [],
-        [scaled],
-        masks,
-        blocks,
-        tile,
-        layers,
-        lambda t, s: (0, (s[2] ^ t) * SPLIT + SPLIT - 1),
-    )
+    apart = blend(place, all_weights[:1], [], [scaled], masks, blocks, tile, layers)
     apart = passed(apart, "blk", blocks)
     apart = fold(apart)
     apart = passed(apart, "lay", layers)
 
     shares = blend(
-        place,
-        all_weights,
-        pairs,
-        [near_rows, far_rows],
-        masks,
-        blocks,
-        keep // 2,
-        2,
-        lambda t, s: (0, jnp.minimum(t, 1)),
+        place, all_weights, pairs, [near_rows, far_rows], masks, blocks, keep // 4, 4
     )
     shares = passed(shares, "blk", blocks)
     return finish(place, shares, apart, wedge, tile)

time: 184 us -> 175 us (0.951)
  Pallas kernels: 62.7 us -> 30.4 us
  waiting for transfers between devices: 64.4 us -> 95.1 us
  starting transfers between devices: 47.6 us -> 43.9 us
  local copies, waits for them, and re-layouts: 5.98 us -> 4.11 us
  other arithmetic: 1.93 us -> 0.08 us
    ppermute x19, waiting for transfers between devices: 52.9 us -> 75.6 us  [passed(): lax.ppermute(values[p], axis, [(d, d ^ p) for d in range(size)])]
    pallas_call x3, Pallas kernels: 15.3 us -> 5.57 us  [the longest x1 3.73 us: correl(): pl.pallas_call(functools.partial(correl_kernel, blocks, tile), in_specs=[...]
    pallas_call x3, Pallas kernels: 21 us -> 12.5 us  [select(): pl.pallas_call(functools.partial(select_kernel, len(blocks)), grid_spec=p...]
    pallas_call x2, Pallas kernels: 10.5 us -> 4.56 us  [blend(): pl.pallas_call(functools.partial(blend_kernel, layers, len(scaled), block...]
    ppermute x1, waiting for transfers between devices: 8.31 us -> 13.2 us  [per_device(): high_x = lax.ppermute(high, 'blk', over_x)]
    ppermute x19, starting transfers between devices: 31.6 us -> 27.7 us  [passed(): lax.ppermute(values[p], axis, [(d, d ^ p) for d in range(size)])]
    ppermute x1, waiting for transfers between devices: 2.1 us -> 5.07 us  [per_device(): high_xy = lax.ppermute(high_y, 'blk', over_x)]
    pallas_call x1, Pallas kernels: 5.12 us -> 2.96 us  [brief(): pl.pallas_call(brief_kernel, grid_spec=pltpu.PrefetchScalarGridSpec(num_s...]
  transfers between devices with their start and end apart: 30 -> 30, of which waited for: 10 -> 10; matrix products, arithmetic and copies ran while one was open for 1% -> 0% of each run, Pallas kernels for 30% -> 15%
where the time goes in v6:
time: 175 us; the launch traced here: 174 us
  waiting for transfers between devices  95.1 us (54%)
  starting transfers between devices  43.9 us (25%)
  Pallas kernels  30.4 us (17%)
  local copies, waits for them, and re-layouts  4.11 us (2%)
    ppermute x19, waiting for transfers between devices, passed(): lax.ppermute(values[p], axis, [(d, d ^ p) for d in range(size)])  75.6 us
    ppermute x19, starting transfers between devices, passed(): lax.ppermute(values[p], axis, [(d, d ^ p) for d in range(size)])  27.7 us
    ppermute x1, waiting for transfers between devices, per_device(): high_x = lax.ppermute(high, 'blk', over_x)  13.2 us
    pallas_call x3, Pallas kernels, select(): pl.pallas_call(functools.partial(select_kernel, len(blocks)), grid_spec=p...  12.5 us
    ppermute x3, starting transfers between devices, per_device(): lax.ppermute(far[p - 1], 'lay', [(z, z ^ p) for z in range(layers)])  6.73 us
    ppermute x1, waiting for transfers between devices, per_device(): high_xy = lax.ppermute(high_y, 'blk', over_x)  5.07 us
    pallas_call x2, Pallas kernels, blend(): pl.pallas_call(functools.partial(blend_kernel, layers, len(scaled), block...  4.56 us
    unnamed x16, local copies, waits for them, and re-layouts  4.11 us
  transfers between devices with their start and end apart: 30, of which 10 were waited for; matrix products, arithmetic and copies ran while one was open for 0% of the time, Pallas kernels for 15%

profile of v6, /device:TPU:0, one launch (start us, length us, event | category | flops | bytes accessed | tf_op | source)
XLA Modules:
  0.0 174.4 jit_solution(14916665162114629606)
XLA Ops:
  0.1 2.2 %copy-done = bf16[64,32768]{1,0:T(8,128)(2,1)S(1)} copy-done((bf16[64,32768]{1,0:T(8,128)(2,1)S(1)}, bf16[64,32768]{1,0:T(8,128)(2,1)}, u32[]{:S(2)}) %copy-start) | copy-done | bytes 4194328
  5.7 2.6 %collective-permute-start.8 = (bf16[48,8192]{1,0:T(8,128)(2,1)S(1)}, bf16[48,8192]{1,0:T(8,128)(2,1)S(1)}, u32[]{:S(2)}, u32[]{:S(2)}) collective-permute-start(bf16[48,8192]{1,0:T(8,128)(2,1)S(1)} %get-tuple-element.25.rest_1_), channel_id=1, source_target_pairs={{0,2},{1,3},{2,0},{3,1},{4,6},{5,7},{6,4},{7,5},{8,10},{9,11},{10,... | collective-permute-start | bytes 2359304 | tf_op jit(solution)/shard_map/ppermute | solution.py:548
  10.5 3.0 %brief.1.rest_0_ = f32[16,128]{1,0:T(8,128)S(1)} custom-call(s32[1]{0:T(128)S(6)} %copy.8.live, bf16[48,32768]{1,0:T(8,128)(2,1)S(1)} %copy-done.3, f32[8,32768]{1,0:T(8,128)S(1)} %copy-done.4, s32[1,64]{1,0:T(1,128)S(1)} %bitcast.10, s32[1,64]{1,0:T(1,128)S(1)} %bitcast.11, s32[1,64]{1,0:T(1,128)S(1)} %bitcast.12), custom_call_target="tpu_custom_call" | custom-call | flops 150994944 | bytes 4194304 | tf_op jit(solution)/shard_map/brief/pallas_call | solution.py:164
  14.8 13.3 %collective-permute-done.1.rest_1_ = f32[16,128]{1,0:T(8,128)S(1)} collective-permute-done((f32[16,128]{1,0:T(8,128)S(1)}, f32[16,128]{1,0:T(8,128)S(1)}, u32[]{:S(2)}, u32[]{:S(2)}) %collective-permute-start.1) | collective-permute-done | bytes 8224 | tf_op jit(solution)/shard_map/ppermute | solution.py:523
  29.5 3.1 %collective-permute-done.3.rest_3_ = f32[16,128]{1,0:T(8,128)S(1)} collective-permute-done((f32[16,128]{1,0:T(8,128)S(1)}, f32[16,128]{1,0:T(8,128)S(1)}, u32[]{:S(2)}, u32[]{:S(2)}) %collective-permute-start.3) | collective-permute-done | bytes 8224 | tf_op jit(solution)/shard_map/ppermute | solution.py:523
  40.9 13.2 %collective-permute-done.6.rest_3_ = bf16[48,8192]{1,0:T(8,128)(2,1)S(1)} collective-permute-done((bf16[48,8192]{1,0:T(8,128)(2,1)S(1)}, bf16[48,8192]{1,0:T(8,128)(2,1)S(1)}, u32[]{:S(2)}, u32[]{:S(2)}) %collective-permute-start.6) | collective-permute-done | bytes 786464 | tf_op jit(solution)/shard_map/ppermute | solution.py:549
  54.1 2.6 %collective-permute-start.16 = (bf16[128,3072]{1,0:T(8,128)(2,1)S(1)}, bf16[128,3072]{1,0:T(8,128)(2,1)S(1)}, u32[]{:S(2)}, u32[]{:S(2)}) collective-permute-start(bf16[128,3072]{1,0:T(8,128)(2,1)S(1)} %get-tuple-element.27), channel_id=1, source_target_pairs={{0,16},{8,24},{16,0},{24,8},{1,17},{9,25},{17,1},{25,9},{2,18},{10... | collective-permute-start | bytes 2359304 | tf_op jit(solution)/shard_map/ppermute | solution.py:559
  56.7 2.5 %collective-permute-start.17 = (bf16[128,3072]{1,0:T(8,128)(2,1)S(1)}, bf16[128,3072]{1,0:T(8,128)(2,1)S(1)}, u32[]{:S(2)}, u32[]{:S(2)}) collective-permute-start(bf16[128,3072]{1,0:T(8,128)(2,1)S(1)} %get-tuple-element.28), channel_id=1, source_target_pairs={{0,24},{8,16},{16,8},{24,0},{1,25},{9,17},{17,9},{25,1},{2,26},{10... | collective-permute-start | bytes 2359304 | tf_op jit(solution)/shard_map/ppermute | solution.py:559
  59.2 6.2 %select.3.scaled.rest_1_ = bf16[256,16384]{1,0:T(8,128)(2,1)S(1)} custom-call(s32[4]{0:T(128)S(1)} %pad_add_fusion.place, bf16[64,32768]{1,0:T(8,128)(2,1)S(1)} %copy-done.1, bf16[64,16384]{1,0:T(8,128)(2,1)S(1)} %collective-permute-done.rest_1_.mate, f32[2,8,128]{2,1,0:T(8,128)S(1)} %pad_maximum_fusion.rest_2_.pair.rest_6_, f32[8,32768]{1,0:T(8,128)S(1)} %copy-done.4), custom_call_target="tpu_custom_call" | custom-call | flops 4294967296 | bytes 12582912 | tf_op jit(solution)/shard_map/select/pallas_call | solution.py:276
  65.4 5.1 %collective-permute-done.10.rest_7_ = bf16[48,8192]{1,0:T(8,128)(2,1)S(1)} collective-permute-done((bf16[48,8192]{1,0:T(8,128)(2,1)S(1)}, bf16[48,8192]{1,0:T(8,128)(2,1)S(1)}, u32[]{:S(2)}, u32[]{:S(2)}) %collective-permute-start.10) | collective-permute-done | bytes 786464 | tf_op jit(solution)/shard_map/ppermute | solution.py:552
  71.7 3.7 %correl.1.own = f32[256,192]{1,0:T(8,128)S(1)} custom-call(bf16[256,16384]{1,0:T(8,128)(2,1)S(1)} %select.3.scaled.rest_1_, bf16[48,8192]{1,0:T(8,128)(2,1)S(1)} %get-tuple-element.24.rest_0_, bf16[48,8192]{1,0:T(8,128)(2,1)S(1)} %get-tuple-element.25.rest_1_, bf16[48,8192]{1,0:T(8,128)(2,1)S(1)} %collective-permute-done.5.rest_2_, ...), custom_call_target="tpu_custom_call" | custom-call | flops 1610612736 | bytes 14680064 | tf_op jit(solution)/shard_map/correl/pallas_call | solution.py:323
  77.2 2.6 %collective-permute-start.19 = (f32[2,8,128]{2,1,0:T(8,128)S(1)}, f32[2,8,128]{2,1,0:T(8,128)S(1)}, u32[]{:S(2)}, u32[]{:S(2)}) collective-permute-start(f32[2,8,128]{2,1,0:T(8,128)S(1)} %pad_maximum_fusion.rest_2_.pair.rest_6_), channel_id=1, source_target_pairs={{0,16},{8,24},{16,0},{24,8},{1,17},{9,25},{17,1},{25,9},{2,18},{10... | collective-permute-start | bytes 24584 | tf_op jit(solution)/shard_map/ppermute | solution.py:523
  80.9 11.7 %collective-permute-done.18.rest_3_.rest_7_ = f32[2,8,128]{2,1,0:T(8,128)S(1)} collective-permute-done((f32[2,8,128]{2,1,0:T(8,128)S(1)}, f32[2,8,128]{2,1,0:T(8,128)S(1)}, u32[]{:S(2)}, u32[]{:S(2)}) %collective-permute-start.18) | collective-permute-done | bytes 8224 | tf_op jit(solution)/shard_map/ppermute | solution.py:523
  92.6 3.0 %collective-permute-start.20 = (f32[2,8,128]{2,1,0:T(8,128)S(1)}, f32[2,8,128]{2,1,0:T(8,128)S(1)}, u32[]{:S(2)}, u32[]{:S(2)}) collective-permute-start(f32[2,8,128]{2,1,0:T(8,128)S(1)} %pad_maximum_fusion.rest_2_.pair.rest_6_), channel_id=1, source_target_pairs={{0,24},{8,16},{16,8},{24,0},{1,25},{9,17},{17,9},{25,1},{2,26},{10... | collective-permute-start | bytes 24584 | tf_op jit(solution)/shard_map/ppermute | solution.py:523
  95.6 29.3 %collective-permute-done.19.rest_4_.rest_8_ = f32[2,8,128]{2,1,0:T(8,128)S(1)} collective-permute-done((f32[2,8,128]{2,1,0:T(8,128)S(1)}, f32[2,8,128]{2,1,0:T(8,128)S(1)}, u32[]{:S(2)}, u32[]{:S(2)}) %collective-permute-start.19) | collective-permute-done | bytes 8224 | tf_op jit(solution)/shard_map/ppermute | solution.py:523
  128.8 2.1 %select.4.rest_4_ = bf16[256,3072]{1,0:T(8,128)(2,1)S(1)} custom-call(s32[4]{0:T(128)S(1)} %pad_add_fusion.place, bf16[64,32768]{1,0:T(8,128)(2,1)S(1)} %copy-done.1, bf16[64,16384]{1,0:T(8,128)(2,1)S(1)} %collective-permute-done.rest_1_.mate, f32[2,8,128]{2,1,0:T(8,128)S(1)} %pad_maximum_fusion.rest_2_.pair.rest_6_, f32[8,32768]{1,0:T(8,128)S(1)} %copy-done.4), custom_call_target="tpu_custom_call" | custom-call | flops 805306368 | bytes 2359296 | tf_op jit(solution)/shard_map/select/pallas_call | solution.py:276
  130.9 3.4 %collective-permute-start.13 = (bf16[2,192,128]{2,1,0:T(8,128)(2,1)S(1)}, bf16[2,192,128]{2,1,0:T(8,128)(2,1)S(1)}, u32[]{:S(2)}, u32[]{:S(2)}) collective-permute-start(bf16[2,192,128]{2,1,0:T(8,128)(2,1)S(1)} %weigh.1.rest_0_), channel_id=1, source_target_pairs={{0,16},{8,24},{16,0},{24,8},{1,17},{9,25},{17,1},{25,9},{2,18},{10... | collective-permute-start | bytes 294920 | tf_op jit(solution)/shard_map/ppermute | solution.py:523
  136.7 4.2 %select.5.rest_5_ = bf16[768,3072]{1,0:T(8,128)(2,1)S(1)} custom-call(s32[4]{0:T(128)S(1)} %pad_add_fusion.place, bf16[128,3072]{1,0:T(8,128)(2,1)S(1)} %collective-permute-done.15.rest_0_, bf16[128,3072]{1,0:T(8,128)(2,1)S(1)} %collective-permute-done.16.rest_1_, bf16[128,3072]{1,0:T(8,128)(2,1)S(1)} %collective-permute-done.17.rest_2_, ...), custom_call_target="tpu_custom_call" | custom-call | flops 2415919104 | bytes 7077888 | tf_op jit(solution)/shard_map/select/pallas_call | solution.py:276
  140.9 2.9 %blend.2 = (bf16[48,3200]{1,0:T(8,128)(2,1)S(1)}, bf16[48,3200]{1,0:T(8,128)(2,1)S(1)}, bf16[48,3200]{1,0:T(8,128)(2,1)S(1)}, bf16[48,3200]{1,0:T(8,128)(2,1)S(1)}) custom-call(s32[4]{0:T(128)S(1)} %pad_add_fusion.place, bf16[2,192,128]{2,1,0:T(8,128)(2,1)S(1)} %weigh.1.rest_0_, bf16[2,192,128]{2,1,0:T(8,128)(2,1)S(1)} %collective-permute-done.12.rest_1_, ...), custom_call_target="tpu_custom_call" | custom-call | flops 1207959552 | bytes 7471104 | tf_op jit(solution)/shard_map/blend/pallas_call | solution.py:429
  147.4 13.3 %collective-permute-done.25.refs_2_ = bf16[4,48,1024]{2,1,0:T(8,128)(2,1)S(1)} collective-permute-done((bf16[4,48,1024]{2,1,0:T(8,128)(2,1)S(1)}, bf16[4,48,1024]{2,1,0:T(8,128)(2,1)S(1)}, u32[]{:S(2)}, u32[]{:S(2)}) %collective-permute-start.25) | collective-permute-done | bytes 393248 | tf_op jit(solution)/shard_map/ppermute | solution.py:523
  161.2 3.1 %collective-permute-start.28 = (bf16[48,1024]{1,0:T(8,128)(2,1)S(1)}, bf16[48,1024]{1,0:T(8,128)(2,1)S(1)}, u32[]{:S(2)}, u32[]{:S(2)}) collective-permute-start(bf16[48,1024]{1,0:T(8,128)(2,1)S(1)} %get-tuple-element.39), channel_id=1, source_target_pairs={{0,16},{8,24},{16,0},{24,8},{1,17},{9,25},{17,1},{25,9},{2,18},{10... | collective-permute-start | bytes 294920 | tf_op jit(solution)/shard_map/ppermute | solution.py:523
  165.5 2.8 %collective-permute-start.29 = (bf16[48,1024]{1,0:T(8,128)(2,1)S(1)}, bf16[48,1024]{1,0:T(8,128)(2,1)S(1)}, u32[]{:S(2)}, u32[]{:S(2)}) collective-permute-start(bf16[48,1024]{1,0:T(8,128)(2,1)S(1)} %get-tuple-element.40), channel_id=1, source_target_pairs={{0,24},{8,16},{16,8},{24,0},{1,25},{9,17},{17,9},{25,1},{2,26},{10... | collective-permute-start | bytes 294920 | tf_op jit(solution)/shard_map/ppermute | solution.py:523
  168.4 3.6 %collective-permute-done.29.rest_7_ = bf16[48,1024]{1,0:T(8,128)(2,1)S(1)} collective-permute-done((bf16[48,1024]{1,0:T(8,128)(2,1)S(1)}, bf16[48,1024]{1,0:T(8,128)(2,1)S(1)}, u32[]{:S(2)}, u32[]{:S(2)}) %collective-permute-start.29) | collective-permute-done | bytes 98336 | tf_op jit(solution)/shard_map/ppermute | solution.py:523
  172.0 2.4 %finish.1 = f32[48,4096]{1,0:T(8,128)} custom-call(s32[4]{0:T(128)S(1)} %pad_add_fusion.place, bf16[48,3200]{1,0:T(8,128)(2,1)S(1)} %get-tuple-element.29.rest_0_, bf16[48,3200]{1,0:T(8,128)(2,1)S(1)} %collective-permute-done.21.rest_1_, bf16[48,3200]{1,0:T(8,128)(2,1)S(1)} %collective-permute-done.22.rest_2_, ...), custom_call_target="tpu_custom_call" | custom-call | bytes 1572864 | tf_op jit(solution)/shard_map/finish/pallas_call | solution.py:501
  (67 shorter events, 31.7 us)
Async XLA Ops:
  5.2 33.2 %collective-permute-start = (bf16[64,16384]{1,0:T(8,128)(2,1)S(1)}, bf16[64,16384]{1,0:T(8,128)(2,1)S(1)}, u32[]{:S(2)}, u32[]{:S(2)}) collective-permute-start(bf16[64,16384]{1,0:T(8,128)(2,1)S(1)} %get-tuple-element.23), channel_id=1, source_target_pairs={{0,4},{4,0},{1,5},{5,1},{2,6},{6,2},{3,7},{7,3},{8,12},{12,8},{9,1... | collective-permute-start | bytes 6291464 | tf_op jit(solution)/shard_map/ppermute | solution.py:544
  5.7 30.0 %collective-permute-start.8 = (bf16[48,8192]{1,0:T(8,128)(2,1)S(1)}, bf16[48,8192]{1,0:T(8,128)(2,1)S(1)}, u32[]{:S(2)}, u32[]{:S(2)}) collective-permute-start(bf16[48,8192]{1,0:T(8,128)(2,1)S(1)} %get-tuple-element.25.rest_1_), channel_id=1, source_target_pairs={{0,2},{1,3},{2,0},{3,1},{4,6},{5,7},{6,4},{7,5},{8,10},{9,11},{10,... | collective-permute-start | bytes 2359304 | tf_op jit(solution)/shard_map/ppermute | solution.py:548
  8.3 28.5 %collective-permute-start.5 = (bf16[48,8192]{1,0:T(8,128)(2,1)S(1)}, bf16[48,8192]{1,0:T(8,128)(2,1)S(1)}, u32[]{:S(2)}, u32[]{:S(2)}) collective-permute-start(bf16[48,8192]{1,0:T(8,128)(2,1)S(1)} %get-tuple-element.24.rest_0_), channel_id=1, source_target_pairs={{0,1},{1,0},{2,3},{3,2},{4,5},{5,4},{6,7},{7,6},{8,9},{9,8},{10,11... | collective-permute-start | bytes 2359304 | tf_op jit(solution)/shard_map/ppermute | solution.py:547
  13.5 14.6 %collective-permute-start.1 = (f32[16,128]{1,0:T(8,128)S(1)}, f32[16,128]{1,0:T(8,128)S(1)}, u32[]{:S(2)}, u32[]{:S(2)}) collective-permute-start(f32[16,128]{1,0:T(8,128)S(1)} %brief.1.rest_0_), channel_id=1, source_target_pairs={{0,1},{1,0},{2,3},{3,2},{4,5},{5,4},{6,7},{7,6},{8,9},{9,8},{10,11... | collective-permute-start | bytes 24584 | tf_op jit(solution)/shard_map/ppermute | solution.py:523
  14.1 15.5 %collective-permute-start.2 = (f32[16,128]{1,0:T(8,128)S(1)}, f32[16,128]{1,0:T(8,128)S(1)}, u32[]{:S(2)}, u32[]{:S(2)}) collective-permute-start(f32[16,128]{1,0:T(8,128)S(1)} %brief.1.rest_0_), channel_id=1, source_target_pairs={{0,2},{1,3},{2,0},{3,1},{4,6},{5,7},{6,4},{7,5},{8,10},{9,11},{10,... | collective-permute-start | bytes 24584 | tf_op jit(solution)/shard_map/ppermute | solution.py:523
  33.7 20.5 %collective-permute-start.6 = (bf16[48,8192]{1,0:T(8,128)(2,1)S(1)}, bf16[48,8192]{1,0:T(8,128)(2,1)S(1)}, u32[]{:S(2)}, u32[]{:S(2)}) collective-permute-start(bf16[48,8192]{1,0:T(8,128)(2,1)S(1)} %get-tuple-element.25.rest_1_), channel_id=1, source_target_pairs={{0,1},{1,0},{2,3},{3,2},{4,5},{5,4},{6,7},{7,6},{8,9},{9,8},{10,11... | collective-permute-start | bytes 2359304 | tf_op jit(solution)/shard_map/ppermute | solution.py:549
  35.2 21.5 %collective-permute-start.7 = (bf16[48,8192]{1,0:T(8,128)(2,1)S(1)}, bf16[48,8192]{1,0:T(8,128)(2,1)S(1)}, u32[]{:S(2)}, u32[]{:S(2)}) collective-permute-start(bf16[48,8192]{1,0:T(8,128)(2,1)S(1)} %get-tuple-element.24.rest_0_), channel_id=1, source_target_pairs={{0,2},{1,3},{2,0},{3,1},{4,6},{5,7},{6,4},{7,5},{8,10},{9,11},{10,... | collective-permute-start | bytes 2359304 | tf_op jit(solution)/shard_map/ppermute | solution.py:550
  35.7 34.8 %collective-permute-start.10 = (bf16[48,8192]{1,0:T(8,128)(2,1)S(1)}, bf16[48,8192]{1,0:T(8,128)(2,1)S(1)}, u32[]{:S(2)}, u32[]{:S(2)}) collective-permute-start(bf16[48,8192]{1,0:T(8,128)(2,1)S(1)} %collective-permute-done.8.rest_5_), channel_id=1, source_target_pairs={{0,1},{1,0},{2,3},{3,2},{4,5},{5,4},{6,7},{7,6},{8,9},{9,8},{10,11... | collective-permute-start | bytes 2359304 | tf_op jit(solution)/shard_map/ppermute | solution.py:552
  36.9 34.9 %collective-permute-start.9 = (bf16[48,8192]{1,0:T(8,128)(2,1)S(1)}, bf16[48,8192]{1,0:T(8,128)(2,1)S(1)}, u32[]{:S(2)}, u32[]{:S(2)}) collective-permute-start(bf16[48,8192]{1,0:T(8,128)(2,1)S(1)} %collective-permute-done.5.rest_2_), channel_id=1, source_target_pairs={{0,2},{1,3},{2,0},{3,1},{4,6},{5,7},{6,4},{7,5},{8,10},{9,11},{10,... | collective-permute-start | bytes 2359304 | tf_op jit(solution)/shard_map/ppermute | solution.py:551
  39.3 95.1 %collective-permute-start.15 = (bf16[128,3072]{1,0:T(8,128)(2,1)S(1)}, bf16[128,3072]{1,0:T(8,128)(2,1)S(1)}, u32[]{:S(2)}, u32[]{:S(2)}) collective-permute-start(bf16[128,3072]{1,0:T(8,128)(2,1)S(1)} %get-tuple-element.26), channel_id=1, source_target_pairs={{0,8},{8,0},{16,24},{24,16},{1,9},{9,1},{17,25},{25,17},{2,10},{10... | collective-permute-start | bytes 2359304 | tf_op jit(solution)/shard_map/ppermute | solution.py:559
  54.1 80.6 %collective-permute-start.16 = (bf16[128,3072]{1,0:T(8,128)(2,1)S(1)}, bf16[128,3072]{1,0:T(8,128)(2,1)S(1)}, u32[]{:S(2)}, u32[]{:S(2)}) collective-permute-start(bf16[128,3072]{1,0:T(8,128)(2,1)S(1)} %get-tuple-element.27), channel_id=1, source_target_pairs={{0,16},{8,24},{16,0},{24,8},{1,17},{9,25},{17,1},{25,9},{2,18},{10... | collective-permute-start | bytes 2359304 | tf_op jit(solution)/shard_map/ppermute | solution.py:559
  56.7 78.5 %collective-permute-start.17 = (bf16[128,3072]{1,0:T(8,128)(2,1)S(1)}, bf16[128,3072]{1,0:T(8,128)(2,1)S(1)}, u32[]{:S(2)}, u32[]{:S(2)}) collective-permute-start(bf16[128,3072]{1,0:T(8,128)(2,1)S(1)} %get-tuple-element.28), channel_id=1, source_target_pairs={{0,24},{8,16},{16,8},{24,0},{1,25},{9,17},{17,9},{25,1},{2,26},{10... | collective-permute-start | bytes 2359304 | tf_op jit(solution)/shard_map/ppermute | solution.py:559
  75.5 17.1 %collective-permute-start.18 = (f32[2,8,128]{2,1,0:T(8,128)S(1)}, f32[2,8,128]{2,1,0:T(8,128)S(1)}, u32[]{:S(2)}, u32[]{:S(2)}) collective-permute-start(f32[2,8,128]{2,1,0:T(8,128)S(1)} %pad_maximum_fusion.rest_2_.pair.rest_6_), channel_id=1, source_target_pairs={{0,8},{8,0},{16,24},{24,16},{1,9},{9,1},{17,25},{25,17},{2,10},{10... | collective-permute-start | bytes 24584 | tf_op jit(solution)/shard_map/ppermute | solution.py:523
  77.2 47.7 %collective-permute-start.19 = (f32[2,8,128]{2,1,0:T(8,128)S(1)}, f32[2,8,128]{2,1,0:T(8,128)S(1)}, u32[]{:S(2)}, u32[]{:S(2)}) collective-permute-start(f32[2,8,128]{2,1,0:T(8,128)S(1)} %pad_maximum_fusion.rest_2_.pair.rest_6_), channel_id=1, source_target_pairs={{0,16},{8,24},{16,0},{24,8},{1,17},{9,25},{17,1},{25,9},{2,18},{10... | collective-permute-start | bytes 24584 | tf_op jit(solution)/shard_map/ppermute | solution.py:523
  92.6 34.6 %collective-permute-start.20 = (f32[2,8,128]{2,1,0:T(8,128)S(1)}, f32[2,8,128]{2,1,0:T(8,128)S(1)}, u32[]{:S(2)}, u32[]{:S(2)}) collective-permute-start(f32[2,8,128]{2,1,0:T(8,128)S(1)} %pad_maximum_fusion.rest_2_.pair.rest_6_), channel_id=1, source_target_pairs={{0,24},{8,16},{16,8},{24,0},{1,25},{9,17},{17,9},{25,1},{2,26},{10... | collective-permute-start | bytes 24584 | tf_op jit(solution)/shard_map/ppermute | solution.py:523
  127.2 18.7 %collective-permute-start.24 = (bf16[4,48,1024]{2,1,0:T(8,128)(2,1)S(1)}, bf16[4,48,1024]{2,1,0:T(8,128)(2,1)S(1)}, u32[]{:S(2)}, u32[]{:S(2)}) collective-permute-start(bf16[4,48,1024]{2,1,0:T(8,128)(2,1)S(1)} %get-tuple-element.34), channel_id=1, source_target_pairs={{0,1},{1,0},{2,3},{3,2},{4,5},{5,4},{6,7},{7,6},{8,9},{9,8},{10,11... | collective-permute-start | bytes 1179656 | tf_op jit(solution)/shard_map/ppermute | solution.py:523
  130.9 9.9 %collective-permute-start.13 = (bf16[2,192,128]{2,1,0:T(8,128)(2,1)S(1)}, bf16[2,192,128]{2,1,0:T(8,128)(2,1)S(1)}, u32[]{:S(2)}, u32[]{:S(2)}) collective-permute-start(bf16[2,192,128]{2,1,0:T(8,128)(2,1)S(1)} %weigh.1.rest_0_), channel_id=1, source_target_pairs={{0,16},{8,24},{16,0},{24,8},{1,17},{9,25},{17,1},{25,9},{2,18},{10... | collective-permute-start | bytes 294920 | tf_op jit(solution)/shard_map/ppermute | solution.py:523
  134.4 6.5 %collective-permute-start.14 = (bf16[2,192,128]{2,1,0:T(8,128)(2,1)S(1)}, bf16[2,192,128]{2,1,0:T(8,128)(2,1)S(1)}, u32[]{:S(2)}, u32[]{:S(2)}) collective-permute-start(bf16[2,192,128]{2,1,0:T(8,128)(2,1)S(1)} %weigh.1.rest_0_), channel_id=1, source_target_pairs={{0,24},{8,16},{16,8},{24,0},{1,25},{9,17},{17,9},{25,1},{2,26},{10... | collective-permute-start | bytes 294920 | tf_op jit(solution)/shard_map/ppermute | solution.py:523
  134.7 25.9 %collective-permute-start.25 = (bf16[4,48,1024]{2,1,0:T(8,128)(2,1)S(1)}, bf16[4,48,1024]{2,1,0:T(8,128)(2,1)S(1)}, u32[]{:S(2)}, u32[]{:S(2)}) collective-permute-start(bf16[4,48,1024]{2,1,0:T(8,128)(2,1)S(1)} %get-tuple-element.35), channel_id=1, source_target_pairs={{0,2},{1,3},{2,0},{3,1},{4,6},{5,7},{6,4},{7,5},{8,10},{9,11},{10,... | collective-permute-start | bytes 1179656 | tf_op jit(solution)/shard_map/ppermute | solution.py:523
  135.2 25.4 %collective-permute-start.26 = (bf16[4,48,1024]{2,1,0:T(8,128)(2,1)S(1)}, bf16[4,48,1024]{2,1,0:T(8,128)(2,1)S(1)}, u32[]{:S(2)}, u32[]{:S(2)}) collective-permute-start(bf16[4,48,1024]{2,1,0:T(8,128)(2,1)S(1)} %get-tuple-element.36), channel_id=1, source_target_pairs={{0,3},{1,2},{2,1},{3,0},{4,7},{5,6},{6,5},{7,4},{8,11},{9,10},{10,... | collective-permute-start | bytes 1179656 | tf_op jit(solution)/shard_map/ppermute | solution.py:523
  143.8 28.1 %collective-permute-start.21 = (bf16[48,3200]{1,0:T(8,128)(2,1)S(1)}, bf16[48,3200]{1,0:T(8,128)(2,1)S(1)}, u32[]{:S(2)}, u32[]{:S(2)}) collective-permute-start(bf16[48,3200]{1,0:T(8,128)(2,1)S(1)} %get-tuple-element.30), channel_id=1, source_target_pairs={{0,1},{1,0},{2,3},{3,2},{4,5},{5,4},{6,7},{7,6},{8,9},{9,8},{10,11... | collective-permute-start | bytes 921608 | tf_op jit(solution)/shard_map/ppermute | solution.py:523
  145.4 26.6 %collective-permute-start.22 = (bf16[48,3200]{1,0:T(8,128)(2,1)S(1)}, bf16[48,3200]{1,0:T(8,128)(2,1)S(1)}, u32[]{:S(2)}, u32[]{:S(2)}) collective-permute-start(bf16[48,3200]{1,0:T(8,128)(2,1)S(1)} %get-tuple-element.31), channel_id=1, source_target_pairs={{0,2},{1,3},{2,0},{3,1},{4,6},{5,7},{6,4},{7,5},{8,10},{9,11},{10,... | collective-permute-start | bytes 921608 | tf_op jit(solution)/shard_map/ppermute | solution.py:523
  145.9 26.1 %collective-permute-start.23 = (bf16[48,3200]{1,0:T(8,128)(2,1)S(1)}, bf16[48,3200]{1,0:T(8,128)(2,1)S(1)}, u32[]{:S(2)}, u32[]{:S(2)}) collective-permute-start(bf16[48,3200]{1,0:T(8,128)(2,1)S(1)} %get-tuple-element.32), channel_id=1, source_target_pairs={{0,3},{1,2},{2,1},{3,0},{4,7},{5,6},{6,5},{7,4},{8,11},{9,10},{10,... | collective-permute-start | bytes 921608 | tf_op jit(solution)/shard_map/ppermute | solution.py:523
  161.2 7.1 %collective-permute-start.28 = (bf16[48,1024]{1,0:T(8,128)(2,1)S(1)}, bf16[48,1024]{1,0:T(8,128)(2,1)S(1)}, u32[]{:S(2)}, u32[]{:S(2)}) collective-permute-start(bf16[48,1024]{1,0:T(8,128)(2,1)S(1)} %get-tuple-element.39), channel_id=1, source_target_pairs={{0,16},{8,24},{16,0},{24,8},{1,17},{9,25},{17,1},{25,9},{2,18},{10... | collective-permute-start | bytes 294920 | tf_op jit(solution)/shard_map/ppermute | solution.py:523
  (14 other events, 93.9 us)

commit v7 on v6

--- a/solution.py
+++ b/solution.py
@@ -540,7 +540,10 @@
     layer = lax.axis_index("lay").astype(jnp.int32)
     place = jnp.stack([core, layer * 2 + core, layer, block])
 
-    low, high, aside = cut(place, references, slab, layers, per_vox)
+    slab_hbm, refs_hbm = (
+        pltpu.with_memory_space_constraint(value, pltpu.HBM) for value in (slab, references)
+    )
+    low, high, aside = cut(place, refs_hbm, slab_hbm, layers, per_vox)
     mate = lax.ppermute(aside, "core", [(0, 1), (1, 0)])
     if blocks == 4:
         over_x, over_y = [(b, b ^ 1) for b in range(4)], [(b, b ^ 2) for b in range(4)]
@@ -553,7 +556,7 @@
         tables = [[low, low_x, low_y, low_xy], [high, high_x, high_y, high_xy]]
     else:
         tables = [passed([s] * blocks, "blk", blocks) for s in (low, high)]
-    far = deal(place, slab, mate, layers, keep)
+    far = deal(place, slab_hbm, mate, layers, keep)
     pieces = [None] * layers
     for p in range(1, layers):
         pieces[p] = lax.ppermute(far[p - 1], "lay", [(z, z ^ p) for z in range(layers)])

time: 175 us -> 172 us (0.983)
  local copies, waits for them, and re-layouts: 4.11 us -> 0.02 us
  Pallas kernels: 30.4 us -> 33.5 us
  waiting for transfers between devices: 95.1 us -> 92.9 us
    unnamed x16 -> x12, local copies, waits for them, and re-layouts: 4.11 us -> 0.02 us
    pallas_call x1, Pallas kernels: 0.99 us -> 2.92 us  [cut(): pl.pallas_call(cut_kernel, in_specs=[SMEM, HBM, HBM], out_specs=[VMEM] *...]
  transfers between devices with their start and end apart: 30 -> 30, of which waited for: 10 -> 11; matrix products, arithmetic and copies ran while one was open for 0% -> 0% of each run, Pallas kernels for 15% -> 16%
where the time goes in v7:
time: 172 us
  waiting for transfers between devices  92.9 us (54%)
  starting transfers between devices  44.6 us (26%)
  Pallas kernels  33.5 us (19%)
    ppermute x19, waiting for transfers between devices, passed(): lax.ppermute(values[p], axis, [(d, d ^ p) for d in range(size)])  74.6 us
    ppermute x19, starting transfers between devices, passed(): lax.ppermute(values[p], axis, [(d, d ^ p) for d in range(size)])  28.5 us
    pallas_call x3, Pallas kernels, select(): pl.pallas_call(functools.partial(select_kernel, len(blocks)), grid_spec=p...  12.5 us
    ppermute x1, waiting for transfers between devices, per_device(): high_x = lax.ppermute(high, 'blk', over_x)  12 us
    ppermute x3, starting transfers between devices, per_device(): lax.ppermute(far[p - 1], 'lay', [(z, z ^ p) for z in range(layers)])  6.73 us
    ppermute x1, waiting for transfers between devices, per_device(): high_xy = lax.ppermute(high_y, 'blk', over_x)  5.07 us
    pallas_call x2, Pallas kernels, blend(): pl.pallas_call(functools.partial(blend_kernel, layers, len(scaled), block...  4.57 us
    pallas_call x1, Pallas kernels, correl(): pl.pallas_call(functools.partial(correl_kernel, blocks, tile), in_specs=[...  3.72 us
  transfers between devices with their start and end apart: 30, of which 11 were waited for; matrix products, arithmetic and copies ran while one was open for 0% of the time, Pallas kernels for 16%

profile of v7, /device:TPU:0, one launch (start us, length us, event | category | flops | bytes accessed | tf_op | source)
XLA Modules:
  0.0 172.0 jit_solution(9674279053145641565)
XLA Ops:
  0.1 2.9 %cut.1 = (bf16[48,8192]{1,0:T(8,128)(2,1)S(1)}, bf16[48,8192]{1,0:T(8,128)(2,1)S(1)}, bf16[64,16384]{1,0:T(8,128)(2,1)S(1)}) custom-call(s32[4]{0:T(128)S(1)} %pad_add_fusion.place, bf16[48,32768]{1,0:T(8,128)(2,1)} %refs.3, bf16[64,32768]{1,0:T(8,128)(2,1)} %slab.3), custom_call_target="tpu_custom_call" | custom-call | bytes 7340032 | tf_op jit(solution)/shard_map/cut/pallas_call | solution.py:79
  3.6 2.6 %collective-permute-start.8 = (bf16[48,8192]{1,0:T(8,128)(2,1)S(1)}, bf16[48,8192]{1,0:T(8,128)(2,1)S(1)}, u32[]{:S(2)}, u32[]{:S(2)}) collective-permute-start(bf16[48,8192]{1,0:T(8,128)(2,1)S(1)} %get-tuple-element.25.rest_1_), channel_id=1, source_target_pairs={{0,2},{1,3},{2,0},{3,1},{4,6},{5,7},{6,4},{7,5},{8,10},{9,11},{10,... | collective-permute-start | bytes 2359304 | tf_op jit(solution)/shard_map/ppermute | solution.py:551
  8.4 3.0 %brief.1.rest_0_ = f32[16,128]{1,0:T(8,128)S(1)} custom-call(s32[1]{0:T(128)S(6)} %copy.8.live, bf16[48,32768]{1,0:T(8,128)(2,1)S(1)} %copy-done.1, f32[8,32768]{1,0:T(8,128)S(1)} %copy-done.2, s32[1,64]{1,0:T(1,128)S(1)} %bitcast.10, s32[1,64]{1,0:T(1,128)S(1)} %bitcast.11, s32[1,64]{1,0:T(1,128)S(1)} %bitcast.12), custom_call_target="tpu_custom_call" | custom-call | flops 150994944 | bytes 4194304 | tf_op jit(solution)/shard_map/brief/pallas_call | solution.py:164
  12.0 13.9 %collective-permute-done.1.rest_1_ = f32[16,128]{1,0:T(8,128)S(1)} collective-permute-done((f32[16,128]{1,0:T(8,128)S(1)}, f32[16,128]{1,0:T(8,128)S(1)}, u32[]{:S(2)}, u32[]{:S(2)}) %collective-permute-start.1) | collective-permute-done | bytes 8224 | tf_op jit(solution)/shard_map/ppermute | solution.py:523
  27.4 3.1 %collective-permute-done.3.rest_3_ = f32[16,128]{1,0:T(8,128)S(1)} collective-permute-done((f32[16,128]{1,0:T(8,128)S(1)}, f32[16,128]{1,0:T(8,128)S(1)}, u32[]{:S(2)}, u32[]{:S(2)}) %collective-permute-start.3) | collective-permute-done | bytes 8224 | tf_op jit(solution)/shard_map/ppermute | solution.py:523
  40.0 12.0 %collective-permute-done.6.rest_3_ = bf16[48,8192]{1,0:T(8,128)(2,1)S(1)} collective-permute-done((bf16[48,8192]{1,0:T(8,128)(2,1)S(1)}, bf16[48,8192]{1,0:T(8,128)(2,1)S(1)}, u32[]{:S(2)}, u32[]{:S(2)}) %collective-permute-start.6) | collective-permute-done | bytes 786464 | tf_op jit(solution)/shard_map/ppermute | solution.py:552
  52.0 2.6 %collective-permute-start.16 = (bf16[128,3072]{1,0:T(8,128)(2,1)S(1)}, bf16[128,3072]{1,0:T(8,128)(2,1)S(1)}, u32[]{:S(2)}, u32[]{:S(2)}) collective-permute-start(bf16[128,3072]{1,0:T(8,128)(2,1)S(1)} %get-tuple-element.27), channel_id=1, source_target_pairs={{0,16},{8,24},{16,0},{24,8},{1,17},{9,25},{17,1},{25,9},{2,18},{10... | collective-permute-start | bytes 2359304 | tf_op jit(solution)/shard_map/ppermute | solution.py:562
  54.6 2.5 %collective-permute-start.17 = (bf16[128,3072]{1,0:T(8,128)(2,1)S(1)}, bf16[128,3072]{1,0:T(8,128)(2,1)S(1)}, u32[]{:S(2)}, u32[]{:S(2)}) collective-permute-start(bf16[128,3072]{1,0:T(8,128)(2,1)S(1)} %get-tuple-element.28), channel_id=1, source_target_pairs={{0,24},{8,16},{16,8},{24,0},{1,25},{9,17},{17,9},{25,1},{2,26},{10... | collective-permute-start | bytes 2359304 | tf_op jit(solution)/shard_map/ppermute | solution.py:562
  57.1 6.2 %select.3.scaled.rest_1_ = bf16[256,16384]{1,0:T(8,128)(2,1)S(1)} custom-call(s32[4]{0:T(128)S(1)} %pad_add_fusion.place, bf16[64,32768]{1,0:T(8,128)(2,1)S(1)} %copy-done, bf16[64,16384]{1,0:T(8,128)(2,1)S(1)} %collective-permute-done.rest_1_.mate, f32[2,8,128]{2,1,0:T(8,128)S(1)} %pad_maximum_fusion.rest_2_.pair.rest_6_, f32[8,32768]{1,0:T(8,128)S(1)} %copy-done.2), custom_call_target="tpu_custom_call" | custom-call | flops 4294967296 | bytes 12582912 | tf_op jit(solution)/shard_map/select/pallas_call | solution.py:276
  63.3 5.1 %collective-permute-done.10.rest_7_ = bf16[48,8192]{1,0:T(8,128)(2,1)S(1)} collective-permute-done((bf16[48,8192]{1,0:T(8,128)(2,1)S(1)}, bf16[48,8192]{1,0:T(8,128)(2,1)S(1)}, u32[]{:S(2)}, u32[]{:S(2)}) %collective-permute-start.10) | collective-permute-done | bytes 786464 | tf_op jit(solution)/shard_map/ppermute | solution.py:555
  69.6 3.7 %correl.1.own = f32[256,192]{1,0:T(8,128)S(1)} custom-call(bf16[256,16384]{1,0:T(8,128)(2,1)S(1)} %select.3.scaled.rest_1_, bf16[48,8192]{1,0:T(8,128)(2,1)S(1)} %get-tuple-element.24.rest_0_, bf16[48,8192]{1,0:T(8,128)(2,1)S(1)} %get-tuple-element.25.rest_1_, bf16[48,8192]{1,0:T(8,128)(2,1)S(1)} %collective-permute-done.5.rest_2_, ...), custom_call_target="tpu_custom_call" | custom-call | flops 1610612736 | bytes 14680064 | tf_op jit(solution)/shard_map/correl/pallas_call | solution.py:323
  75.0 2.6 %collective-permute-start.19 = (f32[2,8,128]{2,1,0:T(8,128)S(1)}, f32[2,8,128]{2,1,0:T(8,128)S(1)}, u32[]{:S(2)}, u32[]{:S(2)}) collective-permute-start(f32[2,8,128]{2,1,0:T(8,128)S(1)} %pad_maximum_fusion.rest_2_.pair.rest_6_), channel_id=1, source_target_pairs={{0,16},{8,24},{16,0},{24,8},{1,17},{9,25},{17,1},{25,9},{2,18},{10... | collective-permute-start | bytes 24584 | tf_op jit(solution)/shard_map/ppermute | solution.py:523
  78.7 11.6 %collective-permute-done.18.rest_3_.rest_7_ = f32[2,8,128]{2,1,0:T(8,128)S(1)} collective-permute-done((f32[2,8,128]{2,1,0:T(8,128)S(1)}, f32[2,8,128]{2,1,0:T(8,128)S(1)}, u32[]{:S(2)}, u32[]{:S(2)}) %collective-permute-start.18) | collective-permute-done | bytes 8224 | tf_op jit(solution)/shard_map/ppermute | solution.py:523
  90.3 4.3 %collective-permute-start.20 = (f32[2,8,128]{2,1,0:T(8,128)S(1)}, f32[2,8,128]{2,1,0:T(8,128)S(1)}, u32[]{:S(2)}, u32[]{:S(2)}) collective-permute-start(f32[2,8,128]{2,1,0:T(8,128)S(1)} %pad_maximum_fusion.rest_2_.pair.rest_6_), channel_id=1, source_target_pairs={{0,24},{8,16},{16,8},{24,0},{1,25},{9,17},{17,9},{25,1},{2,26},{10... | collective-permute-start | bytes 24584 | tf_op jit(solution)/shard_map/ppermute | solution.py:523
  94.7 28.0 %collective-permute-done.19.rest_4_.rest_8_ = f32[2,8,128]{2,1,0:T(8,128)S(1)} collective-permute-done((f32[2,8,128]{2,1,0:T(8,128)S(1)}, f32[2,8,128]{2,1,0:T(8,128)S(1)}, u32[]{:S(2)}, u32[]{:S(2)}) %collective-permute-start.19) | collective-permute-done | bytes 8224 | tf_op jit(solution)/shard_map/ppermute | solution.py:523
  126.7 2.1 %select.4.rest_4_ = bf16[256,3072]{1,0:T(8,128)(2,1)S(1)} custom-call(s32[4]{0:T(128)S(1)} %pad_add_fusion.place, bf16[64,32768]{1,0:T(8,128)(2,1)S(1)} %copy-done, bf16[64,16384]{1,0:T(8,128)(2,1)S(1)} %collective-permute-done.rest_1_.mate, f32[2,8,128]{2,1,0:T(8,128)S(1)} %pad_maximum_fusion.rest_2_.pair.rest_6_, f32[8,32768]{1,0:T(8,128)S(1)} %copy-done.2), custom_call_target="tpu_custom_call" | custom-call | flops 805306368 | bytes 2359296 | tf_op jit(solution)/shard_map/select/pallas_call | solution.py:276
  128.8 3.4 %collective-permute-start.13 = (bf16[2,192,128]{2,1,0:T(8,128)(2,1)S(1)}, bf16[2,192,128]{2,1,0:T(8,128)(2,1)S(1)}, u32[]{:S(2)}, u32[]{:S(2)}) collective-permute-start(bf16[2,192,128]{2,1,0:T(8,128)(2,1)S(1)} %weigh.1.rest_0_), channel_id=1, source_target_pairs={{0,16},{8,24},{16,0},{24,8},{1,17},{9,25},{17,1},{25,9},{2,18},{10... | collective-permute-start | bytes 294920 | tf_op jit(solution)/shard_map/ppermute | solution.py:523
  134.5 4.2 %select.5.rest_5_ = bf16[768,3072]{1,0:T(8,128)(2,1)S(1)} custom-call(s32[4]{0:T(128)S(1)} %pad_add_fusion.place, bf16[128,3072]{1,0:T(8,128)(2,1)S(1)} %collective-permute-done.15.rest_0_, bf16[128,3072]{1,0:T(8,128)(2,1)S(1)} %collective-permute-done.16.rest_1_, bf16[128,3072]{1,0:T(8,128)(2,1)S(1)} %collective-permute-done.17.rest_2_, ...), custom_call_target="tpu_custom_call" | custom-call | flops 2415919104 | bytes 7077888 | tf_op jit(solution)/shard_map/select/pallas_call | solution.py:276
  138.8 2.9 %blend.2 = (bf16[48,3200]{1,0:T(8,128)(2,1)S(1)}, bf16[48,3200]{1,0:T(8,128)(2,1)S(1)}, bf16[48,3200]{1,0:T(8,128)(2,1)S(1)}, bf16[48,3200]{1,0:T(8,128)(2,1)S(1)}) custom-call(s32[4]{0:T(128)S(1)} %pad_add_fusion.place, bf16[2,192,128]{2,1,0:T(8,128)(2,1)S(1)} %weigh.1.rest_0_, bf16[2,192,128]{2,1,0:T(8,128)(2,1)S(1)} %collective-permute-done.12.rest_1_, ...), custom_call_target="tpu_custom_call" | custom-call | flops 1207959552 | bytes 7471104 | tf_op jit(solution)/shard_map/blend/pallas_call | solution.py:429
  145.3 12.9 %collective-permute-done.25.refs_2_ = bf16[4,48,1024]{2,1,0:T(8,128)(2,1)S(1)} collective-permute-done((bf16[4,48,1024]{2,1,0:T(8,128)(2,1)S(1)}, bf16[4,48,1024]{2,1,0:T(8,128)(2,1)S(1)}, u32[]{:S(2)}, u32[]{:S(2)}) %collective-permute-start.25) | collective-permute-done | bytes 393248 | tf_op jit(solution)/shard_map/ppermute | solution.py:523
  159.0 2.8 %collective-permute-start.28 = (bf16[48,1024]{1,0:T(8,128)(2,1)S(1)}, bf16[48,1024]{1,0:T(8,128)(2,1)S(1)}, u32[]{:S(2)}, u32[]{:S(2)}) collective-permute-start(bf16[48,1024]{1,0:T(8,128)(2,1)S(1)} %get-tuple-element.39), channel_id=1, source_target_pairs={{0,16},{8,24},{16,0},{24,8},{1,17},{9,25},{17,1},{25,9},{2,18},{10... | collective-permute-start | bytes 294920 | tf_op jit(solution)/shard_map/ppermute | solution.py:523
  163.1 2.8 %collective-permute-start.29 = (bf16[48,1024]{1,0:T(8,128)(2,1)S(1)}, bf16[48,1024]{1,0:T(8,128)(2,1)S(1)}, u32[]{:S(2)}, u32[]{:S(2)}) collective-permute-start(bf16[48,1024]{1,0:T(8,128)(2,1)S(1)} %get-tuple-element.40), channel_id=1, source_target_pairs={{0,24},{8,16},{16,8},{24,0},{1,25},{9,17},{17,9},{25,1},{2,26},{10... | collective-permute-start | bytes 294920 | tf_op jit(solution)/shard_map/ppermute | solution.py:523
  165.9 3.6 %collective-permute-done.29.rest_7_ = bf16[48,1024]{1,0:T(8,128)(2,1)S(1)} collective-permute-done((bf16[48,1024]{1,0:T(8,128)(2,1)S(1)}, bf16[48,1024]{1,0:T(8,128)(2,1)S(1)}, u32[]{:S(2)}, u32[]{:S(2)}) %collective-permute-start.29) | collective-permute-done | bytes 98336 | tf_op jit(solution)/shard_map/ppermute | solution.py:523
  169.5 2.4 %finish.1 = f32[48,4096]{1,0:T(8,128)} custom-call(s32[4]{0:T(128)S(1)} %pad_add_fusion.place, bf16[48,3200]{1,0:T(8,128)(2,1)S(1)} %get-tuple-element.29.rest_0_, bf16[48,3200]{1,0:T(8,128)(2,1)S(1)} %collective-permute-done.21.rest_1_, bf16[48,3200]{1,0:T(8,128)(2,1)S(1)} %collective-permute-done.22.rest_2_, ...), custom_call_target="tpu_custom_call" | custom-call | bytes 1572864 | tf_op jit(solution)/shard_map/finish/pallas_call | solution.py:501
  (63 shorter events, 29.8 us)
Async XLA Ops:
  3.0 33.2 %collective-permute-start = (bf16[64,16384]{1,0:T(8,128)(2,1)S(1)}, bf16[64,16384]{1,0:T(8,128)(2,1)S(1)}, u32[]{:S(2)}, u32[]{:S(2)}) collective-permute-start(bf16[64,16384]{1,0:T(8,128)(2,1)S(1)} %get-tuple-element.23), channel_id=1, source_target_pairs={{0,4},{4,0},{1,5},{5,1},{2,6},{6,2},{3,7},{7,3},{8,12},{12,8},{9,1... | collective-permute-start | bytes 6291464 | tf_op jit(solution)/shard_map/ppermute | solution.py:547
  3.6 30.0 %collective-permute-start.8 = (bf16[48,8192]{1,0:T(8,128)(2,1)S(1)}, bf16[48,8192]{1,0:T(8,128)(2,1)S(1)}, u32[]{:S(2)}, u32[]{:S(2)}) collective-permute-start(bf16[48,8192]{1,0:T(8,128)(2,1)S(1)} %get-tuple-element.25.rest_1_), channel_id=1, source_target_pairs={{0,2},{1,3},{2,0},{3,1},{4,6},{5,7},{6,4},{7,5},{8,10},{9,11},{10,... | collective-permute-start | bytes 2359304 | tf_op jit(solution)/shard_map/ppermute | solution.py:551
  6.2 28.5 %collective-permute-start.5 = (bf16[48,8192]{1,0:T(8,128)(2,1)S(1)}, bf16[48,8192]{1,0:T(8,128)(2,1)S(1)}, u32[]{:S(2)}, u32[]{:S(2)}) collective-permute-start(bf16[48,8192]{1,0:T(8,128)(2,1)S(1)} %get-tuple-element.24.rest_0_), channel_id=1, source_target_pairs={{0,1},{1,0},{2,3},{3,2},{4,5},{5,4},{6,7},{7,6},{8,9},{9,8},{10,11... | collective-permute-start | bytes 2359304 | tf_op jit(solution)/shard_map/ppermute | solution.py:550
  11.3 14.6 %collective-permute-start.1 = (f32[16,128]{1,0:T(8,128)S(1)}, f32[16,128]{1,0:T(8,128)S(1)}, u32[]{:S(2)}, u32[]{:S(2)}) collective-permute-start(f32[16,128]{1,0:T(8,128)S(1)} %brief.1.rest_0_), channel_id=1, source_target_pairs={{0,1},{1,0},{2,3},{3,2},{4,5},{5,4},{6,7},{7,6},{8,9},{9,8},{10,11... | collective-permute-start | bytes 24584 | tf_op jit(solution)/shard_map/ppermute | solution.py:523
  11.9 15.5 %collective-permute-start.2 = (f32[16,128]{1,0:T(8,128)S(1)}, f32[16,128]{1,0:T(8,128)S(1)}, u32[]{:S(2)}, u32[]{:S(2)}) collective-permute-start(f32[16,128]{1,0:T(8,128)S(1)} %brief.1.rest_0_), channel_id=1, source_target_pairs={{0,2},{1,3},{2,0},{3,1},{4,6},{5,7},{6,4},{7,5},{8,10},{9,11},{10,... | collective-permute-start | bytes 24584 | tf_op jit(solution)/shard_map/ppermute | solution.py:523
  31.5 20.5 %collective-permute-start.6 = (bf16[48,8192]{1,0:T(8,128)(2,1)S(1)}, bf16[48,8192]{1,0:T(8,128)(2,1)S(1)}, u32[]{:S(2)}, u32[]{:S(2)}) collective-permute-start(bf16[48,8192]{1,0:T(8,128)(2,1)S(1)} %get-tuple-element.25.rest_1_), channel_id=1, source_target_pairs={{0,1},{1,0},{2,3},{3,2},{4,5},{5,4},{6,7},{7,6},{8,9},{9,8},{10,11... | collective-permute-start | bytes 2359304 | tf_op jit(solution)/shard_map/ppermute | solution.py:552
  33.0 21.5 %collective-permute-start.7 = (bf16[48,8192]{1,0:T(8,128)(2,1)S(1)}, bf16[48,8192]{1,0:T(8,128)(2,1)S(1)}, u32[]{:S(2)}, u32[]{:S(2)}) collective-permute-start(bf16[48,8192]{1,0:T(8,128)(2,1)S(1)} %get-tuple-element.24.rest_0_), channel_id=1, source_target_pairs={{0,2},{1,3},{2,0},{3,1},{4,6},{5,7},{6,4},{7,5},{8,10},{9,11},{10,... | collective-permute-start | bytes 2359304 | tf_op jit(solution)/shard_map/ppermute | solution.py:553
  33.6 34.8 %collective-permute-start.10 = (bf16[48,8192]{1,0:T(8,128)(2,1)S(1)}, bf16[48,8192]{1,0:T(8,128)(2,1)S(1)}, u32[]{:S(2)}, u32[]{:S(2)}) collective-permute-start(bf16[48,8192]{1,0:T(8,128)(2,1)S(1)} %collective-permute-done.8.rest_5_), channel_id=1, source_target_pairs={{0,1},{1,0},{2,3},{3,2},{4,5},{5,4},{6,7},{7,6},{8,9},{9,8},{10,11... | collective-permute-start | bytes 2359304 | tf_op jit(solution)/shard_map/ppermute | solution.py:555
  34.7 34.9 %collective-permute-start.9 = (bf16[48,8192]{1,0:T(8,128)(2,1)S(1)}, bf16[48,8192]{1,0:T(8,128)(2,1)S(1)}, u32[]{:S(2)}, u32[]{:S(2)}) collective-permute-start(bf16[48,8192]{1,0:T(8,128)(2,1)S(1)} %collective-permute-done.5.rest_2_), channel_id=1, source_target_pairs={{0,2},{1,3},{2,0},{3,1},{4,6},{5,7},{6,4},{7,5},{8,10},{9,11},{10,... | collective-permute-start | bytes 2359304 | tf_op jit(solution)/shard_map/ppermute | solution.py:554
  38.3 93.9 %collective-permute-start.15 = (bf16[128,3072]{1,0:T(8,128)(2,1)S(1)}, bf16[128,3072]{1,0:T(8,128)(2,1)S(1)}, u32[]{:S(2)}, u32[]{:S(2)}) collective-permute-start(bf16[128,3072]{1,0:T(8,128)(2,1)S(1)} %get-tuple-element.26), channel_id=1, source_target_pairs={{0,8},{8,0},{16,24},{24,16},{1,9},{9,1},{17,25},{25,17},{2,10},{10... | collective-permute-start | bytes 2359304 | tf_op jit(solution)/shard_map/ppermute | solution.py:562
  52.0 80.5 %collective-permute-start.16 = (bf16[128,3072]{1,0:T(8,128)(2,1)S(1)}, bf16[128,3072]{1,0:T(8,128)(2,1)S(1)}, u32[]{:S(2)}, u32[]{:S(2)}) collective-permute-start(bf16[128,3072]{1,0:T(8,128)(2,1)S(1)} %get-tuple-element.27), channel_id=1, source_target_pairs={{0,16},{8,24},{16,0},{24,8},{1,17},{9,25},{17,1},{25,9},{2,18},{10... | collective-permute-start | bytes 2359304 | tf_op jit(solution)/shard_map/ppermute | solution.py:562
  54.6 78.5 %collective-permute-start.17 = (bf16[128,3072]{1,0:T(8,128)(2,1)S(1)}, bf16[128,3072]{1,0:T(8,128)(2,1)S(1)}, u32[]{:S(2)}, u32[]{:S(2)}) collective-permute-start(bf16[128,3072]{1,0:T(8,128)(2,1)S(1)} %get-tuple-element.28), channel_id=1, source_target_pairs={{0,24},{8,16},{16,8},{24,0},{1,25},{9,17},{17,9},{25,1},{2,26},{10... | collective-permute-start | bytes 2359304 | tf_op jit(solution)/shard_map/ppermute | solution.py:562
  73.4 17.0 %collective-permute-start.18 = (f32[2,8,128]{2,1,0:T(8,128)S(1)}, f32[2,8,128]{2,1,0:T(8,128)S(1)}, u32[]{:S(2)}, u32[]{:S(2)}) collective-permute-start(f32[2,8,128]{2,1,0:T(8,128)S(1)} %pad_maximum_fusion.rest_2_.pair.rest_6_), channel_id=1, source_target_pairs={{0,8},{8,0},{16,24},{24,16},{1,9},{9,1},{17,25},{25,17},{2,10},{10... | collective-permute-start | bytes 24584 | tf_op jit(solution)/shard_map/ppermute | solution.py:523
  75.0 47.7 %collective-permute-start.19 = (f32[2,8,128]{2,1,0:T(8,128)S(1)}, f32[2,8,128]{2,1,0:T(8,128)S(1)}, u32[]{:S(2)}, u32[]{:S(2)}) collective-permute-start(f32[2,8,128]{2,1,0:T(8,128)S(1)} %pad_maximum_fusion.rest_2_.pair.rest_6_), channel_id=1, source_target_pairs={{0,16},{8,24},{16,0},{24,8},{1,17},{9,25},{17,1},{25,9},{2,18},{10... | collective-permute-start | bytes 24584 | tf_op jit(solution)/shard_map/ppermute | solution.py:523
  90.3 34.8 %collective-permute-start.20 = (f32[2,8,128]{2,1,0:T(8,128)S(1)}, f32[2,8,128]{2,1,0:T(8,128)S(1)}, u32[]{:S(2)}, u32[]{:S(2)}) collective-permute-start(f32[2,8,128]{2,1,0:T(8,128)S(1)} %pad_maximum_fusion.rest_2_.pair.rest_6_), channel_id=1, source_target_pairs={{0,24},{8,16},{16,8},{24,0},{1,25},{9,17},{17,9},{25,1},{2,26},{10... | collective-permute-start | bytes 24584 | tf_op jit(solution)/shard_map/ppermute | solution.py:523
  125.1 18.6 %collective-permute-start.24 = (bf16[4,48,1024]{2,1,0:T(8,128)(2,1)S(1)}, bf16[4,48,1024]{2,1,0:T(8,128)(2,1)S(1)}, u32[]{:S(2)}, u32[]{:S(2)}) collective-permute-start(bf16[4,48,1024]{2,1,0:T(8,128)(2,1)S(1)} %get-tuple-element.34), channel_id=1, source_target_pairs={{0,1},{1,0},{2,3},{3,2},{4,5},{5,4},{6,7},{7,6},{8,9},{9,8},{10,11... | collective-permute-start | bytes 1179656 | tf_op jit(solution)/shard_map/ppermute | solution.py:523
  128.8 9.8 %collective-permute-start.13 = (bf16[2,192,128]{2,1,0:T(8,128)(2,1)S(1)}, bf16[2,192,128]{2,1,0:T(8,128)(2,1)S(1)}, u32[]{:S(2)}, u32[]{:S(2)}) collective-permute-start(bf16[2,192,128]{2,1,0:T(8,128)(2,1)S(1)} %weigh.1.rest_0_), channel_id=1, source_target_pairs={{0,16},{8,24},{16,0},{24,8},{1,17},{9,25},{17,1},{25,9},{2,18},{10... | collective-permute-start | bytes 294920 | tf_op jit(solution)/shard_map/ppermute | solution.py:523
  132.3 6.5 %collective-permute-start.14 = (bf16[2,192,128]{2,1,0:T(8,128)(2,1)S(1)}, bf16[2,192,128]{2,1,0:T(8,128)(2,1)S(1)}, u32[]{:S(2)}, u32[]{:S(2)}) collective-permute-start(bf16[2,192,128]{2,1,0:T(8,128)(2,1)S(1)} %weigh.1.rest_0_), channel_id=1, source_target_pairs={{0,24},{8,16},{16,8},{24,0},{1,25},{9,17},{17,9},{25,1},{2,26},{10... | collective-permute-start | bytes 294920 | tf_op jit(solution)/shard_map/ppermute | solution.py:523
  132.5 25.7 %collective-permute-start.25 = (bf16[4,48,1024]{2,1,0:T(8,128)(2,1)S(1)}, bf16[4,48,1024]{2,1,0:T(8,128)(2,1)S(1)}, u32[]{:S(2)}, u32[]{:S(2)}) collective-permute-start(bf16[4,48,1024]{2,1,0:T(8,128)(2,1)S(1)} %get-tuple-element.35), channel_id=1, source_target_pairs={{0,2},{1,3},{2,0},{3,1},{4,6},{5,7},{6,4},{7,5},{8,10},{9,11},{10,... | collective-permute-start | bytes 1179656 | tf_op jit(solution)/shard_map/ppermute | solution.py:523
  133.0 25.2 %collective-permute-start.26 = (bf16[4,48,1024]{2,1,0:T(8,128)(2,1)S(1)}, bf16[4,48,1024]{2,1,0:T(8,128)(2,1)S(1)}, u32[]{:S(2)}, u32[]{:S(2)}) collective-permute-start(bf16[4,48,1024]{2,1,0:T(8,128)(2,1)S(1)} %get-tuple-element.36), channel_id=1, source_target_pairs={{0,3},{1,2},{2,1},{3,0},{4,7},{5,6},{6,5},{7,4},{8,11},{9,10},{10,... | collective-permute-start | bytes 1179656 | tf_op jit(solution)/shard_map/ppermute | solution.py:523
  141.7 27.8 %collective-permute-start.21 = (bf16[48,3200]{1,0:T(8,128)(2,1)S(1)}, bf16[48,3200]{1,0:T(8,128)(2,1)S(1)}, u32[]{:S(2)}, u32[]{:S(2)}) collective-permute-start(bf16[48,3200]{1,0:T(8,128)(2,1)S(1)} %get-tuple-element.30), channel_id=1, source_target_pairs={{0,1},{1,0},{2,3},{3,2},{4,5},{5,4},{6,7},{7,6},{8,9},{9,8},{10,11... | collective-permute-start | bytes 921608 | tf_op jit(solution)/shard_map/ppermute | solution.py:523
  143.2 26.3 %collective-permute-start.22 = (bf16[48,3200]{1,0:T(8,128)(2,1)S(1)}, bf16[48,3200]{1,0:T(8,128)(2,1)S(1)}, u32[]{:S(2)}, u32[]{:S(2)}) collective-permute-start(bf16[48,3200]{1,0:T(8,128)(2,1)S(1)} %get-tuple-element.31), channel_id=1, source_target_pairs={{0,2},{1,3},{2,0},{3,1},{4,6},{5,7},{6,4},{7,5},{8,10},{9,11},{10,... | collective-permute-start | bytes 921608 | tf_op jit(solution)/shard_map/ppermute | solution.py:523
  143.7 25.8 %collective-permute-start.23 = (bf16[48,3200]{1,0:T(8,128)(2,1)S(1)}, bf16[48,3200]{1,0:T(8,128)(2,1)S(1)}, u32[]{:S(2)}, u32[]{:S(2)}) collective-permute-start(bf16[48,3200]{1,0:T(8,128)(2,1)S(1)} %get-tuple-element.32), channel_id=1, source_target_pairs={{0,3},{1,2},{2,1},{3,0},{4,7},{5,6},{6,5},{7,4},{8,11},{9,10},{10,... | collective-permute-start | bytes 921608 | tf_op jit(solution)/shard_map/ppermute | solution.py:523
  159.0 6.9 %collective-permute-start.28 = (bf16[48,1024]{1,0:T(8,128)(2,1)S(1)}, bf16[48,1024]{1,0:T(8,128)(2,1)S(1)}, u32[]{:S(2)}, u32[]{:S(2)}) collective-permute-start(bf16[48,1024]{1,0:T(8,128)(2,1)S(1)} %get-tuple-element.39), channel_id=1, source_target_pairs={{0,16},{8,24},{16,0},{24,8},{1,17},{9,25},{17,1},{25,9},{2,18},{10... | collective-permute-start | bytes 294920 | tf_op jit(solution)/shard_map/ppermute | solution.py:523
  (12 other events, 87.1 us)

commit v8 on v7

--- a/solution.py
+++ b/solution.py
@@ -16,7 +16,7 @@
 VMEM = pl.BlockSpec(memory_space=pltpu.VMEM)
 SMEM = pl.BlockSpec(memory_space=pltpu.SMEM)
 HBM = pl.BlockSpec(memory_space=pltpu.HBM)
-SPLIT = 4
+APART = (5, 16)
 
 
 def dot(left, right, dims=ROWS):
@@ -467,34 +467,35 @@
     wedge, out, tables, held, came, went = rest[-6:]
     masks = wedge.shape[0]
     span = tables.shape[1]
-    tile = held.shape[2]
+    keep = span - apart[0].shape[1]
     at = pl.multiple_of(place[1] * span, span)
     fetch = pltpu.make_async_copy(wedge.at[:, pl.ds(at, span)], tables, came)
     fetch.start()
-    keep = span - tile
     mass = 0.0
     for part in shares:
         mass = mass + part[:, keep : keep + 3 * masks].astype(F32)
     mass = mass[:, :masks] + mass[:, masks : 2 * masks] + mass[:, 2 * masks : 3 * masks]
     fetch.wait()
     leaves = []
-    for t in range(SPLIT):
-        cols = slice(t * tile, (t + 1) * tile)
-        below = jnp.ones(held.shape[1:], F32)
+    half = keep // 256 * 128
+    for i, (first, end) in enumerate(((0, half), (half, keep), (keep, span))):
+        below = jnp.ones((held.shape[0], end - first), F32)
         for w in range(masks):
-            below = below + mass[:, w : w + 1] * tables[w : w + 1, cols]
+            below = below + mass[:, w : w + 1] * tables[w : w + 1, first:end]
         total = 0.0
-        for part in shares if t < SPLIT - 1 else apart:
-            total = total + (part[:, cols] if t < SPLIT - 1 else part[...]).astype(F32)
-        held[t] = total / below
-        leave = pltpu.make_async_copy(held.at[t], out.at[:, pl.ds(t * tile, tile)], went.at[t])
+        for part in apart if i == 2 else shares:
+            total = total + (part[...] if i == 2 else part[:, first:end]).astype(F32)
+        held[:, first:end] = total / below
+        leave = pltpu.make_async_copy(
+            held.at[:, pl.ds(first, end - first)], out.at[:, pl.ds(first, end - first)], went.at[i]
+        )
         leave.start()
         leaves.append(leave)
     for leave in leaves:
         leave.wait()
 
 
-def finish(place, shares, apart, wedge, tile):
+def finish(place, shares, apart, wedge, span):
     per_ref = shares[0].shape[0]
     masks = wedge.shape[0]
     blocks = len(shares)
@@ -502,15 +503,15 @@
         functools.partial(finish_kernel, blocks),
         in_specs=[SMEM] + [VMEM] * (blocks + len(apart)) + [HBM],
         out_specs=HBM,
-        out_shape=jax.ShapeDtypeStruct((per_ref, SPLIT * tile), F32),
+        out_shape=jax.ShapeDtypeStruct((per_ref, span), F32),
         scratch_shapes=[
-            pltpu.VMEM((masks, SPLIT * tile), F32),
-            pltpu.VMEM((SPLIT, per_ref, tile), F32),
+            pltpu.VMEM((masks, span), F32),
+            pltpu.VMEM((per_ref, span), F32),
             pltpu.SemaphoreType.DMA,
-            pltpu.SemaphoreType.DMA((SPLIT,)),
+            pltpu.SemaphoreType.DMA((3,)),
         ],
-        cost_estimate=cost(0, 8 * per_ref * SPLIT * tile),
         compiler_params=room(16),
+        cost_estimate=cost(0, 8 * per_ref * span),
         name="finish",
     )(place, *shares, *apart, wedge)
 
@@ -531,8 +532,9 @@
     groups = 2 * layers
     blocks = lax.axis_size("blk")
     per_vox = voxels // groups
-    tile = per_vox // SPLIT
+    tile = per_vox * APART[0] // APART[1]
     keep = per_vox - tile
+    steps = 2 if keep % 256 == 0 else 1
     half = voxels // 2
     cap = 2 * slot_count
     block = lax.axis_index("blk").astype(jnp.int32)
@@ -599,8 +601,8 @@
         wedge,
         here,
         slot_count,
-        keep // 2,
-        2,
+        keep // steps,
+        steps,
     )
     pairs = passed([pair] * layers, "lay", layers)
     sums = correl(scaled, tables, half // 8)
@@ -616,8 +618,8 @@
         wedge,
         here,
         slot_count,
-        keep // 2,
-        2,
+        keep // steps,
+        steps,
     )
 
     apart = blend(place, all_weights[:1], [], [scaled], masks, blocks, tile, layers)
@@ -626,10 +628,10 @@
     apart = passed(apart, "lay", layers)
 
     shares = blend(
-        place, all_weights, pairs, [near_rows, far_rows], masks, blocks, keep // 4, 4
+        place, all_weights, pairs, [near_rows, far_rows], masks, blocks, keep // steps, steps
     )
     shares = passed(shares, "blk", blocks)
-    return finish(place, shares, apart, wedge, tile)
+    return finish(place, shares, apart, wedge, per_vox)
 
 
 def solution(mesh):

time: 172 us -> 164 us (0.953)
  waiting for transfers between devices: 92.9 us -> 88.3 us
  starting transfers between devices: 44.6 us -> 42 us
    ppermute x19, waiting for transfers between devices: 74.6 us -> 70 us  [passed(): lax.ppermute(values[p], axis, [(d, d ^ p) for d in range(size)])]
    ppermute x19, starting transfers between devices: 28.5 us -> 25.9 us  [passed(): lax.ppermute(values[p], axis, [(d, d ^ p) for d in range(size)])]
  transfers between devices with their start and end apart: 30 -> 30, of which waited for: 11 -> 12; matrix products, arithmetic and copies ran while one was open for 0% -> 0% of each run, Pallas kernels for 16% -> 17%
where the time goes in v8:
time: 164 us
  waiting for transfers between devices  88.3 us (54%)
  starting transfers between devices  42 us (26%)
  Pallas kernels  33 us (20%)
    ppermute x19, waiting for transfers between devices, passed(): lax.ppermute(values[p], axis, [(d, d ^ p) for d in range(size)])  70 us
    ppermute x19, starting transfers between devices, passed(): lax.ppermute(values[p], axis, [(d, d ^ p) for d in range(size)])  25.9 us
    pallas_call x3, Pallas kernels, select(): pl.pallas_call(functools.partial(select_kernel, len(blocks)), grid_spec=p...  12.2 us
    ppermute x1, waiting for transfers between devices, per_device(): high_x = lax.ppermute(high, 'blk', over_x)  12 us
    ppermute x3, starting transfers between devices, per_device(): lax.ppermute(far[p - 1], 'lay', [(z, z ^ p) for z in range(layers)])  6.73 us
    ppermute x1, waiting for transfers between devices, per_device(): high_xy = lax.ppermute(high_y, 'blk', over_x)  5.07 us
    pallas_call x2, Pallas kernels, blend(): pl.pallas_call(functools.partial(blend_kernel, layers, len(scaled), block...  4.31 us
    pallas_call x1, Pallas kernels, correl(): pl.pallas_call(functools.partial(correl_kernel, blocks, tile), in_specs=[...  3.72 us
  transfers between devices with their start and end apart: 30, of which 12 were waited for; matrix products, arithmetic and copies ran while one was open for 0% of the time, Pallas kernels for 17%

profile of v8, /device:TPU:0, one launch (start us, length us, event | category | flops | bytes accessed | tf_op | source)
XLA Modules:
  0.0 164.3 jit_solution(9234393107309072001)
XLA Ops:
  0.1 2.9 %cut.1 = (bf16[48,8192]{1,0:T(8,128)(2,1)S(1)}, bf16[48,8192]{1,0:T(8,128)(2,1)S(1)}, bf16[64,16384]{1,0:T(8,128)(2,1)S(1)}) custom-call(s32[4]{0:T(128)S(1)} %pad_add_fusion.place, bf16[48,32768]{1,0:T(8,128)(2,1)} %refs.3, bf16[64,32768]{1,0:T(8,128)(2,1)} %slab.3), custom_call_target="tpu_custom_call" | custom-call | bytes 7340032 | tf_op jit(solution)/shard_map/cut/pallas_call | solution.py:79
  3.6 2.6 %collective-permute-start.8 = (bf16[48,8192]{1,0:T(8,128)(2,1)S(1)}, bf16[48,8192]{1,0:T(8,128)(2,1)S(1)}, u32[]{:S(2)}, u32[]{:S(2)}) collective-permute-start(bf16[48,8192]{1,0:T(8,128)(2,1)S(1)} %get-tuple-element.25.rest_1_), channel_id=1, source_target_pairs={{0,2},{1,3},{2,0},{3,1},{4,6},{5,7},{6,4},{7,5},{8,10},{9,11},{10,... | collective-permute-start | bytes 2359304 | tf_op jit(solution)/shard_map/ppermute | solution.py:553
  8.4 3.0 %brief.1.rest_0_ = f32[16,128]{1,0:T(8,128)S(1)} custom-call(s32[1]{0:T(128)S(6)} %copy.8.live, bf16[48,32768]{1,0:T(8,128)(2,1)S(1)} %copy-done.1, f32[8,32768]{1,0:T(8,128)S(1)} %copy-done.2, s32[1,64]{1,0:T(1,128)S(1)} %bitcast.10, s32[1,64]{1,0:T(1,128)S(1)} %bitcast.11, s32[1,64]{1,0:T(1,128)S(1)} %bitcast.12), custom_call_target="tpu_custom_call" | custom-call | flops 150994944 | bytes 4194304 | tf_op jit(solution)/shard_map/brief/pallas_call | solution.py:164
  12.0 13.9 %collective-permute-done.1.rest_1_ = f32[16,128]{1,0:T(8,128)S(1)} collective-permute-done((f32[16,128]{1,0:T(8,128)S(1)}, f32[16,128]{1,0:T(8,128)S(1)}, u32[]{:S(2)}, u32[]{:S(2)}) %collective-permute-start.1) | collective-permute-done | bytes 8224 | tf_op jit(solution)/shard_map/ppermute | solution.py:524
  27.4 3.1 %collective-permute-done.3.rest_3_ = f32[16,128]{1,0:T(8,128)S(1)} collective-permute-done((f32[16,128]{1,0:T(8,128)S(1)}, f32[16,128]{1,0:T(8,128)S(1)}, u32[]{:S(2)}, u32[]{:S(2)}) %collective-permute-start.3) | collective-permute-done | bytes 8224 | tf_op jit(solution)/shard_map/ppermute | solution.py:524
  36.2 2.1 %deal.1 = (bf16[128,2816]{1,0:T(8,128)(2,1)S(1)}, bf16[128,2816]{1,0:T(8,128)(2,1)S(1)}, bf16[128,2816]{1,0:T(8,128)(2,1)S(1)}) custom-call(s32[4]{0:T(128)S(1)} %pad_add_fusion.place, bf16[64,32768]{1,0:T(8,128)(2,1)} %slab.3, bf16[64,16384]{1,0:T(8,128)(2,1)S(1)} %collective-permute-done.rest_1_.mate), custom_call_target="tpu_custom_call" | custom-call | bytes 4325376 | tf_op jit(solution)/shard_map/deal/pallas_call | solution.py:119
  40.0 12.0 %collective-permute-done.6.rest_3_ = bf16[48,8192]{1,0:T(8,128)(2,1)S(1)} collective-permute-done((bf16[48,8192]{1,0:T(8,128)(2,1)S(1)}, bf16[48,8192]{1,0:T(8,128)(2,1)S(1)}, u32[]{:S(2)}, u32[]{:S(2)}) %collective-permute-start.6) | collective-permute-done | bytes 786464 | tf_op jit(solution)/shard_map/ppermute | solution.py:554
  52.0 2.6 %collective-permute-start.16 = (bf16[128,2816]{1,0:T(8,128)(2,1)S(1)}, bf16[128,2816]{1,0:T(8,128)(2,1)S(1)}, u32[]{:S(2)}, u32[]{:S(2)}) collective-permute-start(bf16[128,2816]{1,0:T(8,128)(2,1)S(1)} %get-tuple-element.27), channel_id=1, source_target_pairs={{0,16},{8,24},{16,0},{24,8},{1,17},{9,25},{17,1},{25,9},{2,18},{10... | collective-permute-start | bytes 2162696 | tf_op jit(solution)/shard_map/ppermute | solution.py:564
  54.6 2.5 %collective-permute-start.17 = (bf16[128,2816]{1,0:T(8,128)(2,1)S(1)}, bf16[128,2816]{1,0:T(8,128)(2,1)S(1)}, u32[]{:S(2)}, u32[]{:S(2)}) collective-permute-start(bf16[128,2816]{1,0:T(8,128)(2,1)S(1)} %get-tuple-element.28), channel_id=1, source_target_pairs={{0,24},{8,16},{16,8},{24,0},{1,25},{9,17},{17,9},{25,1},{2,26},{10... | collective-permute-start | bytes 2162696 | tf_op jit(solution)/shard_map/ppermute | solution.py:564
  57.1 6.2 %select.3.scaled.rest_1_ = bf16[256,16384]{1,0:T(8,128)(2,1)S(1)} custom-call(s32[4]{0:T(128)S(1)} %pad_add_fusion.place, bf16[64,32768]{1,0:T(8,128)(2,1)S(1)} %copy-done, bf16[64,16384]{1,0:T(8,128)(2,1)S(1)} %collective-permute-done.rest_1_.mate, f32[2,8,128]{2,1,0:T(8,128)S(1)} %pad_maximum_fusion.rest_2_.pair.rest_6_, f32[8,32768]{1,0:T(8,128)S(1)} %copy-done.2), custom_call_target="tpu_custom_call" | custom-call | flops 4294967296 | bytes 12582912 | tf_op jit(solution)/shard_map/select/pallas_call | solution.py:276
  63.3 5.1 %collective-permute-done.10.rest_7_ = bf16[48,8192]{1,0:T(8,128)(2,1)S(1)} collective-permute-done((bf16[48,8192]{1,0:T(8,128)(2,1)S(1)}, bf16[48,8192]{1,0:T(8,128)(2,1)S(1)}, u32[]{:S(2)}, u32[]{:S(2)}) %collective-permute-start.10) | collective-permute-done | bytes 786464 | tf_op jit(solution)/shard_map/ppermute | solution.py:557
  69.6 3.7 %correl.1.own = f32[256,192]{1,0:T(8,128)S(1)} custom-call(bf16[256,16384]{1,0:T(8,128)(2,1)S(1)} %select.3.scaled.rest_1_, bf16[48,8192]{1,0:T(8,128)(2,1)S(1)} %get-tuple-element.24.rest_0_, bf16[48,8192]{1,0:T(8,128)(2,1)S(1)} %get-tuple-element.25.rest_1_, bf16[48,8192]{1,0:T(8,128)(2,1)S(1)} %collective-permute-done.5.rest_2_, ...), custom_call_target="tpu_custom_call" | custom-call | flops 1610612736 | bytes 14680064 | tf_op jit(solution)/shard_map/correl/pallas_call | solution.py:323
  77.7 22.1 %collective-permute-done.18.rest_3_.rest_7_ = f32[2,8,128]{2,1,0:T(8,128)S(1)} collective-permute-done((f32[2,8,128]{2,1,0:T(8,128)S(1)}, f32[2,8,128]{2,1,0:T(8,128)S(1)}, u32[]{:S(2)}, u32[]{:S(2)}) %collective-permute-start.18) | collective-permute-done | bytes 8224 | tf_op jit(solution)/shard_map/ppermute | solution.py:524
  99.8 17.1 %collective-permute-done.19.rest_4_.rest_8_ = f32[2,8,128]{2,1,0:T(8,128)S(1)} collective-permute-done((f32[2,8,128]{2,1,0:T(8,128)S(1)}, f32[2,8,128]{2,1,0:T(8,128)S(1)}, u32[]{:S(2)}, u32[]{:S(2)}) %collective-permute-start.19) | collective-permute-done | bytes 8224 | tf_op jit(solution)/shard_map/ppermute | solution.py:524
  116.9 3.6 %collective-permute-start.20 = (f32[2,8,128]{2,1,0:T(8,128)S(1)}, f32[2,8,128]{2,1,0:T(8,128)S(1)}, u32[]{:S(2)}, u32[]{:S(2)}) collective-permute-start(f32[2,8,128]{2,1,0:T(8,128)S(1)} %pad_maximum_fusion.rest_2_.pair.rest_6_), channel_id=1, source_target_pairs={{0,24},{8,16},{16,8},{24,0},{1,25},{9,17},{17,9},{25,1},{2,26},{10... | collective-permute-start | bytes 24584 | tf_op jit(solution)/shard_map/ppermute | solution.py:524
  128.0 3.6 %collective-permute-start.14 = (bf16[2,192,128]{2,1,0:T(8,128)(2,1)S(1)}, bf16[2,192,128]{2,1,0:T(8,128)(2,1)S(1)}, u32[]{:S(2)}, u32[]{:S(2)}) collective-permute-start(bf16[2,192,128]{2,1,0:T(8,128)(2,1)S(1)} %weigh.1.rest_0_), channel_id=1, source_target_pairs={{0,24},{8,16},{16,8},{24,0},{1,25},{9,17},{17,9},{25,1},{2,26},{10... | collective-permute-start | bytes 294920 | tf_op jit(solution)/shard_map/ppermute | solution.py:524
  131.6 4.0 %select.5.rest_5_ = bf16[768,2816]{1,0:T(8,128)(2,1)S(1)} custom-call(s32[4]{0:T(128)S(1)} %pad_add_fusion.place, bf16[128,2816]{1,0:T(8,128)(2,1)S(1)} %collective-permute-done.15.rest_0_, bf16[128,2816]{1,0:T(8,128)(2,1)S(1)} %collective-permute-done.16.rest_1_, bf16[128,2816]{1,0:T(8,128)(2,1)S(1)} %collective-permute-done.17.rest_2_, ...), custom_call_target="tpu_custom_call" | custom-call | flops 2214592512 | bytes 6488064 | tf_op jit(solution)/shard_map/select/pallas_call | solution.py:276
  136.6 2.5 %blend.2 = (bf16[48,2944]{1,0:T(8,128)(2,1)S(1)}, bf16[48,2944]{1,0:T(8,128)(2,1)S(1)}, bf16[48,2944]{1,0:T(8,128)(2,1)S(1)}, bf16[48,2944]{1,0:T(8,128)(2,1)S(1)}) custom-call(s32[4]{0:T(128)S(1)} %pad_add_fusion.place, bf16[2,192,128]{2,1,0:T(8,128)(2,1)S(1)} %weigh.1.rest_0_, bf16[2,192,128]{2,1,0:T(8,128)(2,1)S(1)} %collective-permute-done.12.rest_1_, ...), custom_call_target="tpu_custom_call" | custom-call | flops 1107296256 | bytes 6848512 | tf_op jit(solution)/shard_map/blend/pallas_call | solution.py:429
  142.7 4.8 %collective-permute-done.25.refs_2_ = bf16[4,48,1280]{2,1,0:T(8,128)(2,1)S(1)} collective-permute-done((bf16[4,48,1280]{2,1,0:T(8,128)(2,1)S(1)}, bf16[4,48,1280]{2,1,0:T(8,128)(2,1)S(1)}, u32[]{:S(2)}, u32[]{:S(2)}) %collective-permute-start.25) | collective-permute-done | bytes 491552 | tf_op jit(solution)/shard_map/ppermute | solution.py:524
  147.9 3.5 %collective-permute-start.28 = (bf16[48,1280]{1,0:T(8,128)(2,1)S(1)}, bf16[48,1280]{1,0:T(8,128)(2,1)S(1)}, u32[]{:S(2)}, u32[]{:S(2)}) collective-permute-start(bf16[48,1280]{1,0:T(8,128)(2,1)S(1)} %get-tuple-element.39), channel_id=1, source_target_pairs={{0,16},{8,24},{16,0},{24,8},{1,17},{9,25},{17,1},{25,9},{2,18},{10... | collective-permute-start | bytes 368648 | tf_op jit(solution)/shard_map/ppermute | solution.py:524
  151.4 3.8 %collective-permute-done.27.rest_5_ = bf16[48,1280]{1,0:T(8,128)(2,1)S(1)} collective-permute-done((bf16[48,1280]{1,0:T(8,128)(2,1)S(1)}, bf16[48,1280]{1,0:T(8,128)(2,1)S(1)}, u32[]{:S(2)}, u32[]{:S(2)}) %collective-permute-start.27) | collective-permute-done | bytes 122912 | tf_op jit(solution)/shard_map/ppermute | solution.py:524
  155.2 2.7 %collective-permute-start.29 = (bf16[48,1280]{1,0:T(8,128)(2,1)S(1)}, bf16[48,1280]{1,0:T(8,128)(2,1)S(1)}, u32[]{:S(2)}, u32[]{:S(2)}) collective-permute-start(bf16[48,1280]{1,0:T(8,128)(2,1)S(1)} %get-tuple-element.40), channel_id=1, source_target_pairs={{0,24},{8,16},{16,8},{24,0},{1,25},{9,17},{17,9},{25,1},{2,26},{10... | collective-permute-start | bytes 368648 | tf_op jit(solution)/shard_map/ppermute | solution.py:524
  157.9 4.0 %collective-permute-done.29.rest_7_ = bf16[48,1280]{1,0:T(8,128)(2,1)S(1)} collective-permute-done((bf16[48,1280]{1,0:T(8,128)(2,1)S(1)}, bf16[48,1280]{1,0:T(8,128)(2,1)S(1)}, u32[]{:S(2)}, u32[]{:S(2)}) %collective-permute-start.29) | collective-permute-done | bytes 122912 | tf_op jit(solution)/shard_map/ppermute | solution.py:524
  161.9 2.4 %finish.1 = f32[48,4096]{1,0:T(8,128)} custom-call(s32[4]{0:T(128)S(1)} %pad_add_fusion.place, bf16[48,2944]{1,0:T(8,128)(2,1)S(1)} %get-tuple-element.29.rest_0_, bf16[48,2944]{1,0:T(8,128)(2,1)S(1)} %collective-permute-done.21.rest_1_, bf16[48,2944]{1,0:T(8,128)(2,1)S(1)} %collective-permute-done.22.rest_2_, ...), custom_call_target="tpu_custom_call" | custom-call | bytes 1572864 | tf_op jit(solution)/shard_map/finish/pallas_call | solution.py:502
  (63 shorter events, 29.6 us)
Async XLA Ops:
  3.0 33.2 %collective-permute-start = (bf16[64,16384]{1,0:T(8,128)(2,1)S(1)}, bf16[64,16384]{1,0:T(8,128)(2,1)S(1)}, u32[]{:S(2)}, u32[]{:S(2)}) collective-permute-start(bf16[64,16384]{1,0:T(8,128)(2,1)S(1)} %get-tuple-element.23), channel_id=1, source_target_pairs={{0,4},{4,0},{1,5},{5,1},{2,6},{6,2},{3,7},{7,3},{8,12},{12,8},{9,1... | collective-permute-start | bytes 6291464 | tf_op jit(solution)/shard_map/ppermute | solution.py:549
  3.6 30.0 %collective-permute-start.8 = (bf16[48,8192]{1,0:T(8,128)(2,1)S(1)}, bf16[48,8192]{1,0:T(8,128)(2,1)S(1)}, u32[]{:S(2)}, u32[]{:S(2)}) collective-permute-start(bf16[48,8192]{1,0:T(8,128)(2,1)S(1)} %get-tuple-element.25.rest_1_), channel_id=1, source_target_pairs={{0,2},{1,3},{2,0},{3,1},{4,6},{5,7},{6,4},{7,5},{8,10},{9,11},{10,... | collective-permute-start | bytes 2359304 | tf_op jit(solution)/shard_map/ppermute | solution.py:553
  6.2 28.5 %collective-permute-start.5 = (bf16[48,8192]{1,0:T(8,128)(2,1)S(1)}, bf16[48,8192]{1,0:T(8,128)(2,1)S(1)}, u32[]{:S(2)}, u32[]{:S(2)}) collective-permute-start(bf16[48,8192]{1,0:T(8,128)(2,1)S(1)} %get-tuple-element.24.rest_0_), channel_id=1, source_target_pairs={{0,1},{1,0},{2,3},{3,2},{4,5},{5,4},{6,7},{7,6},{8,9},{9,8},{10,11... | collective-permute-start | bytes 2359304 | tf_op jit(solution)/shard_map/ppermute | solution.py:552
  11.3 14.6 %collective-permute-start.1 = (f32[16,128]{1,0:T(8,128)S(1)}, f32[16,128]{1,0:T(8,128)S(1)}, u32[]{:S(2)}, u32[]{:S(2)}) collective-permute-start(f32[16,128]{1,0:T(8,128)S(1)} %brief.1.rest_0_), channel_id=1, source_target_pairs={{0,1},{1,0},{2,3},{3,2},{4,5},{5,4},{6,7},{7,6},{8,9},{9,8},{10,11... | collective-permute-start | bytes 24584 | tf_op jit(solution)/shard_map/ppermute | solution.py:524
  11.9 15.5 %collective-permute-start.2 = (f32[16,128]{1,0:T(8,128)S(1)}, f32[16,128]{1,0:T(8,128)S(1)}, u32[]{:S(2)}, u32[]{:S(2)}) collective-permute-start(f32[16,128]{1,0:T(8,128)S(1)} %brief.1.rest_0_), channel_id=1, source_target_pairs={{0,2},{1,3},{2,0},{3,1},{4,6},{5,7},{6,4},{7,5},{8,10},{9,11},{10,... | collective-permute-start | bytes 24584 | tf_op jit(solution)/shard_map/ppermute | solution.py:524
  31.5 20.5 %collective-permute-start.6 = (bf16[48,8192]{1,0:T(8,128)(2,1)S(1)}, bf16[48,8192]{1,0:T(8,128)(2,1)S(1)}, u32[]{:S(2)}, u32[]{:S(2)}) collective-permute-start(bf16[48,8192]{1,0:T(8,128)(2,1)S(1)} %get-tuple-element.25.rest_1_), channel_id=1, source_target_pairs={{0,1},{1,0},{2,3},{3,2},{4,5},{5,4},{6,7},{7,6},{8,9},{9,8},{10,11... | collective-permute-start | bytes 2359304 | tf_op jit(solution)/shard_map/ppermute | solution.py:554
  33.0 21.5 %collective-permute-start.7 = (bf16[48,8192]{1,0:T(8,128)(2,1)S(1)}, bf16[48,8192]{1,0:T(8,128)(2,1)S(1)}, u32[]{:S(2)}, u32[]{:S(2)}) collective-permute-start(bf16[48,8192]{1,0:T(8,128)(2,1)S(1)} %get-tuple-element.24.rest_0_), channel_id=1, source_target_pairs={{0,2},{1,3},{2,0},{3,1},{4,6},{5,7},{6,4},{7,5},{8,10},{9,11},{10,... | collective-permute-start | bytes 2359304 | tf_op jit(solution)/shard_map/ppermute | solution.py:555
  33.6 34.8 %collective-permute-start.10 = (bf16[48,8192]{1,0:T(8,128)(2,1)S(1)}, bf16[48,8192]{1,0:T(8,128)(2,1)S(1)}, u32[]{:S(2)}, u32[]{:S(2)}) collective-permute-start(bf16[48,8192]{1,0:T(8,128)(2,1)S(1)} %collective-permute-done.8.rest_5_), channel_id=1, source_target_pairs={{0,1},{1,0},{2,3},{3,2},{4,5},{5,4},{6,7},{7,6},{8,9},{9,8},{10,11... | collective-permute-start | bytes 2359304 | tf_op jit(solution)/shard_map/ppermute | solution.py:557
  34.7 34.9 %collective-permute-start.9 = (bf16[48,8192]{1,0:T(8,128)(2,1)S(1)}, bf16[48,8192]{1,0:T(8,128)(2,1)S(1)}, u32[]{:S(2)}, u32[]{:S(2)}) collective-permute-start(bf16[48,8192]{1,0:T(8,128)(2,1)S(1)} %collective-permute-done.5.rest_2_), channel_id=1, source_target_pairs={{0,2},{1,3},{2,0},{3,1},{4,6},{5,7},{6,4},{7,5},{8,10},{9,11},{10,... | collective-permute-start | bytes 2359304 | tf_op jit(solution)/shard_map/ppermute | solution.py:556
  38.3 86.0 %collective-permute-start.15 = (bf16[128,2816]{1,0:T(8,128)(2,1)S(1)}, bf16[128,2816]{1,0:T(8,128)(2,1)S(1)}, u32[]{:S(2)}, u32[]{:S(2)}) collective-permute-start(bf16[128,2816]{1,0:T(8,128)(2,1)S(1)} %get-tuple-element.26), channel_id=1, source_target_pairs={{0,8},{8,0},{16,24},{24,16},{1,9},{9,1},{17,25},{25,17},{2,10},{10... | collective-permute-start | bytes 2162696 | tf_op jit(solution)/shard_map/ppermute | solution.py:564
  52.0 75.9 %collective-permute-start.16 = (bf16[128,2816]{1,0:T(8,128)(2,1)S(1)}, bf16[128,2816]{1,0:T(8,128)(2,1)S(1)}, u32[]{:S(2)}, u32[]{:S(2)}) collective-permute-start(bf16[128,2816]{1,0:T(8,128)(2,1)S(1)} %get-tuple-element.27), channel_id=1, source_target_pairs={{0,16},{8,24},{16,0},{24,8},{1,17},{9,25},{17,1},{25,9},{2,18},{10... | collective-permute-start | bytes 2162696 | tf_op jit(solution)/shard_map/ppermute | solution.py:564
  54.6 73.4 %collective-permute-start.17 = (bf16[128,2816]{1,0:T(8,128)(2,1)S(1)}, bf16[128,2816]{1,0:T(8,128)(2,1)S(1)}, u32[]{:S(2)}, u32[]{:S(2)}) collective-permute-start(bf16[128,2816]{1,0:T(8,128)(2,1)S(1)} %get-tuple-element.28), channel_id=1, source_target_pairs={{0,24},{8,16},{16,8},{24,0},{1,25},{9,17},{17,9},{25,1},{2,26},{10... | collective-permute-start | bytes 2162696 | tf_op jit(solution)/shard_map/ppermute | solution.py:564
  73.4 26.4 %collective-permute-start.18 = (f32[2,8,128]{2,1,0:T(8,128)S(1)}, f32[2,8,128]{2,1,0:T(8,128)S(1)}, u32[]{:S(2)}, u32[]{:S(2)}) collective-permute-start(f32[2,8,128]{2,1,0:T(8,128)S(1)} %pad_maximum_fusion.rest_2_.pair.rest_6_), channel_id=1, source_target_pairs={{0,8},{8,0},{16,24},{24,16},{1,9},{9,1},{17,25},{25,17},{2,10},{10... | collective-permute-start | bytes 24584 | tf_op jit(solution)/shard_map/ppermute | solution.py:524
  76.2 47.6 %collective-permute-start.12 = (bf16[2,192,128]{2,1,0:T(8,128)(2,1)S(1)}, bf16[2,192,128]{2,1,0:T(8,128)(2,1)S(1)}, u32[]{:S(2)}, u32[]{:S(2)}) collective-permute-start(bf16[2,192,128]{2,1,0:T(8,128)(2,1)S(1)} %weigh.1.rest_0_), channel_id=1, source_target_pairs={{0,8},{8,0},{16,24},{24,16},{1,9},{9,1},{17,25},{25,17},{2,10},{10... | collective-permute-start | bytes 294920 | tf_op jit(solution)/shard_map/ppermute | solution.py:524
  99.8 17.1 %collective-permute-start.19 = (f32[2,8,128]{2,1,0:T(8,128)S(1)}, f32[2,8,128]{2,1,0:T(8,128)S(1)}, u32[]{:S(2)}, u32[]{:S(2)}) collective-permute-start(f32[2,8,128]{2,1,0:T(8,128)S(1)} %pad_maximum_fusion.rest_2_.pair.rest_6_), channel_id=1, source_target_pairs={{0,16},{8,24},{16,0},{24,8},{1,17},{9,25},{17,1},{25,9},{2,18},{10... | collective-permute-start | bytes 24584 | tf_op jit(solution)/shard_map/ppermute | solution.py:524
  122.3 18.9 %collective-permute-start.24 = (bf16[4,48,1280]{2,1,0:T(8,128)(2,1)S(1)}, bf16[4,48,1280]{2,1,0:T(8,128)(2,1)S(1)}, u32[]{:S(2)}, u32[]{:S(2)}) collective-permute-start(bf16[4,48,1280]{2,1,0:T(8,128)(2,1)S(1)} %get-tuple-element.34), channel_id=1, source_target_pairs={{0,1},{1,0},{2,3},{3,2},{4,5},{5,4},{6,7},{7,6},{8,9},{9,8},{10,11... | collective-permute-start | bytes 1474568 | tf_op jit(solution)/shard_map/ppermute | solution.py:524
  123.8 23.7 %collective-permute-start.25 = (bf16[4,48,1280]{2,1,0:T(8,128)(2,1)S(1)}, bf16[4,48,1280]{2,1,0:T(8,128)(2,1)S(1)}, u32[]{:S(2)}, u32[]{:S(2)}) collective-permute-start(bf16[4,48,1280]{2,1,0:T(8,128)(2,1)S(1)} %get-tuple-element.35), channel_id=1, source_target_pairs={{0,2},{1,3},{2,0},{3,1},{4,6},{5,7},{6,4},{7,5},{8,10},{9,11},{10,... | collective-permute-start | bytes 1474568 | tf_op jit(solution)/shard_map/ppermute | solution.py:524
  124.3 23.2 %collective-permute-start.26 = (bf16[4,48,1280]{2,1,0:T(8,128)(2,1)S(1)}, bf16[4,48,1280]{2,1,0:T(8,128)(2,1)S(1)}, u32[]{:S(2)}, u32[]{:S(2)}) collective-permute-start(bf16[4,48,1280]{2,1,0:T(8,128)(2,1)S(1)} %get-tuple-element.36), channel_id=1, source_target_pairs={{0,3},{1,2},{2,1},{3,0},{4,7},{5,6},{6,5},{7,4},{8,11},{9,10},{10,... | collective-permute-start | bytes 1474568 | tf_op jit(solution)/shard_map/ppermute | solution.py:524
  127.9 8.7 %collective-permute-start.13 = (bf16[2,192,128]{2,1,0:T(8,128)(2,1)S(1)}, bf16[2,192,128]{2,1,0:T(8,128)(2,1)S(1)}, u32[]{:S(2)}, u32[]{:S(2)}) collective-permute-start(bf16[2,192,128]{2,1,0:T(8,128)(2,1)S(1)} %weigh.1.rest_0_), channel_id=1, source_target_pairs={{0,16},{8,24},{16,0},{24,8},{1,17},{9,25},{17,1},{25,9},{2,18},{10... | collective-permute-start | bytes 294920 | tf_op jit(solution)/shard_map/ppermute | solution.py:524
  128.0 8.7 %collective-permute-start.14 = (bf16[2,192,128]{2,1,0:T(8,128)(2,1)S(1)}, bf16[2,192,128]{2,1,0:T(8,128)(2,1)S(1)}, u32[]{:S(2)}, u32[]{:S(2)}) collective-permute-start(bf16[2,192,128]{2,1,0:T(8,128)(2,1)S(1)} %weigh.1.rest_0_), channel_id=1, source_target_pairs={{0,24},{8,16},{16,8},{24,0},{1,25},{9,17},{17,9},{25,1},{2,26},{10... | collective-permute-start | bytes 294920 | tf_op jit(solution)/shard_map/ppermute | solution.py:524
  139.2 22.7 %collective-permute-start.21 = (bf16[48,2944]{1,0:T(8,128)(2,1)S(1)}, bf16[48,2944]{1,0:T(8,128)(2,1)S(1)}, u32[]{:S(2)}, u32[]{:S(2)}) collective-permute-start(bf16[48,2944]{1,0:T(8,128)(2,1)S(1)} %get-tuple-element.30), channel_id=1, source_target_pairs={{0,1},{1,0},{2,3},{3,2},{4,5},{5,4},{6,7},{7,6},{8,9},{9,8},{10,11... | collective-permute-start | bytes 847880 | tf_op jit(solution)/shard_map/ppermute | solution.py:524
  140.7 21.1 %collective-permute-start.22 = (bf16[48,2944]{1,0:T(8,128)(2,1)S(1)}, bf16[48,2944]{1,0:T(8,128)(2,1)S(1)}, u32[]{:S(2)}, u32[]{:S(2)}) collective-permute-start(bf16[48,2944]{1,0:T(8,128)(2,1)S(1)} %get-tuple-element.31), channel_id=1, source_target_pairs={{0,2},{1,3},{2,0},{3,1},{4,6},{5,7},{6,4},{7,5},{8,10},{9,11},{10,... | collective-permute-start | bytes 847880 | tf_op jit(solution)/shard_map/ppermute | solution.py:524
  141.2 20.6 %collective-permute-start.23 = (bf16[48,2944]{1,0:T(8,128)(2,1)S(1)}, bf16[48,2944]{1,0:T(8,128)(2,1)S(1)}, u32[]{:S(2)}, u32[]{:S(2)}) collective-permute-start(bf16[48,2944]{1,0:T(8,128)(2,1)S(1)} %get-tuple-element.32), channel_id=1, source_target_pairs={{0,3},{1,2},{2,1},{3,0},{4,7},{5,6},{6,5},{7,4},{8,11},{9,10},{10,... | collective-permute-start | bytes 847880 | tf_op jit(solution)/shard_map/ppermute | solution.py:524
  147.9 10.0 %collective-permute-start.28 = (bf16[48,1280]{1,0:T(8,128)(2,1)S(1)}, bf16[48,1280]{1,0:T(8,128)(2,1)S(1)}, u32[]{:S(2)}, u32[]{:S(2)}) collective-permute-start(bf16[48,1280]{1,0:T(8,128)(2,1)S(1)} %get-tuple-element.39), channel_id=1, source_target_pairs={{0,16},{8,24},{16,0},{24,8},{1,17},{9,25},{17,1},{25,9},{2,18},{10... | collective-permute-start | bytes 368648 | tf_op jit(solution)/shard_map/ppermute | solution.py:524
  (12 other events, 89.4 us)

commit v9 on v8

--- a/solution.py
+++ b/solution.py
@@ -298,38 +298,39 @@
     )(place, *blocks, *pairs, wedge)
 
 
-def correl_kernel(blocks, tile, scaled, *rest):
-    refs, out, table = rest[:-2], rest[-2], rest[-1]
+def correl_kernel(blocks, tile, first, steps, shifts, scaled, *rest):
+    refs, seeds, out, table = rest[: 2 * blocks], rest[2 * blocks : -2], rest[-2], rest[-1]
     per_ref, span = refs[0].shape
-    out[...] = jnp.zeros_like(out)
+    out[...] = seeds[0][...] if seeds else jnp.zeros_like(out)
     for side in range(2):
 
         def step(t, carry, side=side):
-            at = pl.multiple_of(t * tile, tile)
+            at = first + t * tile
             for p in range(blocks):
-                table[p * per_ref : (p + 1) * per_ref, :] = refs[2 * p + side][:, pl.ds(at, tile)]
-            rows = scaled[:, pl.ds(pl.multiple_of(side * span + t * tile, tile), tile)]
+                cols = pl.ds(pl.multiple_of(at - shifts[p], tile), tile)
+                table[p * per_ref : (p + 1) * per_ref, :] = refs[2 * p + side][:, cols]
+            rows = scaled[:, pl.ds(pl.multiple_of(side * span + at, tile), tile)]
             out[...] += dot(rows, table[...], LANES)
             return carry
 
-        lax.fori_loop(0, span // tile, step, 0)
-
-
-def correl(scaled, tables, tile):
-    height, span = scaled.shape
+        lax.fori_loop(0, steps, step, 0)
+
+
+def correl(scaled, tables, shifts, tile, first, steps, seeds):
+    height = scaled.shape[0]
     blocks = len(tables[0])
     count = blocks * tables[0][0].shape[0]
     refs = [tables[i][p] for p in range(blocks) for i in range(2)]
     return pl.pallas_call(
-        functools.partial(correl_kernel, blocks, tile),
-        in_specs=[VMEM] * (1 + len(refs)),
+        functools.partial(correl_kernel, blocks, tile, first, steps, shifts),
+        in_specs=[VMEM] * (1 + len(refs) + len(seeds)),
         out_specs=VMEM,
         out_shape=jax.ShapeDtypeStruct((height, count), F32),
         scratch_shapes=[pltpu.VMEM((count, tile), BF16)],
         compiler_params=room(24),
-        cost_estimate=cost(2 * height * count * span, 2 * span * (height + count)),
+        cost_estimate=cost(4 * height * count * steps * tile, 4 * steps * tile * (height + count)),
         name="correl",
-    )(scaled, *refs)
+    )(scaled, *refs, *seeds)
 
 
 def weigh_kernel(scale, masks, own, got, pair, *rest):
@@ -463,25 +464,23 @@
 
 
 def finish_kernel(blocks, place, *rest):
-    shares, apart = rest[:blocks], rest[blocks:-6]
-    wedge, out, tables, held, came, went = rest[-6:]
+    shares, apart = rest[:blocks], rest[blocks:-4]
+    wedge, out, held, went = rest[-4:]
     masks = wedge.shape[0]
-    span = tables.shape[1]
+    span = held.shape[1]
     keep = span - apart[0].shape[1]
     at = pl.multiple_of(place[1] * span, span)
-    fetch = pltpu.make_async_copy(wedge.at[:, pl.ds(at, span)], tables, came)
-    fetch.start()
     mass = 0.0
     for part in shares:
         mass = mass + part[:, keep : keep + 3 * masks].astype(F32)
     mass = mass[:, :masks] + mass[:, masks : 2 * masks] + mass[:, 2 * masks : 3 * masks]
-    fetch.wait()
     leaves = []
     half = keep // 256 * 128
     for i, (first, end) in enumerate(((0, half), (half, keep), (keep, span))):
         below = jnp.ones((held.shape[0], end - first), F32)
         for w in range(masks):
-            below = below + mass[:, w : w + 1] * tables[w : w + 1, first:end]
+            row = wedge[w : w + 1, pl.ds(pl.multiple_of(at + first, 128), end - first)]
+            below = below + mass[:, w : w + 1] * row
         total = 0.0
         for part in apart if i == 2 else shares:
             total = total + (part[...] if i == 2 else part[:, first:end]).astype(F32)
@@ -497,17 +496,14 @@
 
 def finish(place, shares, apart, wedge, span):
     per_ref = shares[0].shape[0]
-    masks = wedge.shape[0]
     blocks = len(shares)
     return pl.pallas_call(
         functools.partial(finish_kernel, blocks),
-        in_specs=[SMEM] + [VMEM] * (blocks + len(apart)) + [HBM],
+        in_specs=[SMEM] + [VMEM] * (blocks + len(apart) + 1),
         out_specs=HBM,
         out_shape=jax.ShapeDtypeStruct((per_ref, span), F32),
         scratch_shapes=[
-            pltpu.VMEM((masks, span), F32),
             pltpu.VMEM((per_ref, span), F32),
-            pltpu.SemaphoreType.DMA,
             pltpu.SemaphoreType.DMA((3,)),
         ],
         compiler_params=room(16),
@@ -545,6 +541,8 @@
     slab_hbm, refs_hbm = (
         pltpu.with_memory_space_constraint(value, pltpu.HBM) for value in (slab, references)
     )
+    quarter = half // 8
+    most = 3 * quarter
     low, high, aside = cut(place, refs_hbm, slab_hbm, layers, per_vox)
     mate = lax.ppermute(aside, "core", [(0, 1), (1, 0)])
     if blocks == 4:
@@ -553,11 +551,16 @@
         high_y = lax.ppermute(high, "blk", over_y)
         high_x = lax.ppermute(high, "blk", over_x)
         low_y = lax.ppermute(low, "blk", over_y)
-        low_xy = lax.ppermute(low_x, "blk", over_y)
-        high_xy = lax.ppermute(high_y, "blk", over_x)
+        low_xy = lax.ppermute(low_x[:, :most], "blk", over_y)
+        high_xy = lax.ppermute(high_y[:, :most], "blk", over_x)
+        low_end = lax.ppermute(low_x[:, most:], "blk", over_y)
+        high_end = lax.ppermute(high_y[:, most:], "blk", over_x)
         tables = [[low, low_x, low_y, low_xy], [high, high_x, high_y, high_xy]]
+        ends = [[low, low_x, low_y, low_end], [high, high_x, high_y, high_end]]
+        shifts = [0, 0, 0, most]
     else:
         tables = [passed([s] * blocks, "blk", blocks) for s in (low, high)]
+        ends, shifts = tables, [0] * blocks
     far = deal(place, slab_hbm, mate, layers, keep)
     pieces = [None] * layers
     for p in range(1, layers):
@@ -605,7 +608,8 @@
         steps,
     )
     pairs = passed([pair] * layers, "lay", layers)
-    sums = correl(scaled, tables, half // 8)
+    sums = correl(scaled, tables, [0] * blocks, quarter, 0, 3, [])
+    sums = correl(scaled, ends, shifts, quarter, most, 1, [sums])
     got = lax.ppermute(sums, "core", [(0, 1), (1, 0)])
     weights = weigh(sums, got, pair, notes, masks, 1.0 / (32.0 * math.sqrt(voxels)))
     all_weights = passed([weights] * layers, "lay", layers)

time: 164 us -> 170 us (1.037)
  starting transfers between devices: 42 us -> 45.9 us
    ppermute x2 -> x4, waiting for transfers between devices: 6.28 us -> 10.6 us  [the longest x1 10.6 us: per_device(): low_xy = lax.ppermute(low_x[:, :most], 'blk', over_y)]
    ppermute x19, starting transfers between devices: 25.9 us -> 30.2 us  [passed(): lax.ppermute(values[p], axis, [(d, d ^ p) for d in range(size)])]
    ppermute x19, waiting for transfers between devices: 70 us -> 66.1 us  [passed(): lax.ppermute(values[p], axis, [(d, d ^ p) for d in range(size)])]
    pallas_call x1 -> x2, Pallas kernels: 3.72 us -> 3.55 us  [correl(): pl.pallas_call(functools.partial(correl_kernel, blocks, tile, first, step...]
  transfers between devices with their start and end apart: 30 -> 32, of which waited for: 12 -> 15; matrix products, arithmetic and copies ran while one was open for 0% -> 0% of each run, Pallas kernels for 17% -> 16%
where the time goes in v9:
time: 170 us; the launch traced here: 169 us
  waiting for transfers between devices  89.7 us (53%)
  starting transfers between devices  45.9 us (27%)
  Pallas kernels  32.6 us (19%)
    ppermute x19, waiting for transfers between devices, passed(): lax.ppermute(values[p], axis, [(d, d ^ p) for d in range(size)])  66.1 us
    ppermute x19, starting transfers between devices, passed(): lax.ppermute(values[p], axis, [(d, d ^ p) for d in range(size)])  30.2 us
    pallas_call x3, Pallas kernels, select(): pl.pallas_call(functools.partial(select_kernel, len(blocks)), grid_spec=p...  12.2 us
    ppermute x1, waiting for transfers between devices, per_device(): low_xy = lax.ppermute(low_x[:, :most], 'blk', over_y)  10.6 us
    ppermute x1, waiting for transfers between devices, per_device(): high_x = lax.ppermute(high, 'blk', over_x)  10.4 us
    ppermute x3, starting transfers between devices, per_device(): lax.ppermute(far[p - 1], 'lay', [(z, z ^ p) for z in range(layers)])  5.8 us
    pallas_call x2, Pallas kernels, blend(): pl.pallas_call(functools.partial(blend_kernel, layers, len(scaled), block...  4.31 us
    pallas_call x2, Pallas kernels, correl(): pl.pallas_call(functools.partial(correl_kernel, blocks, tile, first, step...  3.55 us
  transfers between devices with their start and end apart: 32, of which 15 were waited for; matrix products, arithmetic and copies ran while one was open for 0% of the time, Pallas kernels for 16%

profile of v9, /device:TPU:0, one launch (start us, length us, event | category | flops | bytes accessed | tf_op | source)
XLA Modules:
  0.0 169.4 jit_solution(2872227516361986054)
XLA Ops:
  0.1 2.9 %cut.1 = (bf16[48,8192]{1,0:T(8,128)(2,1)S(1)}, bf16[48,8192]{1,0:T(8,128)(2,1)S(1)}, bf16[64,16384]{1,0:T(8,128)(2,1)S(1)}) custom-call(s32[4]{0:T(128)S(1)} %pad_add_fusion.place, bf16[48,32768]{1,0:T(8,128)(2,1)} %refs.3, bf16[64,32768]{1,0:T(8,128)(2,1)} %slab.3), custom_call_target="tpu_custom_call" | custom-call | bytes 7340032 | tf_op jit(solution)/shard_map/cut/pallas_call | solution.py:79
  3.6 2.6 %collective-permute-start.5 = (bf16[48,8192]{1,0:T(8,128)(2,1)S(1)}, bf16[48,8192]{1,0:T(8,128)(2,1)S(1)}, u32[]{:S(2)}, u32[]{:S(2)}) collective-permute-start(bf16[48,8192]{1,0:T(8,128)(2,1)S(1)} %get-tuple-element.24.rest_0_), channel_id=1, source_target_pairs={{0,1},{1,0},{2,3},{3,2},{4,5},{5,4},{6,7},{7,6},{8,9},{9,8},{10,11... | collective-permute-start | bytes 2359304 | tf_op jit(solution)/shard_map/ppermute | solution.py:550
  8.4 3.0 %brief.1.rest_0_ = f32[16,128]{1,0:T(8,128)S(1)} custom-call(s32[1]{0:T(128)S(6)} %copy.8.live, bf16[48,32768]{1,0:T(8,128)(2,1)S(1)} %copy-done.1, f32[8,32768]{1,0:T(8,128)S(1)} %copy-done.2, s32[1,64]{1,0:T(1,128)S(1)} %bitcast.10, s32[1,64]{1,0:T(1,128)S(1)} %bitcast.11, s32[1,64]{1,0:T(1,128)S(1)} %bitcast.12), custom_call_target="tpu_custom_call" | custom-call | flops 150994944 | bytes 4194304 | tf_op jit(solution)/shard_map/brief/pallas_call | solution.py:164
  12.0 12.5 %collective-permute-done.1.rest_1_ = f32[16,128]{1,0:T(8,128)S(1)} collective-permute-done((f32[16,128]{1,0:T(8,128)S(1)}, f32[16,128]{1,0:T(8,128)S(1)}, u32[]{:S(2)}, u32[]{:S(2)}) %collective-permute-start.1) | collective-permute-done | bytes 8224 | tf_op jit(solution)/shard_map/ppermute | solution.py:520
  24.4 2.7 %collective-permute-start.3 = (f32[16,128]{1,0:T(8,128)S(1)}, f32[16,128]{1,0:T(8,128)S(1)}, u32[]{:S(2)}, u32[]{:S(2)}) collective-permute-start(f32[16,128]{1,0:T(8,128)S(1)} %brief.1.rest_0_), channel_id=1, source_target_pairs={{0,3},{1,2},{2,1},{3,0},{4,7},{5,6},{6,5},{7,4},{8,11},{9,10},{10,... | collective-permute-start | bytes 24584 | tf_op jit(solution)/shard_map/ppermute | solution.py:520
  35.2 1.9 %deal.1 = (bf16[128,2816]{1,0:T(8,128)(2,1)S(1)}, bf16[128,2816]{1,0:T(8,128)(2,1)S(1)}, bf16[128,2816]{1,0:T(8,128)(2,1)S(1)}) custom-call(s32[4]{0:T(128)S(1)} %pad_add_fusion.place, bf16[64,32768]{1,0:T(8,128)(2,1)} %slab.3, bf16[64,16384]{1,0:T(8,128)(2,1)S(1)} %collective-permute-done.rest_1_.mate), custom_call_target="tpu_custom_call" | custom-call | bytes 4325376 | tf_op jit(solution)/shard_map/deal/pallas_call | solution.py:119
  37.1 10.4 %collective-permute-done.6.rest_3_ = bf16[48,8192]{1,0:T(8,128)(2,1)S(1)} collective-permute-done((bf16[48,8192]{1,0:T(8,128)(2,1)S(1)}, bf16[48,8192]{1,0:T(8,128)(2,1)S(1)}, u32[]{:S(2)}, u32[]{:S(2)}) %collective-permute-start.6) | collective-permute-done | bytes 786464 | tf_op jit(solution)/shard_map/ppermute | solution.py:552
  51.3 10.6 %collective-permute-done.11.rest_6_ = bf16[48,6144]{1,0:T(8,128)(2,1)S(1)} collective-permute-done((bf16[48,6144]{1,0:T(8,128)(2,1)S(1)}, bf16[48,6144]{1,0:T(8,128)(2,1)S(1)}, u32[]{:S(2)}, u32[]{:S(2)}) %collective-permute-start.11) | collective-permute-done | bytes 589856 | tf_op jit(solution)/shard_map/ppermute | solution.py:554
  61.9 2.6 %collective-permute-start.18 = (bf16[128,2816]{1,0:T(8,128)(2,1)S(1)}, bf16[128,2816]{1,0:T(8,128)(2,1)S(1)}, u32[]{:S(2)}, u32[]{:S(2)}) collective-permute-start(bf16[128,2816]{1,0:T(8,128)(2,1)S(1)} %get-tuple-element.27), channel_id=1, source_target_pairs={{0,16},{8,24},{16,0},{24,8},{1,17},{9,25},{17,1},{25,9},{2,18},{10... | collective-permute-start | bytes 2162696 | tf_op jit(solution)/shard_map/ppermute | solution.py:567
  65.8 6.2 %select.3.scaled.rest_1_ = bf16[256,16384]{1,0:T(8,128)(2,1)S(1)} custom-call(s32[4]{0:T(128)S(1)} %pad_add_fusion.place, bf16[64,32768]{1,0:T(8,128)(2,1)S(1)} %copy-done, bf16[64,16384]{1,0:T(8,128)(2,1)S(1)} %collective-permute-done.rest_1_.mate, f32[2,8,128]{2,1,0:T(8,128)S(1)} %pad_maximum_fusion.rest_2_.pair.rest_6_, f32[8,32768]{1,0:T(8,128)S(1)} %copy-done.2), custom_call_target="tpu_custom_call" | custom-call | flops 4294967296 | bytes 12582912 | tf_op jit(solution)/shard_map/select/pallas_call | solution.py:276
  72.0 2.8 %correl.2.rest_8_ = f32[256,192]{1,0:T(8,128)S(1)} custom-call(bf16[256,16384]{1,0:T(8,128)(2,1)S(1)} %select.3.scaled.rest_1_, bf16[48,8192]{1,0:T(8,128)(2,1)S(1)} %get-tuple-element.24.rest_0_, bf16[48,8192]{1,0:T(8,128)(2,1)S(1)} %get-tuple-element.25.rest_1_, bf16[48,8192]{1,0:T(8,128)(2,1)S(1)} %collective-permute-done.5.rest_2_, ...), custom_call_target="tpu_custom_call" | custom-call | flops 1207959552 | bytes 11010048 | tf_op jit(solution)/shard_map/correl/pallas_call | solution.py:324
  79.0 15.2 %collective-permute-done.20.rest_3_.rest_7_ = f32[2,8,128]{2,1,0:T(8,128)S(1)} collective-permute-done((f32[2,8,128]{2,1,0:T(8,128)S(1)}, f32[2,8,128]{2,1,0:T(8,128)S(1)}, u32[]{:S(2)}, u32[]{:S(2)}) %collective-permute-start.20) | collective-permute-done | bytes 8224 | tf_op jit(solution)/shard_map/ppermute | solution.py:520
  94.2 3.5 %collective-permute-start.21 = (f32[2,8,128]{2,1,0:T(8,128)S(1)}, f32[2,8,128]{2,1,0:T(8,128)S(1)}, u32[]{:S(2)}, u32[]{:S(2)}) collective-permute-start(f32[2,8,128]{2,1,0:T(8,128)S(1)} %pad_maximum_fusion.rest_2_.pair.rest_6_), channel_id=1, source_target_pairs={{0,16},{8,24},{16,0},{24,8},{1,17},{9,25},{17,1},{25,9},{2,18},{10... | collective-permute-start | bytes 24584 | tf_op jit(solution)/shard_map/ppermute | solution.py:520
  97.7 25.6 %collective-permute-done.21.rest_4_.rest_8_ = f32[2,8,128]{2,1,0:T(8,128)S(1)} collective-permute-done((f32[2,8,128]{2,1,0:T(8,128)S(1)}, f32[2,8,128]{2,1,0:T(8,128)S(1)}, u32[]{:S(2)}, u32[]{:S(2)}) %collective-permute-start.21) | collective-permute-done | bytes 8224 | tf_op jit(solution)/shard_map/ppermute | solution.py:520
  123.3 3.3 %collective-permute-start.22 = (f32[2,8,128]{2,1,0:T(8,128)S(1)}, f32[2,8,128]{2,1,0:T(8,128)S(1)}, u32[]{:S(2)}, u32[]{:S(2)}) collective-permute-start(f32[2,8,128]{2,1,0:T(8,128)S(1)} %pad_maximum_fusion.rest_2_.pair.rest_6_), channel_id=1, source_target_pairs={{0,24},{8,16},{16,8},{24,0},{1,25},{9,17},{17,9},{25,1},{2,26},{10... | collective-permute-start | bytes 24584 | tf_op jit(solution)/shard_map/ppermute | solution.py:520
  132.2 2.0 %select.4.rest_4_ = bf16[256,2816]{1,0:T(8,128)(2,1)S(1)} custom-call(s32[4]{0:T(128)S(1)} %pad_add_fusion.place, bf16[64,32768]{1,0:T(8,128)(2,1)S(1)} %copy-done, bf16[64,16384]{1,0:T(8,128)(2,1)S(1)} %collective-permute-done.rest_1_.mate, f32[2,8,128]{2,1,0:T(8,128)S(1)} %pad_maximum_fusion.rest_2_.pair.rest_6_, f32[8,32768]{1,0:T(8,128)S(1)} %copy-done.2), custom_call_target="tpu_custom_call" | custom-call | flops 738197504 | bytes 2162688 | tf_op jit(solution)/shard_map/select/pallas_call | solution.py:276
  134.4 3.3 %collective-permute-start.16 = (bf16[2,192,128]{2,1,0:T(8,128)(2,1)S(1)}, bf16[2,192,128]{2,1,0:T(8,128)(2,1)S(1)}, u32[]{:S(2)}, u32[]{:S(2)}) collective-permute-start(bf16[2,192,128]{2,1,0:T(8,128)(2,1)S(1)} %weigh.1.rest_0_), channel_id=1, source_target_pairs={{0,24},{8,16},{16,8},{24,0},{1,25},{9,17},{17,9},{25,1},{2,26},{10... | collective-permute-start | bytes 294920 | tf_op jit(solution)/shard_map/ppermute | solution.py:520
  137.7 4.0 %select.5.rest_5_ = bf16[768,2816]{1,0:T(8,128)(2,1)S(1)} custom-call(s32[4]{0:T(128)S(1)} %pad_add_fusion.place, bf16[128,2816]{1,0:T(8,128)(2,1)S(1)} %collective-permute-done.17.rest_0_, bf16[128,2816]{1,0:T(8,128)(2,1)S(1)} %collective-permute-done.18.rest_1_, bf16[128,2816]{1,0:T(8,128)(2,1)S(1)} %collective-permute-done.19.rest_2_, ...), custom_call_target="tpu_custom_call" | custom-call | flops 2214592512 | bytes 6488064 | tf_op jit(solution)/shard_map/select/pallas_call | solution.py:276
  142.0 2.5 %blend.2 = (bf16[48,2944]{1,0:T(8,128)(2,1)S(1)}, bf16[48,2944]{1,0:T(8,128)(2,1)S(1)}, bf16[48,2944]{1,0:T(8,128)(2,1)S(1)}, bf16[48,2944]{1,0:T(8,128)(2,1)S(1)}) custom-call(s32[4]{0:T(128)S(1)} %pad_add_fusion.place, bf16[2,192,128]{2,1,0:T(8,128)(2,1)S(1)} %weigh.1.rest_0_, bf16[2,192,128]{2,1,0:T(8,128)(2,1)S(1)} %collective-permute-done.14.rest_1_, ...), custom_call_target="tpu_custom_call" | custom-call | flops 1107296256 | bytes 6848512 | tf_op jit(solution)/shard_map/blend/pallas_call | solution.py:430
  149.6 4.4 %collective-permute-done.28.refs_3_ = bf16[4,48,1280]{2,1,0:T(8,128)(2,1)S(1)} collective-permute-done((bf16[4,48,1280]{2,1,0:T(8,128)(2,1)S(1)}, bf16[4,48,1280]{2,1,0:T(8,128)(2,1)S(1)}, u32[]{:S(2)}, u32[]{:S(2)}) %collective-permute-start.28) | collective-permute-done | bytes 491552 | tf_op jit(solution)/shard_map/ppermute | solution.py:520
  154.4 4.1 %collective-permute-start.30 = (bf16[48,1280]{1,0:T(8,128)(2,1)S(1)}, bf16[48,1280]{1,0:T(8,128)(2,1)S(1)}, u32[]{:S(2)}, u32[]{:S(2)}) collective-permute-start(bf16[48,1280]{1,0:T(8,128)(2,1)S(1)} %get-tuple-element.39), channel_id=1, source_target_pairs={{0,16},{8,24},{16,0},{24,8},{1,17},{9,25},{17,1},{25,9},{2,18},{10... | collective-permute-start | bytes 368648 | tf_op jit(solution)/shard_map/ppermute | solution.py:520
  159.7 4.5 %collective-permute-start.31 = (bf16[48,1280]{1,0:T(8,128)(2,1)S(1)}, bf16[48,1280]{1,0:T(8,128)(2,1)S(1)}, u32[]{:S(2)}, u32[]{:S(2)}) collective-permute-start(bf16[48,1280]{1,0:T(8,128)(2,1)S(1)} %get-tuple-element.40), channel_id=1, source_target_pairs={{0,24},{8,16},{16,8},{24,0},{1,25},{9,17},{17,9},{25,1},{2,26},{10... | collective-permute-start | bytes 368648 | tf_op jit(solution)/shard_map/ppermute | solution.py:520
  164.1 2.9 %collective-permute-done.31.rest_7_ = bf16[48,1280]{1,0:T(8,128)(2,1)S(1)} collective-permute-done((bf16[48,1280]{1,0:T(8,128)(2,1)S(1)}, bf16[48,1280]{1,0:T(8,128)(2,1)S(1)}, u32[]{:S(2)}, u32[]{:S(2)}) %collective-permute-start.31) | collective-permute-done | bytes 122912 | tf_op jit(solution)/shard_map/ppermute | solution.py:520
  167.0 2.3 %finish.1 = f32[48,4096]{1,0:T(8,128)} custom-call(s32[4]{0:T(128)S(1)} %pad_add_fusion.place, bf16[48,2944]{1,0:T(8,128)(2,1)S(1)} %get-tuple-element.29.rest_0_, bf16[48,2944]{1,0:T(8,128)(2,1)S(1)} %collective-permute-done.23.rest_1_, bf16[48,2944]{1,0:T(8,128)(2,1)S(1)} %collective-permute-done.24.rest_2_, ...), custom_call_target="tpu_custom_call" | custom-call | bytes 1572864 | tf_op jit(solution)/shard_map/finish/pallas_call | solution.py:500
  (72 shorter events, 32.7 us)
Async XLA Ops:
  3.0 31.6 %collective-permute-start = (bf16[64,16384]{1,0:T(8,128)(2,1)S(1)}, bf16[64,16384]{1,0:T(8,128)(2,1)S(1)}, u32[]{:S(2)}, u32[]{:S(2)}) collective-permute-start(bf16[64,16384]{1,0:T(8,128)(2,1)S(1)} %get-tuple-element.23), channel_id=1, source_target_pairs={{0,4},{4,0},{1,5},{5,1},{2,6},{6,2},{3,7},{7,3},{8,12},{12,8},{9,1... | collective-permute-start | bytes 6291464 | tf_op jit(solution)/shard_map/ppermute | solution.py:547
  3.6 28.3 %collective-permute-start.5 = (bf16[48,8192]{1,0:T(8,128)(2,1)S(1)}, bf16[48,8192]{1,0:T(8,128)(2,1)S(1)}, u32[]{:S(2)}, u32[]{:S(2)}) collective-permute-start(bf16[48,8192]{1,0:T(8,128)(2,1)S(1)} %get-tuple-element.24.rest_0_), channel_id=1, source_target_pairs={{0,1},{1,0},{2,3},{3,2},{4,5},{5,4},{6,7},{7,6},{8,9},{9,8},{10,11... | collective-permute-start | bytes 2359304 | tf_op jit(solution)/shard_map/ppermute | solution.py:550
  6.1 25.8 %collective-permute-start.8 = (bf16[48,8192]{1,0:T(8,128)(2,1)S(1)}, bf16[48,8192]{1,0:T(8,128)(2,1)S(1)}, u32[]{:S(2)}, u32[]{:S(2)}) collective-permute-start(bf16[48,8192]{1,0:T(8,128)(2,1)S(1)} %get-tuple-element.25.rest_1_), channel_id=1, source_target_pairs={{0,2},{1,3},{2,0},{3,1},{4,6},{5,7},{6,4},{7,5},{8,10},{9,11},{10,... | collective-permute-start | bytes 2359304 | tf_op jit(solution)/shard_map/ppermute | solution.py:551
  11.3 13.1 %collective-permute-start.1 = (f32[16,128]{1,0:T(8,128)S(1)}, f32[16,128]{1,0:T(8,128)S(1)}, u32[]{:S(2)}, u32[]{:S(2)}) collective-permute-start(f32[16,128]{1,0:T(8,128)S(1)} %brief.1.rest_0_), channel_id=1, source_target_pairs={{0,1},{1,0},{2,3},{3,2},{4,5},{5,4},{6,7},{7,6},{8,9},{9,8},{10,11... | collective-permute-start | bytes 24584 | tf_op jit(solution)/shard_map/ppermute | solution.py:520
  11.9 15.2 %collective-permute-start.2 = (f32[16,128]{1,0:T(8,128)S(1)}, f32[16,128]{1,0:T(8,128)S(1)}, u32[]{:S(2)}, u32[]{:S(2)}) collective-permute-start(f32[16,128]{1,0:T(8,128)S(1)} %brief.1.rest_0_), channel_id=1, source_target_pairs={{0,2},{1,3},{2,0},{3,1},{4,6},{5,7},{6,4},{7,5},{8,10},{9,11},{10,... | collective-permute-start | bytes 24584 | tf_op jit(solution)/shard_map/ppermute | solution.py:520
  27.2 20.4 %collective-permute-start.6 = (bf16[48,8192]{1,0:T(8,128)(2,1)S(1)}, bf16[48,8192]{1,0:T(8,128)(2,1)S(1)}, u32[]{:S(2)}, u32[]{:S(2)}) collective-permute-start(bf16[48,8192]{1,0:T(8,128)(2,1)S(1)} %get-tuple-element.25.rest_1_), channel_id=1, source_target_pairs={{0,1},{1,0},{2,3},{3,2},{4,5},{5,4},{6,7},{7,6},{8,9},{9,8},{10,11... | collective-permute-start | bytes 2359304 | tf_op jit(solution)/shard_map/ppermute | solution.py:552
  29.0 20.4 %collective-permute-start.7 = (bf16[48,8192]{1,0:T(8,128)(2,1)S(1)}, bf16[48,8192]{1,0:T(8,128)(2,1)S(1)}, u32[]{:S(2)}, u32[]{:S(2)}) collective-permute-start(bf16[48,8192]{1,0:T(8,128)(2,1)S(1)} %get-tuple-element.24.rest_0_), channel_id=1, source_target_pairs={{0,2},{1,3},{2,0},{3,1},{4,6},{5,7},{6,4},{7,5},{8,10},{9,11},{10,... | collective-permute-start | bytes 2359304 | tf_op jit(solution)/shard_map/ppermute | solution.py:553
  32.0 29.9 %collective-permute-start.11 = (bf16[48,6144]{1,0:T(8,128)(2,1)S(1)}, bf16[48,6144]{1,0:T(8,128)(2,1)S(1)}, u32[]{:S(2)}, u32[]{:S(2)}) collective-permute-start(bf16[48,6144]{1,0:T(8,128)(2,1)S(1)} %slice.18), channel_id=1, source_target_pairs={{0,2},{1,3},{2,0},{3,1},{4,6},{5,7},{6,4},{7,5},{8,10},{9,11},{10,... | collective-permute-start | bytes 1769480 | tf_op jit(solution)/shard_map/ppermute | solution.py:554
  33.1 31.4 %collective-permute-start.12 = (bf16[48,6144]{1,0:T(8,128)(2,1)S(1)}, bf16[48,6144]{1,0:T(8,128)(2,1)S(1)}, u32[]{:S(2)}, u32[]{:S(2)}) collective-permute-start(bf16[48,6144]{1,0:T(8,128)(2,1)S(1)} %slice.19), channel_id=1, source_target_pairs={{0,1},{1,0},{2,3},{3,2},{4,5},{5,4},{6,7},{7,6},{8,9},{9,8},{10,11... | collective-permute-start | bytes 1769480 | tf_op jit(solution)/shard_map/ppermute | solution.py:555
  34.6 40.2 %collective-permute-start.10 = (bf16[48,2048]{1,0:T(8,128)(2,1)S(1)}, bf16[48,2048]{1,0:T(8,128)(2,1)S(1)}, u32[]{:S(2)}, u32[]{:S(2)}) collective-permute-start(bf16[48,2048]{1,0:T(8,128)(2,1)S(1)} %slice.17), channel_id=1, source_target_pairs={{0,1},{1,0},{2,3},{3,2},{4,5},{5,4},{6,7},{7,6},{8,9},{9,8},{10,11... | collective-permute-start | bytes 589832 | tf_op jit(solution)/shard_map/ppermute | solution.py:557
  47.6 27.3 %collective-permute-start.9 = (bf16[48,2048]{1,0:T(8,128)(2,1)S(1)}, bf16[48,2048]{1,0:T(8,128)(2,1)S(1)}, u32[]{:S(2)}, u32[]{:S(2)}) collective-permute-start(bf16[48,2048]{1,0:T(8,128)(2,1)S(1)} %slice.16), channel_id=1, source_target_pairs={{0,2},{1,3},{2,0},{3,1},{4,6},{5,7},{6,4},{7,5},{8,10},{9,11},{10,... | collective-permute-start | bytes 589832 | tf_op jit(solution)/shard_map/ppermute | solution.py:556
  49.4 82.0 %collective-permute-start.17 = (bf16[128,2816]{1,0:T(8,128)(2,1)S(1)}, bf16[128,2816]{1,0:T(8,128)(2,1)S(1)}, u32[]{:S(2)}, u32[]{:S(2)}) collective-permute-start(bf16[128,2816]{1,0:T(8,128)(2,1)S(1)} %get-tuple-element.26), channel_id=1, source_target_pairs={{0,8},{8,0},{16,24},{24,16},{1,9},{9,1},{17,25},{25,17},{2,10},{10... | collective-permute-start | bytes 2162696 | tf_op jit(solution)/shard_map/ppermute | solution.py:567
  61.9 72.4 %collective-permute-start.18 = (bf16[128,2816]{1,0:T(8,128)(2,1)S(1)}, bf16[128,2816]{1,0:T(8,128)(2,1)S(1)}, u32[]{:S(2)}, u32[]{:S(2)}) collective-permute-start(bf16[128,2816]{1,0:T(8,128)(2,1)S(1)} %get-tuple-element.27), channel_id=1, source_target_pairs={{0,16},{8,24},{16,0},{24,8},{1,17},{9,25},{17,1},{25,9},{2,18},{10... | collective-permute-start | bytes 2162696 | tf_op jit(solution)/shard_map/ppermute | solution.py:567
  64.5 69.9 %collective-permute-start.19 = (bf16[128,2816]{1,0:T(8,128)(2,1)S(1)}, bf16[128,2816]{1,0:T(8,128)(2,1)S(1)}, u32[]{:S(2)}, u32[]{:S(2)}) collective-permute-start(bf16[128,2816]{1,0:T(8,128)(2,1)S(1)} %get-tuple-element.28), channel_id=1, source_target_pairs={{0,24},{8,16},{16,8},{24,0},{1,25},{9,17},{17,9},{25,1},{2,26},{10... | collective-permute-start | bytes 2162696 | tf_op jit(solution)/shard_map/ppermute | solution.py:567
  75.7 18.5 %collective-permute-start.20 = (f32[2,8,128]{2,1,0:T(8,128)S(1)}, f32[2,8,128]{2,1,0:T(8,128)S(1)}, u32[]{:S(2)}, u32[]{:S(2)}) collective-permute-start(f32[2,8,128]{2,1,0:T(8,128)S(1)} %pad_maximum_fusion.rest_2_.pair.rest_6_), channel_id=1, source_target_pairs={{0,8},{8,0},{16,24},{24,16},{1,9},{9,1},{17,25},{25,17},{2,10},{10... | collective-permute-start | bytes 24584 | tf_op jit(solution)/shard_map/ppermute | solution.py:520
  78.4 51.6 %collective-permute-start.14 = (bf16[2,192,128]{2,1,0:T(8,128)(2,1)S(1)}, bf16[2,192,128]{2,1,0:T(8,128)(2,1)S(1)}, u32[]{:S(2)}, u32[]{:S(2)}) collective-permute-start(bf16[2,192,128]{2,1,0:T(8,128)(2,1)S(1)} %weigh.1.rest_0_), channel_id=1, source_target_pairs={{0,8},{8,0},{16,24},{24,16},{1,9},{9,1},{17,25},{25,17},{2,10},{10... | collective-permute-start | bytes 294920 | tf_op jit(solution)/shard_map/ppermute | solution.py:520
  94.2 29.1 %collective-permute-start.21 = (f32[2,8,128]{2,1,0:T(8,128)S(1)}, f32[2,8,128]{2,1,0:T(8,128)S(1)}, u32[]{:S(2)}, u32[]{:S(2)}) collective-permute-start(f32[2,8,128]{2,1,0:T(8,128)S(1)} %pad_maximum_fusion.rest_2_.pair.rest_6_), channel_id=1, source_target_pairs={{0,16},{8,24},{16,0},{24,8},{1,17},{9,25},{17,1},{25,9},{2,18},{10... | collective-permute-start | bytes 24584 | tf_op jit(solution)/shard_map/ppermute | solution.py:520
  128.7 18.6 %collective-permute-start.26 = (bf16[4,48,1280]{2,1,0:T(8,128)(2,1)S(1)}, bf16[4,48,1280]{2,1,0:T(8,128)(2,1)S(1)}, u32[]{:S(2)}, u32[]{:S(2)}) collective-permute-start(bf16[4,48,1280]{2,1,0:T(8,128)(2,1)S(1)} %get-tuple-element.34), channel_id=1, source_target_pairs={{0,1},{1,0},{2,3},{3,2},{4,5},{5,4},{6,7},{7,6},{8,9},{9,8},{10,11... | collective-permute-start | bytes 1474568 | tf_op jit(solution)/shard_map/ppermute | solution.py:520
  129.9 19.7 %collective-permute-start.27 = (bf16[4,48,1280]{2,1,0:T(8,128)(2,1)S(1)}, bf16[4,48,1280]{2,1,0:T(8,128)(2,1)S(1)}, u32[]{:S(2)}, u32[]{:S(2)}) collective-permute-start(bf16[4,48,1280]{2,1,0:T(8,128)(2,1)S(1)} %get-tuple-element.35), channel_id=1, source_target_pairs={{0,2},{1,3},{2,0},{3,1},{4,6},{5,7},{6,4},{7,5},{8,10},{9,11},{10,... | collective-permute-start | bytes 1474568 | tf_op jit(solution)/shard_map/ppermute | solution.py:520
  131.4 22.6 %collective-permute-start.28 = (bf16[4,48,1280]{2,1,0:T(8,128)(2,1)S(1)}, bf16[4,48,1280]{2,1,0:T(8,128)(2,1)S(1)}, u32[]{:S(2)}, u32[]{:S(2)}) collective-permute-start(bf16[4,48,1280]{2,1,0:T(8,128)(2,1)S(1)} %get-tuple-element.36), channel_id=1, source_target_pairs={{0,3},{1,2},{2,1},{3,0},{4,7},{5,6},{6,5},{7,4},{8,11},{9,10},{10,... | collective-permute-start | bytes 1474568 | tf_op jit(solution)/shard_map/ppermute | solution.py:520
  144.5 22.5 %collective-permute-start.23 = (bf16[48,2944]{1,0:T(8,128)(2,1)S(1)}, bf16[48,2944]{1,0:T(8,128)(2,1)S(1)}, u32[]{:S(2)}, u32[]{:S(2)}) collective-permute-start(bf16[48,2944]{1,0:T(8,128)(2,1)S(1)} %get-tuple-element.30), channel_id=1, source_target_pairs={{0,1},{1,0},{2,3},{3,2},{4,5},{5,4},{6,7},{7,6},{8,9},{9,8},{10,11... | collective-permute-start | bytes 847880 | tf_op jit(solution)/shard_map/ppermute | solution.py:520
  145.8 21.2 %collective-permute-start.24 = (bf16[48,2944]{1,0:T(8,128)(2,1)S(1)}, bf16[48,2944]{1,0:T(8,128)(2,1)S(1)}, u32[]{:S(2)}, u32[]{:S(2)}) collective-permute-start(bf16[48,2944]{1,0:T(8,128)(2,1)S(1)} %get-tuple-element.31), channel_id=1, source_target_pairs={{0,2},{1,3},{2,0},{3,1},{4,6},{5,7},{6,4},{7,5},{8,10},{9,11},{10,... | collective-permute-start | bytes 847880 | tf_op jit(solution)/shard_map/ppermute | solution.py:520
  147.4 19.6 %collective-permute-start.25 = (bf16[48,2944]{1,0:T(8,128)(2,1)S(1)}, bf16[48,2944]{1,0:T(8,128)(2,1)S(1)}, u32[]{:S(2)}, u32[]{:S(2)}) collective-permute-start(bf16[48,2944]{1,0:T(8,128)(2,1)S(1)} %get-tuple-element.32), channel_id=1, source_target_pairs={{0,3},{1,2},{2,1},{3,0},{4,7},{5,6},{6,5},{7,4},{8,11},{9,10},{10,... | collective-permute-start | bytes 847880 | tf_op jit(solution)/shard_map/ppermute | solution.py:520
  154.4 9.8 %collective-permute-start.30 = (bf16[48,1280]{1,0:T(8,128)(2,1)S(1)}, bf16[48,1280]{1,0:T(8,128)(2,1)S(1)}, u32[]{:S(2)}, u32[]{:S(2)}) collective-permute-start(bf16[48,1280]{1,0:T(8,128)(2,1)S(1)} %get-tuple-element.39), channel_id=1, source_target_pairs={{0,16},{8,24},{16,0},{24,8},{1,17},{9,25},{17,1},{25,9},{2,18},{10... | collective-permute-start | bytes 368648 | tf_op jit(solution)/shard_map/ppermute | solution.py:520
  (14 other events, 113.3 us)

commit v10 on v9

--- a/solution.py
+++ b/solution.py
@@ -333,8 +333,8 @@
     )(scaled, *refs, *seeds)
 
 
-def weigh_kernel(scale, masks, own, got, pair, *rest):
-    notes, out = rest[:-1], rest[-1]
+def weigh_kernel(scale, masks, blocks, place, own, got, pair, scaled, *rest):
+    notes, out, outs, turned = rest[:blocks], rest[blocks], rest[blocks + 1 : -1], rest[-1]
     count, cap = out.shape[1], out.shape[2]
     per_ref = count // len(notes)
     lanes = notes[0].shape[1]
@@ -357,20 +357,36 @@
         score = (mine - 0.5 * dot(wedge_hot, norms)) * scale
         score = jnp.exp(score - jnp.max(score, axis=1, keepdims=True))
         share = score / jnp.sum(score, axis=1, keepdims=True) * columns[:, 2:3]
-        out[side] = share.T.astype(BF16)
-
-
-def weigh(own, got, pair, notes, masks, scale):
+        weights = share.T.astype(BF16)
+        out[side] = weights
+        turned[:, side * cap : (side + 1) * cap] = weights
+    steps, _, tile = outs[0].shape
+    stretch = scaled.shape[1] // steps
+
+    def step(t, carry):
+        at = pl.multiple_of((place[2] ^ t) * stretch + stretch - tile, 128)
+        sums = dot(turned[...], scaled[:, pl.ds(at, tile)]).astype(BF16)
+        for p, apart in enumerate(outs):
+            apart[t] = sums[p * per_ref : (p + 1) * per_ref, :]
+        return carry
+
+    lax.fori_loop(0, steps, step, 0)
+
+
+def weigh(place, own, got, pair, scaled, notes, masks, scale, layers, tile):
     cap, count = own.shape[0] // 2, own.shape[1]
-    return pl.pallas_call(
-        functools.partial(weigh_kernel, scale, masks),
-        in_specs=[VMEM] * (3 + len(notes)),
-        out_specs=VMEM,
-        out_shape=jax.ShapeDtypeStruct((2, count, cap), BF16),
-        cost_estimate=cost(1 << 24, 1 << 18),
-        compiler_params=room(16),
+    blocks = len(notes)
+    shapes = [(2, count, cap)] + [(layers, count // blocks, tile)] * blocks
+    return pl.pallas_call(
+        functools.partial(weigh_kernel, scale, masks, blocks),
+        in_specs=[SMEM] + [VMEM] * (4 + blocks),
+        out_specs=[VMEM] * len(shapes),
+        out_shape=[jax.ShapeDtypeStruct(shape, BF16) for shape in shapes],
+        scratch_shapes=[pltpu.VMEM((count, 2 * cap), BF16)],
+        compiler_params=room(24),
+        cost_estimate=cost(4 * cap * count * layers * tile, 1 << 21),
         name="weigh",
-    )(own, got, pair, *notes)
+    )(place, own, got, pair, scaled, *notes)
 
 
 def blend_kernel(layers, parts, blocks, masks, starts, place, *rest):
@@ -611,7 +627,10 @@
     sums = correl(scaled, tables, [0] * blocks, quarter, 0, 3, [])
     sums = correl(scaled, ends, shifts, quarter, most, 1, [sums])
     got = lax.ppermute(sums, "core", [(0, 1), (1, 0)])
-    weights = weigh(sums, got, pair, notes, masks, 1.0 / (32.0 * math.sqrt(voxels)))
+    scale = 1.0 / (32.0 * math.sqrt(voxels))
+    weights, *apart = weigh(
+        place, sums, got, pair, scaled, notes, masks, scale, layers, tile
+    )
     all_weights = passed([weights] * layers, "lay", layers)
 
     far_rows = select(
@@ -626,7 +645,6 @@
         steps,
     )
 
-    apart = blend(place, all_weights[:1], [], [scaled], masks, blocks, tile, layers)
     apart = passed(apart, "blk", blocks)
     apart = fold(apart)
     apart = passed(apart, "lay", layers)

time: 170 us -> 170 us (level)
    pallas_call x2 -> x1, Pallas kernels: 4.31 us -> 2.54 us  [blend(): pl.pallas_call(functools.partial(blend_kernel, layers, len(scaled), block...]
    pallas_call x1, Pallas kernels: 1.14 us -> 2.89 us  [weigh(): pl.pallas_call(functools.partial(weigh_kernel, scale, masks, blocks), in_...]
  transfers between devices with their start and end apart: 32 -> 32, of which waited for: 15 -> 14; matrix products, arithmetic and copies ran while one was open for 0% -> 0% of each run, Pallas kernels for 16% -> 16%
where the time goes in v10:
time: 170 us; the launch traced here: 169 us
  waiting for transfers between devices  89.2 us (52%)
  starting transfers between devices  46.5 us (27%)
  Pallas kernels  32.6 us (19%)
    ppermute x19, waiting for transfers between devices, passed(): lax.ppermute(values[p], axis, [(d, d ^ p) for d in range(size)])  65.3 us
    ppermute x19, starting transfers between devices, passed(): lax.ppermute(values[p], axis, [(d, d ^ p) for d in range(size)])  30.7 us
    pallas_call x3, Pallas kernels, select(): pl.pallas_call(functools.partial(select_kernel, len(blocks)), grid_spec=p...  12.2 us
    ppermute x1, waiting for transfers between devices, per_device(): low_xy = lax.ppermute(low_x[:, :most], 'blk', over_y)  10.6 us
    ppermute x1, waiting for transfers between devices, per_device(): high_x = lax.ppermute(high, 'blk', over_x)  10.4 us
    ppermute x3, starting transfers between devices, per_device(): lax.ppermute(far[p - 1], 'lay', [(z, z ^ p) for z in range(layers)])  5.8 us
    pallas_call x2, Pallas kernels, correl(): pl.pallas_call(functools.partial(correl_kernel, blocks, tile, first, step...  3.55 us
  transfers between devices with their start and end apart: 32, of which 14 were waited for; matrix products, arithmetic and copies ran while one was open for 0% of the time, Pallas kernels for 16%

profile of v10, /device:TPU:0, one launch (start us, length us, event | category | flops | bytes accessed | tf_op | source)
XLA Modules:
  0.0 169.4 jit_solution(10849306101892927511)
XLA Ops:
  0.1 2.9 %cut.1 = (bf16[48,8192]{1,0:T(8,128)(2,1)S(1)}, bf16[48,8192]{1,0:T(8,128)(2,1)S(1)}, bf16[64,16384]{1,0:T(8,128)(2,1)S(1)}) custom-call(s32[4]{0:T(128)S(1)} %pad_add_fusion.place, bf16[48,32768]{1,0:T(8,128)(2,1)} %refs.3, bf16[64,32768]{1,0:T(8,128)(2,1)} %slab.3), custom_call_target="tpu_custom_call" | custom-call | bytes 7340032 | tf_op jit(solution)/shard_map/cut/pallas_call | solution.py:79
  3.6 2.6 %collective-permute-start.5 = (bf16[48,8192]{1,0:T(8,128)(2,1)S(1)}, bf16[48,8192]{1,0:T(8,128)(2,1)S(1)}, u32[]{:S(2)}, u32[]{:S(2)}) collective-permute-start(bf16[48,8192]{1,0:T(8,128)(2,1)S(1)} %get-tuple-element.25.rest_0_), channel_id=1, source_target_pairs={{0,1},{1,0},{2,3},{3,2},{4,5},{5,4},{6,7},{7,6},{8,9},{9,8},{10,11... | collective-permute-start | bytes 2359304 | tf_op jit(solution)/shard_map/ppermute | solution.py:566
  8.4 3.0 %brief.1.rest_0_ = f32[16,128]{1,0:T(8,128)S(1)} custom-call(s32[1]{0:T(128)S(6)} %copy.8.live, bf16[48,32768]{1,0:T(8,128)(2,1)S(1)} %copy-done.1, f32[8,32768]{1,0:T(8,128)S(1)} %copy-done.2, s32[1,64]{1,0:T(1,128)S(1)} %bitcast.10, s32[1,64]{1,0:T(1,128)S(1)} %bitcast.11, s32[1,64]{1,0:T(1,128)S(1)} %bitcast.12), custom_call_target="tpu_custom_call" | custom-call | flops 150994944 | bytes 4194304 | tf_op jit(solution)/shard_map/brief/pallas_call | solution.py:164
  12.0 12.5 %collective-permute-done.1.rest_1_ = f32[16,128]{1,0:T(8,128)S(1)} collective-permute-done((f32[16,128]{1,0:T(8,128)S(1)}, f32[16,128]{1,0:T(8,128)S(1)}, u32[]{:S(2)}, u32[]{:S(2)}) %collective-permute-start.1) | collective-permute-done | bytes 8224 | tf_op jit(solution)/shard_map/ppermute | solution.py:536
  24.4 2.7 %collective-permute-start.3 = (f32[16,128]{1,0:T(8,128)S(1)}, f32[16,128]{1,0:T(8,128)S(1)}, u32[]{:S(2)}, u32[]{:S(2)}) collective-permute-start(f32[16,128]{1,0:T(8,128)S(1)} %brief.1.rest_0_), channel_id=1, source_target_pairs={{0,3},{1,2},{2,1},{3,0},{4,7},{5,6},{6,5},{7,4},{8,11},{9,10},{10,... | collective-permute-start | bytes 24584 | tf_op jit(solution)/shard_map/ppermute | solution.py:536
  37.1 10.4 %collective-permute-done.6.rest_3_ = bf16[48,8192]{1,0:T(8,128)(2,1)S(1)} collective-permute-done((bf16[48,8192]{1,0:T(8,128)(2,1)S(1)}, bf16[48,8192]{1,0:T(8,128)(2,1)S(1)}, u32[]{:S(2)}, u32[]{:S(2)}) %collective-permute-start.6) | collective-permute-done | bytes 786464 | tf_op jit(solution)/shard_map/ppermute | solution.py:568
  51.3 10.6 %collective-permute-done.11.rest_6_ = bf16[48,6144]{1,0:T(8,128)(2,1)S(1)} collective-permute-done((bf16[48,6144]{1,0:T(8,128)(2,1)S(1)}, bf16[48,6144]{1,0:T(8,128)(2,1)S(1)}, u32[]{:S(2)}, u32[]{:S(2)}) %collective-permute-start.11) | collective-permute-done | bytes 589856 | tf_op jit(solution)/shard_map/ppermute | solution.py:570
  61.9 2.6 %collective-permute-start.18 = (bf16[128,2816]{1,0:T(8,128)(2,1)S(1)}, bf16[128,2816]{1,0:T(8,128)(2,1)S(1)}, u32[]{:S(2)}, u32[]{:S(2)}) collective-permute-start(bf16[128,2816]{1,0:T(8,128)(2,1)S(1)} %get-tuple-element.29), channel_id=1, source_target_pairs={{0,16},{8,24},{16,0},{24,8},{1,17},{9,25},{17,1},{25,9},{2,18},{10... | collective-permute-start | bytes 2162696 | tf_op jit(solution)/shard_map/ppermute | solution.py:583
  65.8 6.2 %select.3.scaled = bf16[256,16384]{1,0:T(8,128)(2,1)S(1)} custom-call(s32[4]{0:T(128)S(1)} %pad_add_fusion.place, bf16[64,32768]{1,0:T(8,128)(2,1)S(1)} %copy-done, bf16[64,16384]{1,0:T(8,128)(2,1)S(1)} %collective-permute-done.rest_1_.mate, f32[2,8,128]{2,1,0:T(8,128)S(1)} %pad_maximum_fusion.rest_2_.pair.rest_6_, f32[8,32768]{1,0:T(8,128)S(1)} %copy-done.2), custom_call_target="tpu_custom_call" | custom-call | flops 4294967296 | bytes 12582912 | tf_op jit(solution)/shard_map/select/pallas_call | solution.py:276
  72.0 2.8 %correl.2.rest_8_ = f32[256,192]{1,0:T(8,128)S(1)} custom-call(bf16[256,16384]{1,0:T(8,128)(2,1)S(1)} %select.3.scaled, bf16[48,8192]{1,0:T(8,128)(2,1)S(1)} %get-tuple-element.25.rest_0_, bf16[48,8192]{1,0:T(8,128)(2,1)S(1)} %get-tuple-element.26.rest_1_, bf16[48,8192]{1,0:T(8,128)(2,1)S(1)} %collective-permute-done.5.rest_2_, ...), custom_call_target="tpu_custom_call" | custom-call | flops 1207959552 | bytes 11010048 | tf_op jit(solution)/shard_map/correl/pallas_call | solution.py:324
  77.2 2.9 %weigh.1 = (bf16[2,192,128]{2,1,0:T(8,128)(2,1)S(1)}, bf16[4,48,1280]{2,1,0:T(8,128)(2,1)S(1)}, bf16[4,48,1280]{2,1,0:T(8,128)(2,1)S(1)}, bf16[4,48,1280]{2,1,0:T(8,128)(2,1)S(1)}, bf16[4,48,1280]{2,1,0:T(8,128)(2,1)S(1)}) custom-call(s32[4]{0:T(128)S(1)} %pad_add_fusion.place, f32[256,192]{1,0:T(8,128)S(1)} %correl.3.own, ...), custom_call_target="tpu_custom_call" | custom-call | flops 503316480 | bytes 2097152 | tf_op jit(solution)/shard_map/weigh/pallas_call | solution.py:380
  82.2 26.3 %collective-permute-done.20.rest_3_.rest_7_ = f32[2,8,128]{2,1,0:T(8,128)S(1)} collective-permute-done((f32[2,8,128]{2,1,0:T(8,128)S(1)}, f32[2,8,128]{2,1,0:T(8,128)S(1)}, u32[]{:S(2)}, u32[]{:S(2)}) %collective-permute-start.20) | collective-permute-done | bytes 8224 | tf_op jit(solution)/shard_map/ppermute | solution.py:536
  108.5 2.5 %collective-permute-start.21 = (f32[2,8,128]{2,1,0:T(8,128)S(1)}, f32[2,8,128]{2,1,0:T(8,128)S(1)}, u32[]{:S(2)}, u32[]{:S(2)}) collective-permute-start(f32[2,8,128]{2,1,0:T(8,128)S(1)} %pad_maximum_fusion.rest_2_.pair.rest_6_), channel_id=1, source_target_pairs={{0,16},{8,24},{16,0},{24,8},{1,17},{9,25},{17,1},{25,9},{2,18},{10... | collective-permute-start | bytes 24584 | tf_op jit(solution)/shard_map/ppermute | solution.py:536
  111.0 12.3 %collective-permute-done.21.rest_4_.rest_8_ = f32[2,8,128]{2,1,0:T(8,128)S(1)} collective-permute-done((f32[2,8,128]{2,1,0:T(8,128)S(1)}, f32[2,8,128]{2,1,0:T(8,128)S(1)}, u32[]{:S(2)}, u32[]{:S(2)}) %collective-permute-start.21) | collective-permute-done | bytes 8224 | tf_op jit(solution)/shard_map/ppermute | solution.py:536
  123.3 3.3 %collective-permute-start.22 = (f32[2,8,128]{2,1,0:T(8,128)S(1)}, f32[2,8,128]{2,1,0:T(8,128)S(1)}, u32[]{:S(2)}, u32[]{:S(2)}) collective-permute-start(f32[2,8,128]{2,1,0:T(8,128)S(1)} %pad_maximum_fusion.rest_2_.pair.rest_6_), channel_id=1, source_target_pairs={{0,24},{8,16},{16,8},{24,0},{1,25},{9,17},{17,9},{25,1},{2,26},{10... | collective-permute-start | bytes 24584 | tf_op jit(solution)/shard_map/ppermute | solution.py:536
  126.6 2.2 %collective-permute-done.22.rest_5_.rest_9_ = f32[2,8,128]{2,1,0:T(8,128)S(1)} collective-permute-done((f32[2,8,128]{2,1,0:T(8,128)S(1)}, f32[2,8,128]{2,1,0:T(8,128)S(1)}, u32[]{:S(2)}, u32[]{:S(2)}) %collective-permute-start.22) | collective-permute-done | bytes 8224 | tf_op jit(solution)/shard_map/ppermute | solution.py:536
  134.4 3.3 %collective-permute-start.16 = (bf16[2,192,128]{2,1,0:T(8,128)(2,1)S(1)}, bf16[2,192,128]{2,1,0:T(8,128)(2,1)S(1)}, u32[]{:S(2)}, u32[]{:S(2)}) collective-permute-start(bf16[2,192,128]{2,1,0:T(8,128)(2,1)S(1)} %get-tuple-element.27.rest_0_), channel_id=1, source_target_pairs={{0,24},{8,16},{16,8},{24,0},{1,25},{9,17},{17,9},{25,1},{2,26},{10... | collective-permute-start | bytes 294920 | tf_op jit(solution)/shard_map/ppermute | solution.py:536
  137.7 4.0 %select.5.rest_5_ = bf16[768,2816]{1,0:T(8,128)(2,1)S(1)} custom-call(s32[4]{0:T(128)S(1)} %pad_add_fusion.place, bf16[128,2816]{1,0:T(8,128)(2,1)S(1)} %collective-permute-done.17.rest_0_, bf16[128,2816]{1,0:T(8,128)(2,1)S(1)} %collective-permute-done.18.rest_1_, bf16[128,2816]{1,0:T(8,128)(2,1)S(1)} %collective-permute-done.19.rest_2_, ...), custom_call_target="tpu_custom_call" | custom-call | flops 2214592512 | bytes 6488064 | tf_op jit(solution)/shard_map/select/pallas_call | solution.py:276
  142.0 2.5 %blend.1 = (bf16[48,2944]{1,0:T(8,128)(2,1)S(1)}, bf16[48,2944]{1,0:T(8,128)(2,1)S(1)}, bf16[48,2944]{1,0:T(8,128)(2,1)S(1)}, bf16[48,2944]{1,0:T(8,128)(2,1)S(1)}) custom-call(s32[4]{0:T(128)S(1)} %pad_add_fusion.place, bf16[2,192,128]{2,1,0:T(8,128)(2,1)S(1)} %get-tuple-element.27.rest_0_, bf16[2,192,128]{2,1,0:T(8,128)(2,1)S(1)} %collective-permute-done.14.rest_1_, ...), custom_call_target="tpu_custom_call" | custom-call | flops 1107296256 | bytes 6848512 | tf_op jit(solution)/shard_map/blend/pallas_call | solution.py:446
  148.1 5.9 %collective-permute-done.28.refs_3_ = bf16[4,48,1280]{2,1,0:T(8,128)(2,1)S(1)} collective-permute-done((bf16[4,48,1280]{2,1,0:T(8,128)(2,1)S(1)}, bf16[4,48,1280]{2,1,0:T(8,128)(2,1)S(1)}, u32[]{:S(2)}, u32[]{:S(2)}) %collective-permute-start.28) | collective-permute-done | bytes 491552 | tf_op jit(solution)/shard_map/ppermute | solution.py:536
  154.4 4.1 %collective-permute-start.30 = (bf16[48,1280]{1,0:T(8,128)(2,1)S(1)}, bf16[48,1280]{1,0:T(8,128)(2,1)S(1)}, u32[]{:S(2)}, u32[]{:S(2)}) collective-permute-start(bf16[48,1280]{1,0:T(8,128)(2,1)S(1)} %get-tuple-element.41), channel_id=1, source_target_pairs={{0,16},{8,24},{16,0},{24,8},{1,17},{9,25},{17,1},{25,9},{2,18},{10... | collective-permute-start | bytes 368648 | tf_op jit(solution)/shard_map/ppermute | solution.py:536
  159.2 4.9 %collective-permute-start.31 = (bf16[48,1280]{1,0:T(8,128)(2,1)S(1)}, bf16[48,1280]{1,0:T(8,128)(2,1)S(1)}, u32[]{:S(2)}, u32[]{:S(2)}) collective-permute-start(bf16[48,1280]{1,0:T(8,128)(2,1)S(1)} %get-tuple-element.42), channel_id=1, source_target_pairs={{0,24},{8,16},{16,8},{24,0},{1,25},{9,17},{17,9},{25,1},{2,26},{10... | collective-permute-start | bytes 368648 | tf_op jit(solution)/shard_map/ppermute | solution.py:536
  164.1 2.9 %collective-permute-done.31.rest_7_ = bf16[48,1280]{1,0:T(8,128)(2,1)S(1)} collective-permute-done((bf16[48,1280]{1,0:T(8,128)(2,1)S(1)}, bf16[48,1280]{1,0:T(8,128)(2,1)S(1)}, u32[]{:S(2)}, u32[]{:S(2)}) %collective-permute-start.31) | collective-permute-done | bytes 122912 | tf_op jit(solution)/shard_map/ppermute | solution.py:536
  167.0 2.3 %finish.1 = f32[48,4096]{1,0:T(8,128)} custom-call(s32[4]{0:T(128)S(1)} %pad_add_fusion.place, bf16[48,2944]{1,0:T(8,128)(2,1)S(1)} %get-tuple-element.31.rest_0_, bf16[48,2944]{1,0:T(8,128)(2,1)S(1)} %collective-permute-done.23.rest_1_, bf16[48,2944]{1,0:T(8,128)(2,1)S(1)} %collective-permute-done.24.rest_2_, ...), custom_call_target="tpu_custom_call" | custom-call | bytes 1572864 | tf_op jit(solution)/shard_map/finish/pallas_call | solution.py:516
  (71 shorter events, 32.8 us)
Async XLA Ops:
  3.0 31.6 %collective-permute-start = (bf16[64,16384]{1,0:T(8,128)(2,1)S(1)}, bf16[64,16384]{1,0:T(8,128)(2,1)S(1)}, u32[]{:S(2)}, u32[]{:S(2)}) collective-permute-start(bf16[64,16384]{1,0:T(8,128)(2,1)S(1)} %get-tuple-element.24), channel_id=1, source_target_pairs={{0,4},{4,0},{1,5},{5,1},{2,6},{6,2},{3,7},{7,3},{8,12},{12,8},{9,1... | collective-permute-start | bytes 6291464 | tf_op jit(solution)/shard_map/ppermute | solution.py:563
  3.6 28.3 %collective-permute-start.5 = (bf16[48,8192]{1,0:T(8,128)(2,1)S(1)}, bf16[48,8192]{1,0:T(8,128)(2,1)S(1)}, u32[]{:S(2)}, u32[]{:S(2)}) collective-permute-start(bf16[48,8192]{1,0:T(8,128)(2,1)S(1)} %get-tuple-element.25.rest_0_), channel_id=1, source_target_pairs={{0,1},{1,0},{2,3},{3,2},{4,5},{5,4},{6,7},{7,6},{8,9},{9,8},{10,11... | collective-permute-start | bytes 2359304 | tf_op jit(solution)/shard_map/ppermute | solution.py:566
  6.1 25.8 %collective-permute-start.8 = (bf16[48,8192]{1,0:T(8,128)(2,1)S(1)}, bf16[48,8192]{1,0:T(8,128)(2,1)S(1)}, u32[]{:S(2)}, u32[]{:S(2)}) collective-permute-start(bf16[48,8192]{1,0:T(8,128)(2,1)S(1)} %get-tuple-element.26.rest_1_), channel_id=1, source_target_pairs={{0,2},{1,3},{2,0},{3,1},{4,6},{5,7},{6,4},{7,5},{8,10},{9,11},{10,... | collective-permute-start | bytes 2359304 | tf_op jit(solution)/shard_map/ppermute | solution.py:567
  11.3 13.1 %collective-permute-start.1 = (f32[16,128]{1,0:T(8,128)S(1)}, f32[16,128]{1,0:T(8,128)S(1)}, u32[]{:S(2)}, u32[]{:S(2)}) collective-permute-start(f32[16,128]{1,0:T(8,128)S(1)} %brief.1.rest_0_), channel_id=1, source_target_pairs={{0,1},{1,0},{2,3},{3,2},{4,5},{5,4},{6,7},{7,6},{8,9},{9,8},{10,11... | collective-permute-start | bytes 24584 | tf_op jit(solution)/shard_map/ppermute | solution.py:536
  11.9 15.2 %collective-permute-start.2 = (f32[16,128]{1,0:T(8,128)S(1)}, f32[16,128]{1,0:T(8,128)S(1)}, u32[]{:S(2)}, u32[]{:S(2)}) collective-permute-start(f32[16,128]{1,0:T(8,128)S(1)} %brief.1.rest_0_), channel_id=1, source_target_pairs={{0,2},{1,3},{2,0},{3,1},{4,6},{5,7},{6,4},{7,5},{8,10},{9,11},{10,... | collective-permute-start | bytes 24584 | tf_op jit(solution)/shard_map/ppermute | solution.py:536
  27.2 20.4 %collective-permute-start.6 = (bf16[48,8192]{1,0:T(8,128)(2,1)S(1)}, bf16[48,8192]{1,0:T(8,128)(2,1)S(1)}, u32[]{:S(2)}, u32[]{:S(2)}) collective-permute-start(bf16[48,8192]{1,0:T(8,128)(2,1)S(1)} %get-tuple-element.26.rest_1_), channel_id=1, source_target_pairs={{0,1},{1,0},{2,3},{3,2},{4,5},{5,4},{6,7},{7,6},{8,9},{9,8},{10,11... | collective-permute-start | bytes 2359304 | tf_op jit(solution)/shard_map/ppermute | solution.py:568
  29.0 20.4 %collective-permute-start.7 = (bf16[48,8192]{1,0:T(8,128)(2,1)S(1)}, bf16[48,8192]{1,0:T(8,128)(2,1)S(1)}, u32[]{:S(2)}, u32[]{:S(2)}) collective-permute-start(bf16[48,8192]{1,0:T(8,128)(2,1)S(1)} %get-tuple-element.25.rest_0_), channel_id=1, source_target_pairs={{0,2},{1,3},{2,0},{3,1},{4,6},{5,7},{6,4},{7,5},{8,10},{9,11},{10,... | collective-permute-start | bytes 2359304 | tf_op jit(solution)/shard_map/ppermute | solution.py:569
  32.0 29.9 %collective-permute-start.11 = (bf16[48,6144]{1,0:T(8,128)(2,1)S(1)}, bf16[48,6144]{1,0:T(8,128)(2,1)S(1)}, u32[]{:S(2)}, u32[]{:S(2)}) collective-permute-start(bf16[48,6144]{1,0:T(8,128)(2,1)S(1)} %slice.18), channel_id=1, source_target_pairs={{0,2},{1,3},{2,0},{3,1},{4,6},{5,7},{6,4},{7,5},{8,10},{9,11},{10,... | collective-permute-start | bytes 1769480 | tf_op jit(solution)/shard_map/ppermute | solution.py:570
  33.1 31.4 %collective-permute-start.12 = (bf16[48,6144]{1,0:T(8,128)(2,1)S(1)}, bf16[48,6144]{1,0:T(8,128)(2,1)S(1)}, u32[]{:S(2)}, u32[]{:S(2)}) collective-permute-start(bf16[48,6144]{1,0:T(8,128)(2,1)S(1)} %slice.19), channel_id=1, source_target_pairs={{0,1},{1,0},{2,3},{3,2},{4,5},{5,4},{6,7},{7,6},{8,9},{9,8},{10,11... | collective-permute-start | bytes 1769480 | tf_op jit(solution)/shard_map/ppermute | solution.py:571
  34.6 40.2 %collective-permute-start.10 = (bf16[48,2048]{1,0:T(8,128)(2,1)S(1)}, bf16[48,2048]{1,0:T(8,128)(2,1)S(1)}, u32[]{:S(2)}, u32[]{:S(2)}) collective-permute-start(bf16[48,2048]{1,0:T(8,128)(2,1)S(1)} %slice.17), channel_id=1, source_target_pairs={{0,1},{1,0},{2,3},{3,2},{4,5},{5,4},{6,7},{7,6},{8,9},{9,8},{10,11... | collective-permute-start | bytes 589832 | tf_op jit(solution)/shard_map/ppermute | solution.py:573
  47.6 27.3 %collective-permute-start.9 = (bf16[48,2048]{1,0:T(8,128)(2,1)S(1)}, bf16[48,2048]{1,0:T(8,128)(2,1)S(1)}, u32[]{:S(2)}, u32[]{:S(2)}) collective-permute-start(bf16[48,2048]{1,0:T(8,128)(2,1)S(1)} %slice.16), channel_id=1, source_target_pairs={{0,2},{1,3},{2,0},{3,1},{4,6},{5,7},{6,4},{7,5},{8,10},{9,11},{10,... | collective-permute-start | bytes 589832 | tf_op jit(solution)/shard_map/ppermute | solution.py:572
  49.4 82.0 %collective-permute-start.17 = (bf16[128,2816]{1,0:T(8,128)(2,1)S(1)}, bf16[128,2816]{1,0:T(8,128)(2,1)S(1)}, u32[]{:S(2)}, u32[]{:S(2)}) collective-permute-start(bf16[128,2816]{1,0:T(8,128)(2,1)S(1)} %get-tuple-element.28), channel_id=1, source_target_pairs={{0,8},{8,0},{16,24},{24,16},{1,9},{9,1},{17,25},{25,17},{2,10},{10... | collective-permute-start | bytes 2162696 | tf_op jit(solution)/shard_map/ppermute | solution.py:583
  61.9 72.4 %collective-permute-start.18 = (bf16[128,2816]{1,0:T(8,128)(2,1)S(1)}, bf16[128,2816]{1,0:T(8,128)(2,1)S(1)}, u32[]{:S(2)}, u32[]{:S(2)}) collective-permute-start(bf16[128,2816]{1,0:T(8,128)(2,1)S(1)} %get-tuple-element.29), channel_id=1, source_target_pairs={{0,16},{8,24},{16,0},{24,8},{1,17},{9,25},{17,1},{25,9},{2,18},{10... | collective-permute-start | bytes 2162696 | tf_op jit(solution)/shard_map/ppermute | solution.py:583
  64.5 69.9 %collective-permute-start.19 = (bf16[128,2816]{1,0:T(8,128)(2,1)S(1)}, bf16[128,2816]{1,0:T(8,128)(2,1)S(1)}, u32[]{:S(2)}, u32[]{:S(2)}) collective-permute-start(bf16[128,2816]{1,0:T(8,128)(2,1)S(1)} %get-tuple-element.30), channel_id=1, source_target_pairs={{0,24},{8,16},{16,8},{24,0},{1,25},{9,17},{17,9},{25,1},{2,26},{10... | collective-permute-start | bytes 2162696 | tf_op jit(solution)/shard_map/ppermute | solution.py:583
  80.1 49.8 %collective-permute-start.14 = (bf16[2,192,128]{2,1,0:T(8,128)(2,1)S(1)}, bf16[2,192,128]{2,1,0:T(8,128)(2,1)S(1)}, u32[]{:S(2)}, u32[]{:S(2)}) collective-permute-start(bf16[2,192,128]{2,1,0:T(8,128)(2,1)S(1)} %get-tuple-element.27.rest_0_), channel_id=1, source_target_pairs={{0,8},{8,0},{16,24},{24,16},{1,9},{9,1},{17,25},{25,17},{2,10},{10... | collective-permute-start | bytes 294920 | tf_op jit(solution)/shard_map/ppermute | solution.py:536
  80.4 28.1 %collective-permute-start.20 = (f32[2,8,128]{2,1,0:T(8,128)S(1)}, f32[2,8,128]{2,1,0:T(8,128)S(1)}, u32[]{:S(2)}, u32[]{:S(2)}) collective-permute-start(f32[2,8,128]{2,1,0:T(8,128)S(1)} %pad_maximum_fusion.rest_2_.pair.rest_6_), channel_id=1, source_target_pairs={{0,8},{8,0},{16,24},{24,16},{1,9},{9,1},{17,25},{25,17},{2,10},{10... | collective-permute-start | bytes 24584 | tf_op jit(solution)/shard_map/ppermute | solution.py:536
  108.5 14.8 %collective-permute-start.21 = (f32[2,8,128]{2,1,0:T(8,128)S(1)}, f32[2,8,128]{2,1,0:T(8,128)S(1)}, u32[]{:S(2)}, u32[]{:S(2)}) collective-permute-start(f32[2,8,128]{2,1,0:T(8,128)S(1)} %pad_maximum_fusion.rest_2_.pair.rest_6_), channel_id=1, source_target_pairs={{0,16},{8,24},{16,0},{24,8},{1,17},{9,25},{17,1},{25,9},{2,18},{10... | collective-permute-start | bytes 24584 | tf_op jit(solution)/shard_map/ppermute | solution.py:536
  128.7 18.6 %collective-permute-start.26 = (bf16[4,48,1280]{2,1,0:T(8,128)(2,1)S(1)}, bf16[4,48,1280]{2,1,0:T(8,128)(2,1)S(1)}, u32[]{:S(2)}, u32[]{:S(2)}) collective-permute-start(bf16[4,48,1280]{2,1,0:T(8,128)(2,1)S(1)} %get-tuple-element.36), channel_id=1, source_target_pairs={{0,1},{1,0},{2,3},{3,2},{4,5},{5,4},{6,7},{7,6},{8,9},{9,8},{10,11... | collective-permute-start | bytes 1474568 | tf_op jit(solution)/shard_map/ppermute | solution.py:536
  129.9 18.2 %collective-permute-start.27 = (bf16[4,48,1280]{2,1,0:T(8,128)(2,1)S(1)}, bf16[4,48,1280]{2,1,0:T(8,128)(2,1)S(1)}, u32[]{:S(2)}, u32[]{:S(2)}) collective-permute-start(bf16[4,48,1280]{2,1,0:T(8,128)(2,1)S(1)} %get-tuple-element.37), channel_id=1, source_target_pairs={{0,2},{1,3},{2,0},{3,1},{4,6},{5,7},{6,4},{7,5},{8,10},{9,11},{10,... | collective-permute-start | bytes 1474568 | tf_op jit(solution)/shard_map/ppermute | solution.py:536
  131.4 22.6 %collective-permute-start.28 = (bf16[4,48,1280]{2,1,0:T(8,128)(2,1)S(1)}, bf16[4,48,1280]{2,1,0:T(8,128)(2,1)S(1)}, u32[]{:S(2)}, u32[]{:S(2)}) collective-permute-start(bf16[4,48,1280]{2,1,0:T(8,128)(2,1)S(1)} %get-tuple-element.38), channel_id=1, source_target_pairs={{0,3},{1,2},{2,1},{3,0},{4,7},{5,6},{6,5},{7,4},{8,11},{9,10},{10,... | collective-permute-start | bytes 1474568 | tf_op jit(solution)/shard_map/ppermute | solution.py:536
  144.6 22.4 %collective-permute-start.23 = (bf16[48,2944]{1,0:T(8,128)(2,1)S(1)}, bf16[48,2944]{1,0:T(8,128)(2,1)S(1)}, u32[]{:S(2)}, u32[]{:S(2)}) collective-permute-start(bf16[48,2944]{1,0:T(8,128)(2,1)S(1)} %get-tuple-element.32), channel_id=1, source_target_pairs={{0,1},{1,0},{2,3},{3,2},{4,5},{5,4},{6,7},{7,6},{8,9},{9,8},{10,11... | collective-permute-start | bytes 847880 | tf_op jit(solution)/shard_map/ppermute | solution.py:536
  145.8 21.2 %collective-permute-start.24 = (bf16[48,2944]{1,0:T(8,128)(2,1)S(1)}, bf16[48,2944]{1,0:T(8,128)(2,1)S(1)}, u32[]{:S(2)}, u32[]{:S(2)}) collective-permute-start(bf16[48,2944]{1,0:T(8,128)(2,1)S(1)} %get-tuple-element.33), channel_id=1, source_target_pairs={{0,2},{1,3},{2,0},{3,1},{4,6},{5,7},{6,4},{7,5},{8,10},{9,11},{10,... | collective-permute-start | bytes 847880 | tf_op jit(solution)/shard_map/ppermute | solution.py:536
  147.4 19.6 %collective-permute-start.25 = (bf16[48,2944]{1,0:T(8,128)(2,1)S(1)}, bf16[48,2944]{1,0:T(8,128)(2,1)S(1)}, u32[]{:S(2)}, u32[]{:S(2)}) collective-permute-start(bf16[48,2944]{1,0:T(8,128)(2,1)S(1)} %get-tuple-element.34), channel_id=1, source_target_pairs={{0,3},{1,2},{2,1},{3,0},{4,7},{5,6},{6,5},{7,4},{8,11},{9,10},{10,... | collective-permute-start | bytes 847880 | tf_op jit(solution)/shard_map/ppermute | solution.py:536
  154.4 9.8 %collective-permute-start.30 = (bf16[48,1280]{1,0:T(8,128)(2,1)S(1)}, bf16[48,1280]{1,0:T(8,128)(2,1)S(1)}, u32[]{:S(2)}, u32[]{:S(2)}) collective-permute-start(bf16[48,1280]{1,0:T(8,128)(2,1)S(1)} %get-tuple-element.41), channel_id=1, source_target_pairs={{0,16},{8,24},{16,0},{24,8},{1,17},{9,25},{17,1},{25,9},{2,18},{10... | collective-permute-start | bytes 368648 | tf_op jit(solution)/shard_map/ppermute | solution.py:536
  (14 other events, 113.3 us)

commit v11 on v10

--- a/solution.py
+++ b/solution.py
@@ -491,15 +491,18 @@
         mass = mass + part[:, keep : keep + 3 * masks].astype(F32)
     mass = mass[:, :masks] + mass[:, masks : 2 * masks] + mass[:, 2 * masks : 3 * masks]
     leaves = []
-    half = keep // 256 * 128
-    for i, (first, end) in enumerate(((0, half), (half, keep), (keep, span))):
+    third = keep // 384 * 128
+    edges = [keep, (keep + span) // 256 * 128, span]
+    ranges = [*zip(edges[:-1], edges[1:]), (0, third), (third, 2 * third), (2 * third, keep)]
+    for i, (first, end) in enumerate(ranges):
         below = jnp.ones((held.shape[0], end - first), F32)
         for w in range(masks):
             row = wedge[w : w + 1, pl.ds(pl.multiple_of(at + first, 128), end - first)]
             below = below + mass[:, w : w + 1] * row
         total = 0.0
-        for part in apart if i == 2 else shares:
-            total = total + (part[...] if i == 2 else part[:, first:end]).astype(F32)
+        for part in apart if first >= keep else shares:
+            shift = keep if first >= keep else 0
+            total = total + part[:, first - shift : end - shift].astype(F32)
         held[:, first:end] = total / below
         leave = pltpu.make_async_copy(
             held.at[:, pl.ds(first, end - first)], out.at[:, pl.ds(first, end - first)], went.at[i]
@@ -520,7 +523,7 @@
         out_shape=jax.ShapeDtypeStruct((per_ref, span), F32),
         scratch_shapes=[
             pltpu.VMEM((per_ref, span), F32),
-            pltpu.SemaphoreType.DMA((3,)),
+            pltpu.SemaphoreType.DMA((5,)),
         ],
         compiler_params=room(16),
         cost_estimate=cost(0, 8 * per_ref * span),

time: 170 us -> 170 us (level)
  no operation moved by 1% of the time
where the time goes in v11:
time: 170 us; the launch traced here: 169 us
  waiting for transfers between devices  89.2 us (52%)
  starting transfers between devices  46.5 us (27%)
  Pallas kernels  32.6 us (19%)
    ppermute x19, waiting for transfers between devices, passed(): lax.ppermute(values[p], axis, [(d, d ^ p) for d in range(size)])  65.3 us
    ppermute x19, starting transfers between devices, passed(): lax.ppermute(values[p], axis, [(d, d ^ p) for d in range(size)])  30.7 us
    pallas_call x3, Pallas kernels, select(): pl.pallas_call(functools.partial(select_kernel, len(blocks)), grid_spec=p...  12.2 us
    ppermute x1, waiting for transfers between devices, per_device(): low_xy = lax.ppermute(low_x[:, :most], 'blk', over_y)  10.6 us
    ppermute x1, waiting for transfers between devices, per_device(): high_x = lax.ppermute(high, 'blk', over_x)  10.4 us
    ppermute x3, starting transfers between devices, per_device(): lax.ppermute(far[p - 1], 'lay', [(z, z ^ p) for z in range(layers)])  5.8 us
    pallas_call x2, Pallas kernels, correl(): pl.pallas_call(functools.partial(correl_kernel, blocks, tile, first, step...  3.55 us
  transfers between devices with their start and end apart: 32, of which 14 were waited for; matrix products, arithmetic and copies ran while one was open for 0% of the time, Pallas kernels for 16%

profile of v11, /device:TPU:0, one launch (start us, length us, event | category | flops | bytes accessed | tf_op | source)
XLA Modules:
  0.0 169.4 jit_solution(8095857068497002628)
XLA Ops:
  0.1 2.9 %cut.1 = (bf16[48,8192]{1,0:T(8,128)(2,1)S(1)}, bf16[48,8192]{1,0:T(8,128)(2,1)S(1)}, bf16[64,16384]{1,0:T(8,128)(2,1)S(1)}) custom-call(s32[4]{0:T(128)S(1)} %pad_add_fusion.place, bf16[48,32768]{1,0:T(8,128)(2,1)} %refs.3, bf16[64,32768]{1,0:T(8,128)(2,1)} %slab.3), custom_call_target="tpu_custom_call" | custom-call | bytes 7340032 | tf_op jit(solution)/shard_map/cut/pallas_call | solution.py:79
  3.6 2.6 %collective-permute-start.5 = (bf16[48,8192]{1,0:T(8,128)(2,1)S(1)}, bf16[48,8192]{1,0:T(8,128)(2,1)S(1)}, u32[]{:S(2)}, u32[]{:S(2)}) collective-permute-start(bf16[48,8192]{1,0:T(8,128)(2,1)S(1)} %get-tuple-element.25.rest_0_), channel_id=1, source_target_pairs={{0,1},{1,0},{2,3},{3,2},{4,5},{5,4},{6,7},{7,6},{8,9},{9,8},{10,11... | collective-permute-start | bytes 2359304 | tf_op jit(solution)/shard_map/ppermute | solution.py:569
  8.4 3.0 %brief.1.rest_0_ = f32[16,128]{1,0:T(8,128)S(1)} custom-call(s32[1]{0:T(128)S(6)} %copy.8.live, bf16[48,32768]{1,0:T(8,128)(2,1)S(1)} %copy-done.1, f32[8,32768]{1,0:T(8,128)S(1)} %copy-done.2, s32[1,64]{1,0:T(1,128)S(1)} %bitcast.10, s32[1,64]{1,0:T(1,128)S(1)} %bitcast.11, s32[1,64]{1,0:T(1,128)S(1)} %bitcast.12), custom_call_target="tpu_custom_call" | custom-call | flops 150994944 | bytes 4194304 | tf_op jit(solution)/shard_map/brief/pallas_call | solution.py:164
  12.0 12.5 %collective-permute-done.1.rest_1_ = f32[16,128]{1,0:T(8,128)S(1)} collective-permute-done((f32[16,128]{1,0:T(8,128)S(1)}, f32[16,128]{1,0:T(8,128)S(1)}, u32[]{:S(2)}, u32[]{:S(2)}) %collective-permute-start.1) | collective-permute-done | bytes 8224 | tf_op jit(solution)/shard_map/ppermute | solution.py:539
  24.4 2.7 %collective-permute-start.3 = (f32[16,128]{1,0:T(8,128)S(1)}, f32[16,128]{1,0:T(8,128)S(1)}, u32[]{:S(2)}, u32[]{:S(2)}) collective-permute-start(f32[16,128]{1,0:T(8,128)S(1)} %brief.1.rest_0_), channel_id=1, source_target_pairs={{0,3},{1,2},{2,1},{3,0},{4,7},{5,6},{6,5},{7,4},{8,11},{9,10},{10,... | collective-permute-start | bytes 24584 | tf_op jit(solution)/shard_map/ppermute | solution.py:539
  37.1 10.4 %collective-permute-done.6.rest_3_ = bf16[48,8192]{1,0:T(8,128)(2,1)S(1)} collective-permute-done((bf16[48,8192]{1,0:T(8,128)(2,1)S(1)}, bf16[48,8192]{1,0:T(8,128)(2,1)S(1)}, u32[]{:S(2)}, u32[]{:S(2)}) %collective-permute-start.6) | collective-permute-done | bytes 786464 | tf_op jit(solution)/shard_map/ppermute | solution.py:571
  51.3 10.6 %collective-permute-done.11.rest_6_ = bf16[48,6144]{1,0:T(8,128)(2,1)S(1)} collective-permute-done((bf16[48,6144]{1,0:T(8,128)(2,1)S(1)}, bf16[48,6144]{1,0:T(8,128)(2,1)S(1)}, u32[]{:S(2)}, u32[]{:S(2)}) %collective-permute-start.11) | collective-permute-done | bytes 589856 | tf_op jit(solution)/shard_map/ppermute | solution.py:573
  61.9 2.6 %collective-permute-start.18 = (bf16[128,2816]{1,0:T(8,128)(2,1)S(1)}, bf16[128,2816]{1,0:T(8,128)(2,1)S(1)}, u32[]{:S(2)}, u32[]{:S(2)}) collective-permute-start(bf16[128,2816]{1,0:T(8,128)(2,1)S(1)} %get-tuple-element.29), channel_id=1, source_target_pairs={{0,16},{8,24},{16,0},{24,8},{1,17},{9,25},{17,1},{25,9},{2,18},{10... | collective-permute-start | bytes 2162696 | tf_op jit(solution)/shard_map/ppermute | solution.py:586
  65.8 6.2 %select.3.scaled = bf16[256,16384]{1,0:T(8,128)(2,1)S(1)} custom-call(s32[4]{0:T(128)S(1)} %pad_add_fusion.place, bf16[64,32768]{1,0:T(8,128)(2,1)S(1)} %copy-done, bf16[64,16384]{1,0:T(8,128)(2,1)S(1)} %collective-permute-done.rest_1_.mate, f32[2,8,128]{2,1,0:T(8,128)S(1)} %pad_maximum_fusion.rest_2_.pair.rest_6_, f32[8,32768]{1,0:T(8,128)S(1)} %copy-done.2), custom_call_target="tpu_custom_call" | custom-call | flops 4294967296 | bytes 12582912 | tf_op jit(solution)/shard_map/select/pallas_call | solution.py:276
  72.0 2.8 %correl.2.rest_8_ = f32[256,192]{1,0:T(8,128)S(1)} custom-call(bf16[256,16384]{1,0:T(8,128)(2,1)S(1)} %select.3.scaled, bf16[48,8192]{1,0:T(8,128)(2,1)S(1)} %get-tuple-element.25.rest_0_, bf16[48,8192]{1,0:T(8,128)(2,1)S(1)} %get-tuple-element.26.rest_1_, bf16[48,8192]{1,0:T(8,128)(2,1)S(1)} %collective-permute-done.5.rest_2_, ...), custom_call_target="tpu_custom_call" | custom-call | flops 1207959552 | bytes 11010048 | tf_op jit(solution)/shard_map/correl/pallas_call | solution.py:324
  77.2 2.9 %weigh.1 = (bf16[2,192,128]{2,1,0:T(8,128)(2,1)S(1)}, bf16[4,48,1280]{2,1,0:T(8,128)(2,1)S(1)}, bf16[4,48,1280]{2,1,0:T(8,128)(2,1)S(1)}, bf16[4,48,1280]{2,1,0:T(8,128)(2,1)S(1)}, bf16[4,48,1280]{2,1,0:T(8,128)(2,1)S(1)}) custom-call(s32[4]{0:T(128)S(1)} %pad_add_fusion.place, f32[256,192]{1,0:T(8,128)S(1)} %correl.3.own, ...), custom_call_target="tpu_custom_call" | custom-call | flops 503316480 | bytes 2097152 | tf_op jit(solution)/shard_map/weigh/pallas_call | solution.py:380
  82.2 26.3 %collective-permute-done.20.rest_3_.rest_7_ = f32[2,8,128]{2,1,0:T(8,128)S(1)} collective-permute-done((f32[2,8,128]{2,1,0:T(8,128)S(1)}, f32[2,8,128]{2,1,0:T(8,128)S(1)}, u32[]{:S(2)}, u32[]{:S(2)}) %collective-permute-start.20) | collective-permute-done | bytes 8224 | tf_op jit(solution)/shard_map/ppermute | solution.py:539
  108.5 2.5 %collective-permute-start.21 = (f32[2,8,128]{2,1,0:T(8,128)S(1)}, f32[2,8,128]{2,1,0:T(8,128)S(1)}, u32[]{:S(2)}, u32[]{:S(2)}) collective-permute-start(f32[2,8,128]{2,1,0:T(8,128)S(1)} %pad_maximum_fusion.rest_2_.pair.rest_6_), channel_id=1, source_target_pairs={{0,16},{8,24},{16,0},{24,8},{1,17},{9,25},{17,1},{25,9},{2,18},{10... | collective-permute-start | bytes 24584 | tf_op jit(solution)/shard_map/ppermute | solution.py:539
  111.0 12.3 %collective-permute-done.21.rest_4_.rest_8_ = f32[2,8,128]{2,1,0:T(8,128)S(1)} collective-permute-done((f32[2,8,128]{2,1,0:T(8,128)S(1)}, f32[2,8,128]{2,1,0:T(8,128)S(1)}, u32[]{:S(2)}, u32[]{:S(2)}) %collective-permute-start.21) | collective-permute-done | bytes 8224 | tf_op jit(solution)/shard_map/ppermute | solution.py:539
  123.3 3.3 %collective-permute-start.22 = (f32[2,8,128]{2,1,0:T(8,128)S(1)}, f32[2,8,128]{2,1,0:T(8,128)S(1)}, u32[]{:S(2)}, u32[]{:S(2)}) collective-permute-start(f32[2,8,128]{2,1,0:T(8,128)S(1)} %pad_maximum_fusion.rest_2_.pair.rest_6_), channel_id=1, source_target_pairs={{0,24},{8,16},{16,8},{24,0},{1,25},{9,17},{17,9},{25,1},{2,26},{10... | collective-permute-start | bytes 24584 | tf_op jit(solution)/shard_map/ppermute | solution.py:539
  126.6 2.2 %collective-permute-done.22.rest_5_.rest_9_ = f32[2,8,128]{2,1,0:T(8,128)S(1)} collective-permute-done((f32[2,8,128]{2,1,0:T(8,128)S(1)}, f32[2,8,128]{2,1,0:T(8,128)S(1)}, u32[]{:S(2)}, u32[]{:S(2)}) %collective-permute-start.22) | collective-permute-done | bytes 8224 | tf_op jit(solution)/shard_map/ppermute | solution.py:539
  134.4 3.3 %collective-permute-start.16 = (bf16[2,192,128]{2,1,0:T(8,128)(2,1)S(1)}, bf16[2,192,128]{2,1,0:T(8,128)(2,1)S(1)}, u32[]{:S(2)}, u32[]{:S(2)}) collective-permute-start(bf16[2,192,128]{2,1,0:T(8,128)(2,1)S(1)} %get-tuple-element.27.rest_0_), channel_id=1, source_target_pairs={{0,24},{8,16},{16,8},{24,0},{1,25},{9,17},{17,9},{25,1},{2,26},{10... | collective-permute-start | bytes 294920 | tf_op jit(solution)/shard_map/ppermute | solution.py:539
  137.7 4.0 %select.5.rest_5_ = bf16[768,2816]{1,0:T(8,128)(2,1)S(1)} custom-call(s32[4]{0:T(128)S(1)} %pad_add_fusion.place, bf16[128,2816]{1,0:T(8,128)(2,1)S(1)} %collective-permute-done.17.rest_0_, bf16[128,2816]{1,0:T(8,128)(2,1)S(1)} %collective-permute-done.18.rest_1_, bf16[128,2816]{1,0:T(8,128)(2,1)S(1)} %collective-permute-done.19.rest_2_, ...), custom_call_target="tpu_custom_call" | custom-call | flops 2214592512 | bytes 6488064 | tf_op jit(solution)/shard_map/select/pallas_call | solution.py:276
  142.0 2.5 %blend.1 = (bf16[48,2944]{1,0:T(8,128)(2,1)S(1)}, bf16[48,2944]{1,0:T(8,128)(2,1)S(1)}, bf16[48,2944]{1,0:T(8,128)(2,1)S(1)}, bf16[48,2944]{1,0:T(8,128)(2,1)S(1)}) custom-call(s32[4]{0:T(128)S(1)} %pad_add_fusion.place, bf16[2,192,128]{2,1,0:T(8,128)(2,1)S(1)} %get-tuple-element.27.rest_0_, bf16[2,192,128]{2,1,0:T(8,128)(2,1)S(1)} %collective-permute-done.14.rest_1_, ...), custom_call_target="tpu_custom_call" | custom-call | flops 1107296256 | bytes 6848512 | tf_op jit(solution)/shard_map/blend/pallas_call | solution.py:446
  148.1 5.9 %collective-permute-done.28.refs_3_ = bf16[4,48,1280]{2,1,0:T(8,128)(2,1)S(1)} collective-permute-done((bf16[4,48,1280]{2,1,0:T(8,128)(2,1)S(1)}, bf16[4,48,1280]{2,1,0:T(8,128)(2,1)S(1)}, u32[]{:S(2)}, u32[]{:S(2)}) %collective-permute-start.28) | collective-permute-done | bytes 491552 | tf_op jit(solution)/shard_map/ppermute | solution.py:539
  154.4 4.1 %collective-permute-start.30 = (bf16[48,1280]{1,0:T(8,128)(2,1)S(1)}, bf16[48,1280]{1,0:T(8,128)(2,1)S(1)}, u32[]{:S(2)}, u32[]{:S(2)}) collective-permute-start(bf16[48,1280]{1,0:T(8,128)(2,1)S(1)} %get-tuple-element.41), channel_id=1, source_target_pairs={{0,16},{8,24},{16,0},{24,8},{1,17},{9,25},{17,1},{25,9},{2,18},{10... | collective-permute-start | bytes 368648 | tf_op jit(solution)/shard_map/ppermute | solution.py:539
  159.2 4.9 %collective-permute-start.31 = (bf16[48,1280]{1,0:T(8,128)(2,1)S(1)}, bf16[48,1280]{1,0:T(8,128)(2,1)S(1)}, u32[]{:S(2)}, u32[]{:S(2)}) collective-permute-start(bf16[48,1280]{1,0:T(8,128)(2,1)S(1)} %get-tuple-element.42), channel_id=1, source_target_pairs={{0,24},{8,16},{16,8},{24,0},{1,25},{9,17},{17,9},{25,1},{2,26},{10... | collective-permute-start | bytes 368648 | tf_op jit(solution)/shard_map/ppermute | solution.py:539
  164.1 2.9 %collective-permute-done.31.rest_7_ = bf16[48,1280]{1,0:T(8,128)(2,1)S(1)} collective-permute-done((bf16[48,1280]{1,0:T(8,128)(2,1)S(1)}, bf16[48,1280]{1,0:T(8,128)(2,1)S(1)}, u32[]{:S(2)}, u32[]{:S(2)}) %collective-permute-start.31) | collective-permute-done | bytes 122912 | tf_op jit(solution)/shard_map/ppermute | solution.py:539
  167.0 2.3 %finish.1 = f32[48,4096]{1,0:T(8,128)} custom-call(s32[4]{0:T(128)S(1)} %pad_add_fusion.place, bf16[48,2944]{1,0:T(8,128)(2,1)S(1)} %get-tuple-element.31.rest_0_, bf16[48,2944]{1,0:T(8,128)(2,1)S(1)} %collective-permute-done.23.rest_1_, bf16[48,2944]{1,0:T(8,128)(2,1)S(1)} %collective-permute-done.24.rest_2_, ...), custom_call_target="tpu_custom_call" | custom-call | bytes 1572864 | tf_op jit(solution)/shard_map/finish/pallas_call | solution.py:519
  (71 shorter events, 32.8 us)
Async XLA Ops:
  3.0 31.6 %collective-permute-start = (bf16[64,16384]{1,0:T(8,128)(2,1)S(1)}, bf16[64,16384]{1,0:T(8,128)(2,1)S(1)}, u32[]{:S(2)}, u32[]{:S(2)}) collective-permute-start(bf16[64,16384]{1,0:T(8,128)(2,1)S(1)} %get-tuple-element.24), channel_id=1, source_target_pairs={{0,4},{4,0},{1,5},{5,1},{2,6},{6,2},{3,7},{7,3},{8,12},{12,8},{9,1... | collective-permute-start | bytes 6291464 | tf_op jit(solution)/shard_map/ppermute | solution.py:566
  3.6 28.3 %collective-permute-start.5 = (bf16[48,8192]{1,0:T(8,128)(2,1)S(1)}, bf16[48,8192]{1,0:T(8,128)(2,1)S(1)}, u32[]{:S(2)}, u32[]{:S(2)}) collective-permute-start(bf16[48,8192]{1,0:T(8,128)(2,1)S(1)} %get-tuple-element.25.rest_0_), channel_id=1, source_target_pairs={{0,1},{1,0},{2,3},{3,2},{4,5},{5,4},{6,7},{7,6},{8,9},{9,8},{10,11... | collective-permute-start | bytes 2359304 | tf_op jit(solution)/shard_map/ppermute | solution.py:569
  6.1 25.8 %collective-permute-start.8 = (bf16[48,8192]{1,0:T(8,128)(2,1)S(1)}, bf16[48,8192]{1,0:T(8,128)(2,1)S(1)}, u32[]{:S(2)}, u32[]{:S(2)}) collective-permute-start(bf16[48,8192]{1,0:T(8,128)(2,1)S(1)} %get-tuple-element.26.rest_1_), channel_id=1, source_target_pairs={{0,2},{1,3},{2,0},{3,1},{4,6},{5,7},{6,4},{7,5},{8,10},{9,11},{10,... | collective-permute-start | bytes 2359304 | tf_op jit(solution)/shard_map/ppermute | solution.py:570
  11.3 13.1 %collective-permute-start.1 = (f32[16,128]{1,0:T(8,128)S(1)}, f32[16,128]{1,0:T(8,128)S(1)}, u32[]{:S(2)}, u32[]{:S(2)}) collective-permute-start(f32[16,128]{1,0:T(8,128)S(1)} %brief.1.rest_0_), channel_id=1, source_target_pairs={{0,1},{1,0},{2,3},{3,2},{4,5},{5,4},{6,7},{7,6},{8,9},{9,8},{10,11... | collective-permute-start | bytes 24584 | tf_op jit(solution)/shard_map/ppermute | solution.py:539
  11.9 15.2 %collective-permute-start.2 = (f32[16,128]{1,0:T(8,128)S(1)}, f32[16,128]{1,0:T(8,128)S(1)}, u32[]{:S(2)}, u32[]{:S(2)}) collective-permute-start(f32[16,128]{1,0:T(8,128)S(1)} %brief.1.rest_0_), channel_id=1, source_target_pairs={{0,2},{1,3},{2,0},{3,1},{4,6},{5,7},{6,4},{7,5},{8,10},{9,11},{10,... | collective-permute-start | bytes 24584 | tf_op jit(solution)/shard_map/ppermute | solution.py:539
  27.2 20.4 %collective-permute-start.6 = (bf16[48,8192]{1,0:T(8,128)(2,1)S(1)}, bf16[48,8192]{1,0:T(8,128)(2,1)S(1)}, u32[]{:S(2)}, u32[]{:S(2)}) collective-permute-start(bf16[48,8192]{1,0:T(8,128)(2,1)S(1)} %get-tuple-element.26.rest_1_), channel_id=1, source_target_pairs={{0,1},{1,0},{2,3},{3,2},{4,5},{5,4},{6,7},{7,6},{8,9},{9,8},{10,11... | collective-permute-start | bytes 2359304 | tf_op jit(solution)/shard_map/ppermute | solution.py:571
  29.0 20.4 %collective-permute-start.7 = (bf16[48,8192]{1,0:T(8,128)(2,1)S(1)}, bf16[48,8192]{1,0:T(8,128)(2,1)S(1)}, u32[]{:S(2)}, u32[]{:S(2)}) collective-permute-start(bf16[48,8192]{1,0:T(8,128)(2,1)S(1)} %get-tuple-element.25.rest_0_), channel_id=1, source_target_pairs={{0,2},{1,3},{2,0},{3,1},{4,6},{5,7},{6,4},{7,5},{8,10},{9,11},{10,... | collective-permute-start | bytes 2359304 | tf_op jit(solution)/shard_map/ppermute | solution.py:572
  32.0 29.9 %collective-permute-start.11 = (bf16[48,6144]{1,0:T(8,128)(2,1)S(1)}, bf16[48,6144]{1,0:T(8,128)(2,1)S(1)}, u32[]{:S(2)}, u32[]{:S(2)}) collective-permute-start(bf16[48,6144]{1,0:T(8,128)(2,1)S(1)} %slice.18), channel_id=1, source_target_pairs={{0,2},{1,3},{2,0},{3,1},{4,6},{5,7},{6,4},{7,5},{8,10},{9,11},{10,... | collective-permute-start | bytes 1769480 | tf_op jit(solution)/shard_map/ppermute | solution.py:573
  33.1 31.4 %collective-permute-start.12 = (bf16[48,6144]{1,0:T(8,128)(2,1)S(1)}, bf16[48,6144]{1,0:T(8,128)(2,1)S(1)}, u32[]{:S(2)}, u32[]{:S(2)}) collective-permute-start(bf16[48,6144]{1,0:T(8,128)(2,1)S(1)} %slice.19), channel_id=1, source_target_pairs={{0,1},{1,0},{2,3},{3,2},{4,5},{5,4},{6,7},{7,6},{8,9},{9,8},{10,11... | collective-permute-start | bytes 1769480 | tf_op jit(solution)/shard_map/ppermute | solution.py:574
  34.6 40.2 %collective-permute-start.10 = (bf16[48,2048]{1,0:T(8,128)(2,1)S(1)}, bf16[48,2048]{1,0:T(8,128)(2,1)S(1)}, u32[]{:S(2)}, u32[]{:S(2)}) collective-permute-start(bf16[48,2048]{1,0:T(8,128)(2,1)S(1)} %slice.17), channel_id=1, source_target_pairs={{0,1},{1,0},{2,3},{3,2},{4,5},{5,4},{6,7},{7,6},{8,9},{9,8},{10,11... | collective-permute-start | bytes 589832 | tf_op jit(solution)/shard_map/ppermute | solution.py:576
  47.6 27.3 %collective-permute-start.9 = (bf16[48,2048]{1,0:T(8,128)(2,1)S(1)}, bf16[48,2048]{1,0:T(8,128)(2,1)S(1)}, u32[]{:S(2)}, u32[]{:S(2)}) collective-permute-start(bf16[48,2048]{1,0:T(8,128)(2,1)S(1)} %slice.16), channel_id=1, source_target_pairs={{0,2},{1,3},{2,0},{3,1},{4,6},{5,7},{6,4},{7,5},{8,10},{9,11},{10,... | collective-permute-start | bytes 589832 | tf_op jit(solution)/shard_map/ppermute | solution.py:575
  49.4 82.0 %collective-permute-start.17 = (bf16[128,2816]{1,0:T(8,128)(2,1)S(1)}, bf16[128,2816]{1,0:T(8,128)(2,1)S(1)}, u32[]{:S(2)}, u32[]{:S(2)}) collective-permute-start(bf16[128,2816]{1,0:T(8,128)(2,1)S(1)} %get-tuple-element.28), channel_id=1, source_target_pairs={{0,8},{8,0},{16,24},{24,16},{1,9},{9,1},{17,25},{25,17},{2,10},{10... | collective-permute-start | bytes 2162696 | tf_op jit(solution)/shard_map/ppermute | solution.py:586
  61.9 72.4 %collective-permute-start.18 = (bf16[128,2816]{1,0:T(8,128)(2,1)S(1)}, bf16[128,2816]{1,0:T(8,128)(2,1)S(1)}, u32[]{:S(2)}, u32[]{:S(2)}) collective-permute-start(bf16[128,2816]{1,0:T(8,128)(2,1)S(1)} %get-tuple-element.29), channel_id=1, source_target_pairs={{0,16},{8,24},{16,0},{24,8},{1,17},{9,25},{17,1},{25,9},{2,18},{10... | collective-permute-start | bytes 2162696 | tf_op jit(solution)/shard_map/ppermute | solution.py:586
  64.5 69.9 %collective-permute-start.19 = (bf16[128,2816]{1,0:T(8,128)(2,1)S(1)}, bf16[128,2816]{1,0:T(8,128)(2,1)S(1)}, u32[]{:S(2)}, u32[]{:S(2)}) collective-permute-start(bf16[128,2816]{1,0:T(8,128)(2,1)S(1)} %get-tuple-element.30), channel_id=1, source_target_pairs={{0,24},{8,16},{16,8},{24,0},{1,25},{9,17},{17,9},{25,1},{2,26},{10... | collective-permute-start | bytes 2162696 | tf_op jit(solution)/shard_map/ppermute | solution.py:586
  80.1 49.8 %collective-permute-start.14 = (bf16[2,192,128]{2,1,0:T(8,128)(2,1)S(1)}, bf16[2,192,128]{2,1,0:T(8,128)(2,1)S(1)}, u32[]{:S(2)}, u32[]{:S(2)}) collective-permute-start(bf16[2,192,128]{2,1,0:T(8,128)(2,1)S(1)} %get-tuple-element.27.rest_0_), channel_id=1, source_target_pairs={{0,8},{8,0},{16,24},{24,16},{1,9},{9,1},{17,25},{25,17},{2,10},{10... | collective-permute-start | bytes 294920 | tf_op jit(solution)/shard_map/ppermute | solution.py:539
  80.4 28.1 %collective-permute-start.20 = (f32[2,8,128]{2,1,0:T(8,128)S(1)}, f32[2,8,128]{2,1,0:T(8,128)S(1)}, u32[]{:S(2)}, u32[]{:S(2)}) collective-permute-start(f32[2,8,128]{2,1,0:T(8,128)S(1)} %pad_maximum_fusion.rest_2_.pair.rest_6_), channel_id=1, source_target_pairs={{0,8},{8,0},{16,24},{24,16},{1,9},{9,1},{17,25},{25,17},{2,10},{10... | collective-permute-start | bytes 24584 | tf_op jit(solution)/shard_map/ppermute | solution.py:539
  108.5 14.8 %collective-permute-start.21 = (f32[2,8,128]{2,1,0:T(8,128)S(1)}, f32[2,8,128]{2,1,0:T(8,128)S(1)}, u32[]{:S(2)}, u32[]{:S(2)}) collective-permute-start(f32[2,8,128]{2,1,0:T(8,128)S(1)} %pad_maximum_fusion.rest_2_.pair.rest_6_), channel_id=1, source_target_pairs={{0,16},{8,24},{16,0},{24,8},{1,17},{9,25},{17,1},{25,9},{2,18},{10... | collective-permute-start | bytes 24584 | tf_op jit(solution)/shard_map/ppermute | solution.py:539
  128.7 18.6 %collective-permute-start.26 = (bf16[4,48,1280]{2,1,0:T(8,128)(2,1)S(1)}, bf16[4,48,1280]{2,1,0:T(8,128)(2,1)S(1)}, u32[]{:S(2)}, u32[]{:S(2)}) collective-permute-start(bf16[4,48,1280]{2,1,0:T(8,128)(2,1)S(1)} %get-tuple-element.36), channel_id=1, source_target_pairs={{0,1},{1,0},{2,3},{3,2},{4,5},{5,4},{6,7},{7,6},{8,9},{9,8},{10,11... | collective-permute-start | bytes 1474568 | tf_op jit(solution)/shard_map/ppermute | solution.py:539
  129.9 18.2 %collective-permute-start.27 = (bf16[4,48,1280]{2,1,0:T(8,128)(2,1)S(1)}, bf16[4,48,1280]{2,1,0:T(8,128)(2,1)S(1)}, u32[]{:S(2)}, u32[]{:S(2)}) collective-permute-start(bf16[4,48,1280]{2,1,0:T(8,128)(2,1)S(1)} %get-tuple-element.37), channel_id=1, source_target_pairs={{0,2},{1,3},{2,0},{3,1},{4,6},{5,7},{6,4},{7,5},{8,10},{9,11},{10,... | collective-permute-start | bytes 1474568 | tf_op jit(solution)/shard_map/ppermute | solution.py:539
  131.4 22.6 %collective-permute-start.28 = (bf16[4,48,1280]{2,1,0:T(8,128)(2,1)S(1)}, bf16[4,48,1280]{2,1,0:T(8,128)(2,1)S(1)}, u32[]{:S(2)}, u32[]{:S(2)}) collective-permute-start(bf16[4,48,1280]{2,1,0:T(8,128)(2,1)S(1)} %get-tuple-element.38), channel_id=1, source_target_pairs={{0,3},{1,2},{2,1},{3,0},{4,7},{5,6},{6,5},{7,4},{8,11},{9,10},{10,... | collective-permute-start | bytes 1474568 | tf_op jit(solution)/shard_map/ppermute | solution.py:539
  144.6 22.4 %collective-permute-start.23 = (bf16[48,2944]{1,0:T(8,128)(2,1)S(1)}, bf16[48,2944]{1,0:T(8,128)(2,1)S(1)}, u32[]{:S(2)}, u32[]{:S(2)}) collective-permute-start(bf16[48,2944]{1,0:T(8,128)(2,1)S(1)} %get-tuple-element.32), channel_id=1, source_target_pairs={{0,1},{1,0},{2,3},{3,2},{4,5},{5,4},{6,7},{7,6},{8,9},{9,8},{10,11... | collective-permute-start | bytes 847880 | tf_op jit(solution)/shard_map/ppermute | solution.py:539
  145.8 21.2 %collective-permute-start.24 = (bf16[48,2944]{1,0:T(8,128)(2,1)S(1)}, bf16[48,2944]{1,0:T(8,128)(2,1)S(1)}, u32[]{:S(2)}, u32[]{:S(2)}) collective-permute-start(bf16[48,2944]{1,0:T(8,128)(2,1)S(1)} %get-tuple-element.33), channel_id=1, source_target_pairs={{0,2},{1,3},{2,0},{3,1},{4,6},{5,7},{6,4},{7,5},{8,10},{9,11},{10,... | collective-permute-start | bytes 847880 | tf_op jit(solution)/shard_map/ppermute | solution.py:539
  147.4 19.6 %collective-permute-start.25 = (bf16[48,2944]{1,0:T(8,128)(2,1)S(1)}, bf16[48,2944]{1,0:T(8,128)(2,1)S(1)}, u32[]{:S(2)}, u32[]{:S(2)}) collective-permute-start(bf16[48,2944]{1,0:T(8,128)(2,1)S(1)} %get-tuple-element.34), channel_id=1, source_target_pairs={{0,3},{1,2},{2,1},{3,0},{4,7},{5,6},{6,5},{7,4},{8,11},{9,10},{10,... | collective-permute-start | bytes 847880 | tf_op jit(solution)/shard_map/ppermute | solution.py:539
  154.4 9.8 %collective-permute-start.30 = (bf16[48,1280]{1,0:T(8,128)(2,1)S(1)}, bf16[48,1280]{1,0:T(8,128)(2,1)S(1)}, u32[]{:S(2)}, u32[]{:S(2)}) collective-permute-start(bf16[48,1280]{1,0:T(8,128)(2,1)S(1)} %get-tuple-element.41), channel_id=1, source_target_pairs={{0,16},{8,24},{16,0},{24,8},{1,17},{9,25},{17,1},{25,9},{2,18},{10... | collective-permute-start | bytes 368648 | tf_op jit(solution)/shard_map/ppermute | solution.py:539
  (14 other events, 113.3 us)
